TPU v7x, 512 devices: a whole 4x4x16 slice. The times are simulated.
512 devices in a mesh: ctx: 128 (over z_hi, y, x, core), head: 4 (over z_lo).
Axes of the slice: x: 4, y: 4, z: 16 (z_hi: 4, z_lo: 4; z = z_hi * 4 + z_lo), core: 2. Of those that a mesh axis runs over, the one named last changes fastest.
Arguments:
- queries: bfloat16 [32768, 2048], P(('ctx', 'head')), may hold values from -8.5 to 8.5
- keys: bfloat16 [32768, 1024], P(('ctx', 'head')), may hold values from -8.5 to 8.5
- values: bfloat16 [32768, 1024], P(('ctx', 'head')), may hold values from -5 to 5
- grad_attn: bfloat16 [32768, 2048], P(('ctx', 'head')), may hold values from -5 to 5
- parent_gap: int32 [128], replicated, may hold values from 0 to 2, as said below
Outputs:
- attended: bfloat16 [32768, 2048], P(('ctx', 'head'))
- grad_query: bfloat16 [32768, 2048], P(('ctx', 'head'))
- grad_key: bfloat16 [32768, 1024], P(('ctx', 'head'))
- grad_value: bfloat16 [32768, 1024], P(('ctx', 'head'))
Inputs may be any that keep to these rules, and one draw needn't show every extreme that they name: Shards are in depth-first order of a tree rooted at shard 0: the parent of shard s > 0 is shard s - parent_gap[s], and parent_gap[0] = 0. The ancestor 4 levels above a shard, where it exists, lies at most 8 shards before it.
All inputs are finite; a program needn't handle non-finite values.
Results may differ from a plain program's by a relative error of at most 0.011.
Values may be sent and summed in bfloat16 or wider, within the bound.
No kernel may reach another device: no remote copies, remote signals or barrier semaphores. Data moves between devices by JAX's collectives and lax.ppermute only.
A program may use at most 64 MiB of HBM per device.

v0:
```python
import math

import jax
import jax.numpy as jnp
from jax import lax
from jax.sharding import PartitionSpec as P

HD = 256
GROUP = 2
WINDOW = 1024
FORK = 2


BASE = 10000.0


def from_behind(block, axis, distance):
    devices = range(lax.axis_size(axis))
    route = [(i - distance, i) for i in devices if i - distance in devices]
    return lax.ppermute(block, axis, route)


def tree_tables(parent_gap):
    shard_count = parent_gap.shape[0]
    ordinal = jnp.arange(shard_count, dtype=jnp.int32)
    parent = jnp.where(parent_gap > 0, ordinal - parent_gap, shard_count)
    pointer = jnp.concatenate([parent, jnp.full((1,), shard_count, jnp.int32)])
    depths = jnp.concatenate([(parent_gap > 0).astype(jnp.int32), jnp.zeros((1,), jnp.int32)])
    jumped = pointer
    for rounds in range(shard_count.bit_length()):
        depths = depths + jnp.take(depths, jumped)
        jumped = jnp.take(jumped, jumped)
    return (pointer, depths)


def rotate(inputs, position, direction):
    half_dim = inputs.shape[-1] // 2
    frequency = jnp.exp(
        jnp.arange(half_dim, dtype=jnp.float32) * (-2.0 * math.log(BASE) / inputs.shape[-1])
    )
    angles = position.astype(jnp.float32)[:, None] * frequency[None, :]
    cosine = jnp.cos(angles)[:, None, :]
    sine_part = direction * jnp.sin(angles)[:, None, :]
    first_half = inputs[..., :half_dim]
    second = inputs[..., half_dim:]
    return jnp.concatenate(
        [first_half * cosine - second * sine_part, second * cosine + first_half * sine_part], -1
    )


def visible_mask(length, levels, present):
    within = jnp.arange(length, dtype=jnp.int32)
    later_key = within[None, :] > within[:, None]
    blocks_list = [jnp.logical_not(later_key)]
    for height in range(1, levels + 1):
        blocks_list.append(
            jnp.logical_and(present[height - 1], jnp.logical_or(height < levels, later_key))
        )
    return jnp.stack(blocks_list, 1).reshape(length, (levels + 1) * length)


def attend(query, key_all, value_all, grad_out, visible):
    scaling = query.shape[-1] ** (-0.5)
    scores = (
        jnp.einsum("tkgd,ukd->kgtu", query, key_all, preferred_element_type=jnp.float32) * scaling
    )
    scores = jnp.where(visible, scores, -1e30)
    highest = jnp.max(scores, -1, keepdims=True)
    raw_weights = jnp.where(visible, jnp.exp(scores - highest), 0.0)
    probabilities = raw_weights / jnp.sum(raw_weights, -1, keepdims=True)
    probs_low = probabilities.astype(jnp.bfloat16)
    attended = jnp.einsum(
        "kgtu,ukd->tkgd", probs_low, value_all, preferred_element_type=jnp.float32
    ).astype(jnp.bfloat16)
    grad_prob = jnp.einsum(
        "tkgd,ukd->kgtu", grad_out, value_all, preferred_element_type=jnp.float32
    )
    row_delta = jnp.sum(probabilities * grad_prob, -1, keepdims=True)
    grad_score = (probabilities * (grad_prob - row_delta) * scaling).astype(jnp.bfloat16)
    grad_qrot = jnp.einsum(
        "kgtu,ukd->tkgd", grad_score, key_all, preferred_element_type=jnp.float32
    )
    part_key = jnp.einsum("kgtu,tkgd->ukd", grad_score, query, preferred_element_type=jnp.float32)
    part_value = jnp.einsum(
        "kgtu,tkgd->ukd", probs_low, grad_out, preferred_element_type=jnp.float32
    )
    return (attended, grad_qrot, part_key, part_value)


def shards(queries, keys, values, grad_attn, parent_gap):
    query_in, key_in, value_in, grad_in = (
        lax.all_to_all(queries, "head", split_axis=1, concat_axis=0, tiled=True),
        lax.all_to_all(keys, "head", split_axis=1, concat_axis=0, tiled=True),
        lax.all_to_all(values, "head", split_axis=1, concat_axis=0, tiled=True),
        lax.all_to_all(grad_attn, "head", split_axis=1, concat_axis=0, tiled=True),
    )
    tokens = query_in.shape[0]
    kv_local = key_in.shape[1] // HD
    levels = WINDOW // tokens
    reach = levels * FORK
    shard_count = lax.axis_size("ctx")
    own_shard = lax.axis_index("ctx")
    pointer, depths = tree_tables(parent_gap)
    within = jnp.arange(tokens, dtype=jnp.int32)
    position = jnp.take(depths, own_shard) * tokens + within
    query_rot = rotate(
        query_in.astype(jnp.float32).reshape(tokens, kv_local * GROUP, HD), position, 1.0
    ).astype(jnp.bfloat16)
    query_rot = query_rot.reshape(tokens, kv_local, GROUP, HD)
    key_rot = rotate(
        key_in.astype(jnp.float32).reshape(tokens, kv_local, HD), position, 1.0
    ).astype(jnp.bfloat16)
    value_own = value_in.reshape(tokens, kv_local, HD)
    grad_out = grad_in.reshape(tokens, kv_local, GROUP, HD)
    elders = []
    current = jnp.take(pointer, own_shard)
    for height in range(levels):
        elders.append(current)
        current = jnp.take(pointer, current)
    elders = jnp.stack(elders)
    present = elders < shard_count
    slot_index = jnp.where(present, own_shard - elders, 0)
    chosen = jnp.concatenate([jnp.zeros((1,), jnp.int32), slot_index])
    sections = []
    stride = 1
    while stride <= reach:
        amount = min(stride, reach + 1 - stride)
        sections.append((stride, amount))
        stride = stride + amount
    key_list = [key_rot]
    value_list = [value_own]
    for offset in range(1, reach + 1):
        got_key, got_value = from_behind((key_rot, value_own), "ctx", offset)
        key_list.append(got_key)
        value_list.append(got_value)
    stack_key = jnp.stack(key_list)
    stack_value = jnp.stack(value_list)
    key_all = jnp.take(stack_key, chosen, axis=0).reshape((levels + 1) * tokens, kv_local, HD)
    value_all = jnp.take(stack_value, chosen, axis=0).reshape((levels + 1) * tokens, kv_local, HD)
    visible = visible_mask(tokens, levels, present)
    attended, grad_qrot, part_key, part_value = attend(
        query_rot, key_all, value_all, grad_out, visible
    )
    attended_out = lax.all_to_all(
        attended.reshape(tokens, kv_local * GROUP * HD),
        "head",
        split_axis=0,
        concat_axis=1,
        tiled=True,
    )
    empty = jnp.zeros((reach + 1, tokens, kv_local, HD), jnp.float32)
    return_key = empty.at[chosen].add(part_key.reshape(levels + 1, tokens, kv_local, HD))
    return_value = empty.at[chosen].add(part_value.reshape(levels + 1, tokens, kv_local, HD))
    total_key = return_key[0]
    total_value = return_value[0]
    for offset in range(1, reach + 1):
        got_key, got_value = from_behind((return_key[offset], return_value[offset]), "ctx", -offset)
        total_key = total_key + got_key
        total_value = total_value + got_value
    grad_query = rotate(grad_qrot.reshape(tokens, kv_local * GROUP, HD), position, -1.0).astype(
        jnp.bfloat16
    )
    grad_key = rotate(total_key, position, -1.0).astype(jnp.bfloat16)
    grad_value = total_value.astype(jnp.bfloat16)
    query_back, key_back, value_back = (
        lax.all_to_all(
            grad_query.reshape(tokens, kv_local * GROUP * HD),
            "head",
            split_axis=0,
            concat_axis=1,
            tiled=True,
        ),
        lax.all_to_all(
            grad_key.reshape(tokens, kv_local * HD), "head", split_axis=0, concat_axis=1, tiled=True
        ),
        lax.all_to_all(
            grad_value.reshape(tokens, kv_local * HD),
            "head",
            split_axis=0,
            concat_axis=1,
            tiled=True,
        ),
    )
    return (attended_out, query_back, key_back, value_back)


def solution(mesh):
    in_specs = (
        P(("ctx", "head"), None),
        P(("ctx", "head"), None),
        P(("ctx", "head"), None),
        P(("ctx", "head"), None),
        P(),
    )
    out_specs = (
        P(("ctx", "head"), None),
        P(("ctx", "head"), None),
        P(("ctx", "head"), None),
        P(("ctx", "head"), None),
    )
    return jax.shard_map(shards, mesh=mesh, in_specs=in_specs, out_specs=out_specs, check_vma=False)
```

profile of v0, /device:TPU:191, one launch (start us, length us, event | category | flops | bytes accessed | tf_op | source)
XLA Modules:
  0.0 647.4 jit_solution(11392795030194415651)
XLA Ops:
  2.2 5.4 all-to-all-start.1
  45.1 4.5 all-to-all-start
  51.8 7.5 %collective-permute-start.8 = (bf16[256,1,256]{2,0,1:T(8,128)(2,1)S(1)}, bf16[256,1,256]{2,0,1:T(8,128)(2,1)S(1)}, u32[]{:S(2)}, u32[]{:S(2)}) collective-permute-start(bf16[256,1,256]{2,0,1:T(8,128)(2,1)S(1)} %pad_maximum_fusion.4), channel_id=1, source_target_pairs={{0,4},{4,8},{8,12},{12,16},{16,20},{20,24},{24,28},{28,32},{32,36}... | collective-permute-start | bytes 393224 | tf_op jit(solution)/shard_map/ppermute | solution.py:20
  72.4 4.5 all-to-all-start.2
  77.0 4.1 collective-permute-start.13
  94.8 4.5 collective-permute-start.1
  99.3 18.0 %collective-permute-done.13 = bf16[256,1,256]{2,0,1:T(8,128)(2,1)S(1)} collective-permute-done((bf16[256,1,256]{2,0,1:T(8,128)(2,1)S(1)}, bf16[256,1,256]{2,0,1:T(8,128)(2,1)S(1)}, u32[]{:S(2)}, u32[]{:S(2)}) %collective-permute-start.13) | collective-permute-done | bytes 131104 | tf_op jit(solution)/shard_map/ppermute | solution.py:20
  124.7 6.3 collective-permute-start.4
  131.0 4.7 collective-permute-start.5
  138.2 5.1 collective-permute-start.7
  147.2 90.7 %collective-permute-done.6 = bf16[256,1,256]{2,0,1:T(8,128)(2,1)S(1)} collective-permute-done((bf16[256,1,256]{2,0,1:T(8,128)(2,1)S(1)}, bf16[256,1,256]{2,0,1:T(8,128)(2,1)S(1)}, u32[]{:S(2)}, u32[]{:S(2)}) %collective-permute-start.6) | collective-permute-done | bytes 131104 | tf_op jit(solution)/shard_map/ppermute | solution.py:20
  237.9 8.5 %all-to-all-start.4 = ((bf16[64,4,512]{2,0,1:T(8,128)(2,1)}), bf16[64,4,512]{2,0,1:T(8,128)(2,1)S(1)}, u32[]{:S(2)}, u32[]{:S(2)}) async-start(bf16[64,4,512]{2,0,1:T(8,128)(2,1)} %bitcast.245), calls=%async_computation.4 | async-start | bytes 524288 | tf_op jit(solution)/shard_map/all_to_all | solution.py:95
  280.3 21.7 %collective-permute-done.23 = f32[256,1,256]{2,0,1:T(8,128)} collective-permute-done((f32[256,1,256]{2,0,1:T(8,128)}, f32[256,1,256]{2,0,1:T(8,128)}, u32[]{:S(2)}, u32[]{:S(2)}) %collective-permute-start.23) | collective-permute-done | bytes 262176 | tf_op jit(solution)/shard_map/ppermute | solution.py:20
  302.1 12.8 %collective-permute-start.18 = (f32[256,1,256]{2,0,1:T(8,128)}, f32[256,1,256]{2,0,1:T(8,128)S(1)}, u32[]{:S(2)}, u32[]{:S(2)}) collective-permute-start(f32[256,1,256]{2,0,1:T(8,128)} %get-tuple-element.90), channel_id=1, source_target_pairs={{12,0},{16,4},{20,8},{24,12},{28,16},{32,20},{36,24},{40,28},{44,3... | collective-permute-start | bytes 786440 | tf_op jit(solution)/shard_map/ppermute | solution.py:20
  314.9 16.9 %collective-permute-start.17 = (f32[256,1,256]{2,0,1:T(8,128)}, f32[256,1,256]{2,0,1:T(8,128)S(1)}, u32[]{:S(2)}, u32[]{:S(2)}) collective-permute-start(f32[256,1,256]{2,0,1:T(8,128)} %get-tuple-element.91), channel_id=1, source_target_pairs={{8,0},{12,4},{16,8},{20,12},{24,16},{28,20},{32,24},{36,28},{40,32... | collective-permute-start | bytes 786440 | tf_op jit(solution)/shard_map/ppermute | solution.py:20
  331.8 23.8 %collective-permute-done.21 = f32[256,1,256]{2,0,1:T(8,128)} collective-permute-done((f32[256,1,256]{2,0,1:T(8,128)}, f32[256,1,256]{2,0,1:T(8,128)}, u32[]{:S(2)}, u32[]{:S(2)}) %collective-permute-start.21) | collective-permute-done | bytes 262176 | tf_op jit(solution)/shard_map/ppermute | solution.py:20
  365.8 67.2 %collective-permute-done.17 = f32[256,1,256]{2,0,1:T(8,128)S(1)} collective-permute-done((f32[256,1,256]{2,0,1:T(8,128)}, f32[256,1,256]{2,0,1:T(8,128)S(1)}, u32[]{:S(2)}, u32[]{:S(2)}) %collective-permute-start.17) | collective-permute-done | bytes 262176 | tf_op jit(solution)/shard_map/ppermute | solution.py:20
  445.7 10.9 %collective-permute-start.24 = (f32[256,1,256]{2,0,1:T(8,128)}, f32[256,1,256]{2,0,1:T(8,128)}, u32[]{:S(2)}, u32[]{:S(2)}) collective-permute-start(f32[256,1,256]{2,0,1:T(8,128)} %get-tuple-element.77), channel_id=1, source_target_pairs={{4,0},{8,4},{12,8},{16,12},{20,16},{24,20},{28,24},{32,28},{36,32}... | collective-permute-start | bytes 786440 | tf_op jit(solution)/shard_map/ppermute | solution.py:20
  457.9 82.5 %all-to-all-start.6 = ((bf16[4,64,256]{2,1,0:T(8,128)(2,1)}), bf16[4,64,256]{2,1,0:T(8,128)(2,1)}, u32[]{:S(2)}, u32[]{:S(2)}) async-start(bf16[4,64,256]{2,1,0:T(8,128)(2,1)} %pad_maximum_fusion.5), calls=%async_computation.6 | async-start | bytes 262144 | tf_op jit(solution)/shard_map/all_to_all | solution.py:173
  544.8 73.7 %all-to-all-start.7 = ((bf16[4,64,256]{2,1,0:T(8,128)(2,1)}), bf16[4,64,256]{2,1,0:T(8,128)(2,1)S(1)}, u32[]{:S(2)}, u32[]{:S(2)}) async-start(bf16[4,64,256]{2,1,0:T(8,128)(2,1)} %bitcast.267), calls=%async_computation.7 | async-start | bytes 262144 | tf_op jit(solution)/shard_map/all_to_all | solution.py:176
  622.9 4.1 all-to-all-start.3
  629.2 4.8 all-to-all-done.3
  633.9 5.1 all-to-all-start.5
  642.0 4.7 all-to-all-done.5
  (209 shorter events, 150.5 us)
Async XLA Ops:
  2.2 42.9 %all-to-all-start.1 = ((bf16[64,4,256]{2,0,1:T(8,128)(2,1)}), bf16[64,4,256]{2,0,1:T(8,128)(2,1)S(1)}, u32[]{:S(2)}, u32[]{:S(2)}) async-start(bf16[64,4,256]{2,0,1:T(8,128)(2,1)} %bitcast.247), calls=%async_computation.1 | async-start | bytes 262144 | tf_op jit(solution)/shard_map/all_to_all | solution.py:93
  72.4 165.5 %all-to-all-start.2 = ((bf16[64,4,512]{2,0,1:T(8,128)(2,1)}), bf16[64,4,512]{2,0,1:T(8,128)(2,1)S(1)}, u32[]{:S(2)}, u32[]{:S(2)}) async-start(bf16[64,4,512]{2,0,1:T(8,128)(2,1)} %bitcast.246), calls=%async_computation.2 | async-start | bytes 524288 | tf_op jit(solution)/shard_map/all_to_all | solution.py:92
  81.1 40.8 %collective-permute-start.14 = (bf16[256,1,256]{2,0,1:T(8,128)(2,1)S(1)}, bf16[256,1,256]{2,0,1:T(8,128)(2,1)S(1)}, u32[]{:S(2)}, u32[]{:S(2)}) collective-permute-start(bf16[256,1,256]{2,0,1:T(8,128)(2,1)S(1)} %pad_maximum_fusion.4), channel_id=1, source_target_pairs={{0,28},{4,32},{8,36},{12,40},{16,44},{20,48},{24,52},{28,56},{32,6... | collective-permute-start | bytes 393224 | tf_op jit(solution)/shard_map/ppermute | solution.py:20
  89.3 41.7 %collective-permute-start = (bf16[256,1,256]{2,0,1:T(8,128)(2,1)S(1)}, bf16[256,1,256]{2,0,1:T(8,128)(2,1)S(1)}, u32[]{:S(2)}, u32[]{:S(2)}) collective-permute-start(bf16[256,1,256]{2,0,1:T(8,128)(2,1)S(1)} %bitcast.271), channel_id=1, source_target_pairs={{0,4},{4,8},{8,12},{12,16},{16,20},{20,24},{24,28},{28,32},{32,36}... | collective-permute-start | bytes 393224 | tf_op jit(solution)/shard_map/ppermute | solution.py:20
  94.8 41.0 %collective-permute-start.1 = (bf16[256,1,256]{2,0,1:T(8,128)(2,1)S(1)}, bf16[256,1,256]{2,0,1:T(8,128)(2,1)S(1)}, u32[]{:S(2)}, u32[]{:S(2)}) collective-permute-start(bf16[256,1,256]{2,0,1:T(8,128)(2,1)S(1)} %bitcast.272), channel_id=1, source_target_pairs={{0,8},{4,12},{8,16},{12,20},{16,24},{20,28},{24,32},{28,36},{32,40... | collective-permute-start | bytes 393224 | tf_op jit(solution)/shard_map/ppermute | solution.py:20
  135.7 102.1 %collective-permute-start.6 = (bf16[256,1,256]{2,0,1:T(8,128)(2,1)S(1)}, bf16[256,1,256]{2,0,1:T(8,128)(2,1)S(1)}, u32[]{:S(2)}, u32[]{:S(2)}) collective-permute-start(bf16[256,1,256]{2,0,1:T(8,128)(2,1)S(1)} %bitcast.277), channel_id=1, source_target_pairs={{0,28},{4,32},{8,36},{12,40},{16,44},{20,48},{24,52},{28,56},{32,6... | collective-permute-start | bytes 393224 | tf_op jit(solution)/shard_map/ppermute | solution.py:20
  138.2 108.2 %collective-permute-start.7 = (bf16[256,1,256]{2,0,1:T(8,128)(2,1)S(1)}, bf16[256,1,256]{2,0,1:T(8,128)(2,1)S(1)}, u32[]{:S(2)}, u32[]{:S(2)}) collective-permute-start(bf16[256,1,256]{2,0,1:T(8,128)(2,1)S(1)} %bitcast.278), channel_id=1, source_target_pairs={{0,32},{4,36},{8,40},{12,44},{16,48},{20,52},{24,56},{28,60},{32,6... | collective-permute-start | bytes 393224 | tf_op jit(solution)/shard_map/ppermute | solution.py:20
  266.8 48.1 %collective-permute-start.22 = (f32[256,1,256]{2,0,1:T(8,128)}, f32[256,1,256]{2,0,1:T(8,128)}, u32[]{:S(2)}, u32[]{:S(2)}) collective-permute-start(f32[256,1,256]{2,0,1:T(8,128)} %get-tuple-element.86), channel_id=1, source_target_pairs={{28,0},{32,4},{36,8},{40,12},{44,16},{48,20},{52,24},{56,28},{60,3... | collective-permute-start | bytes 786440 | tf_op jit(solution)/shard_map/ppermute | solution.py:20
  268.7 86.8 %collective-permute-start.21 = (f32[256,1,256]{2,0,1:T(8,128)}, f32[256,1,256]{2,0,1:T(8,128)}, u32[]{:S(2)}, u32[]{:S(2)}) collective-permute-start(f32[256,1,256]{2,0,1:T(8,128)} %get-tuple-element.87), channel_id=1, source_target_pairs={{24,0},{28,4},{32,8},{36,12},{40,16},{44,20},{48,24},{52,28},{56,3... | collective-permute-start | bytes 786440 | tf_op jit(solution)/shard_map/ppermute | solution.py:20
  272.6 86.4 %collective-permute-start.20 = (f32[256,1,256]{2,0,1:T(8,128)}, f32[256,1,256]{2,0,1:T(8,128)}, u32[]{:S(2)}, u32[]{:S(2)}) collective-permute-start(f32[256,1,256]{2,0,1:T(8,128)} %get-tuple-element.88), channel_id=1, source_target_pairs={{20,0},{24,4},{28,8},{32,12},{36,16},{40,20},{44,24},{48,28},{52,3... | collective-permute-start | bytes 786440 | tf_op jit(solution)/shard_map/ppermute | solution.py:20
  274.5 86.4 %collective-permute-start.19 = (f32[256,1,256]{2,0,1:T(8,128)}, f32[256,1,256]{2,0,1:T(8,128)}, u32[]{:S(2)}, u32[]{:S(2)}) collective-permute-start(f32[256,1,256]{2,0,1:T(8,128)} %get-tuple-element.89), channel_id=1, source_target_pairs={{16,0},{20,4},{24,8},{28,12},{32,16},{36,20},{40,24},{44,28},{48,3... | collective-permute-start | bytes 786440 | tf_op jit(solution)/shard_map/ppermute | solution.py:20
  302.1 61.8 %collective-permute-start.18 = (f32[256,1,256]{2,0,1:T(8,128)}, f32[256,1,256]{2,0,1:T(8,128)S(1)}, u32[]{:S(2)}, u32[]{:S(2)}) collective-permute-start(f32[256,1,256]{2,0,1:T(8,128)} %get-tuple-element.90), channel_id=1, source_target_pairs={{12,0},{16,4},{20,8},{24,12},{28,16},{32,20},{36,24},{40,28},{44,3... | collective-permute-start | bytes 786440 | tf_op jit(solution)/shard_map/ppermute | solution.py:20
  314.9 118.1 %collective-permute-start.17 = (f32[256,1,256]{2,0,1:T(8,128)}, f32[256,1,256]{2,0,1:T(8,128)S(1)}, u32[]{:S(2)}, u32[]{:S(2)}) collective-permute-start(f32[256,1,256]{2,0,1:T(8,128)} %get-tuple-element.91), channel_id=1, source_target_pairs={{8,0},{12,4},{16,8},{20,12},{24,16},{28,20},{32,24},{36,28},{40,32... | collective-permute-start | bytes 786440 | tf_op jit(solution)/shard_map/ppermute | solution.py:20
  355.6 82.8 %collective-permute-start.16 = (f32[256,1,256]{2,0,1:T(8,128)}, f32[256,1,256]{2,0,1:T(8,128)S(1)}, u32[]{:S(2)}, u32[]{:S(2)}) collective-permute-start(f32[256,1,256]{2,0,1:T(8,128)} %get-tuple-element.85), channel_id=1, source_target_pairs={{4,0},{8,4},{12,8},{16,12},{20,16},{24,20},{28,24},{32,28},{36,32}... | collective-permute-start | bytes 786440 | tf_op jit(solution)/shard_map/ppermute | solution.py:20
  359.1 82.7 %collective-permute-start.31 = (f32[256,1,256]{2,0,1:T(8,128)S(1)}, f32[256,1,256]{2,0,1:T(8,128)S(1)}, u32[]{:S(2)}, u32[]{:S(2)}) collective-permute-start(f32[256,1,256]{2,0,1:T(8,128)S(1)} %get-tuple-element.84), channel_id=1, source_target_pairs={{32,0},{36,4},{40,8},{44,12},{48,16},{52,20},{56,24},{60,28},{64,3... | collective-permute-start | bytes 786440 | tf_op jit(solution)/shard_map/ppermute | solution.py:20
  361.0 82.8 %collective-permute-start.30 = (f32[256,1,256]{2,0,1:T(8,128)S(1)}, f32[256,1,256]{2,0,1:T(8,128)S(1)}, u32[]{:S(2)}, u32[]{:S(2)}) collective-permute-start(f32[256,1,256]{2,0,1:T(8,128)S(1)} %get-tuple-element.78), channel_id=1, source_target_pairs={{28,0},{32,4},{36,8},{40,12},{44,16},{48,20},{52,24},{56,28},{60,3... | collective-permute-start | bytes 786440 | tf_op jit(solution)/shard_map/ppermute | solution.py:20
  363.9 81.8 %collective-permute-start.29 = (f32[256,1,256]{2,0,1:T(8,128)S(1)}, f32[256,1,256]{2,0,1:T(8,128)S(1)}, u32[]{:S(2)}, u32[]{:S(2)}) collective-permute-start(f32[256,1,256]{2,0,1:T(8,128)S(1)} %get-tuple-element.79), channel_id=1, source_target_pairs={{24,0},{28,4},{32,8},{36,12},{40,16},{44,20},{48,24},{52,28},{56,3... | collective-permute-start | bytes 786440 | tf_op jit(solution)/shard_map/ppermute | solution.py:20
  433.0 107.4 %collective-permute-start.28 = (f32[256,1,256]{2,0,1:T(8,128)}, f32[256,1,256]{2,0,1:T(8,128)}, u32[]{:S(2)}, u32[]{:S(2)}) collective-permute-start(f32[256,1,256]{2,0,1:T(8,128)} %get-tuple-element.80), channel_id=1, source_target_pairs={{20,0},{24,4},{28,8},{32,12},{36,16},{40,20},{44,24},{48,28},{52,3... | collective-permute-start | bytes 786440 | tf_op jit(solution)/shard_map/ppermute | solution.py:20
  438.4 102.1 %collective-permute-start.27 = (f32[256,1,256]{2,0,1:T(8,128)}, f32[256,1,256]{2,0,1:T(8,128)}, u32[]{:S(2)}, u32[]{:S(2)}) collective-permute-start(f32[256,1,256]{2,0,1:T(8,128)} %get-tuple-element.81), channel_id=1, source_target_pairs={{16,0},{20,4},{24,8},{28,12},{32,16},{36,20},{40,24},{44,28},{48,3... | collective-permute-start | bytes 786440 | tf_op jit(solution)/shard_map/ppermute | solution.py:20
  441.8 98.6 %collective-permute-start.26 = (f32[256,1,256]{2,0,1:T(8,128)}, f32[256,1,256]{2,0,1:T(8,128)}, u32[]{:S(2)}, u32[]{:S(2)}) collective-permute-start(f32[256,1,256]{2,0,1:T(8,128)} %get-tuple-element.82), channel_id=1, source_target_pairs={{12,0},{16,4},{20,8},{24,12},{28,16},{32,20},{36,24},{40,28},{44,3... | collective-permute-start | bytes 786440 | tf_op jit(solution)/shard_map/ppermute | solution.py:20
  443.8 96.7 %collective-permute-start.25 = (f32[256,1,256]{2,0,1:T(8,128)}, f32[256,1,256]{2,0,1:T(8,128)}, u32[]{:S(2)}, u32[]{:S(2)}) collective-permute-start(f32[256,1,256]{2,0,1:T(8,128)} %get-tuple-element.83), channel_id=1, source_target_pairs={{8,0},{12,4},{16,8},{20,12},{24,16},{28,20},{32,24},{36,28},{40,32... | collective-permute-start | bytes 786440 | tf_op jit(solution)/shard_map/ppermute | solution.py:20
  445.7 94.8 %collective-permute-start.24 = (f32[256,1,256]{2,0,1:T(8,128)}, f32[256,1,256]{2,0,1:T(8,128)}, u32[]{:S(2)}, u32[]{:S(2)}) collective-permute-start(f32[256,1,256]{2,0,1:T(8,128)} %get-tuple-element.77), channel_id=1, source_target_pairs={{4,0},{8,4},{12,8},{16,12},{20,16},{24,20},{28,24},{32,28},{36,32}... | collective-permute-start | bytes 786440 | tf_op jit(solution)/shard_map/ppermute | solution.py:20
  457.9 86.9 %all-to-all-start.6 = ((bf16[4,64,256]{2,1,0:T(8,128)(2,1)}), bf16[4,64,256]{2,1,0:T(8,128)(2,1)}, u32[]{:S(2)}, u32[]{:S(2)}) async-start(bf16[4,64,256]{2,1,0:T(8,128)(2,1)} %pad_maximum_fusion.5), calls=%async_computation.6 | async-start | bytes 262144 | tf_op jit(solution)/shard_map/all_to_all | solution.py:173
  544.8 78.0 %all-to-all-start.7 = ((bf16[4,64,256]{2,1,0:T(8,128)(2,1)}), bf16[4,64,256]{2,1,0:T(8,128)(2,1)S(1)}, u32[]{:S(2)}, u32[]{:S(2)}) async-start(bf16[4,64,256]{2,1,0:T(8,128)(2,1)} %bitcast.267), calls=%async_computation.7 | async-start | bytes 262144 | tf_op jit(solution)/shard_map/all_to_all | solution.py:176
  (34 other events, 594.9 us)
where the time goes:
time: 651 us; the launch traced here: 647 us
  starting transfers between devices  317 us (49%)
  waiting for transfers between devices  248 us (38%)
  local copies, waits for them, and re-layouts  52.1 us (8%)
  other arithmetic  17.2 us (3%)
  matrix products  7.32 us (1%)
    ppermute x32, waiting for transfers between devices, from_behind(): return lax.ppermute(block, axis, route)  236 us
    ppermute x32, starting transfers between devices, from_behind(): return lax.ppermute(block, axis, route)  129 us
    all_to_all x1, starting transfers between devices, shards(): lax.all_to_all(grad_key.reshape(tokens, kv_local * HD), 'head', split_axi...  82.5 us
    all_to_all x1, starting transfers between devices, shards(): lax.all_to_all(grad_value.reshape(tokens, kv_local * HD), 'head', split_a...  73.7 us
  transfers between devices with their start and end apart: 40, of which 16 were waited for; matrix products, arithmetic and copies ran while one was open for 9% of the time, Pallas kernels for 0%

commit v1 on v0

v1 whole, which is shorter than its diff:
```python
import functools
import math

import jax
import jax.numpy as jnp
from jax import lax
from jax.experimental import pallas as pl
from jax.experimental.pallas import tpu as pltpu
from jax.sharding import Mesh
from jax.sharding import PartitionSpec as P

HD = 256
HALF = HD // 2
TOK = 256
LEVELS = 4
SLOTS = LEVELS + 1
CHIPS = 4
CORES = 2
PAIR = CORES * TOK
ROW = CHIPS * CORES
HEADS = 4
BASE = 10000.0
BF16 = jnp.bfloat16
F32 = jnp.float32

ANY = pl.BlockSpec(memory_space=pl.ANY)
VMEM = pl.BlockSpec(memory_space=pltpu.VMEM)
SMEM = pl.BlockSpec(memory_space=pltpu.SMEM)


def plan(parent_gap, row, chip, core):
    count = parent_gap.shape[0]
    ordinal = jnp.arange(count, dtype=jnp.int32)
    deeper = (parent_gap == 1).astype(jnp.int32)
    depths = jnp.sum(jnp.where(ordinal[None, :] <= ordinal[:, None], deeper[None, :], 0), 1)
    shard = row * ROW + chip * CORES + core
    first = row * ROW
    asked = jnp.stack([shard, shard + 1 - 2 * core, first, first + ROW])
    own_depth = jnp.sum(
        jnp.where(ordinal[None, :] <= asked[:, None], deeper[None, :], 0), 1
    ) + (asked >= count)
    wanted = own_depth[:, None] - jnp.arange(1, SLOTS, dtype=jnp.int32)[None, :]
    match = (depths[None, None, :] == wanted[:, :, None]) & (
        ordinal[None, None, :] < asked[:, None, None]
    )
    elder = jnp.max(jnp.where(match, ordinal[None, None, :], -1), 2)
    present = (elder >= 0).astype(jnp.int32)

    def place(node):
        return 2 * ((chip - (node - first) // CORES) % CHIPS) + node % CORES

    mine = elder[:2]
    rank = jnp.sum(
        jnp.where(mine[:, :, None] == elder[2][None, None, :], jnp.arange(LEVELS, dtype=jnp.int32), 0),
        2,
    )
    code = jnp.where(mine >= first, place(mine), 2 * CHIPS + (chip - rank) % CHIPS)
    code = jnp.where(mine >= 0, code, 0)
    code = jnp.concatenate([jnp.stack([core, 1 - core])[:, None], code], 1)
    relay = jnp.clip(elder[3], first, first + ROW - 1)
    relay_code = place(relay)
    holder = (chip - jnp.arange(CHIPS, dtype=jnp.int32)) % CHIPS
    sent = jnp.sum(jnp.where(jnp.arange(LEVELS) == chip, relay_code, 0))
    landing = jnp.sum(
        jnp.where(holder[:, None] == jnp.arange(LEVELS)[None, :], relay_code[None, :], 0), 1
    )
    table = jnp.concatenate(
        [code.reshape(-1), present[0], sent[None], landing, core[None]]
    ).astype(jnp.int32)
    pair_depth = jnp.sum(
        jnp.where(
            ordinal[None, :] <= (first + chip * CORES + jnp.arange(CORES))[:, None],
            deeper[None, :],
            0,
        ),
        1,
    )
    return table, pair_depth


def angles_of(depth):
    frequency = jnp.exp(jnp.arange(HALF, dtype=F32) * (-2.0 * math.log(BASE) / HD))
    position = (depth[:, None] * TOK + jnp.arange(TOK, dtype=jnp.int32)[None, :]).reshape(-1)
    return position.astype(F32)[:, None] * frequency[None, :]


def turn(block, cosine, sine):
    first, second = block[:, :HALF], block[:, HALF:]
    return jnp.concatenate(
        [first * cosine - second * sine, second * cosine + first * sine], -1
    )


def turn_kernel(x_ref, cos_ref, sin_ref, o_ref):
    o_ref[...] = turn(x_ref[...].astype(F32), cos_ref[...], sin_ref[...]).astype(BF16)


def call_turn(block, cosine, sine):
    return pl.pallas_call(
        turn_kernel,
        out_shape=jax.ShapeDtypeStruct((PAIR, HD), BF16),
        in_specs=[VMEM] * 3,
        out_specs=VMEM,
    )(block, cosine, sine)


def fetch(code, rows, relayed, target, sem):
    for k in range(CHIPS):
        for half in range(CORES):
            @pl.when(code == CORES * k + half)
            def _(k=k, half=half):
                pltpu.make_async_copy(rows[k].at[pl.ds(half * TOK, TOK)], target, sem).start()

        if relayed is not None:
            @pl.when(code == CORES * CHIPS + k)
            def _(k=k):
                pltpu.make_async_copy(relayed[k], target, sem).start()


def await_fetch(rows, target, sem):
    pltpu.make_async_copy(rows[0].at[pl.ds(0, TOK)], target, sem).wait()


def pick_kernel(offset, number, with_relayed, table, *refs):
    rows = refs[:CHIPS]
    relayed = refs[CHIPS : 2 * CHIPS] if with_relayed else None
    o_ref, sem = refs[-2:]
    for i in range(number):
        fetch(table[offset + i], rows, relayed, o_ref.at[pl.ds(i * TOK, TOK)], sem.at[i])
    for i in range(number):
        await_fetch(rows, o_ref.at[pl.ds(i * TOK, TOK)], sem.at[i])


def call_pick(table, rows, relayed, offset, number):
    operands = list(rows) + (list(relayed) if relayed is not None else [])
    return pl.pallas_call(
        functools.partial(pick_kernel, offset, number, relayed is not None),
        out_shape=jax.ShapeDtypeStruct((number * TOK, HD), BF16),
        in_specs=[SMEM] + [ANY] * len(operands),
        out_specs=VMEM,
        scratch_shapes=[pltpu.SemaphoreType.DMA((number,))],
    )(table, *operands)


def attend_kernel(
    table, q_ref, g_ref, cos_ref, sin_ref, other_ref, *refs
):
    rows, relayed = refs[:CHIPS], refs[CHIPS : 2 * CHIPS]
    att_ref, gq_ref, keep_ref, give_ref = refs[2 * CHIPS : 2 * CHIPS + 4]
    mine_ref, q_all, g_all, low_all, score_all, sem = refs[2 * CHIPS + 4 :]
    for i in range(SLOTS):
        fetch(table[i], rows, relayed, mine_ref.at[pl.ds(i * TOK, TOK)], sem.at[i])
    cosine, sine = cos_ref[...], sin_ref[...]
    for h in range(2):
        cols = slice(h * HD, (h + 1) * HD)
        q_all[h * TOK : (h + 1) * TOK, :] = turn(q_ref[:, cols].astype(F32), cosine, sine).astype(BF16)
        g_all[h * TOK : (h + 1) * TOK, :] = g_ref[:, cols]
    for i in range(SLOTS):
        await_fetch(rows, mine_ref.at[pl.ds(i * TOK, TOK)], sem.at[i])
    is_key = table[19] == 0
    mine, other = mine_ref[...], other_ref[...]
    keys = jnp.where(is_key, mine, other)
    vals = jnp.where(is_key, other, mine)
    scaling = HD ** -0.5
    tile = 128
    row_in = lax.broadcasted_iota(jnp.int32, (tile, TOK), 0)
    col_in = lax.broadcasted_iota(jnp.int32, (tile, TOK), 1)
    nt = (((1,), (1,)), ((), ()))
    nn = (((1,), (0,)), ((), ()))
    tn = (((0,), (0,)), ((), ()))
    for t in range(2 * TOK // tile):
        base = (t * tile) % TOK
        rows_here = slice(t * tile, (t + 1) * tile)
        q_tile, g_tile = q_all[rows_here, :], g_all[rows_here, :]
        scores = lax.dot_general(q_tile, keys, nt, preferred_element_type=F32) * scaling
        later = col_in > row_in + base
        seen = [jnp.logical_not(later)]
        for height in range(1, SLOTS):
            here = table[9 + height] > 0
            if height < LEVELS:
                seen.append(jnp.broadcast_to(here, (tile, TOK)))
            else:
                seen.append(jnp.logical_and(later, here))
        visible = jnp.concatenate(seen, 1)
        scores = jnp.where(visible, scores, -1e30)
        top = jnp.max(scores, -1, keepdims=True)
        raw = jnp.where(visible, jnp.exp(scores - top), 0.0)
        probs = raw / jnp.sum(raw, -1, keepdims=True)
        low = probs.astype(BF16)
        low_all[rows_here, :] = low
        att = lax.dot_general(low, vals, nn, preferred_element_type=F32)
        grad_prob = lax.dot_general(g_tile, vals, nt, preferred_element_type=F32)
        delta = jnp.sum(probs * grad_prob, -1, keepdims=True)
        gs = (probs * (grad_prob - delta) * scaling).astype(BF16)
        score_all[rows_here, :] = gs
        gq = lax.dot_general(gs, keys, nn, preferred_element_type=F32)
        h = t * tile // TOK
        toks = slice(base, base + tile)
        att_ref[toks, h * HD : (h + 1) * HD] = att.astype(BF16)
        gq_ref[toks, h * HD : (h + 1) * HD] = turn(
            gq, cos_ref[toks, :], -sin_ref[toks, :]
        ).astype(BF16)
    q2, g2 = q_all[...], g_all[...]
    for i in range(SLOTS):
        cols = slice(i * TOK, (i + 1) * TOK)
        part_key = lax.dot_general(score_all[:, cols], q2, tn, preferred_element_type=F32).astype(BF16)
        part_value = lax.dot_general(low_all[:, cols], g2, tn, preferred_element_type=F32).astype(BF16)
        keep_ref[cols, :] = jnp.where(is_key, part_key, part_value)
        give_ref[cols, :] = jnp.where(is_key, part_value, part_key)


def call_attend(table, query, grad, cosine, sine, other, rows, relayed):
    keys = SLOTS * TOK
    return pl.pallas_call(
        attend_kernel,
        out_shape=(
            jax.ShapeDtypeStruct((TOK, 2 * HD), BF16),
            jax.ShapeDtypeStruct((TOK, 2 * HD), BF16),
            jax.ShapeDtypeStruct((keys, HD), BF16),
            jax.ShapeDtypeStruct((keys, HD), BF16),
        ),
        in_specs=[SMEM] + [VMEM] * 5 + [ANY] * 8,
        out_specs=(VMEM,) * 4,
        scratch_shapes=[
            pltpu.VMEM((keys, HD), BF16),
            pltpu.VMEM((2 * TOK, HD), BF16),
            pltpu.VMEM((2 * TOK, HD), BF16),
            pltpu.VMEM((2 * TOK, keys), BF16),
            pltpu.VMEM((2 * TOK, keys), BF16),
            pltpu.SemaphoreType.DMA((SLOTS,)),
        ],
    )(table, query, grad, cosine, sine, other, *rows, *relayed)


def spread_kernel(table, keep_ref, got_ref, *refs):
    outs, total = refs[:-1], refs[-1]
    total[...] = jnp.zeros_like(total)
    for source, offset in ((keep_ref, 0), (got_ref, SLOTS)):
        for i in range(SLOTS):
            at = pl.ds(pl.multiple_of(table[offset + i] * TOK, TOK), TOK)
            total[at, :] += source[i * TOK : (i + 1) * TOK, :].astype(F32)
    for k in range(CHIPS):
        outs[k][...] = total[k * PAIR : (k + 1) * PAIR, :].astype(outs[k].dtype)
        low = CHIPS * PAIR + k * TOK
        outs[CHIPS + k][...] = total[low : low + TOK, :].astype(BF16)


def call_spread(table, keep, got):
    return pl.pallas_call(
        spread_kernel,
        out_shape=tuple(
            [jax.ShapeDtypeStruct((PAIR, HD), F32)]
            + [jax.ShapeDtypeStruct((PAIR, HD), BF16)] * (CHIPS - 1)
            + [jax.ShapeDtypeStruct((TOK, HD), BF16)] * CHIPS
        ),
        in_specs=[SMEM, VMEM, VMEM],
        out_specs=(VMEM,) * (2 * CHIPS),
        scratch_shapes=[pltpu.VMEM((CHIPS * PAIR + CHIPS * TOK, HD), F32)],
    )(table, keep, got)


def sum_kernel(*refs):
    total = refs[0][...].astype(F32)
    for ref in refs[1:-1]:
        total = total + ref[...].astype(F32)
    refs[-1][...] = total.astype(refs[-1].dtype)


def call_sum(parts, dtype):
    return pl.pallas_call(
        sum_kernel,
        out_shape=jax.ShapeDtypeStruct(parts[0].shape, dtype),
        in_specs=[VMEM] * len(parts),
        out_specs=VMEM,
    )(*parts)


def close_kernel(table, own_ref, *refs):
    backs = refs[:CHIPS]
    cos_ref, sin_ref, o_ref, total = refs[CHIPS:]
    total[...] = own_ref[...]
    for k in range(CHIPS):
        code = table[15 + k]

        @pl.when(code < CORES)
        def _(k=k, code=code):
            at = pl.ds(pl.multiple_of(code * TOK, TOK), TOK)
            total[at, :] += backs[k][...].astype(F32)

    o_ref[...] = turn(total[...], cos_ref[...], -sin_ref[...]).astype(BF16)


def call_close(table, own, backs, cosine, sine):
    return pl.pallas_call(
        close_kernel,
        out_shape=jax.ShapeDtypeStruct((PAIR, HD), BF16),
        in_specs=[SMEM] + [VMEM] * (3 + CHIPS),
        out_specs=VMEM,
        scratch_shapes=[pltpu.VMEM((PAIR, HD), F32)],
    )(table, own, *backs, cosine, sine)


def ring(block, shift):
    return lax.ppermute(block, "chip", [(i, (i + shift) % CHIPS) for i in range(CHIPS)])


def back_in_row(block, shift):
    return lax.ppermute(block, "chip", [(i, i - shift) for i in range(shift, CHIPS)])


def next_row(block, shift):
    rows = lax.axis_size("row")
    return lax.ppermute(
        block, "row", [(i, i + shift) for i in range(rows) if 0 <= i + shift < rows]
    )


def swap(block):
    return lax.ppermute(block, "core", [(0, 1), (1, 0)])


def gather_ring(block):
    near, far = ring(block, 1), ring(block, -1)
    return [block, near, ring(block, 2), far]


def shards(queries, keys, values, grad_attn, parent_gap):
    row, chip, core = (lax.axis_index(name) for name in ("row", "chip", "core"))
    both = lax.all_to_all(
        jnp.concatenate([keys, values], 1), ("core", "head"), split_axis=1, concat_axis=0, tiled=True
    )
    query_in = lax.all_to_all(queries, "head", split_axis=1, concat_axis=0, tiled=True)
    grad_in = lax.all_to_all(grad_attn, "head", split_axis=1, concat_axis=0, tiled=True)
    table, pair_depth = plan(parent_gap, row, chip, core)
    angles = angles_of(pair_depth)
    cosine, sine = jnp.cos(angles), jnp.sin(angles)
    own_cos = lax.dynamic_slice_in_dim(cosine, core * TOK, TOK, 0)
    own_sin = lax.dynamic_slice_in_dim(sine, core * TOK, TOK, 0)
    pair_cos = jnp.where(core == 0, cosine, 1.0)
    pair_sin = jnp.where(core == 0, sine, 0.0)

    both = call_turn(both, pair_cos, pair_sin)
    rows = gather_ring(both)
    relay = next_row(call_pick(table, rows, None, 14, 1), 1)
    relayed = gather_ring(relay)
    other = swap(call_pick(table, rows, relayed, SLOTS, SLOTS))
    attended, grad_query, keep, give = call_attend(
        table, query_in, grad_in, own_cos, own_sin, other, rows, relayed
    )
    spread = call_spread(table, keep, swap(give))
    own, within, stack = spread[0], spread[1:CHIPS], spread[CHIPS:]
    stack_sum = call_sum([stack[0]] + [ring(stack[k], -k) for k in range(1, CHIPS)], BF16)
    back = gather_ring(next_row(stack_sum, -1))
    own = call_sum([own] + [back_in_row(within[k - 1], k) for k in range(1, CHIPS)], F32)
    grad_both = call_close(table, own, back, pair_cos, pair_sin)
    attended_out = lax.all_to_all(attended, "head", split_axis=0, concat_axis=1, tiled=True)
    query_back = lax.all_to_all(grad_query, "head", split_axis=0, concat_axis=1, tiled=True)
    both_back = lax.all_to_all(
        grad_both, ("core", "head"), split_axis=0, concat_axis=1, tiled=True
    )
    half = HEADS * HD
    return attended_out, query_back, both_back[:, :half], both_back[:, half:]


def solution(mesh):
    devices = mesh.devices
    rows = devices.shape[0] // ROW
    split = Mesh(
        devices.reshape(rows, CHIPS, CORES, devices.shape[1]), ("row", "chip", "core", "head")
    )
    spec = P(("row", "chip", "core", "head"), None)
    return jax.shard_map(
        shards,
        mesh=split,
        in_specs=(spec, spec, spec, spec, P()),
        out_specs=(spec, spec, spec, spec),
        check_vma=False,
    )
```

time: 651 us -> 196 us (0.30)
  the two profiles are of different devices: /device:TPU:191 before, /device:TPU:25 now
where the time goes in v1:
time: 196 us; the launch traced here: 194 us
  starting transfers between devices  99.6 us (51%)
  waiting for transfers between devices  48.2 us (25%)
  Pallas kernels  25.2 us (13%)
  local copies, waits for them, and re-layouts  15.1 us (8%)
  other arithmetic  5.2 us (3%)
    ppermute x12, starting transfers between devices, ring(): lax.ppermute(block, 'chip', [(i, (i + shift) % CHIPS) for i in range(CHIP...  36.8 us
    ppermute x2, waiting for transfers between devices, next_row(): lax.ppermute(block, 'row', [(i, i + shift) for i in range(rows) if 0 <= i...  15.7 us
    ppermute x12, waiting for transfers between devices, ring(): lax.ppermute(block, 'chip', [(i, (i + shift) % CHIPS) for i in range(CHIP...  14.3 us
    all_to_all x1, starting transfers between devices, shards(): lax.all_to_all(grad_attn, 'head', split_axis=1, concat_axis=0, tiled=True)  13.5 us
    all_to_all x1, starting transfers between devices, shards(): lax.all_to_all(grad_both, ('core', 'head'), split_axis=0, concat_axis=1,...  10.7 us
    ppermute x2, starting transfers between devices, next_row(): lax.ppermute(block, 'row', [(i, i + shift) for i in range(rows) if 0 <= i...  10.4 us
    pallas_call x1, Pallas kernels, call_attend(): pl.pallas_call(attend_kernel, out_shape=(jax.ShapeDtypeStruct((TOK, 2 * H...  9.16 us
    unnamed x55, local copies, waits for them, and re-layouts  7.98 us
  transfers between devices with their start and end apart: 25, of which 10 were waited for; matrix products, arithmetic and copies ran while one was open for 5% of the time, Pallas kernels for 8%

profile of v1, /device:TPU:25, one launch (start us, length us, event | category | flops | bytes accessed | tf_op | source)
XLA Modules:
  0.0 194.4 jit_solution(6011625640752385322)
XLA Ops:
  2.3 6.7 %all-to-all-start.2 = ((bf16[64,8,256]{2,0,1:T(8,128)(2,1)}), bf16[64,8,256]{2,0,1:T(8,128)(2,1)S(1)}, u32[]{:S(2)}, u32[]{:S(2)}) async-start(bf16[64,8,256]{2,0,1:T(8,128)(2,1)} %bitcast.55), calls=%async_computation.2 | async-start | bytes 524288 | tf_op jit(solution)/shard_map/all_to_all | solution.py:329
  13.5 4.5 %all-to-all-done.2 = bf16[64,8,256]{2,0,1:T(8,128)(2,1)S(1)} async-done(((bf16[64,8,256]{2,0,1:T(8,128)(2,1)}), bf16[64,8,256]{2,0,1:T(8,128)(2,1)S(1)}, u32[]{:S(2)}, u32[]{:S(2)}) %all-to-all-start.2) | async-done | bytes 262176 | tf_op jit(solution)/shard_map/all_to_all | solution.py:329
  18.8 3.4 %all-to-all-start = ((bf16[64,4,512]{2,0,1:T(8,128)(2,1)}), bf16[64,4,512]{2,0,1:T(8,128)(2,1)S(1)}, u32[]{:S(2)}, u32[]{:S(2)}) async-start(bf16[64,4,512]{2,0,1:T(8,128)(2,1)} %bitcast.57), calls=%async_computation | async-start | bytes 524288 | tf_op jit(solution)/shard_map/all_to_all | solution.py:332
  25.9 4.4 %collective-permute-start.2 = (bf16[512,256]{1,0:T(8,128)(2,1)}, bf16[512,256]{1,0:T(8,128)(2,1)S(1)}, u32[]{:S(2)}, u32[]{:S(2)}) collective-permute-start(bf16[512,256]{1,0:T(8,128)(2,1)} %shard_map.84.refs_0_), channel_id=1, source_target_pairs={{0,24},{8,0},{16,8},{24,16},{1,25},{9,1},{17,9},{25,17},{2,26},{10... | collective-permute-start | bytes 786440 | tf_op jit(solution)/shard_map/ppermute | solution.py:304
  36.7 4.7 %collective-permute-done.2.refs_3_ = bf16[512,256]{1,0:T(8,128)(2,1)S(1)} collective-permute-done((bf16[512,256]{1,0:T(8,128)(2,1)}, bf16[512,256]{1,0:T(8,128)(2,1)S(1)}, u32[]{:S(2)}, u32[]{:S(2)}) %collective-permute-start.2) | collective-permute-done | bytes 262176 | tf_op jit(solution)/shard_map/ppermute | solution.py:304
  41.4 6.4 %collective-permute-done.refs_1_ = bf16[512,256]{1,0:T(8,128)(2,1)S(1)} collective-permute-done((bf16[512,256]{1,0:T(8,128)(2,1)}, bf16[512,256]{1,0:T(8,128)(2,1)S(1)}, u32[]{:S(2)}, u32[]{:S(2)}) %collective-permute-start) | collective-permute-done | bytes 262176 | tf_op jit(solution)/shard_map/ppermute | solution.py:304
  50.7 8.5 %collective-permute-start.3 = (bf16[256,256]{1,0:T(8,128)(2,1)}, bf16[256,256]{1,0:T(8,128)(2,1)S(1)}, u32[]{:S(2)}, u32[]{:S(2)}) collective-permute-start(bf16[256,256]{1,0:T(8,128)(2,1)} %shard_map.85), channel_id=1, source_target_pairs={{0,32},{32,64},{64,96},{96,128},{128,160},{160,192},{192,224},{224... | collective-permute-start | bytes 393224 | tf_op jit(solution)/shard_map/ppermute | solution.py:313
  66.3 2.8 %collective-permute-start.4 = (bf16[256,256]{1,0:T(8,128)(2,1)S(1)}, bf16[256,256]{1,0:T(8,128)(2,1)S(1)}, u32[]{:S(2)}, u32[]{:S(2)}) collective-permute-start(bf16[256,256]{1,0:T(8,128)(2,1)S(1)} %collective-permute-done.3.refs_4_), channel_id=1, source_target_pairs={{0,8},{8,16},{16,24},{24,0},{1,9},{9,17},{17,25},{25,1},{2,10},{10... | collective-permute-start | bytes 393224 | tf_op jit(solution)/shard_map/ppermute | solution.py:304
  69.8 13.5 %all-to-all-start.1 = ((bf16[64,4,512]{2,0,1:T(8,128)(2,1)}), bf16[64,4,512]{2,0,1:T(8,128)(2,1)S(1)}, u32[]{:S(2)}, u32[]{:S(2)}) async-start(bf16[64,4,512]{2,0,1:T(8,128)(2,1)} %bitcast.56), calls=%async_computation.1 | async-start | bytes 524288 | tf_op jit(solution)/shard_map/all_to_all | solution.py:333
  84.7 2.7 %shard_map.86 = bf16[1280,256]{1,0:T(8,128)(2,1)} custom-call(s32[20]{0:T(128)} %concatenate.14.table, bf16[512,256]{1,0:T(8,128)(2,1)} %shard_map.84.refs_0_, bf16[512,256]{1,0:T(8,128)(2,1)} %copy-done.2, bf16[512,256]{1,0:T(8,128)(2,1)} %copy-done.1, bf16[512,256]{1,0:T(8,128)(2,1)} %copy-done, bf16[256,256]{1,0:T(8,128)(2,1)} %copy-done.8, ...), custom_call_target="tpu_custom_call" | custom-call | tf_op jit(solution)/shard_map/pallas_call | solution.py:136
  87.5 3.4 %collective-permute-start.7 = (bf16[1280,256]{1,0:T(8,128)(2,1)}, bf16[1280,256]{1,0:T(8,128)(2,1)S(1)}, u32[]{:S(2)}, u32[]{:S(2)}) collective-permute-start(bf16[1280,256]{1,0:T(8,128)(2,1)} %shard_map.86), channel_id=1, source_target_pairs={{0,4},{4,0},{1,5},{5,1},{2,6},{6,2},{3,7},{7,3},{8,12},{12,8},{9,1... | collective-permute-start | bytes 1966088 | tf_op jit(solution)/shard_map/ppermute | solution.py:319
  93.7 9.2 %shard_map.87 = (bf16[256,512]{1,0:T(8,128)(2,1)}, bf16[256,512]{1,0:T(8,128)(2,1)}, bf16[1280,256]{1,0:T(8,128)(2,1)}, bf16[1280,256]{1,0:T(8,128)(2,1)}) custom-call(s32[20]{0:T(128)} %concatenate.14.table, bf16[256,512]{1,0:T(8,128)(2,1)} %bitcast.58, bf16[256,512]{1,0:T(8,128)(2,1)} %bitcast.59, f32[256,128]{1,0:T(8,128)} %get-tuple-element.39.cos_ref, ...), custom_call_target="tpu_custom_call" | custom-call | tf_op jit(solution)/shard_map/pallas_call | solution.py:214
  102.8 4.8 %all-to-all-start.4 = ((bf16[4,64,512]{2,1,0:T(8,128)(2,1)}), bf16[4,64,512]{2,1,0:T(8,128)(2,1)S(1)}, u32[]{:S(2)}, u32[]{:S(2)}) async-start(bf16[4,64,512]{2,1,0:T(8,128)(2,1)} %bitcast.69), calls=%async_computation.4 | async-start | bytes 524288 | tf_op jit(solution)/shard_map/all_to_all | solution.py:357
  107.7 2.5 %collective-permute-start.8 = (bf16[1280,256]{1,0:T(8,128)(2,1)}, bf16[1280,256]{1,0:T(8,128)(2,1)S(1)}, u32[]{:S(2)}, u32[]{:S(2)}) collective-permute-start(bf16[1280,256]{1,0:T(8,128)(2,1)} %get-tuple-element.19), channel_id=1, source_target_pairs={{0,4},{4,0},{1,5},{5,1},{2,6},{6,2},{3,7},{7,3},{8,12},{12,8},{9,1... | collective-permute-start | bytes 1966088 | tf_op jit(solution)/shard_map/ppermute | solution.py:319
  110.2 4.9 %all-to-all-done.4 = bf16[4,64,512]{2,1,0:T(8,128)(2,1)S(1)} async-done(((bf16[4,64,512]{2,1,0:T(8,128)(2,1)}), bf16[4,64,512]{2,1,0:T(8,128)(2,1)S(1)}, u32[]{:S(2)}, u32[]{:S(2)}) %all-to-all-start.4) | async-done | bytes 262176 | tf_op jit(solution)/shard_map/all_to_all | solution.py:357
  115.1 3.5 %all-to-all-start.3 = ((bf16[4,64,512]{2,1,0:T(8,128)(2,1)}), bf16[4,64,512]{2,1,0:T(8,128)(2,1)S(1)}, u32[]{:S(2)}, u32[]{:S(2)}) async-start(bf16[4,64,512]{2,1,0:T(8,128)(2,1)} %bitcast.18), calls=%async_computation.3 | async-start | bytes 524288 | tf_op jit(solution)/shard_map/all_to_all | solution.py:356
  119.4 3.0 %shard_map.88 = (f32[512,256]{1,0:T(8,128)}, bf16[512,256]{1,0:T(8,128)(2,1)}, bf16[512,256]{1,0:T(8,128)(2,1)}, bf16[512,256]{1,0:T(8,128)(2,1)}, bf16[256,256]...) custom-call(s32[20]{0:T(128)} %concatenate.14.table, ...), custom_call_target="tpu_custom_call" | custom-call | tf_op jit(solution)/shard_map/pallas_call | solution.py:249
  122.4 4.1 %collective-permute-start.12 = (bf16[256,256]{1,0:T(8,128)(2,1)}, bf16[256,256]{1,0:T(8,128)(2,1)S(1)}, u32[]{:S(2)}, u32[]{:S(2)}) collective-permute-start(bf16[256,256]{1,0:T(8,128)(2,1)} %get-tuple-element.25), channel_id=1, source_target_pairs={{0,24},{8,0},{16,8},{24,16},{1,25},{9,1},{17,9},{25,17},{2,26},{10... | collective-permute-start | bytes 393224 | tf_op jit(solution)/shard_map/ppermute | solution.py:304
  126.5 3.4 %collective-permute-start.13 = (bf16[256,256]{1,0:T(8,128)(2,1)}, bf16[256,256]{1,0:T(8,128)(2,1)S(1)}, u32[]{:S(2)}, u32[]{:S(2)}) collective-permute-start(bf16[256,256]{1,0:T(8,128)(2,1)} %get-tuple-element.26), channel_id=1, source_target_pairs={{0,16},{8,24},{16,0},{24,8},{1,17},{9,25},{17,1},{25,9},{2,18},{10... | collective-permute-start | bytes 393224 | tf_op jit(solution)/shard_map/ppermute | solution.py:304
  129.9 2.8 %collective-permute-start.14 = (bf16[256,256]{1,0:T(8,128)(2,1)}, bf16[256,256]{1,0:T(8,128)(2,1)S(1)}, u32[]{:S(2)}, u32[]{:S(2)}) collective-permute-start(bf16[256,256]{1,0:T(8,128)(2,1)} %get-tuple-element.27), channel_id=1, source_target_pairs={{0,8},{8,16},{16,24},{24,0},{1,9},{9,17},{17,25},{25,1},{2,10},{10... | collective-permute-start | bytes 393224 | tf_op jit(solution)/shard_map/ppermute | solution.py:304
  142.8 13.7 %collective-permute-done.15.refs_0_ = bf16[256,256]{1,0:T(8,128)(2,1)S(1)} collective-permute-done((bf16[256,256]{1,0:T(8,128)(2,1)}, bf16[256,256]{1,0:T(8,128)(2,1)S(1)}, u32[]{:S(2)}, u32[]{:S(2)}) %collective-permute-start.15) | collective-permute-done | bytes 131104 | tf_op jit(solution)/shard_map/ppermute | solution.py:313
  156.5 5.6 %collective-permute-start.18 = (bf16[256,256]{1,0:T(8,128)(2,1)S(1)}, bf16[256,256]{1,0:T(8,128)(2,1)S(1)}, u32[]{:S(2)}, u32[]{:S(2)}) collective-permute-start(bf16[256,256]{1,0:T(8,128)(2,1)S(1)} %collective-permute-done.15.refs_0_), channel_id=1, source_target_pairs={{0,24},{8,0},{16,8},{24,16},{1,25},{9,1},{17,9},{25,17},{2,26},{10... | collective-permute-start | bytes 393224 | tf_op jit(solution)/shard_map/ppermute | solution.py:304
  174.0 10.7 %all-to-all-start.5 = ((bf16[8,64,256]{2,1,0:T(8,128)(2,1)}), bf16[8,64,256]{2,1,0:T(8,128)(2,1)S(1)}, u32[]{:S(2)}, u32[]{:S(2)}) async-start(bf16[8,64,256]{2,1,0:T(8,128)(2,1)} %bitcast.66), calls=%async_computation.5 | async-start | bytes 524288 | tf_op jit(solution)/shard_map/all_to_all | solution.py:358
  186.1 7.6 %all-to-all-done.5 = bf16[8,64,256]{2,1,0:T(8,128)(2,1)S(1)} async-done(((bf16[8,64,256]{2,1,0:T(8,128)(2,1)}), bf16[8,64,256]{2,1,0:T(8,128)(2,1)S(1)}, u32[]{:S(2)}, u32[]{:S(2)}) %all-to-all-start.5) | async-done | bytes 262176 | tf_op jit(solution)/shard_map/all_to_all | solution.py:358
  (127 shorter events, 56.6 us)
Async XLA Ops:
  2.3 15.7 %all-to-all-start.2 = ((bf16[64,8,256]{2,0,1:T(8,128)(2,1)}), bf16[64,8,256]{2,0,1:T(8,128)(2,1)S(1)}, u32[]{:S(2)}, u32[]{:S(2)}) async-start(bf16[64,8,256]{2,0,1:T(8,128)(2,1)} %bitcast.55), calls=%async_computation.2 | async-start | bytes 524288 | tf_op jit(solution)/shard_map/all_to_all | solution.py:329
  18.8 50.3 %all-to-all-start = ((bf16[64,4,512]{2,0,1:T(8,128)(2,1)}), bf16[64,4,512]{2,0,1:T(8,128)(2,1)S(1)}, u32[]{:S(2)}, u32[]{:S(2)}) async-start(bf16[64,4,512]{2,0,1:T(8,128)(2,1)} %bitcast.57), calls=%async_computation | async-start | bytes 524288 | tf_op jit(solution)/shard_map/all_to_all | solution.py:332
  25.9 15.5 %collective-permute-start.2 = (bf16[512,256]{1,0:T(8,128)(2,1)}, bf16[512,256]{1,0:T(8,128)(2,1)S(1)}, u32[]{:S(2)}, u32[]{:S(2)}) collective-permute-start(bf16[512,256]{1,0:T(8,128)(2,1)} %shard_map.84.refs_0_), channel_id=1, source_target_pairs={{0,24},{8,0},{16,8},{24,16},{1,25},{9,1},{17,9},{25,17},{2,26},{10... | collective-permute-start | bytes 786440 | tf_op jit(solution)/shard_map/ppermute | solution.py:304
  30.3 11.1 %collective-permute-start.1 = (bf16[512,256]{1,0:T(8,128)(2,1)}, bf16[512,256]{1,0:T(8,128)(2,1)S(1)}, u32[]{:S(2)}, u32[]{:S(2)}) collective-permute-start(bf16[512,256]{1,0:T(8,128)(2,1)} %shard_map.84.refs_0_), channel_id=1, source_target_pairs={{0,16},{8,24},{16,0},{24,8},{1,17},{9,25},{17,1},{25,9},{2,18},{10... | collective-permute-start | bytes 786440 | tf_op jit(solution)/shard_map/ppermute | solution.py:304
  32.8 15.0 %collective-permute-start = (bf16[512,256]{1,0:T(8,128)(2,1)}, bf16[512,256]{1,0:T(8,128)(2,1)S(1)}, u32[]{:S(2)}, u32[]{:S(2)}) collective-permute-start(bf16[512,256]{1,0:T(8,128)(2,1)} %shard_map.84.refs_0_), channel_id=1, source_target_pairs={{0,8},{8,16},{16,24},{24,0},{1,9},{9,17},{17,25},{25,1},{2,10},{10... | collective-permute-start | bytes 786440 | tf_op jit(solution)/shard_map/ppermute | solution.py:304
  50.7 11.2 %collective-permute-start.3 = (bf16[256,256]{1,0:T(8,128)(2,1)}, bf16[256,256]{1,0:T(8,128)(2,1)S(1)}, u32[]{:S(2)}, u32[]{:S(2)}) collective-permute-start(bf16[256,256]{1,0:T(8,128)(2,1)} %shard_map.85), channel_id=1, source_target_pairs={{0,32},{32,64},{64,96},{96,128},{128,160},{160,192},{192,224},{224... | collective-permute-start | bytes 393224 | tf_op jit(solution)/shard_map/ppermute | solution.py:313
  61.9 21.5 %collective-permute-start.6 = (bf16[256,256]{1,0:T(8,128)(2,1)S(1)}, bf16[256,256]{1,0:T(8,128)(2,1)S(1)}, u32[]{:S(2)}, u32[]{:S(2)}) collective-permute-start(bf16[256,256]{1,0:T(8,128)(2,1)S(1)} %collective-permute-done.3.refs_4_), channel_id=1, source_target_pairs={{0,24},{8,0},{16,8},{24,16},{1,25},{9,1},{17,9},{25,17},{2,26},{10... | collective-permute-start | bytes 393224 | tf_op jit(solution)/shard_map/ppermute | solution.py:304
  63.8 19.5 %collective-permute-start.5 = (bf16[256,256]{1,0:T(8,128)(2,1)S(1)}, bf16[256,256]{1,0:T(8,128)(2,1)S(1)}, u32[]{:S(2)}, u32[]{:S(2)}) collective-permute-start(bf16[256,256]{1,0:T(8,128)(2,1)S(1)} %collective-permute-done.3.refs_4_), channel_id=1, source_target_pairs={{0,16},{8,24},{16,0},{24,8},{1,17},{9,25},{17,1},{25,9},{2,18},{10... | collective-permute-start | bytes 393224 | tf_op jit(solution)/shard_map/ppermute | solution.py:304
  66.3 17.1 %collective-permute-start.4 = (bf16[256,256]{1,0:T(8,128)(2,1)S(1)}, bf16[256,256]{1,0:T(8,128)(2,1)S(1)}, u32[]{:S(2)}, u32[]{:S(2)}) collective-permute-start(bf16[256,256]{1,0:T(8,128)(2,1)S(1)} %collective-permute-done.3.refs_4_), channel_id=1, source_target_pairs={{0,8},{8,16},{16,24},{24,0},{1,9},{9,17},{17,25},{25,1},{2,10},{10... | collective-permute-start | bytes 393224 | tf_op jit(solution)/shard_map/ppermute | solution.py:304
  69.8 21.8 %all-to-all-start.1 = ((bf16[64,4,512]{2,0,1:T(8,128)(2,1)}), bf16[64,4,512]{2,0,1:T(8,128)(2,1)S(1)}, u32[]{:S(2)}, u32[]{:S(2)}) async-start(bf16[64,4,512]{2,0,1:T(8,128)(2,1)} %bitcast.56), calls=%async_computation.1 | async-start | bytes 524288 | tf_op jit(solution)/shard_map/all_to_all | solution.py:333
  102.8 12.3 %all-to-all-start.4 = ((bf16[4,64,512]{2,1,0:T(8,128)(2,1)}), bf16[4,64,512]{2,1,0:T(8,128)(2,1)S(1)}, u32[]{:S(2)}, u32[]{:S(2)}) async-start(bf16[4,64,512]{2,1,0:T(8,128)(2,1)} %bitcast.69), calls=%async_computation.4 | async-start | bytes 524288 | tf_op jit(solution)/shard_map/all_to_all | solution.py:357
  107.7 10.9 %collective-permute-start.8 = (bf16[1280,256]{1,0:T(8,128)(2,1)}, bf16[1280,256]{1,0:T(8,128)(2,1)S(1)}, u32[]{:S(2)}, u32[]{:S(2)}) collective-permute-start(bf16[1280,256]{1,0:T(8,128)(2,1)} %get-tuple-element.19), channel_id=1, source_target_pairs={{0,4},{4,0},{1,5},{5,1},{2,6},{6,2},{3,7},{7,3},{8,12},{12,8},{9,1... | collective-permute-start | bytes 1966088 | tf_op jit(solution)/shard_map/ppermute | solution.py:319
  115.1 58.9 %all-to-all-start.3 = ((bf16[4,64,512]{2,1,0:T(8,128)(2,1)}), bf16[4,64,512]{2,1,0:T(8,128)(2,1)S(1)}, u32[]{:S(2)}, u32[]{:S(2)}) async-start(bf16[4,64,512]{2,1,0:T(8,128)(2,1)} %bitcast.18), calls=%async_computation.3 | async-start | bytes 524288 | tf_op jit(solution)/shard_map/all_to_all | solution.py:356
  122.4 12.9 %collective-permute-start.12 = (bf16[256,256]{1,0:T(8,128)(2,1)}, bf16[256,256]{1,0:T(8,128)(2,1)S(1)}, u32[]{:S(2)}, u32[]{:S(2)}) collective-permute-start(bf16[256,256]{1,0:T(8,128)(2,1)} %get-tuple-element.25), channel_id=1, source_target_pairs={{0,24},{8,0},{16,8},{24,16},{1,25},{9,1},{17,9},{25,17},{2,26},{10... | collective-permute-start | bytes 393224 | tf_op jit(solution)/shard_map/ppermute | solution.py:304
  126.5 10.1 %collective-permute-start.13 = (bf16[256,256]{1,0:T(8,128)(2,1)}, bf16[256,256]{1,0:T(8,128)(2,1)S(1)}, u32[]{:S(2)}, u32[]{:S(2)}) collective-permute-start(bf16[256,256]{1,0:T(8,128)(2,1)} %get-tuple-element.26), channel_id=1, source_target_pairs={{0,16},{8,24},{16,0},{24,8},{1,17},{9,25},{17,1},{25,9},{2,18},{10... | collective-permute-start | bytes 393224 | tf_op jit(solution)/shard_map/ppermute | solution.py:304
  129.9 8.5 %collective-permute-start.14 = (bf16[256,256]{1,0:T(8,128)(2,1)}, bf16[256,256]{1,0:T(8,128)(2,1)S(1)}, u32[]{:S(2)}, u32[]{:S(2)}) collective-permute-start(bf16[256,256]{1,0:T(8,128)(2,1)} %get-tuple-element.27), channel_id=1, source_target_pairs={{0,8},{8,16},{16,24},{24,0},{1,9},{9,17},{17,25},{25,1},{2,10},{10... | collective-permute-start | bytes 393224 | tf_op jit(solution)/shard_map/ppermute | solution.py:304
  132.7 31.4 %collective-permute-start.9 = (bf16[512,256]{1,0:T(8,128)(2,1)}, bf16[512,256]{1,0:T(8,128)(2,1)S(1)}, u32[]{:S(2)}, u32[]{:S(2)}) collective-permute-start(bf16[512,256]{1,0:T(8,128)(2,1)} %get-tuple-element.21), channel_id=1, source_target_pairs={{8,0},{16,8},{24,16},{9,1},{17,9},{25,17},{10,2},{18,10},{26,18},{... | collective-permute-start | bytes 786440 | tf_op jit(solution)/shard_map/ppermute | solution.py:308
  134.0 32.7 %collective-permute-start.10 = (bf16[512,256]{1,0:T(8,128)(2,1)}, bf16[512,256]{1,0:T(8,128)(2,1)S(1)}, u32[]{:S(2)}, u32[]{:S(2)}) collective-permute-start(bf16[512,256]{1,0:T(8,128)(2,1)} %get-tuple-element.22), channel_id=1, source_target_pairs={{16,0},{24,8},{17,1},{25,9},{18,2},{26,10},{19,3},{27,11},{20,4},{... | collective-permute-start | bytes 786440 | tf_op jit(solution)/shard_map/ppermute | solution.py:308
  135.3 31.4 %collective-permute-start.11 = (bf16[512,256]{1,0:T(8,128)(2,1)}, bf16[512,256]{1,0:T(8,128)(2,1)S(1)}, u32[]{:S(2)}, u32[]{:S(2)}) collective-permute-start(bf16[512,256]{1,0:T(8,128)(2,1)} %get-tuple-element.23), channel_id=1, source_target_pairs={{24,0},{25,1},{26,2},{27,3},{28,4},{29,5},{30,6},{31,7},{56,32},{5... | collective-permute-start | bytes 786440 | tf_op jit(solution)/shard_map/ppermute | solution.py:308
  140.9 15.6 %collective-permute-start.15 = (bf16[256,256]{1,0:T(8,128)(2,1)}, bf16[256,256]{1,0:T(8,128)(2,1)S(1)}, u32[]{:S(2)}, u32[]{:S(2)}) collective-permute-start(bf16[256,256]{1,0:T(8,128)(2,1)} %shard_map.90), channel_id=1, source_target_pairs={{32,0},{64,32},{96,64},{128,96},{160,128},{192,160},{224,192},{256... | collective-permute-start | bytes 393224 | tf_op jit(solution)/shard_map/ppermute | solution.py:313
  156.5 13.1 %collective-permute-start.18 = (bf16[256,256]{1,0:T(8,128)(2,1)S(1)}, bf16[256,256]{1,0:T(8,128)(2,1)S(1)}, u32[]{:S(2)}, u32[]{:S(2)}) collective-permute-start(bf16[256,256]{1,0:T(8,128)(2,1)S(1)} %collective-permute-done.15.refs_0_), channel_id=1, source_target_pairs={{0,24},{8,0},{16,8},{24,16},{1,25},{9,1},{17,9},{25,17},{2,26},{10... | collective-permute-start | bytes 393224 | tf_op jit(solution)/shard_map/ppermute | solution.py:304
  162.2 7.5 %collective-permute-start.17 = (bf16[256,256]{1,0:T(8,128)(2,1)S(1)}, bf16[256,256]{1,0:T(8,128)(2,1)S(1)}, u32[]{:S(2)}, u32[]{:S(2)}) collective-permute-start(bf16[256,256]{1,0:T(8,128)(2,1)S(1)} %collective-permute-done.15.refs_0_), channel_id=1, source_target_pairs={{0,16},{8,24},{16,0},{24,8},{1,17},{9,25},{17,1},{25,9},{2,18},{10... | collective-permute-start | bytes 393224 | tf_op jit(solution)/shard_map/ppermute | solution.py:304
  164.1 6.9 %collective-permute-start.16 = (bf16[256,256]{1,0:T(8,128)(2,1)S(1)}, bf16[256,256]{1,0:T(8,128)(2,1)S(1)}, u32[]{:S(2)}, u32[]{:S(2)}) collective-permute-start(bf16[256,256]{1,0:T(8,128)(2,1)S(1)} %collective-permute-done.15.refs_0_), channel_id=1, source_target_pairs={{0,8},{8,16},{16,24},{24,0},{1,9},{9,17},{17,25},{25,1},{2,10},{10... | collective-permute-start | bytes 393224 | tf_op jit(solution)/shard_map/ppermute | solution.py:304
  174.0 19.7 %all-to-all-start.5 = ((bf16[8,64,256]{2,1,0:T(8,128)(2,1)}), bf16[8,64,256]{2,1,0:T(8,128)(2,1)S(1)}, u32[]{:S(2)}, u32[]{:S(2)}) async-start(bf16[8,64,256]{2,1,0:T(8,128)(2,1)} %bitcast.66), calls=%async_computation.5 | async-start | bytes 524288 | tf_op jit(solution)/shard_map/all_to_all | solution.py:358
  (29 other events, 94.3 us)

commit v2 on v1

v2 whole, which is shorter than its diff:
```python
import functools
import math

import jax
import jax.numpy as jnp
from jax import lax
from jax.experimental import pallas as pl
from jax.experimental.pallas import tpu as pltpu
from jax.sharding import Mesh
from jax.sharding import PartitionSpec as P


HD = 256
HALF = HD // 2
TOK = 256
LEVELS = 4
SLOTS = LEVELS + 1
CHIPS = 4
CORES = 2
PAIR = CORES * TOK
KEYS = SLOTS * TOK
ROW = CHIPS * CORES
HEADS = 4
WIDE = 2 * HD
OWN, OTHER, SEEN, GOES, COMES, LAND, CORE = 0, 5, 10, 14, 19, 24, 27
BASE = 10000.0
BF16 = jnp.bfloat16
F32 = jnp.float32

MIB = 1024 * 1024


def room(mib):
    return pltpu.CompilerParams(vmem_limit_bytes=mib * MIB)


ANY = pl.BlockSpec(memory_space=pl.ANY)
VMEM = pl.BlockSpec(memory_space=pltpu.VMEM)
SMEM = pl.BlockSpec(memory_space=pltpu.SMEM)


def plan(parent_gap, row, chip, core):
    count = parent_gap.shape[0]
    ordinal = jnp.arange(count, dtype=jnp.int32)
    levels = jnp.arange(LEVELS, dtype=jnp.int32)
    deeper = (parent_gap == 1).astype(jnp.int32)
    depths = jnp.sum(jnp.where(ordinal[None, :] <= ordinal[:, None], deeper[None, :], 0), 1)
    first = row * ROW
    shard = first + chip * CORES + core
    asked = jnp.stack([shard, shard + 1 - 2 * core, first, first + ROW])
    own_depth = jnp.sum(
        jnp.where(ordinal[None, :] <= asked[:, None], deeper[None, :], 0), 1
    ) + (asked >= count)
    wanted = own_depth[:, None] - 1 - levels[None, :]
    match = (depths[None, None, :] == wanted[:, :, None]) & (
        ordinal[None, None, :] < asked[:, None, None]
    )
    elder = jnp.max(jnp.where(match, ordinal[None, None, :], -1), 2)
    mine, stack, relay = elder[:2], elder[2], elder[3]
    in_row = 2 * (chip - (mine - first) // CORES) + mine % CORES
    before = 2 * CHIPS + 2 * ((mine - first + ROW) // CORES - chip) + mine % CORES
    rank = jnp.sum(jnp.where(mine[:, :, None] == stack[None, None, :], levels, 0), 2)
    source = jnp.where(mine >= first, in_row, before)
    source = jnp.clip(jnp.where(mine >= 0, source, 0), 0, 4 * CHIPS - 1)
    target = jnp.where(mine >= first, in_row, 2 * CHIPS + CHIPS - 1 - rank - chip)
    target = jnp.clip(jnp.where(mine >= 0, target, 0), 0, 3 * CHIPS - 1)
    own = jnp.stack([core, 1 - core])[:, None]
    source = jnp.concatenate([own, source], 1).reshape(-1)
    target = jnp.concatenate([own, target], 1).reshape(-1)
    held = jnp.stack([CHIPS - 1 - chip, CHIPS - chip, jnp.where(chip == 2, CHIPS - 1, CHIPS)])
    node = jnp.sum(jnp.where(held[:, None] == levels[None, :], relay[None, :], 0), 1)
    here = (held < LEVELS) & (node >= first) & ((node - first) // CORES == chip)
    land = jnp.where(here, node % CORES, CORES)
    table = jnp.concatenate(
        [source, (elder[0] >= 0).astype(jnp.int32), target, land, core[None]]
    ).astype(jnp.int32)
    slot_depth = own_depth[0] - jnp.arange(SLOTS, dtype=jnp.int32)
    pair_depth = jnp.where(core == 0, own_depth[:2], own_depth[1::-1])
    return table, slot_depth, pair_depth


def angles_of(depth):
    frequency = jnp.exp(jnp.arange(HALF, dtype=F32) * (-2.0 * math.log(BASE) / HD))
    position = (depth[:, None] * TOK + jnp.arange(TOK, dtype=jnp.int32)[None, :]).reshape(-1)
    return position.astype(F32)[:, None] * frequency[None, :]


def turn(block, cosine, sine):
    first, second = block[:, :HALF], block[:, HALF:]
    return jnp.concatenate(
        [first * cosine - second * sine, second * cosine + first * sine], -1
    )


def fetch(code, sources, target, sem):
    for k, ref in enumerate(sources):
        for half in range(CORES):

            @pl.when(code == CORES * k + half)
            def _(ref=ref, half=half):
                pltpu.make_async_copy(ref.at[pl.ds(half * TOK, TOK)], target, sem).start()


def await_fetch(sources, target, sem):
    pltpu.make_async_copy(sources[0].at[pl.ds(0, TOK)], target, sem).wait()


def pick_kernel(table, *refs):
    sources, (o_ref, sem) = refs[:-2], refs[-2:]
    for i in range(SLOTS):
        fetch(table[OTHER + i], sources, o_ref.at[pl.ds(i * TOK, TOK)], sem.at[i])
    for i in range(SLOTS):
        await_fetch(sources, o_ref.at[pl.ds(i * TOK, TOK)], sem.at[i])


def call_pick(table, sources):
    return pl.pallas_call(
        pick_kernel,
        compiler_params=room(4),
        out_shape=jax.ShapeDtypeStruct((KEYS, HD), BF16),
        in_specs=[SMEM] + [ANY] * len(sources),
        out_specs=VMEM,
        scratch_shapes=[pltpu.SemaphoreType.DMA((SLOTS,))],
    )(table, *sources)


NT = (((1,), (1,)), ((), ()))
NN = (((1,), (0,)), ((), ()))
TN = (((0,), (0,)), ((), ()))


def dot(a, b, dims):
    return lax.dot_general(a, b, dims, preferred_element_type=F32)


def attend_kernel(table, qg_ref, cos_ref, sin_ref, other_ref, *refs):
    sources = refs[: 2 * CHIPS]
    out_ref, keep_ref, give_ref = refs[2 * CHIPS : 2 * CHIPS + 3]
    mine_ref, keys, vals, q_all, low_all, score_all, sem = refs[2 * CHIPS + 3 :]
    for i in range(SLOTS):
        fetch(table[OWN + i], sources, mine_ref.at[pl.ds(i * TOK, TOK)], sem.at[i])
    for h in range(2):
        q_all[h * TOK : (h + 1) * TOK, :] = turn(
            qg_ref[:, h * HD : (h + 1) * HD].astype(F32), cos_ref[:TOK, :], sin_ref[:TOK, :]
        ).astype(BF16)
    is_key = table[CORE] == 0
    for i in range(SLOTS):
        here = slice(i * TOK, (i + 1) * TOK)
        await_fetch(sources, mine_ref.at[pl.ds(i * TOK, TOK)], sem.at[i])
        mine, other = mine_ref[here, :], other_ref[here, :]
        keys[here, :] = turn(
            jnp.where(is_key, mine, other).astype(F32), cos_ref[here, :], sin_ref[here, :]
        ).astype(BF16)
        vals[here, :] = jnp.where(is_key, other, mine)
    scaling = HD**-0.5
    earlier = lax.broadcasted_iota(jnp.int32, (TOK, TOK), 1) <= lax.broadcasted_iota(
        jnp.int32, (TOK, TOK), 0
    )
    last = SLOTS - 1
    block = lambda ref, i: ref[i * TOK : (i + 1) * TOK, :]
    for h in range(2):
        rows = slice(h * TOK, (h + 1) * TOK)
        q, g = q_all[rows, :], qg_ref[:, WIDE + h * HD : WIDE + (h + 1) * HD]

        def joint(a, which, fill):
            parts = [dot(a, block(which, i), NT) for i in range(SLOTS)]
            if fill is None:
                return [jnp.where(earlier, parts[0], parts[last])] + parts[1:last]
            parts = [parts[0] * scaling] + [
                jnp.where(table[SEEN + i - 1] > 0, parts[i] * scaling, fill)
                for i in range(1, SLOTS)
            ]
            return [jnp.where(earlier, parts[0], parts[last])] + parts[1:last]

        scores = joint(q, keys, -1e30)
        top = functools.reduce(jnp.maximum, scores)
        top = jnp.max(top, -1, keepdims=True)
        raw = [jnp.exp(s - top) for s in scores]
        share = 1.0 / jnp.sum(functools.reduce(jnp.add, raw), -1, keepdims=True)
        probs = [r * share for r in raw]
        grads = joint(g, vals, None)
        delta = functools.reduce(jnp.add, [p * d for p, d in zip(probs, grads)])
        delta = jnp.sum(delta, -1, keepdims=True)
        for ref, parts in (
            (low_all, probs),
            (score_all, [p * (d - delta) * scaling for p, d in zip(probs, grads)]),
        ):
            ref[rows, :TOK] = jnp.where(earlier, parts[0], 0.0).astype(BF16)
            ref[rows, last * TOK :] = jnp.where(earlier, 0.0, parts[0]).astype(BF16)
            for i in range(1, last):
                ref[rows, i * TOK : (i + 1) * TOK] = parts[i].astype(BF16)
        out_ref[:, h * HD : (h + 1) * HD] = dot(low_all[rows, :], vals[...], NN).astype(BF16)
        out_ref[:, WIDE + h * HD : WIDE + (h + 1) * HD] = turn(
            dot(score_all[rows, :], keys[...], NN), cos_ref[:TOK, :], -sin_ref[:TOK, :]
        ).astype(BF16)
    for i in range(SLOTS):
        cols = slice(i * TOK, (i + 1) * TOK)
        part_key = dot(score_all[:, cols], q_all[...], TN)
        part_value = dot(low_all[:TOK, cols], qg_ref[:, WIDE : WIDE + HD], TN) + dot(
            low_all[TOK:, cols], qg_ref[:, WIDE + HD :], TN
        )
        keep_ref[cols, :] = jnp.where(is_key, part_key, part_value).astype(BF16)
        give_ref[cols, :] = jnp.where(is_key, part_value, part_key).astype(BF16)


def call_attend(table, query_grad, cosine, sine, other, sources):
    return pl.pallas_call(
        attend_kernel,
        compiler_params=room(24),
        out_shape=(
            jax.ShapeDtypeStruct((TOK, 2 * WIDE), BF16),
            jax.ShapeDtypeStruct((KEYS, HD), BF16),
            jax.ShapeDtypeStruct((KEYS, HD), BF16),
        ),
        in_specs=[SMEM] + [VMEM] * 4 + [ANY] * len(sources),
        out_specs=(VMEM,) * 3,
        scratch_shapes=[
            pltpu.VMEM((KEYS, HD), BF16),
            pltpu.VMEM((KEYS, HD), BF16),
            pltpu.VMEM((KEYS, HD), BF16),
            pltpu.VMEM((2 * TOK, HD), BF16),
            pltpu.VMEM((2 * TOK, KEYS), BF16),
            pltpu.VMEM((2 * TOK, KEYS), BF16),
            pltpu.SemaphoreType.DMA((SLOTS,)),
        ],
    )(table, query_grad, cosine, sine, other, *sources)


def spread_kernel(table, keep_ref, got_ref, *refs):
    outs, total = refs[:-1], refs[-1]
    total[...] = jnp.zeros_like(total)
    for source, offset in ((keep_ref, GOES), (got_ref, COMES)):
        for i in range(SLOTS):
            at = pl.ds(pl.multiple_of(table[offset + i] * TOK, TOK), TOK)
            total[at, :] += source[i * TOK : (i + 1) * TOK, :].astype(F32)
    for k in range(CHIPS):
        outs[k][...] = total[k * PAIR : (k + 1) * PAIR, :].astype(outs[k].dtype)
        low = CHIPS * PAIR + k * TOK
        outs[CHIPS + k][...] = total[low : low + TOK, :].astype(BF16)


def call_spread(table, keep, got):
    return pl.pallas_call(
        spread_kernel,
        compiler_params=room(12),
        out_shape=tuple(
            [jax.ShapeDtypeStruct((PAIR, HD), F32)]
            + [jax.ShapeDtypeStruct((PAIR, HD), BF16)] * (CHIPS - 1)
            + [jax.ShapeDtypeStruct((TOK, HD), BF16)] * CHIPS
        ),
        in_specs=[SMEM, VMEM, VMEM],
        out_specs=(VMEM,) * (2 * CHIPS),
        scratch_shapes=[pltpu.VMEM((CHIPS * PAIR + CHIPS * TOK, HD), F32)],
    )(table, keep, got)


def sum_kernel(*refs):
    total = refs[0][...].astype(F32)
    for ref in refs[1:-1]:
        total = total + ref[...].astype(F32)
    refs[-1][...] = total.astype(refs[-1].dtype)


def call_sum(parts, dtype):
    return pl.pallas_call(
        sum_kernel,
        compiler_params=room(6),
        out_shape=jax.ShapeDtypeStruct(parts[0].shape, dtype),
        in_specs=[VMEM] * len(parts),
        out_specs=VMEM,
    )(*parts)


def close_kernel(table, own_ref, *refs):
    backs = refs[:-4]
    cos_ref, sin_ref, o_ref, total = refs[-4:]
    total[...] = own_ref[...]
    for k, back in enumerate(backs):
        code = table[LAND + k]

        @pl.when(code < CORES)
        def _(back=back, code=code):
            at = pl.ds(pl.multiple_of(code * TOK, TOK), TOK)
            total[at, :] += back[...].astype(F32)

    is_key = table[CORE] == 0

    @pl.when(is_key)
    def _():
        o_ref[...] = turn(total[...], cos_ref[...], -sin_ref[...]).astype(BF16)

    @pl.when(jnp.logical_not(is_key))
    def _():
        o_ref[...] = total[...].astype(BF16)


def call_close(table, own, backs, cosine, sine):
    return pl.pallas_call(
        close_kernel,
        compiler_params=room(8),
        out_shape=jax.ShapeDtypeStruct((PAIR, HD), BF16),
        in_specs=[SMEM] + [VMEM] * (3 + len(backs)),
        out_specs=VMEM,
        scratch_shapes=[pltpu.VMEM((PAIR, HD), F32)],
    )(table, own, *backs, cosine, sine)


def along(block, shift, starts=range(CHIPS)):
    return lax.ppermute(
        block, "chip", [(i, i + shift) for i in starts if 0 <= i + shift < CHIPS]
    )


def next_row(block, shift):
    rows = lax.axis_size("row")
    return lax.ppermute(
        block, "row", [(i, i + shift) for i in range(rows) if 0 <= i + shift < rows]
    )


def swap(block):
    return lax.ppermute(block, "core", [(0, 1), (1, 0)])


def shards(queries, keys, values, grad_attn, parent_gap):
    row, chip, core = (lax.axis_index(name) for name in ("row", "chip", "core"))
    tokens = queries.shape[0]
    both = lax.all_to_all(
        jnp.concatenate([keys, values], 1),
        ("core", "head"),
        split_axis=1,
        concat_axis=0,
        tiled=True,
    )
    table, slot_depth, pair_depth = plan(parent_gap, row, chip, core)
    slot_angles, pair_angles = angles_of(slot_depth), angles_of(pair_depth)
    slot_cos, slot_sin = jnp.cos(slot_angles), jnp.sin(slot_angles)
    pair_cos, pair_sin = jnp.cos(pair_angles), jnp.sin(pair_angles)
    table, slot_cos, slot_sin, pair_cos, pair_sin = lax.optimization_barrier(
        (table, slot_cos, slot_sin, pair_cos, pair_sin)
    )

    relay = next_row(both, 1)
    sources = [both] + [along(both, k) for k in (1, 2, 3)]
    query_grad = jnp.concatenate(
        [queries.reshape(tokens, HEADS, WIDE), grad_attn.reshape(tokens, HEADS, WIDE)], 2
    ).reshape(tokens, HEADS * 2 * WIDE)
    query_grad = lax.all_to_all(query_grad, "head", split_axis=1, concat_axis=0, tiled=True)
    sources += [relay] + [along(relay, -k) for k in (1, 2, 3)]
    other = swap(call_pick(table, sources))
    out, keep, give = call_attend(table, query_grad, slot_cos, slot_sin, other, sources)
    got = swap(give)
    out = lax.all_to_all(out, "head", split_axis=0, concat_axis=1, tiled=True)
    out = out.reshape(tokens, HEADS, 2, WIDE)
    attended = out[:, :, 0].reshape(tokens, HEADS * WIDE)
    grad_query = out[:, :, 1].reshape(tokens, HEADS * WIDE)
    spread = call_spread(table, keep, got)
    own, within, stack = spread[0], spread[1:CHIPS], spread[CHIPS:]
    stack_sum = call_sum([stack[0]] + [along(stack[k], k) for k in (1, 2, 3)], BF16)
    back = next_row(stack_sum, -1)
    own = call_sum([own] + [along(within[k - 1], -k) for k in (1, 2, 3)], F32)
    backs = [back, along(back, 1), along(back, 2, (0,))]
    grad_both = call_close(table, own, backs, pair_cos, pair_sin)
    grad_both = lax.all_to_all(grad_both, ("core", "head"), split_axis=0, concat_axis=1, tiled=True)
    half = HEADS * HD
    return attended, grad_query, grad_both[:, :half], grad_both[:, half:]


def solution(mesh):
    devices = mesh.devices
    rows = devices.shape[0] // ROW
    split = Mesh(
        devices.reshape(rows, CHIPS, CORES, devices.shape[1]), ("row", "chip", "core", "head")
    )
    spec = P(("row", "chip", "core", "head"), None)

    return jax.shard_map(
        shards,
        mesh=split,
        in_specs=(spec, spec, spec, spec, P()),
        out_specs=(spec, spec, spec, spec),
        check_vma=False,
    )
```

time: 196 us -> 158 us (0.81)
  the two profiles are of different devices: /device:TPU:25 before, /device:TPU:31 now
where the time goes in v2:
time: 158 us; the launch traced here: 157 us
  starting transfers between devices  91.4 us (58%)
  waiting for transfers between devices  36.1 us (23%)
  Pallas kernels  11.1 us (7%)
  local copies, waits for them, and re-layouts  10.1 us (6%)
  other arithmetic  7.77 us (5%)
    ppermute x14, starting transfers between devices, along(): lax.ppermute(block, 'chip', [(i, i + shift) for i in starts if 0 <= i + s...  32 us
    all_to_all x1, starting transfers between devices, shards(): out = lax.all_to_all(out, 'head', split_axis=0, concat_axis=1, tiled=True)  19.3 us
    all_to_all x1, starting transfers between devices, shards(): lax.all_to_all(grad_both, ('core', 'head'), split_axis=0, concat_axis=1,...  13.2 us
    ppermute x2, waiting for transfers between devices, next_row(): lax.ppermute(block, 'row', [(i, i + shift) for i in range(rows) if 0 <= i...  12 us
    ppermute x14, waiting for transfers between devices, along(): lax.ppermute(block, 'chip', [(i, i + shift) for i in starts if 0 <= i + s...  11.4 us
    ppermute x2, starting transfers between devices, next_row(): lax.ppermute(block, 'row', [(i, i + shift) for i in range(rows) if 0 <= i...  10.4 us
    all_to_all x1, starting transfers between devices, shards(): lax.all_to_all(jnp.concatenate([keys, values], 1), ('core', 'head'), spli...  6.7 us
    unnamed x27, local copies, waits for them, and re-layouts  6.42 us
  transfers between devices with their start and end apart: 22, of which 10 were waited for; matrix products, arithmetic and copies ran while one was open for 7% of the time, Pallas kernels for 3%

profile of v2, /device:TPU:31, one launch (start us, length us, event | category | flops | bytes accessed | tf_op | source)
XLA Modules:
  0.0 157.5 jit_solution(9507537059899964312)
XLA Ops:
  2.3 6.7 %all-to-all-start.1 = ((bf16[64,8,256]{2,0,1:T(8,128)(2,1)}), bf16[64,8,256]{2,0,1:T(8,128)(2,1)S(1)}, u32[]{:S(2)}, u32[]{:S(2)}) async-start(bf16[64,8,256]{2,0,1:T(8,128)(2,1)} %bitcast.52), calls=%async_computation.1 | async-start | bytes 524288 | tf_op jit(solution)/shard_map/all_to_all | solution.py:328
  12.8 2.3 %multiply_sine_fusion = (f32[1280,128]{1,0:T(8,128)S(1)}, f32[1280,128]{1,0:T(8,128)S(1)}) fusion(f32[128]{0:T(128)S(1)} %multiply_exponential_fusion, f32[1280]{0:T(1024)S(1)} %convert_element_type.41), kind=kLoop, calls=%fused_computation | loop fusion | flops 163840 | bytes 1316352 | tf_op jit(solution)/shard_map/sin | solution.py:337
  15.1 3.0 %all-to-all-done.1 = bf16[64,8,256]{2,0,1:T(8,128)(2,1)S(1)} async-done(((bf16[64,8,256]{2,0,1:T(8,128)(2,1)}), bf16[64,8,256]{2,0,1:T(8,128)(2,1)S(1)}, u32[]{:S(2)}, u32[]{:S(2)}) %all-to-all-start.1) | async-done | bytes 262176 | tf_op jit(solution)/shard_map/all_to_all | solution.py:328
  18.1 3.5 %all-to-all-start = ((bf16[64,4,1024]{2,0,1:T(8,128)(2,1)}), bf16[64,4,1024]{2,0,1:T(8,128)(2,1)S(1)}, u32[]{:S(2)}, u32[]{:S(2)}) async-start(bf16[64,4,1024]{2,0,1:T(8,128)(2,1)} %pad_maximum_fusion), calls=%async_computation | async-start | bytes 1048576 | tf_op jit(solution)/shard_map/all_to_all | solution.py:348
  22.9 8.5 %collective-permute-start.3 = (bf16[512,256]{1,0:T(8,128)(2,1)S(1)}, bf16[512,256]{1,0:T(8,128)(2,1)S(1)}, u32[]{:S(2)}, u32[]{:S(2)}) collective-permute-start(bf16[512,256]{1,0:T(8,128)(2,1)S(1)} %bitcast.55), channel_id=1, source_target_pairs={{0,32},{32,64},{64,96},{96,128},{128,160},{160,192},{192,224},{224... | collective-permute-start | bytes 786440 | tf_op jit(solution)/shard_map/ppermute | solution.py:316
  36.9 5.1 %collective-permute-start.6 = (bf16[512,256]{1,0:T(8,128)(2,1)S(1)}, bf16[512,256]{1,0:T(8,128)(2,1)S(1)}, u32[]{:S(2)}, u32[]{:S(2)}) collective-permute-start(bf16[512,256]{1,0:T(8,128)(2,1)S(1)} %collective-permute-done.3.refs_4_), channel_id=1, source_target_pairs={{24,0},{25,1},{26,2},{27,3},{28,4},{29,5},{30,6},{31,7},{56,32},{5... | collective-permute-start | bytes 786440 | tf_op jit(solution)/shard_map/ppermute | solution.py:309
  42.0 2.0 %collective-permute-start.5 = (bf16[512,256]{1,0:T(8,128)(2,1)S(1)}, bf16[512,256]{1,0:T(8,128)(2,1)}, u32[]{:S(2)}, u32[]{:S(2)}) collective-permute-start(bf16[512,256]{1,0:T(8,128)(2,1)S(1)} %collective-permute-done.3.refs_4_), channel_id=1, source_target_pairs={{16,0},{24,8},{17,1},{25,9},{18,2},{26,10},{19,3},{27,11},{20,4},{... | collective-permute-start | bytes 786440 | tf_op jit(solution)/shard_map/ppermute | solution.py:309
  44.0 3.4 %collective-permute-done.2.refs_3_ = bf16[512,256]{1,0:T(8,128)(2,1)S(1)} collective-permute-done((bf16[512,256]{1,0:T(8,128)(2,1)S(1)}, bf16[512,256]{1,0:T(8,128)(2,1)S(1)}, u32[]{:S(2)}, u32[]{:S(2)}) %collective-permute-start.2) | collective-permute-done | bytes 262176 | tf_op jit(solution)/shard_map/ppermute | solution.py:309
  47.4 2.0 %collective-permute-start.4 = (bf16[512,256]{1,0:T(8,128)(2,1)S(1)}, bf16[512,256]{1,0:T(8,128)(2,1)}, u32[]{:S(2)}, u32[]{:S(2)}) collective-permute-start(bf16[512,256]{1,0:T(8,128)(2,1)S(1)} %collective-permute-done.3.refs_4_), channel_id=1, source_target_pairs={{8,0},{16,8},{24,16},{9,1},{17,9},{25,17},{10,2},{18,10},{26,18},{... | collective-permute-start | bytes 786440 | tf_op jit(solution)/shard_map/ppermute | solution.py:309
  49.7 1.8 %multiply_sine_fusion.1 = (f32[512,128]{1,0:T(8,128)}, f32[512,128]{1,0:T(8,128)}) fusion(f32[128]{0:T(128)S(1)} %multiply_exponential_fusion, f32[512]{0:T(512)S(1)} %bitcast.73), kind=kLoop, calls=%fused_computation.3 | loop fusion | flops 65536 | bytes 526848 | tf_op jit(solution)/shard_map/sin | solution.py:338
  53.6 2.6 %shard_map.84 = bf16[1280,256]{1,0:T(8,128)(2,1)} custom-call(s32[28]{0:T(128)S(1)} %concatenate.21.table, bf16[512,256]{1,0:T(8,128)(2,1)S(1)} %bitcast.59, bf16[512,256]{1,0:T(8,128)(2,1)S(1)} %collective-permute-done.refs_1_, bf16[512,256]{1,0:T(8,128)(2,1)S(1)} %collective-permute-done.1.refs_2_, bf16[512,256]{1,0:T(8,128)(2,1)S(1)} %collective-permute-done.2.refs_3_, ...), custom_call_target="tpu_custom_call" | custom-call | tf_op jit(solution)/shard_map/pallas_call | solution.py:117
  56.3 3.7 %collective-permute-start.7 = (bf16[1280,256]{1,0:T(8,128)(2,1)}, bf16[1280,256]{1,0:T(8,128)(2,1)}, u32[]{:S(2)}, u32[]{:S(2)}) collective-permute-start(bf16[1280,256]{1,0:T(8,128)(2,1)} %shard_map.84), channel_id=1, source_target_pairs={{0,4},{4,0},{1,5},{5,1},{2,6},{6,2},{3,7},{7,3},{8,12},{12,8},{9,1... | collective-permute-start | bytes 1966088 | tf_op jit(solution)/shard_map/ppermute | solution.py:322
  60.0 2.0 %collective-permute-done.7.other_ref = bf16[1280,256]{1,0:T(8,128)(2,1)} collective-permute-done((bf16[1280,256]{1,0:T(8,128)(2,1)}, bf16[1280,256]{1,0:T(8,128)(2,1)}, u32[]{:S(2)}, u32[]{:S(2)}) %collective-permute-start.7) | collective-permute-done | bytes 655392 | tf_op jit(solution)/shard_map/ppermute | solution.py:322
  62.0 5.8 %shard_map.85 = (bf16[256,1024]{1,0:T(8,128)(2,1)S(1)}, bf16[1280,256]{1,0:T(8,128)(2,1)S(1)}, bf16[1280,256]{1,0:T(8,128)(2,1)S(1)}) custom-call(s32[28]{0:T(128)S(1)} %concatenate.21.table, bf16[256,1024]{1,0:T(8,128)(2,1)S(1)} %bitcast.61, f32[1280,128]{1,0:T(8,128)S(1)} %get-tuple-element.21.cos_ref, f32[1280,128]{1,0:T(8,128)S(1)} %get-tuple-element.22.sin_ref, ...), custom_call_target="tpu_custom_call" | custom-call | tf_op jit(solution)/shard_map/pallas_call | solution.py:207
  70.4 19.3 %all-to-all-start.2 = ((bf16[4,64,1024]{2,1,0:T(8,128)(2,1)}), bf16[4,64,1024]{2,1,0:T(8,128)(2,1)S(1)}, u32[]{:S(2)}, u32[]{:S(2)}) async-start(bf16[4,64,1024]{2,1,0:T(8,128)(2,1)} %bitcast.62), calls=%async_computation.2 | async-start | bytes 1048576 | tf_op jit(solution)/shard_map/all_to_all | solution.py:353
  89.7 2.5 %collective-permute-start.8 = (bf16[1280,256]{1,0:T(8,128)(2,1)}, bf16[1280,256]{1,0:T(8,128)(2,1)S(1)}, u32[]{:S(2)}, u32[]{:S(2)}) collective-permute-start(bf16[1280,256]{1,0:T(8,128)(2,1)} %copy-done.5), channel_id=1, source_target_pairs={{0,4},{4,0},{1,5},{5,1},{2,6},{6,2},{3,7},{7,3},{8,12},{12,8},{9,1... | collective-permute-start | bytes 1966088 | tf_op jit(solution)/shard_map/ppermute | solution.py:322
  92.2 1.9 %collective-permute-done.8.got_ref = bf16[1280,256]{1,0:T(8,128)(2,1)S(1)} collective-permute-done((bf16[1280,256]{1,0:T(8,128)(2,1)}, bf16[1280,256]{1,0:T(8,128)(2,1)S(1)}, u32[]{:S(2)}, u32[]{:S(2)}) %collective-permute-start.8) | collective-permute-done | bytes 655392 | tf_op jit(solution)/shard_map/ppermute | solution.py:322
  99.2 5.2 %collective-permute-start.9 = (bf16[512,256]{1,0:T(8,128)(2,1)S(1)}, bf16[512,256]{1,0:T(8,128)(2,1)S(1)}, u32[]{:S(2)}, u32[]{:S(2)}) collective-permute-start(bf16[512,256]{1,0:T(8,128)(2,1)S(1)} %get-tuple-element.27), channel_id=1, source_target_pairs={{8,0},{16,8},{24,16},{9,1},{17,9},{25,17},{10,2},{18,10},{26,18},{... | collective-permute-start | bytes 786440 | tf_op jit(solution)/shard_map/ppermute | solution.py:309
  104.4 6.7 %collective-permute-start.10 = (bf16[512,256]{1,0:T(8,128)(2,1)S(1)}, bf16[512,256]{1,0:T(8,128)(2,1)S(1)}, u32[]{:S(2)}, u32[]{:S(2)}) collective-permute-start(bf16[512,256]{1,0:T(8,128)(2,1)S(1)} %get-tuple-element.28), channel_id=1, source_target_pairs={{16,0},{24,8},{17,1},{25,9},{18,2},{26,10},{19,3},{27,11},{20,4},{... | collective-permute-start | bytes 786440 | tf_op jit(solution)/shard_map/ppermute | solution.py:309
  112.6 1.9 %collective-permute-start.15 = (bf16[256,256]{1,0:T(8,128)(2,1)S(1)}, bf16[256,256]{1,0:T(8,128)(2,1)S(1)}, u32[]{:S(2)}, u32[]{:S(2)}) collective-permute-start(bf16[256,256]{1,0:T(8,128)(2,1)S(1)} %shard_map.88), channel_id=1, source_target_pairs={{32,0},{64,32},{96,64},{128,96},{160,128},{192,160},{224,192},{256... | collective-permute-start | bytes 393224 | tf_op jit(solution)/shard_map/ppermute | solution.py:316
  114.5 10.7 %collective-permute-done.15.refs_0_ = bf16[256,256]{1,0:T(8,128)(2,1)S(1)} collective-permute-done((bf16[256,256]{1,0:T(8,128)(2,1)S(1)}, bf16[256,256]{1,0:T(8,128)(2,1)S(1)}, u32[]{:S(2)}, u32[]{:S(2)}) %collective-permute-start.15) | collective-permute-done | bytes 131104 | tf_op jit(solution)/shard_map/ppermute | solution.py:316
  127.3 5.8 %collective-permute-done.16.refs_1_ = bf16[256,256]{1,0:T(8,128)(2,1)S(1)} collective-permute-done((bf16[256,256]{1,0:T(8,128)(2,1)S(1)}, bf16[256,256]{1,0:T(8,128)(2,1)S(1)}, u32[]{:S(2)}, u32[]{:S(2)}) %collective-permute-start.16) | collective-permute-done | bytes 131104 | tf_op jit(solution)/shard_map/ppermute | solution.py:309
  134.5 13.2 %all-to-all-start.3 = ((bf16[8,64,256]{2,1,0:T(8,128)(2,1)}), bf16[8,64,256]{2,1,0:T(8,128)(2,1)S(1)}, u32[]{:S(2)}, u32[]{:S(2)}) async-start(bf16[8,64,256]{2,1,0:T(8,128)(2,1)} %bitcast.21), calls=%async_computation.3 | async-start | bytes 524288 | tf_op jit(solution)/shard_map/all_to_all | solution.py:364
  151.0 5.7 %all-to-all-done.3 = bf16[8,64,256]{2,1,0:T(8,128)(2,1)S(1)} async-done(((bf16[8,64,256]{2,1,0:T(8,128)(2,1)}), bf16[8,64,256]{2,1,0:T(8,128)(2,1)S(1)}, u32[]{:S(2)}, u32[]{:S(2)}) %all-to-all-start.3) | async-done | bytes 262176 | tf_op jit(solution)/shard_map/all_to_all | solution.py:364
  (94 shorter events, 31.0 us)
Async XLA Ops:
  2.3 9.3 %copy-start.7 = (bf16[64,2048]{1,0:T(8,128)(2,1)S(1)}, bf16[64,2048]{1,0:T(8,128)(2,1)}, u32[]{:S(2)}) copy-start(bf16[64,2048]{1,0:T(8,128)(2,1)} %param.5) | copy-start | bytes 786436
  2.3 15.7 %all-to-all-start.1 = ((bf16[64,8,256]{2,0,1:T(8,128)(2,1)}), bf16[64,8,256]{2,0,1:T(8,128)(2,1)S(1)}, u32[]{:S(2)}, u32[]{:S(2)}) async-start(bf16[64,8,256]{2,0,1:T(8,128)(2,1)} %bitcast.52), calls=%async_computation.1 | async-start | bytes 524288 | tf_op jit(solution)/shard_map/all_to_all | solution.py:328
  18.1 41.9 %all-to-all-start = ((bf16[64,4,1024]{2,0,1:T(8,128)(2,1)}), bf16[64,4,1024]{2,0,1:T(8,128)(2,1)S(1)}, u32[]{:S(2)}, u32[]{:S(2)}) async-start(bf16[64,4,1024]{2,0,1:T(8,128)(2,1)} %pad_maximum_fusion), calls=%async_computation | async-start | bytes 1048576 | tf_op jit(solution)/shard_map/all_to_all | solution.py:348
  22.9 13.9 %collective-permute-start.3 = (bf16[512,256]{1,0:T(8,128)(2,1)S(1)}, bf16[512,256]{1,0:T(8,128)(2,1)S(1)}, u32[]{:S(2)}, u32[]{:S(2)}) collective-permute-start(bf16[512,256]{1,0:T(8,128)(2,1)S(1)} %bitcast.55), channel_id=1, source_target_pairs={{0,32},{32,64},{64,96},{96,128},{128,160},{160,192},{192,224},{224... | collective-permute-start | bytes 786440 | tf_op jit(solution)/shard_map/ppermute | solution.py:316
  31.4 16.0 %collective-permute-start.2 = (bf16[512,256]{1,0:T(8,128)(2,1)S(1)}, bf16[512,256]{1,0:T(8,128)(2,1)S(1)}, u32[]{:S(2)}, u32[]{:S(2)}) collective-permute-start(bf16[512,256]{1,0:T(8,128)(2,1)S(1)} %bitcast.56), channel_id=1, source_target_pairs={{0,24},{1,25},{2,26},{3,27},{4,28},{5,29},{6,30},{7,31},{32,56},{3... | collective-permute-start | bytes 786440 | tf_op jit(solution)/shard_map/ppermute | solution.py:309
  32.9 18.6 %collective-permute-start.1 = (bf16[512,256]{1,0:T(8,128)(2,1)S(1)}, bf16[512,256]{1,0:T(8,128)(2,1)S(1)}, u32[]{:S(2)}, u32[]{:S(2)}) collective-permute-start(bf16[512,256]{1,0:T(8,128)(2,1)S(1)} %bitcast.57), channel_id=1, source_target_pairs={{0,16},{8,24},{1,17},{9,25},{2,18},{10,26},{3,19},{11,27},{4,20},{... | collective-permute-start | bytes 786440 | tf_op jit(solution)/shard_map/ppermute | solution.py:309
  34.2 17.3 %collective-permute-start = (bf16[512,256]{1,0:T(8,128)(2,1)S(1)}, bf16[512,256]{1,0:T(8,128)(2,1)S(1)}, u32[]{:S(2)}, u32[]{:S(2)}) collective-permute-start(bf16[512,256]{1,0:T(8,128)(2,1)S(1)} %bitcast.58), channel_id=1, source_target_pairs={{0,8},{8,16},{16,24},{1,9},{9,17},{17,25},{2,10},{10,18},{18,26},{... | collective-permute-start | bytes 786440 | tf_op jit(solution)/shard_map/ppermute | solution.py:309
  36.9 15.2 %collective-permute-start.6 = (bf16[512,256]{1,0:T(8,128)(2,1)S(1)}, bf16[512,256]{1,0:T(8,128)(2,1)S(1)}, u32[]{:S(2)}, u32[]{:S(2)}) collective-permute-start(bf16[512,256]{1,0:T(8,128)(2,1)S(1)} %collective-permute-done.3.refs_4_), channel_id=1, source_target_pairs={{24,0},{25,1},{26,2},{27,3},{28,4},{29,5},{30,6},{31,7},{56,32},{5... | collective-permute-start | bytes 786440 | tf_op jit(solution)/shard_map/ppermute | solution.py:309
  42.0 10.1 %collective-permute-start.5 = (bf16[512,256]{1,0:T(8,128)(2,1)S(1)}, bf16[512,256]{1,0:T(8,128)(2,1)}, u32[]{:S(2)}, u32[]{:S(2)}) collective-permute-start(bf16[512,256]{1,0:T(8,128)(2,1)S(1)} %collective-permute-done.3.refs_4_), channel_id=1, source_target_pairs={{16,0},{24,8},{17,1},{25,9},{18,2},{26,10},{19,3},{27,11},{20,4},{... | collective-permute-start | bytes 786440 | tf_op jit(solution)/shard_map/ppermute | solution.py:309
  47.4 6.2 %collective-permute-start.4 = (bf16[512,256]{1,0:T(8,128)(2,1)S(1)}, bf16[512,256]{1,0:T(8,128)(2,1)}, u32[]{:S(2)}, u32[]{:S(2)}) collective-permute-start(bf16[512,256]{1,0:T(8,128)(2,1)S(1)} %collective-permute-done.3.refs_4_), channel_id=1, source_target_pairs={{8,0},{16,8},{24,16},{9,1},{17,9},{25,17},{10,2},{18,10},{26,18},{... | collective-permute-start | bytes 786440 | tf_op jit(solution)/shard_map/ppermute | solution.py:309
  56.3 5.8 %collective-permute-start.7 = (bf16[1280,256]{1,0:T(8,128)(2,1)}, bf16[1280,256]{1,0:T(8,128)(2,1)}, u32[]{:S(2)}, u32[]{:S(2)}) collective-permute-start(bf16[1280,256]{1,0:T(8,128)(2,1)} %shard_map.84), channel_id=1, source_target_pairs={{0,4},{4,0},{1,5},{5,1},{2,6},{6,2},{3,7},{7,3},{8,12},{12,8},{9,1... | collective-permute-start | bytes 1966088 | tf_op jit(solution)/shard_map/ppermute | solution.py:322
  70.4 23.8 %copy-start.3 = (bf16[1280,256]{1,0:T(8,128)(2,1)S(1)}, bf16[1280,256]{1,0:T(8,128)(2,1)}, u32[]{:S(2)}) copy-start(bf16[1280,256]{1,0:T(8,128)(2,1)} %copy-done.2) | copy-start | bytes 1966084
  70.4 64.1 %all-to-all-start.2 = ((bf16[4,64,1024]{2,1,0:T(8,128)(2,1)}), bf16[4,64,1024]{2,1,0:T(8,128)(2,1)S(1)}, u32[]{:S(2)}, u32[]{:S(2)}) async-start(bf16[4,64,1024]{2,1,0:T(8,128)(2,1)} %bitcast.62), calls=%async_computation.2 | async-start | bytes 1048576 | tf_op jit(solution)/shard_map/all_to_all | solution.py:353
  89.7 4.5 %collective-permute-start.8 = (bf16[1280,256]{1,0:T(8,128)(2,1)}, bf16[1280,256]{1,0:T(8,128)(2,1)S(1)}, u32[]{:S(2)}, u32[]{:S(2)}) collective-permute-start(bf16[1280,256]{1,0:T(8,128)(2,1)} %copy-done.5), channel_id=1, source_target_pairs={{0,4},{4,0},{1,5},{5,1},{2,6},{6,2},{3,7},{7,3},{8,12},{12,8},{9,1... | collective-permute-start | bytes 1966088 | tf_op jit(solution)/shard_map/ppermute | solution.py:322
  95.3 15.8 %collective-permute-start.12 = (bf16[256,256]{1,0:T(8,128)(2,1)S(1)}, bf16[256,256]{1,0:T(8,128)(2,1)S(1)}, u32[]{:S(2)}, u32[]{:S(2)}) collective-permute-start(bf16[256,256]{1,0:T(8,128)(2,1)S(1)} %get-tuple-element.31), channel_id=1, source_target_pairs={{0,8},{8,16},{16,24},{1,9},{9,17},{17,25},{2,10},{10,18},{18,26},{... | collective-permute-start | bytes 393224 | tf_op jit(solution)/shard_map/ppermute | solution.py:309
  96.6 15.9 %collective-permute-start.13 = (bf16[256,256]{1,0:T(8,128)(2,1)S(1)}, bf16[256,256]{1,0:T(8,128)(2,1)S(1)}, u32[]{:S(2)}, u32[]{:S(2)}) collective-permute-start(bf16[256,256]{1,0:T(8,128)(2,1)S(1)} %get-tuple-element.32), channel_id=1, source_target_pairs={{0,16},{8,24},{1,17},{9,25},{2,18},{10,26},{3,19},{11,27},{4,20},{... | collective-permute-start | bytes 393224 | tf_op jit(solution)/shard_map/ppermute | solution.py:309
  97.9 14.6 %collective-permute-start.14 = (bf16[256,256]{1,0:T(8,128)(2,1)S(1)}, bf16[256,256]{1,0:T(8,128)(2,1)S(1)}, u32[]{:S(2)}, u32[]{:S(2)}) collective-permute-start(bf16[256,256]{1,0:T(8,128)(2,1)S(1)} %get-tuple-element.33), channel_id=1, source_target_pairs={{0,24},{1,25},{2,26},{3,27},{4,28},{5,29},{6,30},{7,31},{32,56},{3... | collective-permute-start | bytes 393224 | tf_op jit(solution)/shard_map/ppermute | solution.py:309
  99.2 28.0 %collective-permute-start.9 = (bf16[512,256]{1,0:T(8,128)(2,1)S(1)}, bf16[512,256]{1,0:T(8,128)(2,1)S(1)}, u32[]{:S(2)}, u32[]{:S(2)}) collective-permute-start(bf16[512,256]{1,0:T(8,128)(2,1)S(1)} %get-tuple-element.27), channel_id=1, source_target_pairs={{8,0},{16,8},{24,16},{9,1},{17,9},{25,17},{10,2},{18,10},{26,18},{... | collective-permute-start | bytes 786440 | tf_op jit(solution)/shard_map/ppermute | solution.py:309
  104.4 22.8 %collective-permute-start.10 = (bf16[512,256]{1,0:T(8,128)(2,1)S(1)}, bf16[512,256]{1,0:T(8,128)(2,1)S(1)}, u32[]{:S(2)}, u32[]{:S(2)}) collective-permute-start(bf16[512,256]{1,0:T(8,128)(2,1)S(1)} %get-tuple-element.28), channel_id=1, source_target_pairs={{16,0},{24,8},{17,1},{25,9},{18,2},{26,10},{19,3},{27,11},{20,4},{... | collective-permute-start | bytes 786440 | tf_op jit(solution)/shard_map/ppermute | solution.py:309
  111.1 16.0 %collective-permute-start.11 = (bf16[512,256]{1,0:T(8,128)(2,1)S(1)}, bf16[512,256]{1,0:T(8,128)(2,1)S(1)}, u32[]{:S(2)}, u32[]{:S(2)}) collective-permute-start(bf16[512,256]{1,0:T(8,128)(2,1)S(1)} %get-tuple-element.29), channel_id=1, source_target_pairs={{24,0},{25,1},{26,2},{27,3},{28,4},{29,5},{30,6},{31,7},{56,32},{5... | collective-permute-start | bytes 786440 | tf_op jit(solution)/shard_map/ppermute | solution.py:309
  112.6 12.6 %collective-permute-start.15 = (bf16[256,256]{1,0:T(8,128)(2,1)S(1)}, bf16[256,256]{1,0:T(8,128)(2,1)S(1)}, u32[]{:S(2)}, u32[]{:S(2)}) collective-permute-start(bf16[256,256]{1,0:T(8,128)(2,1)S(1)} %shard_map.88), channel_id=1, source_target_pairs={{32,0},{64,32},{96,64},{128,96},{160,128},{192,160},{224,192},{256... | collective-permute-start | bytes 393224 | tf_op jit(solution)/shard_map/ppermute | solution.py:316
  125.2 2.1 %collective-permute-start.17 = (bf16[256,256]{1,0:T(8,128)(2,1)S(1)}, bf16[256,256]{1,0:T(8,128)(2,1)S(1)}, u32[]{:S(2)}, u32[]{:S(2)}) collective-permute-start(bf16[256,256]{1,0:T(8,128)(2,1)S(1)} %collective-permute-done.15.refs_0_), channel_id=1, source_target_pairs={{0,16},{1,17},{2,18},{3,19},{4,20},{5,21},{6,22},{7,23},{32,48},{3... | collective-permute-start | bytes 393224 | tf_op jit(solution)/shard_map/ppermute | solution.py:309
  125.9 7.3 %collective-permute-start.16 = (bf16[256,256]{1,0:T(8,128)(2,1)S(1)}, bf16[256,256]{1,0:T(8,128)(2,1)S(1)}, u32[]{:S(2)}, u32[]{:S(2)}) collective-permute-start(bf16[256,256]{1,0:T(8,128)(2,1)S(1)} %collective-permute-done.15.refs_0_), channel_id=1, source_target_pairs={{0,8},{8,16},{16,24},{1,9},{9,17},{17,25},{2,10},{10,18},{18,26},{... | collective-permute-start | bytes 393224 | tf_op jit(solution)/shard_map/ppermute | solution.py:309
  134.5 22.2 %all-to-all-start.3 = ((bf16[8,64,256]{2,1,0:T(8,128)(2,1)}), bf16[8,64,256]{2,1,0:T(8,128)(2,1)S(1)}, u32[]{:S(2)}, u32[]{:S(2)}) async-start(bf16[8,64,256]{2,1,0:T(8,128)(2,1)} %bitcast.21), calls=%async_computation.3 | async-start | bytes 524288 | tf_op jit(solution)/shard_map/all_to_all | solution.py:364
  (10 other events, 26.3 us)

commit v3 on v2

--- a/solution.py
+++ b/solution.py
@@ -22,7 +22,7 @@
 ROW = CHIPS * CORES
 HEADS = 4
 WIDE = 2 * HD
-OWN, OTHER, SEEN, GOES, COMES, LAND, CORE = 0, 5, 10, 14, 19, 24, 27
+OWN, OTHER, SEEN, SEND, LAND, CORE = 0, 5, 10, 14, 15, 18
 BASE = 10000.0
 BF16 = jnp.bfloat16
 F32 = jnp.float32
@@ -58,21 +58,21 @@
     elder = jnp.max(jnp.where(match, ordinal[None, None, :], -1), 2)
     mine, stack, relay = elder[:2], elder[2], elder[3]
     in_row = 2 * (chip - (mine - first) // CORES) + mine % CORES
-    before = 2 * CHIPS + 2 * ((mine - first + ROW) // CORES - chip) + mine % CORES
-    rank = jnp.sum(jnp.where(mine[:, :, None] == stack[None, None, :], levels, 0), 2)
-    source = jnp.where(mine >= first, in_row, before)
-    source = jnp.clip(jnp.where(mine >= 0, source, 0), 0, 4 * CHIPS - 1)
-    target = jnp.where(mine >= first, in_row, 2 * CHIPS + CHIPS - 1 - rank - chip)
-    target = jnp.clip(jnp.where(mine >= 0, target, 0), 0, 3 * CHIPS - 1)
-    own = jnp.stack([core, 1 - core])[:, None]
-    source = jnp.concatenate([own, source], 1).reshape(-1)
-    target = jnp.concatenate([own, target], 1).reshape(-1)
+    holder = CHIPS - 1 - jnp.sum(
+        jnp.where(mine[:, :, None] == stack[None, None, :], levels, 0), 2
+    )
+    code = jnp.where(mine >= first, in_row, 2 * CHIPS + holder - chip)
+    code = jnp.clip(jnp.where(mine >= 0, code, 0), 0, 3 * CHIPS - 1)
+    code = jnp.concatenate([jnp.stack([core, 1 - core])[:, None], code], 1).reshape(-1)
+    held = jnp.sum(jnp.where(levels == CHIPS - 1 - chip, relay, 0))
+    far = (held - first) // CORES - chip
+    send = jnp.clip(2 * far + held % CORES, 0, 2 * CHIPS - 3)
     held = jnp.stack([CHIPS - 1 - chip, CHIPS - chip, jnp.where(chip == 2, CHIPS - 1, CHIPS)])
     node = jnp.sum(jnp.where(held[:, None] == levels[None, :], relay[None, :], 0), 1)
     here = (held < LEVELS) & (node >= first) & ((node - first) // CORES == chip)
     land = jnp.where(here, node % CORES, CORES)
     table = jnp.concatenate(
-        [source, (elder[0] >= 0).astype(jnp.int32), target, land, core[None]]
+        [code, (elder[0] >= 0).astype(jnp.int32), send[None], land, core[None]]
     ).astype(jnp.int32)
     slot_depth = own_depth[0] - jnp.arange(SLOTS, dtype=jnp.int32)
     pair_depth = jnp.where(core == 0, own_depth[:2], own_depth[1::-1])
@@ -93,34 +93,41 @@
 
 
 def fetch(code, sources, target, sem):
-    for k, ref in enumerate(sources):
-        for half in range(CORES):
-
-            @pl.when(code == CORES * k + half)
+    at = 0
+    for ref in sources:
+        for half in range(ref.shape[0] // TOK):
+
+            @pl.when(code == at)
             def _(ref=ref, half=half):
                 pltpu.make_async_copy(ref.at[pl.ds(half * TOK, TOK)], target, sem).start()
 
+            at += 1
+
 
 def await_fetch(sources, target, sem):
     pltpu.make_async_copy(sources[0].at[pl.ds(0, TOK)], target, sem).wait()
 
 
-def pick_kernel(table, *refs):
+def part(ref, i):
+    return ref.at[pl.ds(i * TOK, TOK)]
+
+
+def pick_kernel(offset, number, table, *refs):
     sources, (o_ref, sem) = refs[:-2], refs[-2:]
-    for i in range(SLOTS):
-        fetch(table[OTHER + i], sources, o_ref.at[pl.ds(i * TOK, TOK)], sem.at[i])
-    for i in range(SLOTS):
-        await_fetch(sources, o_ref.at[pl.ds(i * TOK, TOK)], sem.at[i])
-
-
-def call_pick(table, sources):
+    for i in range(number):
+        fetch(table[offset + i], sources, part(o_ref, i), sem.at[i])
+    for i in range(number):
+        await_fetch(sources, part(o_ref, i), sem.at[i])
+
+
+def call_pick(table, sources, offset, number):
     return pl.pallas_call(
-        pick_kernel,
+        functools.partial(pick_kernel, offset, number),
         compiler_params=room(4),
-        out_shape=jax.ShapeDtypeStruct((KEYS, HD), BF16),
+        out_shape=jax.ShapeDtypeStruct((number * TOK, HD), BF16),
         in_specs=[SMEM] + [ANY] * len(sources),
         out_specs=VMEM,
-        scratch_shapes=[pltpu.SemaphoreType.DMA((SLOTS,))],
+        scratch_shapes=[pltpu.SemaphoreType.DMA((number,))],
     )(table, *sources)
 
 
@@ -133,12 +140,30 @@
     return lax.dot_general(a, b, dims, preferred_element_type=F32)
 
 
-def attend_kernel(table, qg_ref, cos_ref, sin_ref, other_ref, *refs):
+def attend_kernel(table, qg_hbm, cos_hbm, sin_hbm, other_hbm, *refs):
     sources = refs[: 2 * CHIPS]
-    out_ref, keep_ref, give_ref = refs[2 * CHIPS : 2 * CHIPS + 3]
-    mine_ref, keys, vals, q_all, low_all, score_all, sem = refs[2 * CHIPS + 3 :]
+    out_hbm, keep_hbm, give_hbm = refs[2 * CHIPS : 2 * CHIPS + 3]
+    (qg_ref, cos_ref, sin_ref, mine_ref, other_ref, keys, vals, q_all, low_all, score_all) = refs[
+        2 * CHIPS + 3 : 2 * CHIPS + 13
+    ]
+    out_ref, keep_ref, give_ref, sem, in_sem, out_sem = refs[2 * CHIPS + 13 :]
+    whole_in = [
+        pltpu.make_async_copy(src, dst, in_sem.at[i])
+        for i, (src, dst) in enumerate(
+            ((qg_hbm, qg_ref), (cos_hbm, cos_ref), (sin_hbm, sin_ref))
+        )
+    ]
+    other_in = [
+        pltpu.make_async_copy(part(other_hbm, i), part(other_ref, i), sem.at[SLOTS + i])
+        for i in range(SLOTS)
+    ]
+    for copy in whole_in:
+        copy.start()
     for i in range(SLOTS):
-        fetch(table[OWN + i], sources, mine_ref.at[pl.ds(i * TOK, TOK)], sem.at[i])
+        fetch(table[OWN + i], sources, part(mine_ref, i), sem.at[i])
+        other_in[i].start()
+    for copy in whole_in:
+        copy.wait()
     for h in range(2):
         q_all[h * TOK : (h + 1) * TOK, :] = turn(
             qg_ref[:, h * HD : (h + 1) * HD].astype(F32), cos_ref[:TOK, :], sin_ref[:TOK, :]
@@ -146,7 +171,8 @@
     is_key = table[CORE] == 0
     for i in range(SLOTS):
         here = slice(i * TOK, (i + 1) * TOK)
-        await_fetch(sources, mine_ref.at[pl.ds(i * TOK, TOK)], sem.at[i])
+        await_fetch(sources, part(mine_ref, i), sem.at[i])
+        other_in[i].wait()
         mine, other = mine_ref[here, :], other_ref[here, :]
         keys[here, :] = turn(
             jnp.where(is_key, mine, other).astype(F32), cos_ref[here, :], sin_ref[here, :]
@@ -193,6 +219,8 @@
         out_ref[:, WIDE + h * HD : WIDE + (h + 1) * HD] = turn(
             dot(score_all[rows, :], keys[...], NN), cos_ref[:TOK, :], -sin_ref[:TOK, :]
         ).astype(BF16)
+    outgoing = [pltpu.make_async_copy(out_ref, out_hbm, out_sem.at[0])]
+    outgoing[0].start()
     for i in range(SLOTS):
         cols = slice(i * TOK, (i + 1) * TOK)
         part_key = dot(score_all[:, cols], q_all[...], TN)
@@ -201,42 +229,82 @@
         )
         keep_ref[cols, :] = jnp.where(is_key, part_key, part_value).astype(BF16)
         give_ref[cols, :] = jnp.where(is_key, part_value, part_key).astype(BF16)
+        for k, (src, dst) in enumerate(((give_ref, give_hbm), (keep_ref, keep_hbm))):
+            outgoing.append(
+                pltpu.make_async_copy(part(src, i), part(dst, i), out_sem.at[1 + 2 * i + k])
+            )
+            outgoing[-1].start()
+    for copy in outgoing:
+        copy.wait()
 
 
 def call_attend(table, query_grad, cosine, sine, other, sources):
     return pl.pallas_call(
         attend_kernel,
-        compiler_params=room(24),
         out_shape=(
             jax.ShapeDtypeStruct((TOK, 2 * WIDE), BF16),
             jax.ShapeDtypeStruct((KEYS, HD), BF16),
             jax.ShapeDtypeStruct((KEYS, HD), BF16),
         ),
-        in_specs=[SMEM] + [VMEM] * 4 + [ANY] * len(sources),
-        out_specs=(VMEM,) * 3,
+        in_specs=[SMEM] + [ANY] * (4 + len(sources)),
+        out_specs=(ANY,) * 3,
         scratch_shapes=[
+            pltpu.VMEM((TOK, 2 * WIDE), BF16),
+            pltpu.VMEM((KEYS, HALF), F32),
+            pltpu.VMEM((KEYS, HALF), F32),
+            pltpu.VMEM((KEYS, HD), BF16),
             pltpu.VMEM((KEYS, HD), BF16),
             pltpu.VMEM((KEYS, HD), BF16),
             pltpu.VMEM((KEYS, HD), BF16),
             pltpu.VMEM((2 * TOK, HD), BF16),
             pltpu.VMEM((2 * TOK, KEYS), BF16),
             pltpu.VMEM((2 * TOK, KEYS), BF16),
-            pltpu.SemaphoreType.DMA((SLOTS,)),
+            pltpu.VMEM((TOK, 2 * WIDE), BF16),
+            pltpu.VMEM((KEYS, HD), BF16),
+            pltpu.VMEM((KEYS, HD), BF16),
+            pltpu.SemaphoreType.DMA((2 * SLOTS,)),
+            pltpu.SemaphoreType.DMA((3,)),
+            pltpu.SemaphoreType.DMA((1 + 2 * SLOTS,)),
         ],
     )(table, query_grad, cosine, sine, other, *sources)
 
 
-def spread_kernel(table, keep_ref, got_ref, *refs):
-    outs, total = refs[:-1], refs[-1]
+def spread_kernel(table, keep_hbm, got_hbm, *refs):
+    outs, (total, terms, own_ref, within_ref, stack_ref, sem, out_sem) = refs[:-7], refs[-7:]
+    copies = [
+        [
+            pltpu.make_async_copy(part(src, i), part(terms.at[k], i), sem.at[k, i])
+            for i in range(SLOTS)
+        ]
+        for k, src in enumerate((keep_hbm, got_hbm))
+    ]
+    for group in copies:
+        for copy in group:
+            copy.start()
     total[...] = jnp.zeros_like(total)
-    for source, offset in ((keep_ref, GOES), (got_ref, COMES)):
+    for k, offset in enumerate((OWN, OTHER)):
+        source = terms.at[k]
         for i in range(SLOTS):
+            copies[k][i].wait()
             at = pl.ds(pl.multiple_of(table[offset + i] * TOK, TOK), TOK)
             total[at, :] += source[i * TOK : (i + 1) * TOK, :].astype(F32)
+    outgoing = []
+
+    def leave(src, dst):
+        outgoing.append(pltpu.make_async_copy(src, dst, out_sem.at[len(outgoing)]))
+        outgoing[-1].start()
+
     for k in range(CHIPS):
-        outs[k][...] = total[k * PAIR : (k + 1) * PAIR, :].astype(outs[k].dtype)
         low = CHIPS * PAIR + k * TOK
-        outs[CHIPS + k][...] = total[low : low + TOK, :].astype(BF16)
+        stack_ref[k] = total[low : low + TOK, :].astype(BF16)
+        leave(stack_ref.at[k], outs[CHIPS + k])
+    for k in range(1, CHIPS):
+        within_ref[k - 1] = total[k * PAIR : (k + 1) * PAIR, :].astype(BF16)
+        leave(within_ref.at[k - 1], outs[k])
+    own_ref[...] = total[:PAIR, :]
+    leave(own_ref, outs[0])
+    for copy in outgoing:
+        copy.wait()
 
 
 def call_spread(table, keep, got):
@@ -248,9 +316,17 @@
             + [jax.ShapeDtypeStruct((PAIR, HD), BF16)] * (CHIPS - 1)
             + [jax.ShapeDtypeStruct((TOK, HD), BF16)] * CHIPS
         ),
-        in_specs=[SMEM, VMEM, VMEM],
-        out_specs=(VMEM,) * (2 * CHIPS),
-        scratch_shapes=[pltpu.VMEM((CHIPS * PAIR + CHIPS * TOK, HD), F32)],
+        in_specs=[SMEM, ANY, ANY],
+        out_specs=(ANY,) * (2 * CHIPS),
+        scratch_shapes=[
+            pltpu.VMEM((CHIPS * PAIR + CHIPS * TOK, HD), F32),
+            pltpu.VMEM((CORES, KEYS, HD), BF16),
+            pltpu.VMEM((PAIR, HD), F32),
+            pltpu.VMEM((CHIPS - 1, PAIR, HD), BF16),
+            pltpu.VMEM((CHIPS, TOK, HD), BF16),
+            pltpu.SemaphoreType.DMA((CORES, SLOTS)),
+            pltpu.SemaphoreType.DMA((2 * CHIPS,)),
+        ],
     )(table, keep, got)
 
 
@@ -340,20 +416,18 @@
         (table, slot_cos, slot_sin, pair_cos, pair_sin)
     )
 
-    relay = next_row(both, 1)
+    pairs = [both, along(both, -1), along(both, -2, (2,))]
+    relay = next_row(call_pick(table, pairs, SEND, 1), 1)
     sources = [both] + [along(both, k) for k in (1, 2, 3)]
     query_grad = jnp.concatenate(
         [queries.reshape(tokens, HEADS, WIDE), grad_attn.reshape(tokens, HEADS, WIDE)], 2
     ).reshape(tokens, HEADS * 2 * WIDE)
     query_grad = lax.all_to_all(query_grad, "head", split_axis=1, concat_axis=0, tiled=True)
     sources += [relay] + [along(relay, -k) for k in (1, 2, 3)]
-    other = swap(call_pick(table, sources))
+    other = swap(call_pick(table, sources, OTHER, SLOTS))
     out, keep, give = call_attend(table, query_grad, slot_cos, slot_sin, other, sources)
     got = swap(give)
     out = lax.all_to_all(out, "head", split_axis=0, concat_axis=1, tiled=True)
-    out = out.reshape(tokens, HEADS, 2, WIDE)
-    attended = out[:, :, 0].reshape(tokens, HEADS * WIDE)
-    grad_query = out[:, :, 1].reshape(tokens, HEADS * WIDE)
     spread = call_spread(table, keep, got)
     own, within, stack = spread[0], spread[1:CHIPS], spread[CHIPS:]
     stack_sum = call_sum([stack[0]] + [along(stack[k], k) for k in (1, 2, 3)], BF16)
@@ -361,7 +435,11 @@
     own = call_sum([own] + [along(within[k - 1], -k) for k in (1, 2, 3)], F32)
     backs = [back, along(back, 1), along(back, 2, (0,))]
     grad_both = call_close(table, own, backs, pair_cos, pair_sin)
+    grad_both, out = lax.optimization_barrier((grad_both, out))
     grad_both = lax.all_to_all(grad_both, ("core", "head"), split_axis=0, concat_axis=1, tiled=True)
+    out = out.reshape(tokens, HEADS, 2, WIDE)
+    attended = out[:, :, 0].reshape(tokens, HEADS * WIDE)
+    grad_query = out[:, :, 1].reshape(tokens, HEADS * WIDE)
     half = HEADS * HD
     return attended, grad_query, grad_both[:, :half], grad_both[:, half:]
 

time: 158 us -> 155 us (0.981)
  waiting for transfers between devices: 36.1 us -> 28.5 us
  Pallas kernels: 11.1 us -> 14.8 us
  between operations: 1.04 us -> 3.86 us
  local copies, waits for them, and re-layouts: 10.1 us -> 8.09 us
    all_to_all x1, starting transfers between devices: 19.3 us -> 12.3 us  [shards(): out = lax.all_to_all(out, 'head', split_axis=0, concat_axis=1, tiled=True)]
    ppermute x14 -> x16, starting transfers between devices: 32 us -> 36.1 us  [along(): lax.ppermute(block, 'chip', [(i, i + shift) for i in starts if 0 <= i + s...]
    unnamed x27 -> x37, local copies, waits for them, and re-layouts: 6.42 us -> 2.78 us
    ppermute x14 -> x16, waiting for transfers between devices: 11.4 us -> 8 us  [along(): lax.ppermute(block, 'chip', [(i, i + shift) for i in starts if 0 <= i + s...]
    pallas_call x1, Pallas kernels: 1.14 us -> 3.82 us  [call_spread(): pl.pallas_call(spread_kernel, compiler_params=room(12), out_shape=tuple([...]
    all_to_all x1, waiting for transfers between devices: 2.99 us -> 0.5 us  [shards(): lax.all_to_all(jnp.concatenate([keys, values], 1), ('core', 'head'), spli...]
    slice x1, local copies, waits for them, and re-layouts: 0.73 us -> 2.36 us  [shards(): grad_query = out[:, :, 1].reshape(tokens, HEADS * WIDE)]
    pallas_call x2 -> x3, Pallas kernels: 8.43 us -> 9.46 us  [the longest x1 6.95 us: call_attend(): pl.pallas_call(attend_kernel, out_shape=(jax.ShapeDtypeStruct((TOK, 2 * W...]
  transfers between devices with their start and end apart: 22 -> 24, of which waited for: 10 -> 8; matrix products, arithmetic and copies ran while one was open for 7% -> 8% of each run, Pallas kernels for 3% -> 5%
where the time goes in v3:
time: 155 us; the launch traced here: 154 us
  starting transfers between devices  90.2 us (58%)
  waiting for transfers between devices  28.5 us (18%)
  Pallas kernels  14.8 us (10%)
  other arithmetic  8.98 us (6%)
  local copies, waits for them, and re-layouts  8.09 us (5%)
  between operations  3.86 us (2%)
    ppermute x16, starting transfers between devices, along(): lax.ppermute(block, 'chip', [(i, i + shift) for i in starts if 0 <= i + s...  36.1 us
    all_to_all x1, starting transfers between devices, shards(): lax.all_to_all(grad_both, ('core', 'head'), split_axis=0, concat_axis=1,...  14.2 us
    all_to_all x1, starting transfers between devices, shards(): out = lax.all_to_all(out, 'head', split_axis=0, concat_axis=1, tiled=True)  12.3 us
    ppermute x2, waiting for transfers between devices, next_row(): lax.ppermute(block, 'row', [(i, i + shift) for i in range(rows) if 0 <= i...  11.5 us
    ppermute x2, starting transfers between devices, next_row(): lax.ppermute(block, 'row', [(i, i + shift) for i in range(rows) if 0 <= i...  10.4 us
    ppermute x16, waiting for transfers between devices, along(): lax.ppermute(block, 'chip', [(i, i + shift) for i in starts if 0 <= i + s...  8 us
    pallas_call x1, Pallas kernels, call_attend(): pl.pallas_call(attend_kernel, out_shape=(jax.ShapeDtypeStruct((TOK, 2 * W...  6.95 us
    all_to_all x1, starting transfers between devices, shards(): lax.all_to_all(jnp.concatenate([keys, values], 1), ('core', 'head'), spli...  6.7 us
  transfers between devices with their start and end apart: 24, of which 8 were waited for; matrix products, arithmetic and copies ran while one was open for 8% of the time, Pallas kernels for 5%

profile of v3, /device:TPU:31, one launch (start us, length us, event | category | flops | bytes accessed | tf_op | source)
XLA Modules:
  0.0 154.4 jit_solution(17447823314082987629)
XLA Ops:
  2.3 6.7 %all-to-all-start.1 = ((bf16[64,8,256]{2,0,1:T(8,128)(2,1)}), bf16[64,8,256]{2,0,1:T(8,128)(2,1)S(1)}, u32[]{:S(2)}, u32[]{:S(2)}) async-start(bf16[64,8,256]{2,0,1:T(8,128)(2,1)} %bitcast.51), calls=%async_computation.1 | async-start | bytes 524288 | tf_op jit(solution)/shard_map/all_to_all | solution.py:404
  13.8 3.8 %multiply_sine_fusion = (f32[1280,128]{1,0:T(8,128)}, f32[1280,128]{1,0:T(8,128)}) fusion(f32[128]{0:T(128)S(1)} %multiply_exponential_fusion, f32[1280]{0:T(1024)S(1)} %convert_element_type.41), kind=kLoop, calls=%fused_computation | loop fusion | flops 163840 | bytes 1316352 | tf_op jit(solution)/shard_map/sin | solution.py:413
  18.1 3.9 %all-to-all-start = ((bf16[64,4,1024]{2,0,1:T(8,128)(2,1)}), bf16[64,4,1024]{2,0,1:T(8,128)(2,1)S(1)}, u32[]{:S(2)}, u32[]{:S(2)}) async-start(bf16[64,4,1024]{2,0,1:T(8,128)(2,1)} %pad_maximum_fusion), calls=%async_computation | async-start | bytes 1048576 | tf_op jit(solution)/shard_map/all_to_all | solution.py:425
  23.4 3.9 %collective-permute-start.3 = (bf16[512,256]{1,0:T(8,128)(2,1)S(1)}, bf16[512,256]{1,0:T(8,128)(2,1)S(1)}, u32[]{:S(2)}, u32[]{:S(2)}) collective-permute-start(bf16[512,256]{1,0:T(8,128)(2,1)S(1)} %bitcast.55), channel_id=1, source_target_pairs={{8,0},{16,8},{24,16},{9,1},{17,9},{25,17},{10,2},{18,10},{26,18},{... | collective-permute-start | bytes 786440 | tf_op jit(solution)/shard_map/ppermute | solution.py:385
  34.6 8.5 %collective-permute-start.5 = (bf16[256,256]{1,0:T(8,128)(2,1)S(1)}, bf16[256,256]{1,0:T(8,128)(2,1)S(1)}, u32[]{:S(2)}, u32[]{:S(2)}) collective-permute-start(bf16[256,256]{1,0:T(8,128)(2,1)S(1)} %shard_map.84), channel_id=1, source_target_pairs={{0,32},{32,64},{64,96},{96,128},{128,160},{160,192},{192,224},{224... | collective-permute-start | bytes 393224 | tf_op jit(solution)/shard_map/ppermute | solution.py:392
  45.0 5.8 %collective-permute-start.8 = (bf16[256,256]{1,0:T(8,128)(2,1)S(1)}, bf16[256,256]{1,0:T(8,128)(2,1)S(1)}, u32[]{:S(2)}, u32[]{:S(2)}) collective-permute-start(bf16[256,256]{1,0:T(8,128)(2,1)S(1)} %collective-permute-done.5.refs_4_), channel_id=1, source_target_pairs={{24,0},{25,1},{26,2},{27,3},{28,4},{29,5},{30,6},{31,7},{56,32},{5... | collective-permute-start | bytes 393224 | tf_op jit(solution)/shard_map/ppermute | solution.py:385
  52.1 2.5 %collective-permute-start.6 = (bf16[256,256]{1,0:T(8,128)(2,1)S(1)}, bf16[256,256]{1,0:T(8,128)(2,1)S(1)}, u32[]{:S(2)}, u32[]{:S(2)}) collective-permute-start(bf16[256,256]{1,0:T(8,128)(2,1)S(1)} %collective-permute-done.5.refs_4_), channel_id=1, source_target_pairs={{8,0},{16,8},{24,16},{9,1},{17,9},{25,17},{10,2},{18,10},{26,18},{... | collective-permute-start | bytes 393224 | tf_op jit(solution)/shard_map/ppermute | solution.py:385
  54.7 3.2 %collective-permute-done.6.refs_5_ = bf16[256,256]{1,0:T(8,128)(2,1)S(1)} collective-permute-done((bf16[256,256]{1,0:T(8,128)(2,1)S(1)}, bf16[256,256]{1,0:T(8,128)(2,1)S(1)}, u32[]{:S(2)}, u32[]{:S(2)}) %collective-permute-start.6) | collective-permute-done | bytes 131104 | tf_op jit(solution)/shard_map/ppermute | solution.py:385
  57.9 1.8 %shard_map.85 = bf16[1280,256]{1,0:T(8,128)(2,1)S(1)} custom-call(s32[19]{0:T(128)S(1)} %concatenate.17.table, bf16[512,256]{1,0:T(8,128)(2,1)S(1)} %bitcast.60, bf16[512,256]{1,0:T(8,128)(2,1)S(1)} %collective-permute-done.refs_1_, bf16[512,256]{1,0:T(8,128)(2,1)S(1)} %collective-permute-done.1.refs_2_, ...), custom_call_target="tpu_custom_call" | custom-call | tf_op jit(solution)/shard_map/pallas_call | solution.py:124
  59.7 3.8 %collective-permute-start.9 = (bf16[1280,256]{1,0:T(8,128)(2,1)S(1)}, bf16[1280,256]{1,0:T(8,128)(2,1)}, u32[]{:S(2)}, u32[]{:S(2)}) collective-permute-start(bf16[1280,256]{1,0:T(8,128)(2,1)S(1)} %shard_map.85), channel_id=1, source_target_pairs={{0,4},{4,0},{1,5},{5,1},{2,6},{6,2},{3,7},{7,3},{8,12},{12,8},{9,1... | collective-permute-start | bytes 1966088 | tf_op jit(solution)/shard_map/ppermute | solution.py:398
  63.5 1.8 %collective-permute-done.9.other_hbm = bf16[1280,256]{1,0:T(8,128)(2,1)} collective-permute-done((bf16[1280,256]{1,0:T(8,128)(2,1)S(1)}, bf16[1280,256]{1,0:T(8,128)(2,1)}, u32[]{:S(2)}, u32[]{:S(2)}) %collective-permute-start.9) | collective-permute-done | bytes 655392 | tf_op jit(solution)/shard_map/ppermute | solution.py:398
  65.3 7.0 %shard_map.86 = (bf16[256,1024]{1,0:T(8,128)(2,1)}, bf16[1280,256]{1,0:T(8,128)(2,1)}, bf16[1280,256]{1,0:T(8,128)(2,1)}) custom-call(s32[19]{0:T(128)} %copy-done.9, bf16[256,1024]{1,0:T(8,128)(2,1)} %bitcast.62, f32[1280,128]{1,0:T(8,128)} %get-tuple-element.23.cos_hbm, f32[1280,128]{1,0:T(8,128)} %get-tuple-element.24.sin_hbm, ...), custom_call_target="tpu_custom_call" | custom-call | tf_op jit(solution)/shard_map/pallas_call | solution.py:242
  72.3 12.3 %all-to-all-start.2 = ((bf16[4,64,1024]{2,1,0:T(8,128)(2,1)}), bf16[4,64,1024]{2,1,0:T(8,128)(2,1)S(1)}, u32[]{:S(2)}, u32[]{:S(2)}) async-start(bf16[4,64,1024]{2,1,0:T(8,128)(2,1)} %bitcast.70), calls=%async_computation.2 | async-start | bytes 1048576 | tf_op jit(solution)/shard_map/all_to_all | solution.py:430
  84.7 2.7 %collective-permute-start.10 = (bf16[1280,256]{1,0:T(8,128)(2,1)}, bf16[1280,256]{1,0:T(8,128)(2,1)S(1)}, u32[]{:S(2)}, u32[]{:S(2)}) collective-permute-start(bf16[1280,256]{1,0:T(8,128)(2,1)} %get-tuple-element.26), channel_id=1, source_target_pairs={{0,4},{4,0},{1,5},{5,1},{2,6},{6,2},{3,7},{7,3},{8,12},{12,8},{9,1... | collective-permute-start | bytes 1966088 | tf_op jit(solution)/shard_map/ppermute | solution.py:398
  87.3 1.9 %collective-permute-done.10.got_hbm = bf16[1280,256]{1,0:T(8,128)(2,1)S(1)} collective-permute-done((bf16[1280,256]{1,0:T(8,128)(2,1)}, bf16[1280,256]{1,0:T(8,128)(2,1)S(1)}, u32[]{:S(2)}, u32[]{:S(2)}) %collective-permute-start.10) | collective-permute-done | bytes 655392 | tf_op jit(solution)/shard_map/ppermute | solution.py:398
  89.3 3.8 %shard_map.87 = (f32[512,256]{1,0:T(8,128)S(1)}, bf16[512,256]{1,0:T(8,128)(2,1)S(1)}, bf16[512,256]{1,0:T(8,128)(2,1)S(1)}, bf16[512,256]{1,0:T(8,128)(2,1)S(1)...) custom-call(s32[19]{0:T(128)S(1)} %copy-done.10, ...), custom_call_target="tpu_custom_call" | custom-call | tf_op jit(solution)/shard_map/pallas_call | solution.py:311
  97.0 4.1 %collective-permute-start.11 = (bf16[512,256]{1,0:T(8,128)(2,1)S(1)}, bf16[512,256]{1,0:T(8,128)(2,1)S(1)}, u32[]{:S(2)}, u32[]{:S(2)}) collective-permute-start(bf16[512,256]{1,0:T(8,128)(2,1)S(1)} %get-tuple-element.28), channel_id=1, source_target_pairs={{8,0},{16,8},{24,16},{9,1},{17,9},{25,17},{10,2},{18,10},{26,18},{... | collective-permute-start | bytes 786440 | tf_op jit(solution)/shard_map/ppermute | solution.py:385
  101.1 6.7 %collective-permute-start.12 = (bf16[512,256]{1,0:T(8,128)(2,1)S(1)}, bf16[512,256]{1,0:T(8,128)(2,1)S(1)}, u32[]{:S(2)}, u32[]{:S(2)}) collective-permute-start(bf16[512,256]{1,0:T(8,128)(2,1)S(1)} %get-tuple-element.29), channel_id=1, source_target_pairs={{16,0},{24,8},{17,1},{25,9},{18,2},{26,10},{19,3},{27,11},{20,4},{... | collective-permute-start | bytes 786440 | tf_op jit(solution)/shard_map/ppermute | solution.py:385
  109.3 1.9 %collective-permute-start.17 = (bf16[256,256]{1,0:T(8,128)(2,1)S(1)}, bf16[256,256]{1,0:T(8,128)(2,1)S(1)}, u32[]{:S(2)}, u32[]{:S(2)}) collective-permute-start(bf16[256,256]{1,0:T(8,128)(2,1)S(1)} %shard_map.89), channel_id=1, source_target_pairs={{32,0},{64,32},{96,64},{128,96},{160,128},{192,160},{224,192},{256... | collective-permute-start | bytes 393224 | tf_op jit(solution)/shard_map/ppermute | solution.py:392
  111.2 10.8 %collective-permute-done.17.refs_0_ = bf16[256,256]{1,0:T(8,128)(2,1)S(1)} collective-permute-done((bf16[256,256]{1,0:T(8,128)(2,1)S(1)}, bf16[256,256]{1,0:T(8,128)(2,1)S(1)}, u32[]{:S(2)}, u32[]{:S(2)}) %collective-permute-start.17) | collective-permute-done | bytes 131104 | tf_op jit(solution)/shard_map/ppermute | solution.py:392
  124.2 4.8 %collective-permute-done.18.refs_1_ = bf16[256,256]{1,0:T(8,128)(2,1)S(1)} collective-permute-done((bf16[256,256]{1,0:T(8,128)(2,1)S(1)}, bf16[256,256]{1,0:T(8,128)(2,1)S(1)}, u32[]{:S(2)}, u32[]{:S(2)}) %collective-permute-start.18) | collective-permute-done | bytes 131104 | tf_op jit(solution)/shard_map/ppermute | solution.py:385
  130.4 14.2 %all-to-all-start.3 = ((bf16[8,64,256]{2,1,0:T(8,128)(2,1)}), bf16[8,64,256]{2,1,0:T(8,128)(2,1)S(1)}, u32[]{:S(2)}, u32[]{:S(2)}) async-start(bf16[8,64,256]{2,1,0:T(8,128)(2,1)} %bitcast.22), calls=%async_computation.3 | async-start | bytes 524288 | tf_op jit(solution)/shard_map/all_to_all | solution.py:439
  145.0 2.4 %slice_reduce_fusion = (bf16[64,4,512]{2,1,0:T(4,128)(2,1)S(1)}, bf16[64,4,512]{2,1,0:T(4,128)(2,1)S(1)}) fusion(bf16[64,4,2,512]{3,2,1,0:T(2,128)(2,1)S(1)} %reshape.170), kind=kLoop, calls=%fused_computation.2 | loop fusion | bytes 1048576 | tf_op jit(solution)/shard_map/slice | solution.py:442
  148.9 4.8 %all-to-all-done.3 = bf16[8,64,256]{2,1,0:T(8,128)(2,1)S(1)} async-done(((bf16[8,64,256]{2,1,0:T(8,128)(2,1)}), bf16[8,64,256]{2,1,0:T(8,128)(2,1)S(1)}, u32[]{:S(2)}, u32[]{:S(2)}) %all-to-all-start.3) | async-done | bytes 262176 | tf_op jit(solution)/shard_map/all_to_all | solution.py:439
  (109 shorter events, 27.4 us)
Async XLA Ops:
  2.3 15.7 %all-to-all-start.1 = ((bf16[64,8,256]{2,0,1:T(8,128)(2,1)}), bf16[64,8,256]{2,0,1:T(8,128)(2,1)S(1)}, u32[]{:S(2)}, u32[]{:S(2)}) async-start(bf16[64,8,256]{2,0,1:T(8,128)(2,1)} %bitcast.51), calls=%async_computation.1 | async-start | bytes 524288 | tf_op jit(solution)/shard_map/all_to_all | solution.py:404
  18.1 45.4 %all-to-all-start = ((bf16[64,4,1024]{2,0,1:T(8,128)(2,1)}), bf16[64,4,1024]{2,0,1:T(8,128)(2,1)S(1)}, u32[]{:S(2)}, u32[]{:S(2)}) async-start(bf16[64,4,1024]{2,0,1:T(8,128)(2,1)} %pad_maximum_fusion), calls=%async_computation | async-start | bytes 1048576 | tf_op jit(solution)/shard_map/all_to_all | solution.py:425
  22.7 11.1 %collective-permute-start.4 = (bf16[512,256]{1,0:T(8,128)(2,1)S(1)}, bf16[512,256]{1,0:T(8,128)(2,1)S(1)}, u32[]{:S(2)}, u32[]{:S(2)}) collective-permute-start(bf16[512,256]{1,0:T(8,128)(2,1)S(1)} %bitcast.54), channel_id=1, source_target_pairs={{16,0},{17,1},{18,2},{19,3},{20,4},{21,5},{22,6},{23,7},{48,32},{4... | collective-permute-start | bytes 786440 | tf_op jit(solution)/shard_map/ppermute | solution.py:385
  23.4 10.4 %collective-permute-start.3 = (bf16[512,256]{1,0:T(8,128)(2,1)S(1)}, bf16[512,256]{1,0:T(8,128)(2,1)S(1)}, u32[]{:S(2)}, u32[]{:S(2)}) collective-permute-start(bf16[512,256]{1,0:T(8,128)(2,1)S(1)} %bitcast.55), channel_id=1, source_target_pairs={{8,0},{16,8},{24,16},{9,1},{17,9},{25,17},{10,2},{18,10},{26,18},{... | collective-permute-start | bytes 786440 | tf_op jit(solution)/shard_map/ppermute | solution.py:385
  30.2 21.9 %collective-permute-start.2 = (bf16[512,256]{1,0:T(8,128)(2,1)S(1)}, bf16[512,256]{1,0:T(8,128)(2,1)S(1)}, u32[]{:S(2)}, u32[]{:S(2)}) collective-permute-start(bf16[512,256]{1,0:T(8,128)(2,1)S(1)} %bitcast.56), channel_id=1, source_target_pairs={{0,24},{1,25},{2,26},{3,27},{4,28},{5,29},{6,30},{7,31},{32,56},{3... | collective-permute-start | bytes 786440 | tf_op jit(solution)/shard_map/ppermute | solution.py:385
  32.5 22.1 %collective-permute-start.1 = (bf16[512,256]{1,0:T(8,128)(2,1)S(1)}, bf16[512,256]{1,0:T(8,128)(2,1)S(1)}, u32[]{:S(2)}, u32[]{:S(2)}) collective-permute-start(bf16[512,256]{1,0:T(8,128)(2,1)S(1)} %bitcast.57), channel_id=1, source_target_pairs={{0,16},{8,24},{1,17},{9,25},{2,18},{10,26},{3,19},{11,27},{4,20},{... | collective-permute-start | bytes 786440 | tf_op jit(solution)/shard_map/ppermute | solution.py:385
  34.6 10.4 %collective-permute-start.5 = (bf16[256,256]{1,0:T(8,128)(2,1)S(1)}, bf16[256,256]{1,0:T(8,128)(2,1)S(1)}, u32[]{:S(2)}, u32[]{:S(2)}) collective-permute-start(bf16[256,256]{1,0:T(8,128)(2,1)S(1)} %shard_map.84), channel_id=1, source_target_pairs={{0,32},{32,64},{64,96},{96,128},{128,160},{160,192},{192,224},{224... | collective-permute-start | bytes 393224 | tf_op jit(solution)/shard_map/ppermute | solution.py:392
  43.0 11.6 %collective-permute-start = (bf16[512,256]{1,0:T(8,128)(2,1)S(1)}, bf16[512,256]{1,0:T(8,128)(2,1)S(1)}, u32[]{:S(2)}, u32[]{:S(2)}) collective-permute-start(bf16[512,256]{1,0:T(8,128)(2,1)S(1)} %bitcast.59), channel_id=1, source_target_pairs={{0,8},{8,16},{16,24},{1,9},{9,17},{17,25},{2,10},{10,18},{18,26},{... | collective-permute-start | bytes 786440 | tf_op jit(solution)/shard_map/ppermute | solution.py:385
  45.0 9.7 %collective-permute-start.8 = (bf16[256,256]{1,0:T(8,128)(2,1)S(1)}, bf16[256,256]{1,0:T(8,128)(2,1)S(1)}, u32[]{:S(2)}, u32[]{:S(2)}) collective-permute-start(bf16[256,256]{1,0:T(8,128)(2,1)S(1)} %collective-permute-done.5.refs_4_), channel_id=1, source_target_pairs={{24,0},{25,1},{26,2},{27,3},{28,4},{29,5},{30,6},{31,7},{56,32},{5... | collective-permute-start | bytes 393224 | tf_op jit(solution)/shard_map/ppermute | solution.py:385
  50.8 3.9 %collective-permute-start.7 = (bf16[256,256]{1,0:T(8,128)(2,1)S(1)}, bf16[256,256]{1,0:T(8,128)(2,1)S(1)}, u32[]{:S(2)}, u32[]{:S(2)}) collective-permute-start(bf16[256,256]{1,0:T(8,128)(2,1)S(1)} %collective-permute-done.5.refs_4_), channel_id=1, source_target_pairs={{16,0},{24,8},{17,1},{25,9},{18,2},{26,10},{19,3},{27,11},{20,4},{... | collective-permute-start | bytes 393224 | tf_op jit(solution)/shard_map/ppermute | solution.py:385
  52.1 5.8 %collective-permute-start.6 = (bf16[256,256]{1,0:T(8,128)(2,1)S(1)}, bf16[256,256]{1,0:T(8,128)(2,1)S(1)}, u32[]{:S(2)}, u32[]{:S(2)}) collective-permute-start(bf16[256,256]{1,0:T(8,128)(2,1)S(1)} %collective-permute-done.5.refs_4_), channel_id=1, source_target_pairs={{8,0},{16,8},{24,16},{9,1},{17,9},{25,17},{10,2},{18,10},{26,18},{... | collective-permute-start | bytes 393224 | tf_op jit(solution)/shard_map/ppermute | solution.py:385
  59.7 5.6 %collective-permute-start.9 = (bf16[1280,256]{1,0:T(8,128)(2,1)S(1)}, bf16[1280,256]{1,0:T(8,128)(2,1)}, u32[]{:S(2)}, u32[]{:S(2)}) collective-permute-start(bf16[1280,256]{1,0:T(8,128)(2,1)S(1)} %shard_map.85), channel_id=1, source_target_pairs={{0,4},{4,0},{1,5},{5,1},{2,6},{6,2},{3,7},{7,3},{8,12},{12,8},{9,1... | collective-permute-start | bytes 1966088 | tf_op jit(solution)/shard_map/ppermute | solution.py:398
  72.3 58.0 %all-to-all-start.2 = ((bf16[4,64,1024]{2,1,0:T(8,128)(2,1)}), bf16[4,64,1024]{2,1,0:T(8,128)(2,1)S(1)}, u32[]{:S(2)}, u32[]{:S(2)}) async-start(bf16[4,64,1024]{2,1,0:T(8,128)(2,1)} %bitcast.70), calls=%async_computation.2 | async-start | bytes 1048576 | tf_op jit(solution)/shard_map/all_to_all | solution.py:430
  84.7 4.6 %collective-permute-start.10 = (bf16[1280,256]{1,0:T(8,128)(2,1)}, bf16[1280,256]{1,0:T(8,128)(2,1)S(1)}, u32[]{:S(2)}, u32[]{:S(2)}) collective-permute-start(bf16[1280,256]{1,0:T(8,128)(2,1)} %get-tuple-element.26), channel_id=1, source_target_pairs={{0,4},{4,0},{1,5},{5,1},{2,6},{6,2},{3,7},{7,3},{8,12},{12,8},{9,1... | collective-permute-start | bytes 1966088 | tf_op jit(solution)/shard_map/ppermute | solution.py:398
  93.1 14.8 %collective-permute-start.14 = (bf16[256,256]{1,0:T(8,128)(2,1)S(1)}, bf16[256,256]{1,0:T(8,128)(2,1)S(1)}, u32[]{:S(2)}, u32[]{:S(2)}) collective-permute-start(bf16[256,256]{1,0:T(8,128)(2,1)S(1)} %get-tuple-element.32), channel_id=1, source_target_pairs={{0,8},{8,16},{16,24},{1,9},{9,17},{17,25},{2,10},{10,18},{18,26},{... | collective-permute-start | bytes 393224 | tf_op jit(solution)/shard_map/ppermute | solution.py:385
  94.4 14.8 %collective-permute-start.15 = (bf16[256,256]{1,0:T(8,128)(2,1)S(1)}, bf16[256,256]{1,0:T(8,128)(2,1)S(1)}, u32[]{:S(2)}, u32[]{:S(2)}) collective-permute-start(bf16[256,256]{1,0:T(8,128)(2,1)S(1)} %get-tuple-element.33), channel_id=1, source_target_pairs={{0,16},{8,24},{1,17},{9,25},{2,18},{10,26},{3,19},{11,27},{4,20},{... | collective-permute-start | bytes 393224 | tf_op jit(solution)/shard_map/ppermute | solution.py:385
  95.7 13.5 %collective-permute-start.16 = (bf16[256,256]{1,0:T(8,128)(2,1)S(1)}, bf16[256,256]{1,0:T(8,128)(2,1)S(1)}, u32[]{:S(2)}, u32[]{:S(2)}) collective-permute-start(bf16[256,256]{1,0:T(8,128)(2,1)S(1)} %get-tuple-element.34), channel_id=1, source_target_pairs={{0,24},{1,25},{2,26},{3,27},{4,28},{5,29},{6,30},{7,31},{32,56},{3... | collective-permute-start | bytes 393224 | tf_op jit(solution)/shard_map/ppermute | solution.py:385
  97.0 27.0 %collective-permute-start.11 = (bf16[512,256]{1,0:T(8,128)(2,1)S(1)}, bf16[512,256]{1,0:T(8,128)(2,1)S(1)}, u32[]{:S(2)}, u32[]{:S(2)}) collective-permute-start(bf16[512,256]{1,0:T(8,128)(2,1)S(1)} %get-tuple-element.28), channel_id=1, source_target_pairs={{8,0},{16,8},{24,16},{9,1},{17,9},{25,17},{10,2},{18,10},{26,18},{... | collective-permute-start | bytes 786440 | tf_op jit(solution)/shard_map/ppermute | solution.py:385
  101.1 22.9 %collective-permute-start.12 = (bf16[512,256]{1,0:T(8,128)(2,1)S(1)}, bf16[512,256]{1,0:T(8,128)(2,1)S(1)}, u32[]{:S(2)}, u32[]{:S(2)}) collective-permute-start(bf16[512,256]{1,0:T(8,128)(2,1)S(1)} %get-tuple-element.29), channel_id=1, source_target_pairs={{16,0},{24,8},{17,1},{25,9},{18,2},{26,10},{19,3},{27,11},{20,4},{... | collective-permute-start | bytes 786440 | tf_op jit(solution)/shard_map/ppermute | solution.py:385
  107.9 16.2 %collective-permute-start.13 = (bf16[512,256]{1,0:T(8,128)(2,1)S(1)}, bf16[512,256]{1,0:T(8,128)(2,1)S(1)}, u32[]{:S(2)}, u32[]{:S(2)}) collective-permute-start(bf16[512,256]{1,0:T(8,128)(2,1)S(1)} %get-tuple-element.30), channel_id=1, source_target_pairs={{24,0},{25,1},{26,2},{27,3},{28,4},{29,5},{30,6},{31,7},{56,32},{5... | collective-permute-start | bytes 786440 | tf_op jit(solution)/shard_map/ppermute | solution.py:385
  109.3 12.8 %collective-permute-start.17 = (bf16[256,256]{1,0:T(8,128)(2,1)S(1)}, bf16[256,256]{1,0:T(8,128)(2,1)S(1)}, u32[]{:S(2)}, u32[]{:S(2)}) collective-permute-start(bf16[256,256]{1,0:T(8,128)(2,1)S(1)} %shard_map.89), channel_id=1, source_target_pairs={{32,0},{64,32},{96,64},{128,96},{160,128},{192,160},{224,192},{256... | collective-permute-start | bytes 393224 | tf_op jit(solution)/shard_map/ppermute | solution.py:392
  122.1 2.1 %collective-permute-start.19 = (bf16[256,256]{1,0:T(8,128)(2,1)S(1)}, bf16[256,256]{1,0:T(8,128)(2,1)S(1)}, u32[]{:S(2)}, u32[]{:S(2)}) collective-permute-start(bf16[256,256]{1,0:T(8,128)(2,1)S(1)} %collective-permute-done.17.refs_0_), channel_id=1, source_target_pairs={{0,16},{1,17},{2,18},{3,19},{4,20},{5,21},{6,22},{7,23},{32,48},{3... | collective-permute-start | bytes 393224 | tf_op jit(solution)/shard_map/ppermute | solution.py:385
  122.7 6.2 %collective-permute-start.18 = (bf16[256,256]{1,0:T(8,128)(2,1)S(1)}, bf16[256,256]{1,0:T(8,128)(2,1)S(1)}, u32[]{:S(2)}, u32[]{:S(2)}) collective-permute-start(bf16[256,256]{1,0:T(8,128)(2,1)S(1)} %collective-permute-done.17.refs_0_), channel_id=1, source_target_pairs={{0,8},{8,16},{16,24},{1,9},{9,17},{17,25},{2,10},{10,18},{18,26},{... | collective-permute-start | bytes 393224 | tf_op jit(solution)/shard_map/ppermute | solution.py:385
  130.4 23.3 %all-to-all-start.3 = ((bf16[8,64,256]{2,1,0:T(8,128)(2,1)}), bf16[8,64,256]{2,1,0:T(8,128)(2,1)S(1)}, u32[]{:S(2)}, u32[]{:S(2)}) async-start(bf16[8,64,256]{2,1,0:T(8,128)(2,1)} %bitcast.22), calls=%async_computation.3 | async-start | bytes 524288 | tf_op jit(solution)/shard_map/all_to_all | solution.py:439
  (18 other events, 162.2 us)

commit v4 on v3

--- a/solution.py
+++ b/solution.py
@@ -270,7 +270,7 @@
 
 
 def spread_kernel(table, keep_hbm, got_hbm, *refs):
-    outs, (total, terms, own_ref, within_ref, stack_ref, sem, out_sem) = refs[:-7], refs[-7:]
+    outs, (total, terms, sem) = refs[:-3], refs[-3:]
     copies = [
         [
             pltpu.make_async_copy(part(src, i), part(terms.at[k], i), sem.at[k, i])
@@ -288,23 +288,10 @@
             copies[k][i].wait()
             at = pl.ds(pl.multiple_of(table[offset + i] * TOK, TOK), TOK)
             total[at, :] += source[i * TOK : (i + 1) * TOK, :].astype(F32)
-    outgoing = []
-
-    def leave(src, dst):
-        outgoing.append(pltpu.make_async_copy(src, dst, out_sem.at[len(outgoing)]))
-        outgoing[-1].start()
-
     for k in range(CHIPS):
+        outs[k][...] = total[k * PAIR : (k + 1) * PAIR, :].astype(outs[k].dtype)
         low = CHIPS * PAIR + k * TOK
-        stack_ref[k] = total[low : low + TOK, :].astype(BF16)
-        leave(stack_ref.at[k], outs[CHIPS + k])
-    for k in range(1, CHIPS):
-        within_ref[k - 1] = total[k * PAIR : (k + 1) * PAIR, :].astype(BF16)
-        leave(within_ref.at[k - 1], outs[k])
-    own_ref[...] = total[:PAIR, :]
-    leave(own_ref, outs[0])
-    for copy in outgoing:
-        copy.wait()
+        outs[CHIPS + k][...] = total[low : low + TOK, :].astype(BF16)
 
 
 def call_spread(table, keep, got):
@@ -317,15 +304,11 @@
             + [jax.ShapeDtypeStruct((TOK, HD), BF16)] * CHIPS
         ),
         in_specs=[SMEM, ANY, ANY],
-        out_specs=(ANY,) * (2 * CHIPS),
+        out_specs=(VMEM,) * (2 * CHIPS),
         scratch_shapes=[
             pltpu.VMEM((CHIPS * PAIR + CHIPS * TOK, HD), F32),
             pltpu.VMEM((CORES, KEYS, HD), BF16),
-            pltpu.VMEM((PAIR, HD), F32),
-            pltpu.VMEM((CHIPS - 1, PAIR, HD), BF16),
-            pltpu.VMEM((CHIPS, TOK, HD), BF16),
             pltpu.SemaphoreType.DMA((CORES, SLOTS)),
-            pltpu.SemaphoreType.DMA((2 * CHIPS,)),
         ],
     )(table, keep, got)
 
@@ -409,15 +392,17 @@
         tiled=True,
     )
     table, slot_depth, pair_depth = plan(parent_gap, row, chip, core)
-    slot_angles, pair_angles = angles_of(slot_depth), angles_of(pair_depth)
+    pair_angles = angles_of(pair_depth)
+    pair_cos, pair_sin = jnp.cos(pair_angles), jnp.sin(pair_angles)
+    table, pair_cos, pair_sin = lax.optimization_barrier((table, pair_cos, pair_sin))
+    pairs = [both, along(both, -1), along(both, -2, (2,))]
+    held, slot_depth = lax.optimization_barrier(
+        (call_pick(table, pairs, SEND, 1), slot_depth)
+    )
+    relay = next_row(held, 1)
+    slot_angles = angles_of(slot_depth)
     slot_cos, slot_sin = jnp.cos(slot_angles), jnp.sin(slot_angles)
-    pair_cos, pair_sin = jnp.cos(pair_angles), jnp.sin(pair_angles)
-    table, slot_cos, slot_sin, pair_cos, pair_sin = lax.optimization_barrier(
-        (table, slot_cos, slot_sin, pair_cos, pair_sin)
-    )
-
-    pairs = [both, along(both, -1), along(both, -2, (2,))]
-    relay = next_row(call_pick(table, pairs, SEND, 1), 1)
+    relay, slot_cos, slot_sin = lax.optimization_barrier((relay, slot_cos, slot_sin))
     sources = [both] + [along(both, k) for k in (1, 2, 3)]
     query_grad = jnp.concatenate(
         [queries.reshape(tokens, HEADS, WIDE), grad_attn.reshape(tokens, HEADS, WIDE)], 2

time: 155 us -> 153 us (0.987)
  no operation moved by 1% of the time
where the time goes in v4:
time: 153 us; the launch traced here: 152 us
  starting transfers between devices  89.3 us (58%)
  waiting for transfers between devices  28.7 us (19%)
  Pallas kernels  14 us (9%)
  other arithmetic  9.05 us (6%)
  local copies, waits for them, and re-layouts  7.55 us (5%)
  between operations  3.68 us (2%)
    ppermute x16, starting transfers between devices, along(): lax.ppermute(block, 'chip', [(i, i + shift) for i in starts if 0 <= i + s...  36.6 us
    all_to_all x1, starting transfers between devices, shards(): lax.all_to_all(grad_both, ('core', 'head'), split_axis=0, concat_axis=1,...  14.4 us
    all_to_all x1, starting transfers between devices, shards(): out = lax.all_to_all(out, 'head', split_axis=0, concat_axis=1, tiled=True)  11.4 us
    ppermute x2, waiting for transfers between devices, next_row(): lax.ppermute(block, 'row', [(i, i + shift) for i in range(rows) if 0 <= i...  10.9 us
    ppermute x2, starting transfers between devices, next_row(): lax.ppermute(block, 'row', [(i, i + shift) for i in range(rows) if 0 <= i...  10.4 us
    ppermute x16, waiting for transfers between devices, along(): lax.ppermute(block, 'chip', [(i, i + shift) for i in starts if 0 <= i + s...  7.76 us
    pallas_call x1, Pallas kernels, call_attend(): pl.pallas_call(attend_kernel, out_shape=(jax.ShapeDtypeStruct((TOK, 2 * W...  6.96 us
    all_to_all x1, starting transfers between devices, shards(): lax.all_to_all(jnp.concatenate([keys, values], 1), ('core', 'head'), spli...  6.7 us
  transfers between devices with their start and end apart: 24, of which 8 were waited for; matrix products, arithmetic and copies ran while one was open for 8% of the time, Pallas kernels for 5%

profile of v4, /device:TPU:31, one launch (start us, length us, event | category | flops | bytes accessed | tf_op | source)
XLA Modules:
  0.0 152.2 jit_solution(10072038238776998355)
XLA Ops:
  2.3 6.7 %all-to-all-start.1 = ((bf16[64,8,256]{2,0,1:T(8,128)(2,1)}), bf16[64,8,256]{2,0,1:T(8,128)(2,1)S(1)}, u32[]{:S(2)}, u32[]{:S(2)}) async-start(bf16[64,8,256]{2,0,1:T(8,128)(2,1)} %bitcast.51), calls=%async_computation.1 | async-start | bytes 524288 | tf_op jit(solution)/shard_map/all_to_all | solution.py:387
  18.1 3.5 %all-to-all-start = ((bf16[64,4,1024]{2,0,1:T(8,128)(2,1)}), bf16[64,4,1024]{2,0,1:T(8,128)(2,1)S(1)}, u32[]{:S(2)}, u32[]{:S(2)}) async-start(bf16[64,4,1024]{2,0,1:T(8,128)(2,1)} %pad_maximum_fusion), calls=%async_computation | async-start | bytes 1048576 | tf_op jit(solution)/shard_map/all_to_all | solution.py:410
  22.2 3.9 %collective-permute-start = (bf16[512,256]{1,0:T(8,128)(2,1)S(1)}, bf16[512,256]{1,0:T(8,128)(2,1)S(1)}, u32[]{:S(2)}, u32[]{:S(2)}) collective-permute-start(bf16[512,256]{1,0:T(8,128)(2,1)S(1)} %bitcast.55), channel_id=1, source_target_pairs={{8,0},{16,8},{24,16},{9,1},{17,9},{25,17},{10,2},{18,10},{26,18},{... | collective-permute-start | bytes 786440 | tf_op jit(solution)/shard_map/ppermute | solution.py:368
  32.0 8.5 %collective-permute-start.2 = (bf16[256,256]{1,0:T(8,128)(2,1)S(1)}, bf16[256,256]{1,0:T(8,128)(2,1)S(1)}, u32[]{:S(2)}, u32[]{:S(2)}) collective-permute-start(bf16[256,256]{1,0:T(8,128)(2,1)S(1)} %shard_map.84), channel_id=1, source_target_pairs={{0,32},{32,64},{64,96},{96,128},{128,160},{160,192},{192,224},{224... | collective-permute-start | bytes 393224 | tf_op jit(solution)/shard_map/ppermute | solution.py:375
  40.5 3.8 %multiply_sine_fusion = (f32[1280,128]{1,0:T(8,128)}, f32[1280,128]{1,0:T(8,128)}) fusion(f32[128]{0:T(128)S(1)} %multiply_exponential_fusion, f32[1280]{0:T(1024)S(1)} %convert_element_type.43), kind=kLoop, calls=%fused_computation | loop fusion | flops 163840 | bytes 1316352 | tf_op jit(solution)/shard_map/sin | solution.py:404
  44.3 6.4 %collective-permute-start.8 = (bf16[256,256]{1,0:T(8,128)(2,1)S(1)}, bf16[256,256]{1,0:T(8,128)(2,1)S(1)}, u32[]{:S(2)}, u32[]{:S(2)}) collective-permute-start(bf16[256,256]{1,0:T(8,128)(2,1)S(1)} %collective-permute-done.2.refs_4_), channel_id=1, source_target_pairs={{24,0},{25,1},{26,2},{27,3},{28,4},{29,5},{30,6},{31,7},{56,32},{5... | collective-permute-start | bytes 393224 | tf_op jit(solution)/shard_map/ppermute | solution.py:368
  52.0 2.5 %collective-permute-start.6 = (bf16[256,256]{1,0:T(8,128)(2,1)S(1)}, bf16[256,256]{1,0:T(8,128)(2,1)S(1)}, u32[]{:S(2)}, u32[]{:S(2)}) collective-permute-start(bf16[256,256]{1,0:T(8,128)(2,1)S(1)} %collective-permute-done.2.refs_4_), channel_id=1, source_target_pairs={{8,0},{16,8},{24,16},{9,1},{17,9},{25,17},{10,2},{18,10},{26,18},{... | collective-permute-start | bytes 393224 | tf_op jit(solution)/shard_map/ppermute | solution.py:368
  54.6 2.9 %collective-permute-done.6.refs_5_ = bf16[256,256]{1,0:T(8,128)(2,1)S(1)} collective-permute-done((bf16[256,256]{1,0:T(8,128)(2,1)S(1)}, bf16[256,256]{1,0:T(8,128)(2,1)S(1)}, u32[]{:S(2)}, u32[]{:S(2)}) %collective-permute-start.6) | collective-permute-done | bytes 131104 | tf_op jit(solution)/shard_map/ppermute | solution.py:368
  57.5 1.8 %shard_map.85 = bf16[1280,256]{1,0:T(8,128)(2,1)S(1)} custom-call(s32[19]{0:T(128)S(1)} %concatenate.17.table, bf16[512,256]{1,0:T(8,128)(2,1)S(1)} %bitcast.60, bf16[512,256]{1,0:T(8,128)(2,1)S(1)} %collective-permute-done.3.refs_1_, bf16[512,256]{1,0:T(8,128)(2,1)S(1)} %collective-permute-done.4.refs_2_, ...), custom_call_target="tpu_custom_call" | custom-call | tf_op jit(solution)/shard_map/pallas_call | solution.py:124
  59.3 3.7 %collective-permute-start.9 = (bf16[1280,256]{1,0:T(8,128)(2,1)S(1)}, bf16[1280,256]{1,0:T(8,128)(2,1)}, u32[]{:S(2)}, u32[]{:S(2)}) collective-permute-start(bf16[1280,256]{1,0:T(8,128)(2,1)S(1)} %shard_map.85), channel_id=1, source_target_pairs={{0,4},{4,0},{1,5},{5,1},{2,6},{6,2},{3,7},{7,3},{8,12},{12,8},{9,1... | collective-permute-start | bytes 1966088 | tf_op jit(solution)/shard_map/ppermute | solution.py:381
  63.1 1.8 %collective-permute-done.9.other_hbm = bf16[1280,256]{1,0:T(8,128)(2,1)} collective-permute-done((bf16[1280,256]{1,0:T(8,128)(2,1)S(1)}, bf16[1280,256]{1,0:T(8,128)(2,1)}, u32[]{:S(2)}, u32[]{:S(2)}) %collective-permute-start.9) | collective-permute-done | bytes 655392 | tf_op jit(solution)/shard_map/ppermute | solution.py:381
  64.9 7.0 %shard_map.86 = (bf16[256,1024]{1,0:T(8,128)(2,1)}, bf16[1280,256]{1,0:T(8,128)(2,1)}, bf16[1280,256]{1,0:T(8,128)(2,1)}) custom-call(s32[19]{0:T(128)} %copy-done.9, bf16[256,1024]{1,0:T(8,128)(2,1)} %bitcast.62, f32[1280,128]{1,0:T(8,128)} %get-tuple-element.28.cos_hbm, f32[1280,128]{1,0:T(8,128)} %get-tuple-element.29.sin_hbm, ...), custom_call_target="tpu_custom_call" | custom-call | tf_op jit(solution)/shard_map/pallas_call | solution.py:242
  71.9 11.4 %all-to-all-start.2 = ((bf16[4,64,1024]{2,1,0:T(8,128)(2,1)}), bf16[4,64,1024]{2,1,0:T(8,128)(2,1)S(1)}, u32[]{:S(2)}, u32[]{:S(2)}) async-start(bf16[4,64,1024]{2,1,0:T(8,128)(2,1)} %bitcast.70), calls=%async_computation.2 | async-start | bytes 1048576 | tf_op jit(solution)/shard_map/all_to_all | solution.py:415
  83.3 2.7 %collective-permute-start.10 = (bf16[1280,256]{1,0:T(8,128)(2,1)}, bf16[1280,256]{1,0:T(8,128)(2,1)S(1)}, u32[]{:S(2)}, u32[]{:S(2)}) collective-permute-start(bf16[1280,256]{1,0:T(8,128)(2,1)} %get-tuple-element.32), channel_id=1, source_target_pairs={{0,4},{4,0},{1,5},{5,1},{2,6},{6,2},{3,7},{7,3},{8,12},{12,8},{9,1... | collective-permute-start | bytes 1966088 | tf_op jit(solution)/shard_map/ppermute | solution.py:381
  86.0 1.9 %collective-permute-done.10.got_hbm = bf16[1280,256]{1,0:T(8,128)(2,1)S(1)} collective-permute-done((bf16[1280,256]{1,0:T(8,128)(2,1)}, bf16[1280,256]{1,0:T(8,128)(2,1)S(1)}, u32[]{:S(2)}, u32[]{:S(2)}) %collective-permute-start.10) | collective-permute-done | bytes 655392 | tf_op jit(solution)/shard_map/ppermute | solution.py:381
  87.9 3.0 %shard_map.87 = (f32[512,256]{1,0:T(8,128)S(1)}, bf16[512,256]{1,0:T(8,128)(2,1)S(1)}, bf16[512,256]{1,0:T(8,128)(2,1)S(1)}, bf16[512,256]{1,0:T(8,128)(2,1)S(1)...) custom-call(s32[19]{0:T(128)S(1)} %copy-done.10, ...), custom_call_target="tpu_custom_call" | custom-call | tf_op jit(solution)/shard_map/pallas_call | solution.py:298
  94.7 4.1 %collective-permute-start.11 = (bf16[512,256]{1,0:T(8,128)(2,1)S(1)}, bf16[512,256]{1,0:T(8,128)(2,1)S(1)}, u32[]{:S(2)}, u32[]{:S(2)}) collective-permute-start(bf16[512,256]{1,0:T(8,128)(2,1)S(1)} %get-tuple-element.34), channel_id=1, source_target_pairs={{8,0},{16,8},{24,16},{9,1},{17,9},{25,17},{10,2},{18,10},{26,18},{... | collective-permute-start | bytes 786440 | tf_op jit(solution)/shard_map/ppermute | solution.py:368
  98.9 6.7 %collective-permute-start.12 = (bf16[512,256]{1,0:T(8,128)(2,1)S(1)}, bf16[512,256]{1,0:T(8,128)(2,1)S(1)}, u32[]{:S(2)}, u32[]{:S(2)}) collective-permute-start(bf16[512,256]{1,0:T(8,128)(2,1)S(1)} %get-tuple-element.35), channel_id=1, source_target_pairs={{16,0},{24,8},{17,1},{25,9},{18,2},{26,10},{19,3},{27,11},{20,4},{... | collective-permute-start | bytes 786440 | tf_op jit(solution)/shard_map/ppermute | solution.py:368
  107.0 1.9 %collective-permute-start.17 = (bf16[256,256]{1,0:T(8,128)(2,1)S(1)}, bf16[256,256]{1,0:T(8,128)(2,1)S(1)}, u32[]{:S(2)}, u32[]{:S(2)}) collective-permute-start(bf16[256,256]{1,0:T(8,128)(2,1)S(1)} %shard_map.89), channel_id=1, source_target_pairs={{32,0},{64,32},{96,64},{128,96},{160,128},{192,160},{224,192},{256... | collective-permute-start | bytes 393224 | tf_op jit(solution)/shard_map/ppermute | solution.py:375
  109.0 10.9 %collective-permute-done.17.refs_0_ = bf16[256,256]{1,0:T(8,128)(2,1)S(1)} collective-permute-done((bf16[256,256]{1,0:T(8,128)(2,1)S(1)}, bf16[256,256]{1,0:T(8,128)(2,1)S(1)}, u32[]{:S(2)}, u32[]{:S(2)}) %collective-permute-start.17) | collective-permute-done | bytes 131104 | tf_op jit(solution)/shard_map/ppermute | solution.py:375
  121.9 4.8 %collective-permute-done.18.refs_1_ = bf16[256,256]{1,0:T(8,128)(2,1)S(1)} collective-permute-done((bf16[256,256]{1,0:T(8,128)(2,1)S(1)}, bf16[256,256]{1,0:T(8,128)(2,1)S(1)}, u32[]{:S(2)}, u32[]{:S(2)}) %collective-permute-start.18) | collective-permute-done | bytes 131104 | tf_op jit(solution)/shard_map/ppermute | solution.py:368
  128.1 14.4 %all-to-all-start.3 = ((bf16[8,64,256]{2,1,0:T(8,128)(2,1)}), bf16[8,64,256]{2,1,0:T(8,128)(2,1)S(1)}, u32[]{:S(2)}, u32[]{:S(2)}) async-start(bf16[8,64,256]{2,1,0:T(8,128)(2,1)} %bitcast.22), calls=%async_computation.3 | async-start | bytes 524288 | tf_op jit(solution)/shard_map/all_to_all | solution.py:424
  142.9 2.4 %slice_reduce_fusion = (bf16[64,4,512]{2,1,0:T(4,128)(2,1)S(1)}, bf16[64,4,512]{2,1,0:T(4,128)(2,1)S(1)}) fusion(bf16[64,4,2,512]{3,2,1,0:T(2,128)(2,1)S(1)} %reshape.166), kind=kLoop, calls=%fused_computation.2 | loop fusion | bytes 1048576 | tf_op jit(solution)/shard_map/slice | solution.py:427
  146.7 4.8 %all-to-all-done.3 = bf16[8,64,256]{2,1,0:T(8,128)(2,1)S(1)} async-done(((bf16[8,64,256]{2,1,0:T(8,128)(2,1)}), bf16[8,64,256]{2,1,0:T(8,128)(2,1)S(1)}, u32[]{:S(2)}, u32[]{:S(2)}) %all-to-all-start.3) | async-done | bytes 262176 | tf_op jit(solution)/shard_map/all_to_all | solution.py:424
  (110 shorter events, 27.4 us)
Async XLA Ops:
  2.3 15.7 %all-to-all-start.1 = ((bf16[64,8,256]{2,0,1:T(8,128)(2,1)}), bf16[64,8,256]{2,0,1:T(8,128)(2,1)S(1)}, u32[]{:S(2)}, u32[]{:S(2)}) async-start(bf16[64,8,256]{2,0,1:T(8,128)(2,1)} %bitcast.51), calls=%async_computation.1 | async-start | bytes 524288 | tf_op jit(solution)/shard_map/all_to_all | solution.py:387
  18.1 45.0 %all-to-all-start = ((bf16[64,4,1024]{2,0,1:T(8,128)(2,1)}), bf16[64,4,1024]{2,0,1:T(8,128)(2,1)S(1)}, u32[]{:S(2)}, u32[]{:S(2)}) async-start(bf16[64,4,1024]{2,0,1:T(8,128)(2,1)} %pad_maximum_fusion), calls=%async_computation | async-start | bytes 1048576 | tf_op jit(solution)/shard_map/all_to_all | solution.py:410
  21.6 9.6 %collective-permute-start.1 = (bf16[512,256]{1,0:T(8,128)(2,1)S(1)}, bf16[512,256]{1,0:T(8,128)(2,1)S(1)}, u32[]{:S(2)}, u32[]{:S(2)}) collective-permute-start(bf16[512,256]{1,0:T(8,128)(2,1)S(1)} %bitcast.54), channel_id=1, source_target_pairs={{16,0},{17,1},{18,2},{19,3},{20,4},{21,5},{22,6},{23,7},{48,32},{4... | collective-permute-start | bytes 786440 | tf_op jit(solution)/shard_map/ppermute | solution.py:368
  22.2 9.0 %collective-permute-start = (bf16[512,256]{1,0:T(8,128)(2,1)S(1)}, bf16[512,256]{1,0:T(8,128)(2,1)S(1)}, u32[]{:S(2)}, u32[]{:S(2)}) collective-permute-start(bf16[512,256]{1,0:T(8,128)(2,1)S(1)} %bitcast.55), channel_id=1, source_target_pairs={{8,0},{16,8},{24,16},{9,1},{17,9},{25,17},{10,2},{18,10},{26,18},{... | collective-permute-start | bytes 786440 | tf_op jit(solution)/shard_map/ppermute | solution.py:368
  27.2 24.8 %collective-permute-start.5 = (bf16[512,256]{1,0:T(8,128)(2,1)S(1)}, bf16[512,256]{1,0:T(8,128)(2,1)S(1)}, u32[]{:S(2)}, u32[]{:S(2)}) collective-permute-start(bf16[512,256]{1,0:T(8,128)(2,1)S(1)} %bitcast.56), channel_id=1, source_target_pairs={{0,24},{1,25},{2,26},{3,27},{4,28},{5,29},{6,30},{7,31},{32,56},{3... | collective-permute-start | bytes 786440 | tf_op jit(solution)/shard_map/ppermute | solution.py:368
  28.5 26.0 %collective-permute-start.4 = (bf16[512,256]{1,0:T(8,128)(2,1)S(1)}, bf16[512,256]{1,0:T(8,128)(2,1)S(1)}, u32[]{:S(2)}, u32[]{:S(2)}) collective-permute-start(bf16[512,256]{1,0:T(8,128)(2,1)S(1)} %bitcast.57), channel_id=1, source_target_pairs={{0,16},{8,24},{1,17},{9,25},{2,18},{10,26},{3,19},{11,27},{4,20},{... | collective-permute-start | bytes 786440 | tf_op jit(solution)/shard_map/ppermute | solution.py:368
  29.8 24.7 %collective-permute-start.3 = (bf16[512,256]{1,0:T(8,128)(2,1)S(1)}, bf16[512,256]{1,0:T(8,128)(2,1)S(1)}, u32[]{:S(2)}, u32[]{:S(2)}) collective-permute-start(bf16[512,256]{1,0:T(8,128)(2,1)S(1)} %bitcast.58), channel_id=1, source_target_pairs={{0,8},{8,16},{16,24},{1,9},{9,17},{17,25},{2,10},{10,18},{18,26},{... | collective-permute-start | bytes 786440 | tf_op jit(solution)/shard_map/ppermute | solution.py:368
  32.0 12.3 %collective-permute-start.2 = (bf16[256,256]{1,0:T(8,128)(2,1)S(1)}, bf16[256,256]{1,0:T(8,128)(2,1)S(1)}, u32[]{:S(2)}, u32[]{:S(2)}) collective-permute-start(bf16[256,256]{1,0:T(8,128)(2,1)S(1)} %shard_map.84), channel_id=1, source_target_pairs={{0,32},{32,64},{64,96},{96,128},{128,160},{160,192},{192,224},{224... | collective-permute-start | bytes 393224 | tf_op jit(solution)/shard_map/ppermute | solution.py:375
  44.3 10.2 %collective-permute-start.8 = (bf16[256,256]{1,0:T(8,128)(2,1)S(1)}, bf16[256,256]{1,0:T(8,128)(2,1)S(1)}, u32[]{:S(2)}, u32[]{:S(2)}) collective-permute-start(bf16[256,256]{1,0:T(8,128)(2,1)S(1)} %collective-permute-done.2.refs_4_), channel_id=1, source_target_pairs={{24,0},{25,1},{26,2},{27,3},{28,4},{29,5},{30,6},{31,7},{56,32},{5... | collective-permute-start | bytes 393224 | tf_op jit(solution)/shard_map/ppermute | solution.py:368
  50.7 3.9 %collective-permute-start.7 = (bf16[256,256]{1,0:T(8,128)(2,1)S(1)}, bf16[256,256]{1,0:T(8,128)(2,1)S(1)}, u32[]{:S(2)}, u32[]{:S(2)}) collective-permute-start(bf16[256,256]{1,0:T(8,128)(2,1)S(1)} %collective-permute-done.2.refs_4_), channel_id=1, source_target_pairs={{16,0},{24,8},{17,1},{25,9},{18,2},{26,10},{19,3},{27,11},{20,4},{... | collective-permute-start | bytes 393224 | tf_op jit(solution)/shard_map/ppermute | solution.py:368
  52.0 5.5 %collective-permute-start.6 = (bf16[256,256]{1,0:T(8,128)(2,1)S(1)}, bf16[256,256]{1,0:T(8,128)(2,1)S(1)}, u32[]{:S(2)}, u32[]{:S(2)}) collective-permute-start(bf16[256,256]{1,0:T(8,128)(2,1)S(1)} %collective-permute-done.2.refs_4_), channel_id=1, source_target_pairs={{8,0},{16,8},{24,16},{9,1},{17,9},{25,17},{10,2},{18,10},{26,18},{... | collective-permute-start | bytes 393224 | tf_op jit(solution)/shard_map/ppermute | solution.py:368
  59.3 5.6 %collective-permute-start.9 = (bf16[1280,256]{1,0:T(8,128)(2,1)S(1)}, bf16[1280,256]{1,0:T(8,128)(2,1)}, u32[]{:S(2)}, u32[]{:S(2)}) collective-permute-start(bf16[1280,256]{1,0:T(8,128)(2,1)S(1)} %shard_map.85), channel_id=1, source_target_pairs={{0,4},{4,0},{1,5},{5,1},{2,6},{6,2},{3,7},{7,3},{8,12},{12,8},{9,1... | collective-permute-start | bytes 1966088 | tf_op jit(solution)/shard_map/ppermute | solution.py:381
  71.9 56.2 %all-to-all-start.2 = ((bf16[4,64,1024]{2,1,0:T(8,128)(2,1)}), bf16[4,64,1024]{2,1,0:T(8,128)(2,1)S(1)}, u32[]{:S(2)}, u32[]{:S(2)}) async-start(bf16[4,64,1024]{2,1,0:T(8,128)(2,1)} %bitcast.70), calls=%async_computation.2 | async-start | bytes 1048576 | tf_op jit(solution)/shard_map/all_to_all | solution.py:415
  83.3 4.6 %collective-permute-start.10 = (bf16[1280,256]{1,0:T(8,128)(2,1)}, bf16[1280,256]{1,0:T(8,128)(2,1)S(1)}, u32[]{:S(2)}, u32[]{:S(2)}) collective-permute-start(bf16[1280,256]{1,0:T(8,128)(2,1)} %get-tuple-element.32), channel_id=1, source_target_pairs={{0,4},{4,0},{1,5},{5,1},{2,6},{6,2},{3,7},{7,3},{8,12},{12,8},{9,1... | collective-permute-start | bytes 1966088 | tf_op jit(solution)/shard_map/ppermute | solution.py:381
  90.8 14.8 %collective-permute-start.14 = (bf16[256,256]{1,0:T(8,128)(2,1)S(1)}, bf16[256,256]{1,0:T(8,128)(2,1)S(1)}, u32[]{:S(2)}, u32[]{:S(2)}) collective-permute-start(bf16[256,256]{1,0:T(8,128)(2,1)S(1)} %get-tuple-element.38), channel_id=1, source_target_pairs={{0,8},{8,16},{16,24},{1,9},{9,17},{17,25},{2,10},{10,18},{18,26},{... | collective-permute-start | bytes 393224 | tf_op jit(solution)/shard_map/ppermute | solution.py:368
  92.1 14.8 %collective-permute-start.15 = (bf16[256,256]{1,0:T(8,128)(2,1)S(1)}, bf16[256,256]{1,0:T(8,128)(2,1)S(1)}, u32[]{:S(2)}, u32[]{:S(2)}) collective-permute-start(bf16[256,256]{1,0:T(8,128)(2,1)S(1)} %get-tuple-element.39), channel_id=1, source_target_pairs={{0,16},{8,24},{1,17},{9,25},{2,18},{10,26},{3,19},{11,27},{4,20},{... | collective-permute-start | bytes 393224 | tf_op jit(solution)/shard_map/ppermute | solution.py:368
  93.4 13.5 %collective-permute-start.16 = (bf16[256,256]{1,0:T(8,128)(2,1)S(1)}, bf16[256,256]{1,0:T(8,128)(2,1)S(1)}, u32[]{:S(2)}, u32[]{:S(2)}) collective-permute-start(bf16[256,256]{1,0:T(8,128)(2,1)S(1)} %get-tuple-element.40), channel_id=1, source_target_pairs={{0,24},{1,25},{2,26},{3,27},{4,28},{5,29},{6,30},{7,31},{32,56},{3... | collective-permute-start | bytes 393224 | tf_op jit(solution)/shard_map/ppermute | solution.py:368
  94.7 27.0 %collective-permute-start.11 = (bf16[512,256]{1,0:T(8,128)(2,1)S(1)}, bf16[512,256]{1,0:T(8,128)(2,1)S(1)}, u32[]{:S(2)}, u32[]{:S(2)}) collective-permute-start(bf16[512,256]{1,0:T(8,128)(2,1)S(1)} %get-tuple-element.34), channel_id=1, source_target_pairs={{8,0},{16,8},{24,16},{9,1},{17,9},{25,17},{10,2},{18,10},{26,18},{... | collective-permute-start | bytes 786440 | tf_op jit(solution)/shard_map/ppermute | solution.py:368
  98.9 22.9 %collective-permute-start.12 = (bf16[512,256]{1,0:T(8,128)(2,1)S(1)}, bf16[512,256]{1,0:T(8,128)(2,1)S(1)}, u32[]{:S(2)}, u32[]{:S(2)}) collective-permute-start(bf16[512,256]{1,0:T(8,128)(2,1)S(1)} %get-tuple-element.35), channel_id=1, source_target_pairs={{16,0},{24,8},{17,1},{25,9},{18,2},{26,10},{19,3},{27,11},{20,4},{... | collective-permute-start | bytes 786440 | tf_op jit(solution)/shard_map/ppermute | solution.py:368
  105.6 16.2 %collective-permute-start.13 = (bf16[512,256]{1,0:T(8,128)(2,1)S(1)}, bf16[512,256]{1,0:T(8,128)(2,1)S(1)}, u32[]{:S(2)}, u32[]{:S(2)}) collective-permute-start(bf16[512,256]{1,0:T(8,128)(2,1)S(1)} %get-tuple-element.36), channel_id=1, source_target_pairs={{24,0},{25,1},{26,2},{27,3},{28,4},{29,5},{30,6},{31,7},{56,32},{5... | collective-permute-start | bytes 786440 | tf_op jit(solution)/shard_map/ppermute | solution.py:368
  107.0 12.8 %collective-permute-start.17 = (bf16[256,256]{1,0:T(8,128)(2,1)S(1)}, bf16[256,256]{1,0:T(8,128)(2,1)S(1)}, u32[]{:S(2)}, u32[]{:S(2)}) collective-permute-start(bf16[256,256]{1,0:T(8,128)(2,1)S(1)} %shard_map.89), channel_id=1, source_target_pairs={{32,0},{64,32},{96,64},{128,96},{160,128},{192,160},{224,192},{256... | collective-permute-start | bytes 393224 | tf_op jit(solution)/shard_map/ppermute | solution.py:375
  119.8 2.1 %collective-permute-start.19 = (bf16[256,256]{1,0:T(8,128)(2,1)S(1)}, bf16[256,256]{1,0:T(8,128)(2,1)S(1)}, u32[]{:S(2)}, u32[]{:S(2)}) collective-permute-start(bf16[256,256]{1,0:T(8,128)(2,1)S(1)} %collective-permute-done.17.refs_0_), channel_id=1, source_target_pairs={{0,16},{1,17},{2,18},{3,19},{4,20},{5,21},{6,22},{7,23},{32,48},{3... | collective-permute-start | bytes 393224 | tf_op jit(solution)/shard_map/ppermute | solution.py:368
  120.5 6.2 %collective-permute-start.18 = (bf16[256,256]{1,0:T(8,128)(2,1)S(1)}, bf16[256,256]{1,0:T(8,128)(2,1)S(1)}, u32[]{:S(2)}, u32[]{:S(2)}) collective-permute-start(bf16[256,256]{1,0:T(8,128)(2,1)S(1)} %collective-permute-done.17.refs_0_), channel_id=1, source_target_pairs={{0,8},{8,16},{16,24},{1,9},{9,17},{17,25},{2,10},{10,18},{18,26},{... | collective-permute-start | bytes 393224 | tf_op jit(solution)/shard_map/ppermute | solution.py:368
  128.1 23.4 %all-to-all-start.3 = ((bf16[8,64,256]{2,1,0:T(8,128)(2,1)}), bf16[8,64,256]{2,1,0:T(8,128)(2,1)S(1)}, u32[]{:S(2)}, u32[]{:S(2)}) async-start(bf16[8,64,256]{2,1,0:T(8,128)(2,1)} %bitcast.22), calls=%async_computation.3 | async-start | bytes 524288 | tf_op jit(solution)/shard_map/all_to_all | solution.py:424
  (18 other events, 178.6 us)

commit v5 on v4

--- a/solution.py
+++ b/solution.py
@@ -22,7 +22,7 @@
 ROW = CHIPS * CORES
 HEADS = 4
 WIDE = 2 * HD
-OWN, OTHER, SEEN, SEND, LAND, CORE = 0, 5, 10, 14, 15, 18
+OWN, OTHER, SEEN, SEND, LAND, CORE, DEPTHS, PAIRS, TABLE = 0, 5, 10, 14, 15, 18, 19, 24, 32
 BASE = 10000.0
 BF16 = jnp.bfloat16
 F32 = jnp.float32
@@ -39,44 +39,76 @@
 SMEM = pl.BlockSpec(memory_space=pltpu.SMEM)
 
 
-def plan(parent_gap, row, chip, core):
-    count = parent_gap.shape[0]
-    ordinal = jnp.arange(count, dtype=jnp.int32)
-    levels = jnp.arange(LEVELS, dtype=jnp.int32)
-    deeper = (parent_gap == 1).astype(jnp.int32)
-    depths = jnp.sum(jnp.where(ordinal[None, :] <= ordinal[:, None], deeper[None, :], 0), 1)
+def plan_kernel(gap_ref, table):
+    row, chip, core = (lax.axis_index(name) for name in ("row", "chip", "core"))
+    count = gap_ref.shape[0]
     first = row * ROW
     shard = first + chip * CORES + core
-    asked = jnp.stack([shard, shard + 1 - 2 * core, first, first + ROW])
-    own_depth = jnp.sum(
-        jnp.where(ordinal[None, :] <= asked[:, None], deeper[None, :], 0), 1
-    ) + (asked >= count)
-    wanted = own_depth[:, None] - 1 - levels[None, :]
-    match = (depths[None, None, :] == wanted[:, :, None]) & (
-        ordinal[None, None, :] < asked[:, None, None]
-    )
-    elder = jnp.max(jnp.where(match, ordinal[None, None, :], -1), 2)
-    mine, stack, relay = elder[:2], elder[2], elder[3]
-    in_row = 2 * (chip - (mine - first) // CORES) + mine % CORES
-    holder = CHIPS - 1 - jnp.sum(
-        jnp.where(mine[:, :, None] == stack[None, None, :], levels, 0), 2
-    )
-    code = jnp.where(mine >= first, in_row, 2 * CHIPS + holder - chip)
-    code = jnp.clip(jnp.where(mine >= 0, code, 0), 0, 3 * CHIPS - 1)
-    code = jnp.concatenate([jnp.stack([core, 1 - core])[:, None], code], 1).reshape(-1)
-    held = jnp.sum(jnp.where(levels == CHIPS - 1 - chip, relay, 0))
-    far = (held - first) // CORES - chip
-    send = jnp.clip(2 * far + held % CORES, 0, 2 * CHIPS - 3)
-    held = jnp.stack([CHIPS - 1 - chip, CHIPS - chip, jnp.where(chip == 2, CHIPS - 1, CHIPS)])
-    node = jnp.sum(jnp.where(held[:, None] == levels[None, :], relay[None, :], 0), 1)
-    here = (held < LEVELS) & (node >= first) & ((node - first) // CORES == chip)
-    land = jnp.where(here, node % CORES, CORES)
-    table = jnp.concatenate(
-        [code, (elder[0] >= 0).astype(jnp.int32), send[None], land, core[None]]
-    ).astype(jnp.int32)
-    slot_depth = own_depth[0] - jnp.arange(SLOTS, dtype=jnp.int32)
-    pair_depth = jnp.where(core == 0, own_depth[:2], own_depth[1::-1])
-    return table, slot_depth, pair_depth
+    pick = lambda cond, a, b: jnp.where(cond, a, b)
+
+    def gap_of(node):
+        inside = gap_ref[jnp.clip(node, 0, count - 1)]
+        return pick(node >= count, 1, pick(node < 0, 0, inside))
+
+    def elders_of(node):
+        found = []
+        for _ in range(LEVELS):
+            gap = gap_of(node)
+            node = pick(gap > 0, node - gap, -1)
+            found.append(node)
+        return found
+
+    def deeper(node, depth):
+        return depth + pick(gap_ref[node] == 1, 1, 0)
+
+    depth = lax.fori_loop(0, first + chip * CORES + 1, deeper, jnp.int32(0))
+    pair_depth = [depth, deeper(first + chip * CORES + 1, depth)]
+    own_depth = pick(core == 0, pair_depth[0], pair_depth[1])
+    stack, relay = elders_of(first), elders_of(first + ROW)
+    for start, node, half in (
+        (OWN, shard, core),
+        (OTHER, shard + 1 - 2 * core, 1 - core),
+    ):
+        table[start] = half
+        for i, elder in enumerate(elders_of(node)):
+            in_row = 2 * (chip - ((elder - first) >> 1)) + (elder & 1)
+            before = jnp.int32(0)
+            for j in range(LEVELS):
+                before = pick(elder == stack[j], 3 * CHIPS - 1 - j - chip, before)
+            code = pick(elder < 0, 0, pick(elder >= first, in_row, before))
+            table[start + 1 + i] = jnp.clip(code, 0, 3 * CHIPS - 1)
+            if start == OWN:
+                table[SEEN + i] = pick(elder >= 0, 1, 0)
+
+    def held(rank):
+        node = jnp.int32(-1)
+        for j in range(LEVELS):
+            node = pick(rank == j, relay[j], node)
+        return node
+
+    node = held(CHIPS - 1 - chip)
+    code = 2 * (((node - first) >> 1) - chip) + (node & 1)
+    table[SEND] = jnp.clip(code, 0, 2 * CHIPS - 3)
+    for i, rank in enumerate((CHIPS - 1 - chip, CHIPS - chip, pick(chip == 2, CHIPS - 1, CHIPS))):
+        node = held(rank)
+        here = (node >= first) & (((node - first) >> 1) == chip)
+        table[LAND + i] = pick(here, node & 1, CORES)
+    table[CORE] = core
+    for i in range(SLOTS):
+        table[DEPTHS + i] = own_depth - i
+    for i in range(CORES):
+        table[PAIRS + i] = pair_depth[i]
+    for i in range(PAIRS + CORES, TABLE):
+        table[i] = 0
+
+
+def call_plan(parent_gap):
+    return pl.pallas_call(
+        plan_kernel,
+        out_shape=jax.ShapeDtypeStruct((TABLE,), jnp.int32),
+        in_specs=[SMEM],
+        out_specs=SMEM,
+    )(parent_gap)
 
 
 def angles_of(depth):
@@ -241,6 +273,7 @@
 def call_attend(table, query_grad, cosine, sine, other, sources):
     return pl.pallas_call(
         attend_kernel,
+        compiler_params=room(24),
         out_shape=(
             jax.ShapeDtypeStruct((TOK, 2 * WIDE), BF16),
             jax.ShapeDtypeStruct((KEYS, HD), BF16),
@@ -382,7 +415,6 @@
 
 
 def shards(queries, keys, values, grad_attn, parent_gap):
-    row, chip, core = (lax.axis_index(name) for name in ("row", "chip", "core"))
     tokens = queries.shape[0]
     both = lax.all_to_all(
         jnp.concatenate([keys, values], 1),
@@ -391,23 +423,26 @@
         concat_axis=0,
         tiled=True,
     )
-    table, slot_depth, pair_depth = plan(parent_gap, row, chip, core)
+    table = call_plan(parent_gap)
+    slot_depth, pair_depth = table[DEPTHS : DEPTHS + SLOTS], table[PAIRS : PAIRS + CORES]
     pair_angles = angles_of(pair_depth)
     pair_cos, pair_sin = jnp.cos(pair_angles), jnp.sin(pair_angles)
     table, pair_cos, pair_sin = lax.optimization_barrier((table, pair_cos, pair_sin))
     pairs = [both, along(both, -1), along(both, -2, (2,))]
-    held, slot_depth = lax.optimization_barrier(
-        (call_pick(table, pairs, SEND, 1), slot_depth)
-    )
-    relay = next_row(held, 1)
-    slot_angles = angles_of(slot_depth)
-    slot_cos, slot_sin = jnp.cos(slot_angles), jnp.sin(slot_angles)
-    relay, slot_cos, slot_sin = lax.optimization_barrier((relay, slot_cos, slot_sin))
-    sources = [both] + [along(both, k) for k in (1, 2, 3)]
     query_grad = jnp.concatenate(
         [queries.reshape(tokens, HEADS, WIDE), grad_attn.reshape(tokens, HEADS, WIDE)], 2
     ).reshape(tokens, HEADS * 2 * WIDE)
     query_grad = lax.all_to_all(query_grad, "head", split_axis=1, concat_axis=0, tiled=True)
+    held, slot_depth = lax.optimization_barrier(
+        (call_pick(table, pairs, SEND, 1), slot_depth)
+    )
+    relay = next_row(held, 1)
+    slot_angles = angles_of(slot_depth)
+    slot_cos, slot_sin = jnp.cos(slot_angles), jnp.sin(slot_angles)
+    relay, slot_cos, slot_sin, query_grad = lax.optimization_barrier(
+        (relay, slot_cos, slot_sin, query_grad)
+    )
+    sources = [both] + [along(both, k) for k in (1, 2, 3)]
     sources += [relay] + [along(relay, -k) for k in (1, 2, 3)]
     other = swap(call_pick(table, sources, OTHER, SLOTS))
     out, keep, give = call_attend(table, query_grad, slot_cos, slot_sin, other, sources)

time: 153 us -> 159 us (1.039)
  waiting for transfers between devices: 28.7 us -> 33.4 us
  Pallas kernels: 14 us -> 18.6 us
  other arithmetic: 9.05 us -> 5.4 us
  between operations: 3.68 us -> 1.08 us
  starting transfers between devices: 89.3 us -> 90.9 us
    all_to_all x1, waiting for transfers between devices: 1.55 us -> 6.54 us  [shards(): lax.all_to_all(jnp.concatenate([keys, values], 1), ('core', 'head'), spli...]
    pallas_call x1 -> x2, Pallas kernels: 6.96 us -> 11 us  [the longest x1 9.45 us: call_attend(): pl.pallas_call(attend_kernel, compiler_params=room(24), out_shape=(jax.Sh...]
    unnamed x37 -> x17, local copies, waits for them, and re-layouts: 2.23 us -> 4.05 us
  transfers between devices with their start and end apart: 24 -> 24, of which waited for: 8 -> 7; matrix products, arithmetic and copies ran while one was open for 8% -> 6% of each run, Pallas kernels for 5% -> 5%
where the time goes in v5:
time: 159 us; the launch traced here: 158 us
  starting transfers between devices  90.9 us (57%)
  waiting for transfers between devices  33.4 us (21%)
  Pallas kernels  18.6 us (12%)
  local copies, waits for them, and re-layouts  8.4 us (5%)
  other arithmetic  5.4 us (3%)
    ppermute x16, starting transfers between devices, along(): lax.ppermute(block, 'chip', [(i, i + shift) for i in starts if 0 <= i + s...  36.8 us
    all_to_all x1, starting transfers between devices, shards(): lax.all_to_all(grad_both, ('core', 'head'), split_axis=0, concat_axis=1,...  14.3 us
    all_to_all x1, starting transfers between devices, shards(): out = lax.all_to_all(out, 'head', split_axis=0, concat_axis=1, tiled=True)  12.7 us
    ppermute x2, waiting for transfers between devices, next_row(): lax.ppermute(block, 'row', [(i, i + shift) for i in range(rows) if 0 <= i...  10.7 us
    ppermute x2, starting transfers between devices, next_row(): lax.ppermute(block, 'row', [(i, i + shift) for i in range(rows) if 0 <= i...  10.4 us
    pallas_call x1, Pallas kernels, call_attend(): pl.pallas_call(attend_kernel, compiler_params=room(24), out_shape=(jax.Sh...  9.45 us
    ppermute x16, waiting for transfers between devices, along(): lax.ppermute(block, 'chip', [(i, i + shift) for i in starts if 0 <= i + s...  7.74 us
    all_to_all x1, starting transfers between devices, shards(): lax.all_to_all(jnp.concatenate([keys, values], 1), ('core', 'head'), spli...  6.7 us
  transfers between devices with their start and end apart: 24, of which 7 were waited for; matrix products, arithmetic and copies ran while one was open for 6% of the time, Pallas kernels for 5%

profile of v5, /device:TPU:31, one launch (start us, length us, event | category | flops | bytes accessed | tf_op | source)
XLA Modules:
  0.0 157.9 jit_solution(11185655912116190374)
XLA Ops:
  2.3 6.7 %all-to-all-start = ((bf16[64,8,256]{2,0,1:T(8,128)(2,1)}), bf16[64,8,256]{2,0,1:T(8,128)(2,1)S(1)}, u32[]{:S(2)}, u32[]{:S(2)}) async-start(bf16[64,8,256]{2,0,1:T(8,128)(2,1)} %bitcast.30), calls=%async_computation | async-start | bytes 524288 | tf_op jit(solution)/shard_map/all_to_all | solution.py:419
  11.5 6.5 %all-to-all-done = bf16[64,8,256]{2,0,1:T(8,128)(2,1)S(1)} async-done(((bf16[64,8,256]{2,0,1:T(8,128)(2,1)}), bf16[64,8,256]{2,0,1:T(8,128)(2,1)S(1)}, u32[]{:S(2)}, u32[]{:S(2)}) %all-to-all-start) | async-done | bytes 262176 | tf_op jit(solution)/shard_map/all_to_all | solution.py:419
  18.1 3.5 %all-to-all-start.1 = ((bf16[64,4,1024]{2,0,1:T(8,128)(2,1)}), bf16[64,4,1024]{2,0,1:T(8,128)(2,1)S(1)}, u32[]{:S(2)}, u32[]{:S(2)}) async-start(bf16[64,4,1024]{2,0,1:T(8,128)(2,1)} %pad_maximum_fusion), calls=%async_computation.1 | async-start | bytes 1048576 | tf_op jit(solution)/shard_map/all_to_all | solution.py:435
  22.4 3.9 %collective-permute-start = (bf16[512,256]{1,0:T(8,128)(2,1)S(1)}, bf16[512,256]{1,0:T(8,128)(2,1)S(1)}, u32[]{:S(2)}, u32[]{:S(2)}) collective-permute-start(bf16[512,256]{1,0:T(8,128)(2,1)S(1)} %bitcast.32), channel_id=1, source_target_pairs={{8,0},{16,8},{24,16},{9,1},{17,9},{25,17},{10,2},{18,10},{26,18},{... | collective-permute-start | bytes 786440 | tf_op jit(solution)/shard_map/ppermute | solution.py:401
  32.8 8.5 %collective-permute-start.2 = (bf16[256,256]{1,0:T(8,128)(2,1)}, bf16[256,256]{1,0:T(8,128)(2,1)S(1)}, u32[]{:S(2)}, u32[]{:S(2)}) collective-permute-start(bf16[256,256]{1,0:T(8,128)(2,1)} %shard_map.85), channel_id=1, source_target_pairs={{0,32},{32,64},{64,96},{96,128},{128,160},{160,192},{192,224},{224... | collective-permute-start | bytes 393224 | tf_op jit(solution)/shard_map/ppermute | solution.py:408
  41.3 2.3 %multiply_sine_fusion = (f32[1280,128]{1,0:T(8,128)S(1)}, f32[1280,128]{1,0:T(8,128)S(1)}) fusion(f32[128]{0:T(128)S(1)} %multiply_exponential_fusion, f32[1280]{0:T(1024)S(1)} %convert_element_type.23), kind=kLoop, calls=%fused_computation | loop fusion | flops 163840 | bytes 1316352 | tf_op jit(solution)/shard_map/sin | solution.py:441
  43.7 6.4 %collective-permute-start.8 = (bf16[256,256]{1,0:T(8,128)(2,1)S(1)}, bf16[256,256]{1,0:T(8,128)(2,1)S(1)}, u32[]{:S(2)}, u32[]{:S(2)}) collective-permute-start(bf16[256,256]{1,0:T(8,128)(2,1)S(1)} %collective-permute-done.2.refs_4_), channel_id=1, source_target_pairs={{24,0},{25,1},{26,2},{27,3},{28,4},{29,5},{30,6},{31,7},{56,32},{5... | collective-permute-start | bytes 393224 | tf_op jit(solution)/shard_map/ppermute | solution.py:401
  51.4 2.5 %collective-permute-start.6 = (bf16[256,256]{1,0:T(8,128)(2,1)S(1)}, bf16[256,256]{1,0:T(8,128)(2,1)S(1)}, u32[]{:S(2)}, u32[]{:S(2)}) collective-permute-start(bf16[256,256]{1,0:T(8,128)(2,1)S(1)} %collective-permute-done.2.refs_4_), channel_id=1, source_target_pairs={{8,0},{16,8},{24,16},{9,1},{17,9},{25,17},{10,2},{18,10},{26,18},{... | collective-permute-start | bytes 393224 | tf_op jit(solution)/shard_map/ppermute | solution.py:401
  53.9 3.1 %collective-permute-done.6.refs_5_ = bf16[256,256]{1,0:T(8,128)(2,1)S(1)} collective-permute-done((bf16[256,256]{1,0:T(8,128)(2,1)S(1)}, bf16[256,256]{1,0:T(8,128)(2,1)S(1)}, u32[]{:S(2)}, u32[]{:S(2)}) %collective-permute-start.6) | collective-permute-done | bytes 131104 | tf_op jit(solution)/shard_map/ppermute | solution.py:401
  57.0 1.8 %shard_map.86 = bf16[1280,256]{1,0:T(8,128)(2,1)S(1)} custom-call(s32[32]{0:T(128)S(1)} %copy-done.3, bf16[512,256]{1,0:T(8,128)(2,1)S(1)} %bitcast.37, bf16[512,256]{1,0:T(8,128)(2,1)S(1)} %collective-permute-done.3.refs_1_, bf16[512,256]{1,0:T(8,128)(2,1)S(1)} %collective-permute-done.4.refs_2_, bf16[512,256]{1,0:T(8,128)(2,1)S(1)} %collective-permute-done.5.refs_3_, ...), custom_call_target="tpu_custom_call" | custom-call | tf_op jit(solution)/shard_map/pallas_call | solution.py:156
  58.8 4.0 %collective-permute-start.9 = (bf16[1280,256]{1,0:T(8,128)(2,1)S(1)}, bf16[1280,256]{1,0:T(8,128)(2,1)S(1)}, u32[]{:S(2)}, u32[]{:S(2)}) collective-permute-start(bf16[1280,256]{1,0:T(8,128)(2,1)S(1)} %shard_map.86), channel_id=1, source_target_pairs={{0,4},{4,0},{1,5},{5,1},{2,6},{6,2},{3,7},{7,3},{8,12},{12,8},{9,1... | collective-permute-start | bytes 1966088 | tf_op jit(solution)/shard_map/ppermute | solution.py:414
  64.5 9.4 %shard_map.87 = (bf16[256,1024]{1,0:T(8,128)(2,1)S(1)}, bf16[1280,256]{1,0:T(8,128)(2,1)S(1)}, bf16[1280,256]{1,0:T(8,128)(2,1)S(1)}) custom-call(s32[32]{0:T(128)S(1)} %copy-done.3, bf16[256,1024]{1,0:T(8,128)(2,1)S(1)} %bitcast.39, f32[1280,128]{1,0:T(8,128)S(1)} %get-tuple-element.30.cos_hbm, f32[1280,128]{1,0:T(8,128)S(1)} %get-tuple-element.31.sin_hbm, ...), custom_call_target="tpu_custom_call" | custom-call | tf_op jit(solution)/shard_map/pallas_call | solution.py:274
  76.5 12.7 %all-to-all-start.2 = ((bf16[4,64,1024]{2,1,0:T(8,128)(2,1)}), bf16[4,64,1024]{2,1,0:T(8,128)(2,1)S(1)}, u32[]{:S(2)}, u32[]{:S(2)}) async-start(bf16[4,64,1024]{2,1,0:T(8,128)(2,1)} %bitcast.40), calls=%async_computation.2 | async-start | bytes 1048576 | tf_op jit(solution)/shard_map/all_to_all | solution.py:450
  89.2 2.5 %collective-permute-start.10 = (bf16[1280,256]{1,0:T(8,128)(2,1)}, bf16[1280,256]{1,0:T(8,128)(2,1)S(1)}, u32[]{:S(2)}, u32[]{:S(2)}) collective-permute-start(bf16[1280,256]{1,0:T(8,128)(2,1)} %copy-done.4), channel_id=1, source_target_pairs={{0,4},{4,0},{1,5},{5,1},{2,6},{6,2},{3,7},{7,3},{8,12},{12,8},{9,1... | collective-permute-start | bytes 1966088 | tf_op jit(solution)/shard_map/ppermute | solution.py:414
  91.8 1.9 %collective-permute-done.10.got_hbm = bf16[1280,256]{1,0:T(8,128)(2,1)S(1)} collective-permute-done((bf16[1280,256]{1,0:T(8,128)(2,1)}, bf16[1280,256]{1,0:T(8,128)(2,1)S(1)}, u32[]{:S(2)}, u32[]{:S(2)}) %collective-permute-start.10) | collective-permute-done | bytes 655392 | tf_op jit(solution)/shard_map/ppermute | solution.py:414
  93.7 3.0 %shard_map.88 = (f32[512,256]{1,0:T(8,128)S(1)}, bf16[512,256]{1,0:T(8,128)(2,1)S(1)}, bf16[512,256]{1,0:T(8,128)(2,1)S(1)}, bf16[512,256]{1,0:T(8,128)(2,1)S(1)...) custom-call(s32[32]{0:T(128)S(1)} %copy-done.3, ...), custom_call_target="tpu_custom_call" | custom-call | tf_op jit(solution)/shard_map/pallas_call | solution.py:331
  100.6 4.1 %collective-permute-start.11 = (bf16[512,256]{1,0:T(8,128)(2,1)S(1)}, bf16[512,256]{1,0:T(8,128)(2,1)S(1)}, u32[]{:S(2)}, u32[]{:S(2)}) collective-permute-start(bf16[512,256]{1,0:T(8,128)(2,1)S(1)} %get-tuple-element.36), channel_id=1, source_target_pairs={{8,0},{16,8},{24,16},{9,1},{17,9},{25,17},{10,2},{18,10},{26,18},{... | collective-permute-start | bytes 786440 | tf_op jit(solution)/shard_map/ppermute | solution.py:401
  104.7 6.7 %collective-permute-start.12 = (bf16[512,256]{1,0:T(8,128)(2,1)S(1)}, bf16[512,256]{1,0:T(8,128)(2,1)S(1)}, u32[]{:S(2)}, u32[]{:S(2)}) collective-permute-start(bf16[512,256]{1,0:T(8,128)(2,1)S(1)} %get-tuple-element.37), channel_id=1, source_target_pairs={{16,0},{24,8},{17,1},{25,9},{18,2},{26,10},{19,3},{27,11},{20,4},{... | collective-permute-start | bytes 786440 | tf_op jit(solution)/shard_map/ppermute | solution.py:401
  112.9 1.9 %collective-permute-start.17 = (bf16[256,256]{1,0:T(8,128)(2,1)S(1)}, bf16[256,256]{1,0:T(8,128)(2,1)S(1)}, u32[]{:S(2)}, u32[]{:S(2)}) collective-permute-start(bf16[256,256]{1,0:T(8,128)(2,1)S(1)} %shard_map.90), channel_id=1, source_target_pairs={{32,0},{64,32},{96,64},{128,96},{160,128},{192,160},{224,192},{256... | collective-permute-start | bytes 393224 | tf_op jit(solution)/shard_map/ppermute | solution.py:408
  114.8 10.7 %collective-permute-done.17.refs_0_ = bf16[256,256]{1,0:T(8,128)(2,1)S(1)} collective-permute-done((bf16[256,256]{1,0:T(8,128)(2,1)S(1)}, bf16[256,256]{1,0:T(8,128)(2,1)S(1)}, u32[]{:S(2)}, u32[]{:S(2)}) %collective-permute-start.17) | collective-permute-done | bytes 131104 | tf_op jit(solution)/shard_map/ppermute | solution.py:408
  127.8 4.6 %collective-permute-done.18.refs_1_ = bf16[256,256]{1,0:T(8,128)(2,1)S(1)} collective-permute-done((bf16[256,256]{1,0:T(8,128)(2,1)S(1)}, bf16[256,256]{1,0:T(8,128)(2,1)S(1)}, u32[]{:S(2)}, u32[]{:S(2)}) %collective-permute-start.18) | collective-permute-done | bytes 131104 | tf_op jit(solution)/shard_map/ppermute | solution.py:401
  133.8 14.3 %all-to-all-start.3 = ((bf16[8,64,256]{2,1,0:T(8,128)(2,1)}), bf16[8,64,256]{2,1,0:T(8,128)(2,1)S(1)}, u32[]{:S(2)}, u32[]{:S(2)}) async-start(bf16[8,64,256]{2,1,0:T(8,128)(2,1)} %bitcast.7), calls=%async_computation.3 | async-start | bytes 524288 | tf_op jit(solution)/shard_map/all_to_all | solution.py:459
  148.5 2.4 %slice_reduce_fusion = (bf16[64,4,512]{2,1,0:T(4,128)(2,1)S(1)}, bf16[64,4,512]{2,1,0:T(4,128)(2,1)S(1)}) fusion(bf16[64,4,2,512]{3,2,1,0:T(2,128)(2,1)S(1)} %reshape.72), kind=kLoop, calls=%fused_computation.2 | loop fusion | bytes 1048576 | tf_op jit(solution)/shard_map/slice | solution.py:462
  152.3 4.8 %all-to-all-done.3 = bf16[8,64,256]{2,1,0:T(8,128)(2,1)S(1)} async-done(((bf16[8,64,256]{2,1,0:T(8,128)(2,1)}), bf16[8,64,256]{2,1,0:T(8,128)(2,1)S(1)}, u32[]{:S(2)}, u32[]{:S(2)}) %all-to-all-start.3) | async-done | bytes 262176 | tf_op jit(solution)/shard_map/all_to_all | solution.py:459
  (67 shorter events, 28.5 us)
Async XLA Ops:
  2.3 15.7 %all-to-all-start = ((bf16[64,8,256]{2,0,1:T(8,128)(2,1)}), bf16[64,8,256]{2,0,1:T(8,128)(2,1)S(1)}, u32[]{:S(2)}, u32[]{:S(2)}) async-start(bf16[64,8,256]{2,0,1:T(8,128)(2,1)} %bitcast.30), calls=%async_computation | async-start | bytes 524288 | tf_op jit(solution)/shard_map/all_to_all | solution.py:419
  18.1 25.6 %all-to-all-start.1 = ((bf16[64,4,1024]{2,0,1:T(8,128)(2,1)}), bf16[64,4,1024]{2,0,1:T(8,128)(2,1)S(1)}, u32[]{:S(2)}, u32[]{:S(2)}) async-start(bf16[64,4,1024]{2,0,1:T(8,128)(2,1)} %pad_maximum_fusion), calls=%async_computation.1 | async-start | bytes 1048576 | tf_op jit(solution)/shard_map/all_to_all | solution.py:435
  21.7 9.6 %collective-permute-start.1 = (bf16[512,256]{1,0:T(8,128)(2,1)S(1)}, bf16[512,256]{1,0:T(8,128)(2,1)S(1)}, u32[]{:S(2)}, u32[]{:S(2)}) collective-permute-start(bf16[512,256]{1,0:T(8,128)(2,1)S(1)} %bitcast.31), channel_id=1, source_target_pairs={{16,0},{17,1},{18,2},{19,3},{20,4},{21,5},{22,6},{23,7},{48,32},{4... | collective-permute-start | bytes 786440 | tf_op jit(solution)/shard_map/ppermute | solution.py:401
  22.4 9.0 %collective-permute-start = (bf16[512,256]{1,0:T(8,128)(2,1)S(1)}, bf16[512,256]{1,0:T(8,128)(2,1)S(1)}, u32[]{:S(2)}, u32[]{:S(2)}) collective-permute-start(bf16[512,256]{1,0:T(8,128)(2,1)S(1)} %bitcast.32), channel_id=1, source_target_pairs={{8,0},{16,8},{24,16},{9,1},{17,9},{25,17},{10,2},{18,10},{26,18},{... | collective-permute-start | bytes 786440 | tf_op jit(solution)/shard_map/ppermute | solution.py:401
  27.4 24.0 %collective-permute-start.5 = (bf16[512,256]{1,0:T(8,128)(2,1)S(1)}, bf16[512,256]{1,0:T(8,128)(2,1)S(1)}, u32[]{:S(2)}, u32[]{:S(2)}) collective-permute-start(bf16[512,256]{1,0:T(8,128)(2,1)S(1)} %bitcast.33), channel_id=1, source_target_pairs={{0,24},{1,25},{2,26},{3,27},{4,28},{5,29},{6,30},{7,31},{32,56},{3... | collective-permute-start | bytes 786440 | tf_op jit(solution)/shard_map/ppermute | solution.py:401
  28.7 25.2 %collective-permute-start.4 = (bf16[512,256]{1,0:T(8,128)(2,1)S(1)}, bf16[512,256]{1,0:T(8,128)(2,1)S(1)}, u32[]{:S(2)}, u32[]{:S(2)}) collective-permute-start(bf16[512,256]{1,0:T(8,128)(2,1)S(1)} %bitcast.34), channel_id=1, source_target_pairs={{0,16},{8,24},{1,17},{9,25},{2,18},{10,26},{3,19},{11,27},{4,20},{... | collective-permute-start | bytes 786440 | tf_op jit(solution)/shard_map/ppermute | solution.py:401
  30.0 23.9 %collective-permute-start.3 = (bf16[512,256]{1,0:T(8,128)(2,1)S(1)}, bf16[512,256]{1,0:T(8,128)(2,1)S(1)}, u32[]{:S(2)}, u32[]{:S(2)}) collective-permute-start(bf16[512,256]{1,0:T(8,128)(2,1)S(1)} %bitcast.35), channel_id=1, source_target_pairs={{0,8},{8,16},{16,24},{1,9},{9,17},{17,25},{2,10},{10,18},{18,26},{... | collective-permute-start | bytes 786440 | tf_op jit(solution)/shard_map/ppermute | solution.py:401
  32.8 10.8 %collective-permute-start.2 = (bf16[256,256]{1,0:T(8,128)(2,1)}, bf16[256,256]{1,0:T(8,128)(2,1)S(1)}, u32[]{:S(2)}, u32[]{:S(2)}) collective-permute-start(bf16[256,256]{1,0:T(8,128)(2,1)} %shard_map.85), channel_id=1, source_target_pairs={{0,32},{32,64},{64,96},{96,128},{128,160},{160,192},{192,224},{224... | collective-permute-start | bytes 393224 | tf_op jit(solution)/shard_map/ppermute | solution.py:408
  43.7 10.2 %collective-permute-start.8 = (bf16[256,256]{1,0:T(8,128)(2,1)S(1)}, bf16[256,256]{1,0:T(8,128)(2,1)S(1)}, u32[]{:S(2)}, u32[]{:S(2)}) collective-permute-start(bf16[256,256]{1,0:T(8,128)(2,1)S(1)} %collective-permute-done.2.refs_4_), channel_id=1, source_target_pairs={{24,0},{25,1},{26,2},{27,3},{28,4},{29,5},{30,6},{31,7},{56,32},{5... | collective-permute-start | bytes 393224 | tf_op jit(solution)/shard_map/ppermute | solution.py:401
  50.1 3.8 %collective-permute-start.7 = (bf16[256,256]{1,0:T(8,128)(2,1)S(1)}, bf16[256,256]{1,0:T(8,128)(2,1)S(1)}, u32[]{:S(2)}, u32[]{:S(2)}) collective-permute-start(bf16[256,256]{1,0:T(8,128)(2,1)S(1)} %collective-permute-done.2.refs_4_), channel_id=1, source_target_pairs={{16,0},{24,8},{17,1},{25,9},{18,2},{26,10},{19,3},{27,11},{20,4},{... | collective-permute-start | bytes 393224 | tf_op jit(solution)/shard_map/ppermute | solution.py:401
  51.4 5.6 %collective-permute-start.6 = (bf16[256,256]{1,0:T(8,128)(2,1)S(1)}, bf16[256,256]{1,0:T(8,128)(2,1)S(1)}, u32[]{:S(2)}, u32[]{:S(2)}) collective-permute-start(bf16[256,256]{1,0:T(8,128)(2,1)S(1)} %collective-permute-done.2.refs_4_), channel_id=1, source_target_pairs={{8,0},{16,8},{24,16},{9,1},{17,9},{25,17},{10,2},{18,10},{26,18},{... | collective-permute-start | bytes 393224 | tf_op jit(solution)/shard_map/ppermute | solution.py:401
  58.8 5.7 %collective-permute-start.9 = (bf16[1280,256]{1,0:T(8,128)(2,1)S(1)}, bf16[1280,256]{1,0:T(8,128)(2,1)S(1)}, u32[]{:S(2)}, u32[]{:S(2)}) collective-permute-start(bf16[1280,256]{1,0:T(8,128)(2,1)S(1)} %shard_map.86), channel_id=1, source_target_pairs={{0,4},{4,0},{1,5},{5,1},{2,6},{6,2},{3,7},{7,3},{8,12},{12,8},{9,1... | collective-permute-start | bytes 1966088 | tf_op jit(solution)/shard_map/ppermute | solution.py:414
  76.5 57.3 %all-to-all-start.2 = ((bf16[4,64,1024]{2,1,0:T(8,128)(2,1)}), bf16[4,64,1024]{2,1,0:T(8,128)(2,1)S(1)}, u32[]{:S(2)}, u32[]{:S(2)}) async-start(bf16[4,64,1024]{2,1,0:T(8,128)(2,1)} %bitcast.40), calls=%async_computation.2 | async-start | bytes 1048576 | tf_op jit(solution)/shard_map/all_to_all | solution.py:450
  89.2 4.5 %collective-permute-start.10 = (bf16[1280,256]{1,0:T(8,128)(2,1)}, bf16[1280,256]{1,0:T(8,128)(2,1)S(1)}, u32[]{:S(2)}, u32[]{:S(2)}) collective-permute-start(bf16[1280,256]{1,0:T(8,128)(2,1)} %copy-done.4), channel_id=1, source_target_pairs={{0,4},{4,0},{1,5},{5,1},{2,6},{6,2},{3,7},{7,3},{8,12},{12,8},{9,1... | collective-permute-start | bytes 1966088 | tf_op jit(solution)/shard_map/ppermute | solution.py:414
  96.7 14.8 %collective-permute-start.14 = (bf16[256,256]{1,0:T(8,128)(2,1)S(1)}, bf16[256,256]{1,0:T(8,128)(2,1)S(1)}, u32[]{:S(2)}, u32[]{:S(2)}) collective-permute-start(bf16[256,256]{1,0:T(8,128)(2,1)S(1)} %get-tuple-element.40), channel_id=1, source_target_pairs={{0,8},{8,16},{16,24},{1,9},{9,17},{17,25},{2,10},{10,18},{18,26},{... | collective-permute-start | bytes 393224 | tf_op jit(solution)/shard_map/ppermute | solution.py:401
  98.0 14.8 %collective-permute-start.15 = (bf16[256,256]{1,0:T(8,128)(2,1)S(1)}, bf16[256,256]{1,0:T(8,128)(2,1)S(1)}, u32[]{:S(2)}, u32[]{:S(2)}) collective-permute-start(bf16[256,256]{1,0:T(8,128)(2,1)S(1)} %get-tuple-element.41), channel_id=1, source_target_pairs={{0,16},{8,24},{1,17},{9,25},{2,18},{10,26},{3,19},{11,27},{4,20},{... | collective-permute-start | bytes 393224 | tf_op jit(solution)/shard_map/ppermute | solution.py:401
  99.3 13.5 %collective-permute-start.16 = (bf16[256,256]{1,0:T(8,128)(2,1)S(1)}, bf16[256,256]{1,0:T(8,128)(2,1)S(1)}, u32[]{:S(2)}, u32[]{:S(2)}) collective-permute-start(bf16[256,256]{1,0:T(8,128)(2,1)S(1)} %get-tuple-element.42), channel_id=1, source_target_pairs={{0,24},{1,25},{2,26},{3,27},{4,28},{5,29},{6,30},{7,31},{32,56},{3... | collective-permute-start | bytes 393224 | tf_op jit(solution)/shard_map/ppermute | solution.py:401
  100.6 27.1 %collective-permute-start.11 = (bf16[512,256]{1,0:T(8,128)(2,1)S(1)}, bf16[512,256]{1,0:T(8,128)(2,1)S(1)}, u32[]{:S(2)}, u32[]{:S(2)}) collective-permute-start(bf16[512,256]{1,0:T(8,128)(2,1)S(1)} %get-tuple-element.36), channel_id=1, source_target_pairs={{8,0},{16,8},{24,16},{9,1},{17,9},{25,17},{10,2},{18,10},{26,18},{... | collective-permute-start | bytes 786440 | tf_op jit(solution)/shard_map/ppermute | solution.py:401
  104.7 23.0 %collective-permute-start.12 = (bf16[512,256]{1,0:T(8,128)(2,1)S(1)}, bf16[512,256]{1,0:T(8,128)(2,1)S(1)}, u32[]{:S(2)}, u32[]{:S(2)}) collective-permute-start(bf16[512,256]{1,0:T(8,128)(2,1)S(1)} %get-tuple-element.37), channel_id=1, source_target_pairs={{16,0},{24,8},{17,1},{25,9},{18,2},{26,10},{19,3},{27,11},{20,4},{... | collective-permute-start | bytes 786440 | tf_op jit(solution)/shard_map/ppermute | solution.py:401
  111.5 16.3 %collective-permute-start.13 = (bf16[512,256]{1,0:T(8,128)(2,1)S(1)}, bf16[512,256]{1,0:T(8,128)(2,1)S(1)}, u32[]{:S(2)}, u32[]{:S(2)}) collective-permute-start(bf16[512,256]{1,0:T(8,128)(2,1)S(1)} %get-tuple-element.38), channel_id=1, source_target_pairs={{24,0},{25,1},{26,2},{27,3},{28,4},{29,5},{30,6},{31,7},{56,32},{5... | collective-permute-start | bytes 786440 | tf_op jit(solution)/shard_map/ppermute | solution.py:401
  112.9 12.7 %collective-permute-start.17 = (bf16[256,256]{1,0:T(8,128)(2,1)S(1)}, bf16[256,256]{1,0:T(8,128)(2,1)S(1)}, u32[]{:S(2)}, u32[]{:S(2)}) collective-permute-start(bf16[256,256]{1,0:T(8,128)(2,1)S(1)} %shard_map.90), channel_id=1, source_target_pairs={{32,0},{64,32},{96,64},{128,96},{160,128},{192,160},{224,192},{256... | collective-permute-start | bytes 393224 | tf_op jit(solution)/shard_map/ppermute | solution.py:408
  125.5 2.3 %collective-permute-start.19 = (bf16[256,256]{1,0:T(8,128)(2,1)S(1)}, bf16[256,256]{1,0:T(8,128)(2,1)S(1)}, u32[]{:S(2)}, u32[]{:S(2)}) collective-permute-start(bf16[256,256]{1,0:T(8,128)(2,1)S(1)} %collective-permute-done.17.refs_0_), channel_id=1, source_target_pairs={{0,16},{1,17},{2,18},{3,19},{4,20},{5,21},{6,22},{7,23},{32,48},{3... | collective-permute-start | bytes 393224 | tf_op jit(solution)/shard_map/ppermute | solution.py:401
  126.2 6.2 %collective-permute-start.18 = (bf16[256,256]{1,0:T(8,128)(2,1)S(1)}, bf16[256,256]{1,0:T(8,128)(2,1)S(1)}, u32[]{:S(2)}, u32[]{:S(2)}) collective-permute-start(bf16[256,256]{1,0:T(8,128)(2,1)S(1)} %collective-permute-done.17.refs_0_), channel_id=1, source_target_pairs={{0,8},{8,16},{16,24},{1,9},{9,17},{17,25},{2,10},{10,18},{18,26},{... | collective-permute-start | bytes 393224 | tf_op jit(solution)/shard_map/ppermute | solution.py:401
  133.8 23.3 %all-to-all-start.3 = ((bf16[8,64,256]{2,1,0:T(8,128)(2,1)}), bf16[8,64,256]{2,1,0:T(8,128)(2,1)S(1)}, u32[]{:S(2)}, u32[]{:S(2)}) async-start(bf16[8,64,256]{2,1,0:T(8,128)(2,1)} %bitcast.7), calls=%async_computation.3 | async-start | bytes 524288 | tf_op jit(solution)/shard_map/all_to_all | solution.py:459
  (7 other events, 46.3 us)

commit v6 on v5

--- a/solution.py
+++ b/solution.py
@@ -34,7 +34,6 @@
     return pltpu.CompilerParams(vmem_limit_bytes=mib * MIB)
 
 
-ANY = pl.BlockSpec(memory_space=pl.ANY)
 VMEM = pl.BlockSpec(memory_space=pltpu.VMEM)
 SMEM = pl.BlockSpec(memory_space=pltpu.SMEM)
 
@@ -124,20 +123,16 @@
     )
 
 
-def fetch(code, sources, target, sem):
+def fetch(code, sources, target):
     at = 0
     for ref in sources:
         for half in range(ref.shape[0] // TOK):
 
             @pl.when(code == at)
             def _(ref=ref, half=half):
-                pltpu.make_async_copy(ref.at[pl.ds(half * TOK, TOK)], target, sem).start()
+                target[...] = ref[half * TOK : (half + 1) * TOK, :]
 
             at += 1
-
-
-def await_fetch(sources, target, sem):
-    pltpu.make_async_copy(sources[0].at[pl.ds(0, TOK)], target, sem).wait()
 
 
 def part(ref, i):
@@ -145,11 +140,9 @@
 
 
 def pick_kernel(offset, number, table, *refs):
-    sources, (o_ref, sem) = refs[:-2], refs[-2:]
+    sources, o_ref = refs[:-1], refs[-1]
     for i in range(number):
-        fetch(table[offset + i], sources, part(o_ref, i), sem.at[i])
-    for i in range(number):
-        await_fetch(sources, part(o_ref, i), sem.at[i])
+        fetch(table[offset + i], sources, part(o_ref, i))
 
 
 def call_pick(table, sources, offset, number):
@@ -157,9 +150,8 @@
         functools.partial(pick_kernel, offset, number),
         compiler_params=room(4),
         out_shape=jax.ShapeDtypeStruct((number * TOK, HD), BF16),
-        in_specs=[SMEM] + [ANY] * len(sources),
+        in_specs=[SMEM] + [VMEM] * len(sources),
         out_specs=VMEM,
-        scratch_shapes=[pltpu.SemaphoreType.DMA((number,))],
     )(table, *sources)
 
 
@@ -172,30 +164,12 @@
     return lax.dot_general(a, b, dims, preferred_element_type=F32)
 
 
-def attend_kernel(table, qg_hbm, cos_hbm, sin_hbm, other_hbm, *refs):
+def attend_kernel(table, qg_ref, cos_ref, sin_ref, other_ref, *refs):
     sources = refs[: 2 * CHIPS]
-    out_hbm, keep_hbm, give_hbm = refs[2 * CHIPS : 2 * CHIPS + 3]
-    (qg_ref, cos_ref, sin_ref, mine_ref, other_ref, keys, vals, q_all, low_all, score_all) = refs[
-        2 * CHIPS + 3 : 2 * CHIPS + 13
-    ]
-    out_ref, keep_ref, give_ref, sem, in_sem, out_sem = refs[2 * CHIPS + 13 :]
-    whole_in = [
-        pltpu.make_async_copy(src, dst, in_sem.at[i])
-        for i, (src, dst) in enumerate(
-            ((qg_hbm, qg_ref), (cos_hbm, cos_ref), (sin_hbm, sin_ref))
-        )
-    ]
-    other_in = [
-        pltpu.make_async_copy(part(other_hbm, i), part(other_ref, i), sem.at[SLOTS + i])
-        for i in range(SLOTS)
-    ]
-    for copy in whole_in:
-        copy.start()
+    out_ref, keep_ref, give_ref = refs[2 * CHIPS : 2 * CHIPS + 3]
+    mine_ref, keys, vals, q_all, low_all, score_all = refs[2 * CHIPS + 3 :]
     for i in range(SLOTS):
-        fetch(table[OWN + i], sources, part(mine_ref, i), sem.at[i])
-        other_in[i].start()
-    for copy in whole_in:
-        copy.wait()
+        fetch(table[OWN + i], sources, part(mine_ref, i))
     for h in range(2):
         q_all[h * TOK : (h + 1) * TOK, :] = turn(
             qg_ref[:, h * HD : (h + 1) * HD].astype(F32), cos_ref[:TOK, :], sin_ref[:TOK, :]
@@ -203,8 +177,6 @@
     is_key = table[CORE] == 0
     for i in range(SLOTS):
         here = slice(i * TOK, (i + 1) * TOK)
-        await_fetch(sources, part(mine_ref, i), sem.at[i])
-        other_in[i].wait()
         mine, other = mine_ref[here, :], other_ref[here, :]
         keys[here, :] = turn(
             jnp.where(is_key, mine, other).astype(F32), cos_ref[here, :], sin_ref[here, :]
@@ -251,8 +223,6 @@
         out_ref[:, WIDE + h * HD : WIDE + (h + 1) * HD] = turn(
             dot(score_all[rows, :], keys[...], NN), cos_ref[:TOK, :], -sin_ref[:TOK, :]
         ).astype(BF16)
-    outgoing = [pltpu.make_async_copy(out_ref, out_hbm, out_sem.at[0])]
-    outgoing[0].start()
     for i in range(SLOTS):
         cols = slice(i * TOK, (i + 1) * TOK)
         part_key = dot(score_all[:, cols], q_all[...], TN)
@@ -261,13 +231,6 @@
         )
         keep_ref[cols, :] = jnp.where(is_key, part_key, part_value).astype(BF16)
         give_ref[cols, :] = jnp.where(is_key, part_value, part_key).astype(BF16)
-        for k, (src, dst) in enumerate(((give_ref, give_hbm), (keep_ref, keep_hbm))):
-            outgoing.append(
-                pltpu.make_async_copy(part(src, i), part(dst, i), out_sem.at[1 + 2 * i + k])
-            )
-            outgoing[-1].start()
-    for copy in outgoing:
-        copy.wait()
 
 
 def call_attend(table, query_grad, cosine, sine, other, sources):
@@ -279,46 +242,24 @@
             jax.ShapeDtypeStruct((KEYS, HD), BF16),
             jax.ShapeDtypeStruct((KEYS, HD), BF16),
         ),
-        in_specs=[SMEM] + [ANY] * (4 + len(sources)),
-        out_specs=(ANY,) * 3,
+        in_specs=[SMEM] + [VMEM] * (4 + len(sources)),
+        out_specs=(VMEM,) * 3,
         scratch_shapes=[
-            pltpu.VMEM((TOK, 2 * WIDE), BF16),
-            pltpu.VMEM((KEYS, HALF), F32),
-            pltpu.VMEM((KEYS, HALF), F32),
-            pltpu.VMEM((KEYS, HD), BF16),
             pltpu.VMEM((KEYS, HD), BF16),
             pltpu.VMEM((KEYS, HD), BF16),
             pltpu.VMEM((KEYS, HD), BF16),
             pltpu.VMEM((2 * TOK, HD), BF16),
             pltpu.VMEM((2 * TOK, KEYS), BF16),
             pltpu.VMEM((2 * TOK, KEYS), BF16),
-            pltpu.VMEM((TOK, 2 * WIDE), BF16),
-            pltpu.VMEM((KEYS, HD), BF16),
-            pltpu.VMEM((KEYS, HD), BF16),
-            pltpu.SemaphoreType.DMA((2 * SLOTS,)),
-            pltpu.SemaphoreType.DMA((3,)),
-            pltpu.SemaphoreType.DMA((1 + 2 * SLOTS,)),
         ],
     )(table, query_grad, cosine, sine, other, *sources)
 
 
-def spread_kernel(table, keep_hbm, got_hbm, *refs):
-    outs, (total, terms, sem) = refs[:-3], refs[-3:]
-    copies = [
-        [
-            pltpu.make_async_copy(part(src, i), part(terms.at[k], i), sem.at[k, i])
-            for i in range(SLOTS)
-        ]
-        for k, src in enumerate((keep_hbm, got_hbm))
-    ]
-    for group in copies:
-        for copy in group:
-            copy.start()
+def spread_kernel(table, keep_ref, got_ref, *refs):
+    outs, total = refs[:-1], refs[-1]
     total[...] = jnp.zeros_like(total)
-    for k, offset in enumerate((OWN, OTHER)):
-        source = terms.at[k]
+    for source, offset in ((keep_ref, OWN), (got_ref, OTHER)):
         for i in range(SLOTS):
-            copies[k][i].wait()
             at = pl.ds(pl.multiple_of(table[offset + i] * TOK, TOK), TOK)
             total[at, :] += source[i * TOK : (i + 1) * TOK, :].astype(F32)
     for k in range(CHIPS):
@@ -336,12 +277,10 @@
             + [jax.ShapeDtypeStruct((PAIR, HD), BF16)] * (CHIPS - 1)
             + [jax.ShapeDtypeStruct((TOK, HD), BF16)] * CHIPS
         ),
-        in_specs=[SMEM, ANY, ANY],
+        in_specs=[SMEM, VMEM, VMEM],
         out_specs=(VMEM,) * (2 * CHIPS),
         scratch_shapes=[
             pltpu.VMEM((CHIPS * PAIR + CHIPS * TOK, HD), F32),
-            pltpu.VMEM((CORES, KEYS, HD), BF16),
-            pltpu.SemaphoreType.DMA((CORES, SLOTS)),
         ],
     )(table, keep, got)
 
@@ -424,23 +363,20 @@
         tiled=True,
     )
     table = call_plan(parent_gap)
-    slot_depth, pair_depth = table[DEPTHS : DEPTHS + SLOTS], table[PAIRS : PAIRS + CORES]
-    pair_angles = angles_of(pair_depth)
+    slot_angles = angles_of(table[DEPTHS : DEPTHS + SLOTS])
+    pair_angles = angles_of(table[PAIRS : PAIRS + CORES])
+    slot_cos, slot_sin = jnp.cos(slot_angles), jnp.sin(slot_angles)
     pair_cos, pair_sin = jnp.cos(pair_angles), jnp.sin(pair_angles)
-    table, pair_cos, pair_sin = lax.optimization_barrier((table, pair_cos, pair_sin))
+    both, slot_cos, slot_sin = lax.optimization_barrier((both, slot_cos, slot_sin))
     pairs = [both, along(both, -1), along(both, -2, (2,))]
     query_grad = jnp.concatenate(
         [queries.reshape(tokens, HEADS, WIDE), grad_attn.reshape(tokens, HEADS, WIDE)], 2
     ).reshape(tokens, HEADS * 2 * WIDE)
     query_grad = lax.all_to_all(query_grad, "head", split_axis=1, concat_axis=0, tiled=True)
-    held, slot_depth = lax.optimization_barrier(
-        (call_pick(table, pairs, SEND, 1), slot_depth)
-    )
+    held = call_pick(table, pairs, SEND, 1)
     relay = next_row(held, 1)
-    slot_angles = angles_of(slot_depth)
-    slot_cos, slot_sin = jnp.cos(slot_angles), jnp.sin(slot_angles)
-    relay, slot_cos, slot_sin, query_grad = lax.optimization_barrier(
-        (relay, slot_cos, slot_sin, query_grad)
+    relay, query_grad, pair_cos, pair_sin = lax.optimization_barrier(
+        (relay, query_grad, pair_cos, pair_sin)
     )
     sources = [both] + [along(both, k) for k in (1, 2, 3)]
     sources += [relay] + [along(relay, -k) for k in (1, 2, 3)]

time: 159 us -> 151 us (0.950)
  Pallas kernels: 18.6 us -> 9.59 us
  waiting for transfers between devices: 33.4 us -> 35.5 us
    pallas_call x1, Pallas kernels: 9.45 us -> 3.93 us  [call_attend(): pl.pallas_call(attend_kernel, compiler_params=room(24), out_shape=(jax.Sh...]
    pallas_call x1, Pallas kernels: 2.95 us -> 1.14 us  [call_spread(): pl.pallas_call(spread_kernel, compiler_params=room(12), out_shape=tuple([...]
    pallas_call x2, Pallas kernels: 3.16 us -> 1.44 us  [call_pick(): pl.pallas_call(functools.partial(pick_kernel, offset, number), compiler_p...]
  transfers between devices with their start and end apart: 24 -> 24, of which waited for: 7 -> 9; matrix products, arithmetic and copies ran while one was open for 6% -> 6% of each run, Pallas kernels for 5% -> 3%
where the time goes in v6:
time: 151 us; the launch traced here: 150 us
  starting transfers between devices  90 us (60%)
  waiting for transfers between devices  35.5 us (24%)
  Pallas kernels  9.59 us (6%)
  local copies, waits for them, and re-layouts  8.33 us (6%)
  other arithmetic  5.47 us (4%)
    ppermute x16, starting transfers between devices, along(): lax.ppermute(block, 'chip', [(i, i + shift) for i in starts if 0 <= i + s...  35.7 us
    all_to_all x1, starting transfers between devices, shards(): lax.all_to_all(grad_both, ('core', 'head'), split_axis=0, concat_axis=1,...  14.3 us
    all_to_all x1, starting transfers between devices, shards(): out = lax.all_to_all(out, 'head', split_axis=0, concat_axis=1, tiled=True)  12.7 us
    ppermute x2, waiting for transfers between devices, next_row(): lax.ppermute(block, 'row', [(i, i + shift) for i in range(rows) if 0 <= i...  11.8 us
    ppermute x2, starting transfers between devices, next_row(): lax.ppermute(block, 'row', [(i, i + shift) for i in range(rows) if 0 <= i...  10.4 us
    ppermute x16, waiting for transfers between devices, along(): lax.ppermute(block, 'chip', [(i, i + shift) for i in starts if 0 <= i + s...  8.75 us
    ppermute x2, starting transfers between devices, swap(): return lax.ppermute(block, 'core', [(0, 1), (1, 0)])  6.81 us
    all_to_all x1, starting transfers between devices, shards(): lax.all_to_all(jnp.concatenate([keys, values], 1), ('core', 'head'), spli...  6.7 us
  transfers between devices with their start and end apart: 24, of which 9 were waited for; matrix products, arithmetic and copies ran while one was open for 6% of the time, Pallas kernels for 3%

profile of v6, /device:TPU:31, one launch (start us, length us, event | category | flops | bytes accessed | tf_op | source)
XLA Modules:
  0.0 149.9 jit_solution(9437584496248875500)
XLA Ops:
  2.3 6.7 %all-to-all-start = ((bf16[64,8,256]{2,0,1:T(8,128)(2,1)}), bf16[64,8,256]{2,0,1:T(8,128)(2,1)S(1)}, u32[]{:S(2)}, u32[]{:S(2)}) async-start(bf16[64,8,256]{2,0,1:T(8,128)(2,1)} %bitcast.30), calls=%async_computation | async-start | bytes 524288 | tf_op jit(solution)/shard_map/all_to_all | solution.py:358
  9.1 1.5 %shard_map.84.table = s32[32]{0:T(128)} custom-call(s32[128]{0:T(128)} %gap_ref.1), custom_call_target="tpu_custom_call" | custom-call | tf_op jit(solution)/shard_map/pallas_call | solution.py:105
  11.5 6.5 %all-to-all-done = bf16[64,8,256]{2,0,1:T(8,128)(2,1)S(1)} async-done(((bf16[64,8,256]{2,0,1:T(8,128)(2,1)}), bf16[64,8,256]{2,0,1:T(8,128)(2,1)S(1)}, u32[]{:S(2)}, u32[]{:S(2)}) %all-to-all-start) | async-done | bytes 262176 | tf_op jit(solution)/shard_map/all_to_all | solution.py:358
  18.1 3.5 %all-to-all-start.1 = ((bf16[64,4,1024]{2,0,1:T(8,128)(2,1)}), bf16[64,4,1024]{2,0,1:T(8,128)(2,1)S(1)}, u32[]{:S(2)}, u32[]{:S(2)}) async-start(bf16[64,4,1024]{2,0,1:T(8,128)(2,1)} %pad_maximum_fusion), calls=%async_computation.1 | async-start | bytes 1048576 | tf_op jit(solution)/shard_map/all_to_all | solution.py:375
  21.7 2.3 %multiply_sine_fusion = (f32[1280,128]{1,0:T(8,128)S(1)}, f32[1280,128]{1,0:T(8,128)S(1)}) fusion(f32[128]{0:T(128)S(1)} %multiply_exponential_fusion, f32[1280]{0:T(1024)S(1)} %convert_element_type.21), kind=kLoop, calls=%fused_computation | loop fusion | flops 163840 | bytes 1316352 | tf_op jit(solution)/shard_map/sin | solution.py:368
  24.8 3.9 %collective-permute-start = (bf16[512,256]{1,0:T(8,128)(2,1)S(1)}, bf16[512,256]{1,0:T(8,128)(2,1)S(1)}, u32[]{:S(2)}, u32[]{:S(2)}) collective-permute-start(bf16[512,256]{1,0:T(8,128)(2,1)S(1)} %bitcast.32), channel_id=1, source_target_pairs={{8,0},{16,8},{24,16},{9,1},{17,9},{25,17},{10,2},{18,10},{26,18},{... | collective-permute-start | bytes 786440 | tf_op jit(solution)/shard_map/ppermute | solution.py:340
  34.3 8.5 %collective-permute-start.2 = (bf16[256,256]{1,0:T(8,128)(2,1)S(1)}, bf16[256,256]{1,0:T(8,128)(2,1)S(1)}, u32[]{:S(2)}, u32[]{:S(2)}) collective-permute-start(bf16[256,256]{1,0:T(8,128)(2,1)S(1)} %shard_map.85), channel_id=1, source_target_pairs={{0,32},{32,64},{64,96},{96,128},{128,160},{160,192},{192,224},{224... | collective-permute-start | bytes 393224 | tf_op jit(solution)/shard_map/ppermute | solution.py:347
  44.7 5.4 %collective-permute-start.8 = (bf16[256,256]{1,0:T(8,128)(2,1)S(1)}, bf16[256,256]{1,0:T(8,128)(2,1)S(1)}, u32[]{:S(2)}, u32[]{:S(2)}) collective-permute-start(bf16[256,256]{1,0:T(8,128)(2,1)S(1)} %collective-permute-done.2.refs_4_), channel_id=1, source_target_pairs={{24,0},{25,1},{26,2},{27,3},{28,4},{29,5},{30,6},{31,7},{56,32},{5... | collective-permute-start | bytes 393224 | tf_op jit(solution)/shard_map/ppermute | solution.py:340
  51.5 2.5 %collective-permute-start.6 = (bf16[256,256]{1,0:T(8,128)(2,1)S(1)}, bf16[256,256]{1,0:T(8,128)(2,1)S(1)}, u32[]{:S(2)}, u32[]{:S(2)}) collective-permute-start(bf16[256,256]{1,0:T(8,128)(2,1)S(1)} %collective-permute-done.2.refs_4_), channel_id=1, source_target_pairs={{8,0},{16,8},{24,16},{9,1},{17,9},{25,17},{10,2},{18,10},{26,18},{... | collective-permute-start | bytes 393224 | tf_op jit(solution)/shard_map/ppermute | solution.py:340
  54.0 3.0 %collective-permute-done.6.refs_5_ = bf16[256,256]{1,0:T(8,128)(2,1)S(1)} collective-permute-done((bf16[256,256]{1,0:T(8,128)(2,1)S(1)}, bf16[256,256]{1,0:T(8,128)(2,1)S(1)}, u32[]{:S(2)}, u32[]{:S(2)}) %collective-permute-start.6) | collective-permute-done | bytes 131104 | tf_op jit(solution)/shard_map/ppermute | solution.py:340
  57.9 4.3 %collective-permute-start.9 = (bf16[1280,256]{1,0:T(8,128)(2,1)S(1)}, bf16[1280,256]{1,0:T(8,128)(2,1)S(1)}, u32[]{:S(2)}, u32[]{:S(2)}) collective-permute-start(bf16[1280,256]{1,0:T(8,128)(2,1)S(1)} %shard_map.86), channel_id=1, source_target_pairs={{0,4},{4,0},{1,5},{5,1},{2,6},{6,2},{3,7},{7,3},{8,12},{12,8},{9,1... | collective-permute-start | bytes 1966088 | tf_op jit(solution)/shard_map/ppermute | solution.py:353
  62.1 1.7 %collective-permute-done.9.other_ref = bf16[1280,256]{1,0:T(8,128)(2,1)S(1)} collective-permute-done((bf16[1280,256]{1,0:T(8,128)(2,1)S(1)}, bf16[1280,256]{1,0:T(8,128)(2,1)S(1)}, u32[]{:S(2)}, u32[]{:S(2)}) %collective-permute-start.9) | collective-permute-done | bytes 655392 | tf_op jit(solution)/shard_map/ppermute | solution.py:353
  63.8 3.9 %shard_map.87 = (bf16[256,1024]{1,0:T(8,128)(2,1)S(1)}, bf16[1280,256]{1,0:T(8,128)(2,1)S(1)}, bf16[1280,256]{1,0:T(8,128)(2,1)S(1)}) custom-call(s32[32]{0:T(128)S(1)} %copy-done.3, bf16[256,1024]{1,0:T(8,128)(2,1)S(1)} %bitcast.39, f32[1280,128]{1,0:T(8,128)S(1)} %get-tuple-element.26.cos_ref, f32[1280,128]{1,0:T(8,128)S(1)} %get-tuple-element.27.sin_ref, ...), custom_call_target="tpu_custom_call" | custom-call | tf_op jit(solution)/shard_map/pallas_call | solution.py:237
  70.3 12.7 %all-to-all-start.2 = ((bf16[4,64,1024]{2,1,0:T(8,128)(2,1)}), bf16[4,64,1024]{2,1,0:T(8,128)(2,1)S(1)}, u32[]{:S(2)}, u32[]{:S(2)}) async-start(bf16[4,64,1024]{2,1,0:T(8,128)(2,1)} %bitcast.40), calls=%async_computation.2 | async-start | bytes 1048576 | tf_op jit(solution)/shard_map/all_to_all | solution.py:386
  83.0 2.5 %collective-permute-start.10 = (bf16[1280,256]{1,0:T(8,128)(2,1)}, bf16[1280,256]{1,0:T(8,128)(2,1)S(1)}, u32[]{:S(2)}, u32[]{:S(2)}) collective-permute-start(bf16[1280,256]{1,0:T(8,128)(2,1)} %copy-done.4), channel_id=1, source_target_pairs={{0,4},{4,0},{1,5},{5,1},{2,6},{6,2},{3,7},{7,3},{8,12},{12,8},{9,1... | collective-permute-start | bytes 1966088 | tf_op jit(solution)/shard_map/ppermute | solution.py:353
  85.6 1.9 %collective-permute-done.10.got_ref = bf16[1280,256]{1,0:T(8,128)(2,1)S(1)} collective-permute-done((bf16[1280,256]{1,0:T(8,128)(2,1)}, bf16[1280,256]{1,0:T(8,128)(2,1)S(1)}, u32[]{:S(2)}, u32[]{:S(2)}) %collective-permute-start.10) | collective-permute-done | bytes 655392 | tf_op jit(solution)/shard_map/ppermute | solution.py:353
  92.5 4.1 %collective-permute-start.11 = (bf16[512,256]{1,0:T(8,128)(2,1)S(1)}, bf16[512,256]{1,0:T(8,128)(2,1)S(1)}, u32[]{:S(2)}, u32[]{:S(2)}) collective-permute-start(bf16[512,256]{1,0:T(8,128)(2,1)S(1)} %get-tuple-element.32), channel_id=1, source_target_pairs={{8,0},{16,8},{24,16},{9,1},{17,9},{25,17},{10,2},{18,10},{26,18},{... | collective-permute-start | bytes 786440 | tf_op jit(solution)/shard_map/ppermute | solution.py:340
  96.7 6.7 %collective-permute-start.12 = (bf16[512,256]{1,0:T(8,128)(2,1)S(1)}, bf16[512,256]{1,0:T(8,128)(2,1)S(1)}, u32[]{:S(2)}, u32[]{:S(2)}) collective-permute-start(bf16[512,256]{1,0:T(8,128)(2,1)S(1)} %get-tuple-element.33), channel_id=1, source_target_pairs={{16,0},{24,8},{17,1},{25,9},{18,2},{26,10},{19,3},{27,11},{20,4},{... | collective-permute-start | bytes 786440 | tf_op jit(solution)/shard_map/ppermute | solution.py:340
  104.8 1.9 %collective-permute-start.17 = (bf16[256,256]{1,0:T(8,128)(2,1)S(1)}, bf16[256,256]{1,0:T(8,128)(2,1)S(1)}, u32[]{:S(2)}, u32[]{:S(2)}) collective-permute-start(bf16[256,256]{1,0:T(8,128)(2,1)S(1)} %shard_map.90), channel_id=1, source_target_pairs={{32,0},{64,32},{96,64},{128,96},{160,128},{192,160},{224,192},{256... | collective-permute-start | bytes 393224 | tf_op jit(solution)/shard_map/ppermute | solution.py:347
  106.8 10.8 %collective-permute-done.17.refs_0_ = bf16[256,256]{1,0:T(8,128)(2,1)S(1)} collective-permute-done((bf16[256,256]{1,0:T(8,128)(2,1)S(1)}, bf16[256,256]{1,0:T(8,128)(2,1)S(1)}, u32[]{:S(2)}, u32[]{:S(2)}) %collective-permute-start.17) | collective-permute-done | bytes 131104 | tf_op jit(solution)/shard_map/ppermute | solution.py:347
  119.7 4.8 %collective-permute-done.18.refs_1_ = bf16[256,256]{1,0:T(8,128)(2,1)S(1)} collective-permute-done((bf16[256,256]{1,0:T(8,128)(2,1)S(1)}, bf16[256,256]{1,0:T(8,128)(2,1)S(1)}, u32[]{:S(2)}, u32[]{:S(2)}) %collective-permute-start.18) | collective-permute-done | bytes 131104 | tf_op jit(solution)/shard_map/ppermute | solution.py:340
  125.9 14.3 %all-to-all-start.3 = ((bf16[8,64,256]{2,1,0:T(8,128)(2,1)}), bf16[8,64,256]{2,1,0:T(8,128)(2,1)S(1)}, u32[]{:S(2)}, u32[]{:S(2)}) async-start(bf16[8,64,256]{2,1,0:T(8,128)(2,1)} %bitcast.6), calls=%async_computation.3 | async-start | bytes 524288 | tf_op jit(solution)/shard_map/all_to_all | solution.py:395
  140.6 2.4 %slice_reduce_fusion = (bf16[64,4,512]{2,1,0:T(4,128)(2,1)S(1)}, bf16[64,4,512]{2,1,0:T(4,128)(2,1)S(1)}) fusion(bf16[64,4,2,512]{3,2,1,0:T(2,128)(2,1)S(1)} %reshape.72), kind=kLoop, calls=%fused_computation.2 | loop fusion | bytes 1048576 | tf_op jit(solution)/shard_map/slice | solution.py:398
  144.4 4.8 %all-to-all-done.3 = bf16[8,64,256]{2,1,0:T(8,128)(2,1)S(1)} async-done(((bf16[8,64,256]{2,1,0:T(8,128)(2,1)}), bf16[8,64,256]{2,1,0:T(8,128)(2,1)S(1)}, u32[]{:S(2)}, u32[]{:S(2)}) %all-to-all-start.3) | async-done | bytes 262176 | tf_op jit(solution)/shard_map/all_to_all | solution.py:395
  (66 shorter events, 28.1 us)
Async XLA Ops:
  2.3 15.7 %all-to-all-start = ((bf16[64,8,256]{2,0,1:T(8,128)(2,1)}), bf16[64,8,256]{2,0,1:T(8,128)(2,1)S(1)}, u32[]{:S(2)}, u32[]{:S(2)}) async-start(bf16[64,8,256]{2,0,1:T(8,128)(2,1)} %bitcast.30), calls=%async_computation | async-start | bytes 524288 | tf_op jit(solution)/shard_map/all_to_all | solution.py:358
  18.1 26.6 %all-to-all-start.1 = ((bf16[64,4,1024]{2,0,1:T(8,128)(2,1)}), bf16[64,4,1024]{2,0,1:T(8,128)(2,1)S(1)}, u32[]{:S(2)}, u32[]{:S(2)}) async-start(bf16[64,4,1024]{2,0,1:T(8,128)(2,1)} %pad_maximum_fusion), calls=%async_computation.1 | async-start | bytes 1048576 | tf_op jit(solution)/shard_map/all_to_all | solution.py:375
  24.1 8.7 %collective-permute-start.1 = (bf16[512,256]{1,0:T(8,128)(2,1)S(1)}, bf16[512,256]{1,0:T(8,128)(2,1)S(1)}, u32[]{:S(2)}, u32[]{:S(2)}) collective-permute-start(bf16[512,256]{1,0:T(8,128)(2,1)S(1)} %bitcast.31), channel_id=1, source_target_pairs={{16,0},{17,1},{18,2},{19,3},{20,4},{21,5},{22,6},{23,7},{48,32},{4... | collective-permute-start | bytes 786440 | tf_op jit(solution)/shard_map/ppermute | solution.py:340
  24.8 9.0 %collective-permute-start = (bf16[512,256]{1,0:T(8,128)(2,1)S(1)}, bf16[512,256]{1,0:T(8,128)(2,1)S(1)}, u32[]{:S(2)}, u32[]{:S(2)}) collective-permute-start(bf16[512,256]{1,0:T(8,128)(2,1)S(1)} %bitcast.32), channel_id=1, source_target_pairs={{8,0},{16,8},{24,16},{9,1},{17,9},{25,17},{10,2},{18,10},{26,18},{... | collective-permute-start | bytes 786440 | tf_op jit(solution)/shard_map/ppermute | solution.py:340
  28.8 22.7 %collective-permute-start.5 = (bf16[512,256]{1,0:T(8,128)(2,1)S(1)}, bf16[512,256]{1,0:T(8,128)(2,1)S(1)}, u32[]{:S(2)}, u32[]{:S(2)}) collective-permute-start(bf16[512,256]{1,0:T(8,128)(2,1)S(1)} %bitcast.33), channel_id=1, source_target_pairs={{0,24},{1,25},{2,26},{3,27},{4,28},{5,29},{6,30},{7,31},{32,56},{3... | collective-permute-start | bytes 786440 | tf_op jit(solution)/shard_map/ppermute | solution.py:340
  30.1 23.8 %collective-permute-start.4 = (bf16[512,256]{1,0:T(8,128)(2,1)S(1)}, bf16[512,256]{1,0:T(8,128)(2,1)S(1)}, u32[]{:S(2)}, u32[]{:S(2)}) collective-permute-start(bf16[512,256]{1,0:T(8,128)(2,1)S(1)} %bitcast.34), channel_id=1, source_target_pairs={{0,16},{8,24},{1,17},{9,25},{2,18},{10,26},{3,19},{11,27},{4,20},{... | collective-permute-start | bytes 786440 | tf_op jit(solution)/shard_map/ppermute | solution.py:340
  31.4 22.6 %collective-permute-start.3 = (bf16[512,256]{1,0:T(8,128)(2,1)S(1)}, bf16[512,256]{1,0:T(8,128)(2,1)S(1)}, u32[]{:S(2)}, u32[]{:S(2)}) collective-permute-start(bf16[512,256]{1,0:T(8,128)(2,1)S(1)} %bitcast.35), channel_id=1, source_target_pairs={{0,8},{8,16},{16,24},{1,9},{9,17},{17,25},{2,10},{10,18},{18,26},{... | collective-permute-start | bytes 786440 | tf_op jit(solution)/shard_map/ppermute | solution.py:340
  34.3 10.4 %collective-permute-start.2 = (bf16[256,256]{1,0:T(8,128)(2,1)S(1)}, bf16[256,256]{1,0:T(8,128)(2,1)S(1)}, u32[]{:S(2)}, u32[]{:S(2)}) collective-permute-start(bf16[256,256]{1,0:T(8,128)(2,1)S(1)} %shard_map.85), channel_id=1, source_target_pairs={{0,32},{32,64},{64,96},{96,128},{128,160},{160,192},{192,224},{224... | collective-permute-start | bytes 393224 | tf_op jit(solution)/shard_map/ppermute | solution.py:347
  44.7 9.3 %collective-permute-start.8 = (bf16[256,256]{1,0:T(8,128)(2,1)S(1)}, bf16[256,256]{1,0:T(8,128)(2,1)S(1)}, u32[]{:S(2)}, u32[]{:S(2)}) collective-permute-start(bf16[256,256]{1,0:T(8,128)(2,1)S(1)} %collective-permute-done.2.refs_4_), channel_id=1, source_target_pairs={{24,0},{25,1},{26,2},{27,3},{28,4},{29,5},{30,6},{31,7},{56,32},{5... | collective-permute-start | bytes 393224 | tf_op jit(solution)/shard_map/ppermute | solution.py:340
  50.2 3.8 %collective-permute-start.7 = (bf16[256,256]{1,0:T(8,128)(2,1)S(1)}, bf16[256,256]{1,0:T(8,128)(2,1)S(1)}, u32[]{:S(2)}, u32[]{:S(2)}) collective-permute-start(bf16[256,256]{1,0:T(8,128)(2,1)S(1)} %collective-permute-done.2.refs_4_), channel_id=1, source_target_pairs={{16,0},{24,8},{17,1},{25,9},{18,2},{26,10},{19,3},{27,11},{20,4},{... | collective-permute-start | bytes 393224 | tf_op jit(solution)/shard_map/ppermute | solution.py:340
  51.5 5.5 %collective-permute-start.6 = (bf16[256,256]{1,0:T(8,128)(2,1)S(1)}, bf16[256,256]{1,0:T(8,128)(2,1)S(1)}, u32[]{:S(2)}, u32[]{:S(2)}) collective-permute-start(bf16[256,256]{1,0:T(8,128)(2,1)S(1)} %collective-permute-done.2.refs_4_), channel_id=1, source_target_pairs={{8,0},{16,8},{24,16},{9,1},{17,9},{25,17},{10,2},{18,10},{26,18},{... | collective-permute-start | bytes 393224 | tf_op jit(solution)/shard_map/ppermute | solution.py:340
  57.9 6.0 %collective-permute-start.9 = (bf16[1280,256]{1,0:T(8,128)(2,1)S(1)}, bf16[1280,256]{1,0:T(8,128)(2,1)S(1)}, u32[]{:S(2)}, u32[]{:S(2)}) collective-permute-start(bf16[1280,256]{1,0:T(8,128)(2,1)S(1)} %shard_map.86), channel_id=1, source_target_pairs={{0,4},{4,0},{1,5},{5,1},{2,6},{6,2},{3,7},{7,3},{8,12},{12,8},{9,1... | collective-permute-start | bytes 1966088 | tf_op jit(solution)/shard_map/ppermute | solution.py:353
  70.3 55.6 %all-to-all-start.2 = ((bf16[4,64,1024]{2,1,0:T(8,128)(2,1)}), bf16[4,64,1024]{2,1,0:T(8,128)(2,1)S(1)}, u32[]{:S(2)}, u32[]{:S(2)}) async-start(bf16[4,64,1024]{2,1,0:T(8,128)(2,1)} %bitcast.40), calls=%async_computation.2 | async-start | bytes 1048576 | tf_op jit(solution)/shard_map/all_to_all | solution.py:386
  83.0 4.5 %collective-permute-start.10 = (bf16[1280,256]{1,0:T(8,128)(2,1)}, bf16[1280,256]{1,0:T(8,128)(2,1)S(1)}, u32[]{:S(2)}, u32[]{:S(2)}) collective-permute-start(bf16[1280,256]{1,0:T(8,128)(2,1)} %copy-done.4), channel_id=1, source_target_pairs={{0,4},{4,0},{1,5},{5,1},{2,6},{6,2},{3,7},{7,3},{8,12},{12,8},{9,1... | collective-permute-start | bytes 1966088 | tf_op jit(solution)/shard_map/ppermute | solution.py:353
  88.6 14.8 %collective-permute-start.14 = (bf16[256,256]{1,0:T(8,128)(2,1)S(1)}, bf16[256,256]{1,0:T(8,128)(2,1)S(1)}, u32[]{:S(2)}, u32[]{:S(2)}) collective-permute-start(bf16[256,256]{1,0:T(8,128)(2,1)S(1)} %get-tuple-element.36), channel_id=1, source_target_pairs={{0,8},{8,16},{16,24},{1,9},{9,17},{17,25},{2,10},{10,18},{18,26},{... | collective-permute-start | bytes 393224 | tf_op jit(solution)/shard_map/ppermute | solution.py:340
  89.9 14.8 %collective-permute-start.15 = (bf16[256,256]{1,0:T(8,128)(2,1)S(1)}, bf16[256,256]{1,0:T(8,128)(2,1)S(1)}, u32[]{:S(2)}, u32[]{:S(2)}) collective-permute-start(bf16[256,256]{1,0:T(8,128)(2,1)S(1)} %get-tuple-element.37), channel_id=1, source_target_pairs={{0,16},{8,24},{1,17},{9,25},{2,18},{10,26},{3,19},{11,27},{4,20},{... | collective-permute-start | bytes 393224 | tf_op jit(solution)/shard_map/ppermute | solution.py:340
  91.2 13.5 %collective-permute-start.16 = (bf16[256,256]{1,0:T(8,128)(2,1)S(1)}, bf16[256,256]{1,0:T(8,128)(2,1)S(1)}, u32[]{:S(2)}, u32[]{:S(2)}) collective-permute-start(bf16[256,256]{1,0:T(8,128)(2,1)S(1)} %get-tuple-element.38), channel_id=1, source_target_pairs={{0,24},{1,25},{2,26},{3,27},{4,28},{5,29},{6,30},{7,31},{32,56},{3... | collective-permute-start | bytes 393224 | tf_op jit(solution)/shard_map/ppermute | solution.py:340
  92.5 27.0 %collective-permute-start.11 = (bf16[512,256]{1,0:T(8,128)(2,1)S(1)}, bf16[512,256]{1,0:T(8,128)(2,1)S(1)}, u32[]{:S(2)}, u32[]{:S(2)}) collective-permute-start(bf16[512,256]{1,0:T(8,128)(2,1)S(1)} %get-tuple-element.32), channel_id=1, source_target_pairs={{8,0},{16,8},{24,16},{9,1},{17,9},{25,17},{10,2},{18,10},{26,18},{... | collective-permute-start | bytes 786440 | tf_op jit(solution)/shard_map/ppermute | solution.py:340
  96.7 22.9 %collective-permute-start.12 = (bf16[512,256]{1,0:T(8,128)(2,1)S(1)}, bf16[512,256]{1,0:T(8,128)(2,1)S(1)}, u32[]{:S(2)}, u32[]{:S(2)}) collective-permute-start(bf16[512,256]{1,0:T(8,128)(2,1)S(1)} %get-tuple-element.33), channel_id=1, source_target_pairs={{16,0},{24,8},{17,1},{25,9},{18,2},{26,10},{19,3},{27,11},{20,4},{... | collective-permute-start | bytes 786440 | tf_op jit(solution)/shard_map/ppermute | solution.py:340
  103.4 16.2 %collective-permute-start.13 = (bf16[512,256]{1,0:T(8,128)(2,1)S(1)}, bf16[512,256]{1,0:T(8,128)(2,1)S(1)}, u32[]{:S(2)}, u32[]{:S(2)}) collective-permute-start(bf16[512,256]{1,0:T(8,128)(2,1)S(1)} %get-tuple-element.34), channel_id=1, source_target_pairs={{24,0},{25,1},{26,2},{27,3},{28,4},{29,5},{30,6},{31,7},{56,32},{5... | collective-permute-start | bytes 786440 | tf_op jit(solution)/shard_map/ppermute | solution.py:340
  104.8 12.8 %collective-permute-start.17 = (bf16[256,256]{1,0:T(8,128)(2,1)S(1)}, bf16[256,256]{1,0:T(8,128)(2,1)S(1)}, u32[]{:S(2)}, u32[]{:S(2)}) collective-permute-start(bf16[256,256]{1,0:T(8,128)(2,1)S(1)} %shard_map.90), channel_id=1, source_target_pairs={{32,0},{64,32},{96,64},{128,96},{160,128},{192,160},{224,192},{256... | collective-permute-start | bytes 393224 | tf_op jit(solution)/shard_map/ppermute | solution.py:347
  117.6 2.1 %collective-permute-start.19 = (bf16[256,256]{1,0:T(8,128)(2,1)S(1)}, bf16[256,256]{1,0:T(8,128)(2,1)S(1)}, u32[]{:S(2)}, u32[]{:S(2)}) collective-permute-start(bf16[256,256]{1,0:T(8,128)(2,1)S(1)} %collective-permute-done.17.refs_0_), channel_id=1, source_target_pairs={{0,16},{1,17},{2,18},{3,19},{4,20},{5,21},{6,22},{7,23},{32,48},{3... | collective-permute-start | bytes 393224 | tf_op jit(solution)/shard_map/ppermute | solution.py:340
  118.3 6.2 %collective-permute-start.18 = (bf16[256,256]{1,0:T(8,128)(2,1)S(1)}, bf16[256,256]{1,0:T(8,128)(2,1)S(1)}, u32[]{:S(2)}, u32[]{:S(2)}) collective-permute-start(bf16[256,256]{1,0:T(8,128)(2,1)S(1)} %collective-permute-done.17.refs_0_), channel_id=1, source_target_pairs={{0,8},{8,16},{16,24},{1,9},{9,17},{17,25},{2,10},{10,18},{18,26},{... | collective-permute-start | bytes 393224 | tf_op jit(solution)/shard_map/ppermute | solution.py:340
  125.9 23.3 %all-to-all-start.3 = ((bf16[8,64,256]{2,1,0:T(8,128)(2,1)}), bf16[8,64,256]{2,1,0:T(8,128)(2,1)S(1)}, u32[]{:S(2)}, u32[]{:S(2)}) async-start(bf16[8,64,256]{2,1,0:T(8,128)(2,1)} %bitcast.6), calls=%async_computation.3 | async-start | bytes 524288 | tf_op jit(solution)/shard_map/all_to_all | solution.py:395
  (7 other events, 46.3 us)

commit v7 on v6

--- a/solution.py
+++ b/solution.py
@@ -355,13 +355,12 @@
 
 def shards(queries, keys, values, grad_attn, parent_gap):
     tokens = queries.shape[0]
+    chunks = [
+        x.reshape(tokens, HEADS, HD).transpose(1, 0, 2) for x in (keys, values)
+    ]
     both = lax.all_to_all(
-        jnp.concatenate([keys, values], 1),
-        ("core", "head"),
-        split_axis=1,
-        concat_axis=0,
-        tiled=True,
-    )
+        jnp.concatenate(chunks, 0), ("core", "head"), split_axis=0, concat_axis=0, tiled=True
+    ).reshape(PAIR, HD)
     table = call_plan(parent_gap)
     slot_angles = angles_of(table[DEPTHS : DEPTHS + SLOTS])
     pair_angles = angles_of(table[PAIRS : PAIRS + CORES])
@@ -375,9 +374,7 @@
     query_grad = lax.all_to_all(query_grad, "head", split_axis=1, concat_axis=0, tiled=True)
     held = call_pick(table, pairs, SEND, 1)
     relay = next_row(held, 1)
-    relay, query_grad, pair_cos, pair_sin = lax.optimization_barrier(
-        (relay, query_grad, pair_cos, pair_sin)
-    )
+    relay, query_grad = lax.optimization_barrier((relay, query_grad))
     sources = [both] + [along(both, k) for k in (1, 2, 3)]
     sources += [relay] + [along(relay, -k) for k in (1, 2, 3)]
     other = swap(call_pick(table, sources, OTHER, SLOTS))
@@ -388,6 +385,7 @@
     own, within, stack = spread[0], spread[1:CHIPS], spread[CHIPS:]
     stack_sum = call_sum([stack[0]] + [along(stack[k], k) for k in (1, 2, 3)], BF16)
     back = next_row(stack_sum, -1)
+    back, pair_cos, pair_sin = lax.optimization_barrier((back, pair_cos, pair_sin))
     own = call_sum([own] + [along(within[k - 1], -k) for k in (1, 2, 3)], F32)
     backs = [back, along(back, 1), along(back, 2, (0,))]
     grad_both = call_close(table, own, backs, pair_cos, pair_sin)

time: 151 us -> 156 us (1.033)
  the two profiles are of different devices: /device:TPU:31 before, /device:TPU:29 now
where the time goes in v7:
time: 156 us; the launch traced here: 155 us
  starting transfers between devices  92.8 us (59%)
  waiting for transfers between devices  36.9 us (24%)
  Pallas kernels  9.59 us (6%)
  local copies, waits for them, and re-layouts  8.66 us (6%)
  other arithmetic  5.87 us (4%)
    ppermute x16, starting transfers between devices, along(): lax.ppermute(block, 'chip', [(i, i + shift) for i in starts if 0 <= i + s...  38.2 us
    all_to_all x1, starting transfers between devices, shards(): lax.all_to_all(grad_both, ('core', 'head'), split_axis=0, concat_axis=1,...  15 us
    all_to_all x1, starting transfers between devices, shards(): out = lax.all_to_all(out, 'head', split_axis=0, concat_axis=1, tiled=True)  11.8 us
    ppermute x16, waiting for transfers between devices, along(): lax.ppermute(block, 'chip', [(i, i + shift) for i in starts if 0 <= i + s...  10.8 us
    ppermute x2, starting transfers between devices, next_row(): lax.ppermute(block, 'row', [(i, i + shift) for i in range(rows) if 0 <= i...  10.4 us
    ppermute x2, waiting for transfers between devices, next_row(): lax.ppermute(block, 'row', [(i, i + shift) for i in range(rows) if 0 <= i...  9.87 us
    all_to_all x1, waiting for transfers between devices, shards(): lax.all_to_all(jnp.concatenate(chunks, 0), ('core', 'head'), split_axis=0...  8.1 us
    ppermute x2, starting transfers between devices, swap(): return lax.ppermute(block, 'core', [(0, 1), (1, 0)])  7.21 us
  transfers between devices with their start and end apart: 24, of which 9 were waited for; matrix products, arithmetic and copies ran while one was open for 6% of the time, Pallas kernels for 3%

profile of v7, /device:TPU:29, one launch (start us, length us, event | category | flops | bytes accessed | tf_op | source)
XLA Modules:
  0.0 154.8 jit_solution(11969462681276105381)
XLA Ops:
  2.4 6.7 %all-to-all-start = ((bf16[8,64,256]{2,1,0:T(8,128)(2,1)}), bf16[8,64,256]{2,1,0:T(8,128)(2,1)S(1)}, u32[]{:S(2)}, u32[]{:S(2)}) async-start(bf16[8,64,256]{2,1,0:T(8,128)(2,1)} %pad_maximum_fusion.1), calls=%async_computation | async-start | bytes 524288 | tf_op jit(solution)/shard_map/all_to_all | solution.py:361
  10.0 8.1 %all-to-all-done = bf16[8,64,256]{2,1,0:T(8,128)(2,1)S(1)} async-done(((bf16[8,64,256]{2,1,0:T(8,128)(2,1)}), bf16[8,64,256]{2,1,0:T(8,128)(2,1)S(1)}, u32[]{:S(2)}, u32[]{:S(2)}) %all-to-all-start) | async-done | bytes 262176 | tf_op jit(solution)/shard_map/all_to_all | solution.py:361
  18.1 3.5 %all-to-all-start.1 = ((bf16[64,4,1024]{2,0,1:T(8,128)(2,1)}), bf16[64,4,1024]{2,0,1:T(8,128)(2,1)S(1)}, u32[]{:S(2)}, u32[]{:S(2)}) async-start(bf16[64,4,1024]{2,0,1:T(8,128)(2,1)} %pad_maximum_fusion), calls=%async_computation.1 | async-start | bytes 1048576 | tf_op jit(solution)/shard_map/all_to_all | solution.py:374
  23.9 2.3 %multiply_sine_fusion = (f32[1280,128]{1,0:T(8,128)S(1)}, f32[1280,128]{1,0:T(8,128)S(1)}) fusion(f32[128]{0:T(128)S(1)} %multiply_exponential_fusion, f32[1280]{0:T(1024)S(1)} %convert_element_type.21), kind=kLoop, calls=%fused_computation | loop fusion | flops 163840 | bytes 1316352 | tf_op jit(solution)/shard_map/sin | solution.py:367
  26.3 2.2 %collective-permute-start = (bf16[512,256]{1,0:T(8,128)(2,1)S(1)}, bf16[512,256]{1,0:T(8,128)(2,1)S(1)}, u32[]{:S(2)}, u32[]{:S(2)}) collective-permute-start(bf16[512,256]{1,0:T(8,128)(2,1)S(1)} %bitcast.35), channel_id=1, source_target_pairs={{8,0},{16,8},{24,16},{9,1},{17,9},{25,17},{10,2},{18,10},{26,18},{... | collective-permute-start | bytes 786440 | tf_op jit(solution)/shard_map/ppermute | solution.py:340
  29.7 2.5 %collective-permute-start.3 = (bf16[512,256]{1,0:T(8,128)(2,1)S(1)}, bf16[512,256]{1,0:T(8,128)(2,1)S(1)}, u32[]{:S(2)}, u32[]{:S(2)}) collective-permute-start(bf16[512,256]{1,0:T(8,128)(2,1)S(1)} %bitcast.37), channel_id=1, source_target_pairs={{0,8},{8,16},{16,24},{1,9},{9,17},{17,25},{2,10},{10,18},{18,26},{... | collective-permute-start | bytes 786440 | tf_op jit(solution)/shard_map/ppermute | solution.py:340
  32.3 3.4 %collective-permute-done.refs_1_ = bf16[512,256]{1,0:T(8,128)(2,1)S(1)} collective-permute-done((bf16[512,256]{1,0:T(8,128)(2,1)S(1)}, bf16[512,256]{1,0:T(8,128)(2,1)S(1)}, u32[]{:S(2)}, u32[]{:S(2)}) %collective-permute-start) | collective-permute-done | bytes 262176 | tf_op jit(solution)/shard_map/ppermute | solution.py:340
  36.3 8.5 %collective-permute-start.2 = (bf16[256,256]{1,0:T(8,128)(2,1)S(1)}, bf16[256,256]{1,0:T(8,128)(2,1)S(1)}, u32[]{:S(2)}, u32[]{:S(2)}) collective-permute-start(bf16[256,256]{1,0:T(8,128)(2,1)S(1)} %shard_map.85), channel_id=1, source_target_pairs={{0,32},{32,64},{64,96},{96,128},{128,160},{160,192},{192,224},{224... | collective-permute-start | bytes 393224 | tf_op jit(solution)/shard_map/ppermute | solution.py:347
  46.8 3.0 %collective-permute-start.6 = (bf16[256,256]{1,0:T(8,128)(2,1)S(1)}, bf16[256,256]{1,0:T(8,128)(2,1)S(1)}, u32[]{:S(2)}, u32[]{:S(2)}) collective-permute-start(bf16[256,256]{1,0:T(8,128)(2,1)S(1)} %collective-permute-done.2.refs_4_), channel_id=1, source_target_pairs={{8,0},{16,8},{24,16},{9,1},{17,9},{25,17},{10,2},{18,10},{26,18},{... | collective-permute-start | bytes 393224 | tf_op jit(solution)/shard_map/ppermute | solution.py:340
  49.8 4.4 %collective-permute-start.7 = (bf16[256,256]{1,0:T(8,128)(2,1)S(1)}, bf16[256,256]{1,0:T(8,128)(2,1)S(1)}, u32[]{:S(2)}, u32[]{:S(2)}) collective-permute-start(bf16[256,256]{1,0:T(8,128)(2,1)S(1)} %collective-permute-done.2.refs_4_), channel_id=1, source_target_pairs={{16,0},{24,8},{17,1},{25,9},{18,2},{26,10},{19,3},{27,11},{20,4},{... | collective-permute-start | bytes 393224 | tf_op jit(solution)/shard_map/ppermute | solution.py:340
  57.1 4.7 %collective-permute-start.9 = (bf16[1280,256]{1,0:T(8,128)(2,1)S(1)}, bf16[1280,256]{1,0:T(8,128)(2,1)S(1)}, u32[]{:S(2)}, u32[]{:S(2)}) collective-permute-start(bf16[1280,256]{1,0:T(8,128)(2,1)S(1)} %shard_map.86), channel_id=1, source_target_pairs={{0,4},{4,0},{1,5},{5,1},{2,6},{6,2},{3,7},{7,3},{8,12},{12,8},{9,1... | collective-permute-start | bytes 1966088 | tf_op jit(solution)/shard_map/ppermute | solution.py:353
  64.4 3.9 %shard_map.87 = (bf16[256,1024]{1,0:T(8,128)(2,1)S(1)}, bf16[1280,256]{1,0:T(8,128)(2,1)S(1)}, bf16[1280,256]{1,0:T(8,128)(2,1)S(1)}) custom-call(s32[32]{0:T(128)S(1)} %copy-done.3, bf16[256,1024]{1,0:T(8,128)(2,1)S(1)} %bitcast.43, f32[1280,128]{1,0:T(8,128)S(1)} %get-tuple-element.27.cos_ref, f32[1280,128]{1,0:T(8,128)S(1)} %get-tuple-element.28.sin_ref, ...), custom_call_target="tpu_custom_call" | custom-call | tf_op jit(solution)/shard_map/pallas_call | solution.py:237
  70.0 11.8 %all-to-all-start.2 = ((bf16[4,64,1024]{2,1,0:T(8,128)(2,1)}), bf16[4,64,1024]{2,1,0:T(8,128)(2,1)S(1)}, u32[]{:S(2)}, u32[]{:S(2)}) async-start(bf16[4,64,1024]{2,1,0:T(8,128)(2,1)} %bitcast.44), calls=%async_computation.2 | async-start | bytes 1048576 | tf_op jit(solution)/shard_map/all_to_all | solution.py:383
  81.8 2.6 %collective-permute-start.10 = (bf16[1280,256]{1,0:T(8,128)(2,1)S(1)}, bf16[1280,256]{1,0:T(8,128)(2,1)S(1)}, u32[]{:S(2)}, u32[]{:S(2)}) collective-permute-start(bf16[1280,256]{1,0:T(8,128)(2,1)S(1)} %copy-done.5), channel_id=1, source_target_pairs={{0,4},{4,0},{1,5},{5,1},{2,6},{6,2},{3,7},{7,3},{8,12},{12,8},{9,1... | collective-permute-start | bytes 1966088 | tf_op jit(solution)/shard_map/ppermute | solution.py:353
  87.2 5.9 %collective-permute-start.14 = (bf16[256,256]{1,0:T(8,128)(2,1)S(1)}, bf16[256,256]{1,0:T(8,128)(2,1)S(1)}, u32[]{:S(2)}, u32[]{:S(2)}) collective-permute-start(bf16[256,256]{1,0:T(8,128)(2,1)S(1)} %get-tuple-element.37), channel_id=1, source_target_pairs={{0,8},{8,16},{16,24},{1,9},{9,17},{17,25},{2,10},{10,18},{18,26},{... | collective-permute-start | bytes 393224 | tf_op jit(solution)/shard_map/ppermute | solution.py:340
  95.1 3.1 %collective-permute-start.11 = (bf16[512,256]{1,0:T(8,128)(2,1)S(1)}, bf16[512,256]{1,0:T(8,128)(2,1)S(1)}, u32[]{:S(2)}, u32[]{:S(2)}) collective-permute-start(bf16[512,256]{1,0:T(8,128)(2,1)S(1)} %get-tuple-element.33), channel_id=1, source_target_pairs={{8,0},{16,8},{24,16},{9,1},{17,9},{25,17},{10,2},{18,10},{26,18},{... | collective-permute-start | bytes 786440 | tf_op jit(solution)/shard_map/ppermute | solution.py:340
  98.2 4.3 %collective-permute-start.12 = (bf16[512,256]{1,0:T(8,128)(2,1)S(1)}, bf16[512,256]{1,0:T(8,128)(2,1)S(1)}, u32[]{:S(2)}, u32[]{:S(2)}) collective-permute-start(bf16[512,256]{1,0:T(8,128)(2,1)S(1)} %get-tuple-element.34), channel_id=1, source_target_pairs={{16,0},{24,8},{17,1},{25,9},{18,2},{26,10},{19,3},{27,11},{20,4},{... | collective-permute-start | bytes 786440 | tf_op jit(solution)/shard_map/ppermute | solution.py:340
  103.4 1.9 %collective-permute-start.17 = (bf16[256,256]{1,0:T(8,128)(2,1)S(1)}, bf16[256,256]{1,0:T(8,128)(2,1)S(1)}, u32[]{:S(2)}, u32[]{:S(2)}) collective-permute-start(bf16[256,256]{1,0:T(8,128)(2,1)S(1)} %shard_map.90), channel_id=1, source_target_pairs={{32,0},{64,32},{96,64},{128,96},{160,128},{192,160},{224,192},{256... | collective-permute-start | bytes 393224 | tf_op jit(solution)/shard_map/ppermute | solution.py:347
  106.3 9.9 %collective-permute-done.17.refs_0_ = bf16[256,256]{1,0:T(8,128)(2,1)S(1)} collective-permute-done((bf16[256,256]{1,0:T(8,128)(2,1)S(1)}, bf16[256,256]{1,0:T(8,128)(2,1)S(1)}, u32[]{:S(2)}, u32[]{:S(2)}) %collective-permute-start.17) | collective-permute-done | bytes 131104 | tf_op jit(solution)/shard_map/ppermute | solution.py:347
  116.2 4.9 %collective-permute-start.18 = (bf16[256,256]{1,0:T(8,128)(2,1)S(1)}, bf16[256,256]{1,0:T(8,128)(2,1)S(1)}, u32[]{:S(2)}, u32[]{:S(2)}) collective-permute-start(bf16[256,256]{1,0:T(8,128)(2,1)S(1)} %collective-permute-done.17.refs_0_), channel_id=1, source_target_pairs={{0,8},{8,16},{16,24},{1,9},{9,17},{17,25},{2,10},{10,18},{18,26},{... | collective-permute-start | bytes 393224 | tf_op jit(solution)/shard_map/ppermute | solution.py:340
  123.0 5.7 %collective-permute-done.19.refs_2_ = bf16[256,256]{1,0:T(8,128)(2,1)S(1)} collective-permute-done((bf16[256,256]{1,0:T(8,128)(2,1)S(1)}, bf16[256,256]{1,0:T(8,128)(2,1)S(1)}, u32[]{:S(2)}, u32[]{:S(2)}) %collective-permute-start.19) | collective-permute-done | bytes 131104 | tf_op jit(solution)/shard_map/ppermute | solution.py:340
  130.1 15.0 %all-to-all-start.3 = ((bf16[8,64,256]{2,1,0:T(8,128)(2,1)}), bf16[8,64,256]{2,1,0:T(8,128)(2,1)S(1)}, u32[]{:S(2)}, u32[]{:S(2)}) async-start(bf16[8,64,256]{2,1,0:T(8,128)(2,1)} %bitcast.7), calls=%async_computation.3 | async-start | bytes 524288 | tf_op jit(solution)/shard_map/all_to_all | solution.py:393
  145.4 2.4 %slice_reduce_fusion = (bf16[64,4,512]{2,1,0:T(4,128)(2,1)S(1)}, bf16[64,4,512]{2,1,0:T(4,128)(2,1)S(1)}) fusion(bf16[64,4,2,512]{3,2,1,0:T(2,128)(2,1)S(1)} %reshape.81), kind=kLoop, calls=%fused_computation.2 | loop fusion | bytes 1048576 | tf_op jit(solution)/shard_map/slice | solution.py:396
  149.3 4.8 %all-to-all-done.3 = bf16[8,64,256]{2,1,0:T(8,128)(2,1)S(1)} async-done(((bf16[8,64,256]{2,1,0:T(8,128)(2,1)}), bf16[8,64,256]{2,1,0:T(8,128)(2,1)S(1)}, u32[]{:S(2)}, u32[]{:S(2)}) %all-to-all-start.3) | async-done | bytes 262176 | tf_op jit(solution)/shard_map/all_to_all | solution.py:393
  (68 shorter events, 28.4 us)
Async XLA Ops:
  2.4 15.7 %all-to-all-start = ((bf16[8,64,256]{2,1,0:T(8,128)(2,1)}), bf16[8,64,256]{2,1,0:T(8,128)(2,1)S(1)}, u32[]{:S(2)}, u32[]{:S(2)}) async-start(bf16[8,64,256]{2,1,0:T(8,128)(2,1)} %pad_maximum_fusion.1), calls=%async_computation | async-start | bytes 524288 | tf_op jit(solution)/shard_map/all_to_all | solution.py:361
  18.1 28.7 %all-to-all-start.1 = ((bf16[64,4,1024]{2,0,1:T(8,128)(2,1)}), bf16[64,4,1024]{2,0,1:T(8,128)(2,1)S(1)}, u32[]{:S(2)}, u32[]{:S(2)}) async-start(bf16[64,4,1024]{2,0,1:T(8,128)(2,1)} %pad_maximum_fusion), calls=%async_computation.1 | async-start | bytes 1048576 | tf_op jit(solution)/shard_map/all_to_all | solution.py:374
  26.3 9.4 %collective-permute-start = (bf16[512,256]{1,0:T(8,128)(2,1)S(1)}, bf16[512,256]{1,0:T(8,128)(2,1)S(1)}, u32[]{:S(2)}, u32[]{:S(2)}) collective-permute-start(bf16[512,256]{1,0:T(8,128)(2,1)S(1)} %bitcast.35), channel_id=1, source_target_pairs={{8,0},{16,8},{24,16},{9,1},{17,9},{25,17},{10,2},{18,10},{26,18},{... | collective-permute-start | bytes 786440 | tf_op jit(solution)/shard_map/ppermute | solution.py:340
  28.4 7.3 %collective-permute-start.1 = (bf16[512,256]{1,0:T(8,128)(2,1)S(1)}, bf16[512,256]{1,0:T(8,128)(2,1)S(1)}, u32[]{:S(2)}, u32[]{:S(2)}) collective-permute-start(bf16[512,256]{1,0:T(8,128)(2,1)S(1)} %bitcast.36), channel_id=1, source_target_pairs={{16,0},{17,1},{18,2},{19,3},{20,4},{21,5},{22,6},{23,7},{48,32},{4... | collective-permute-start | bytes 786440 | tf_op jit(solution)/shard_map/ppermute | solution.py:340
  29.7 24.5 %collective-permute-start.3 = (bf16[512,256]{1,0:T(8,128)(2,1)S(1)}, bf16[512,256]{1,0:T(8,128)(2,1)S(1)}, u32[]{:S(2)}, u32[]{:S(2)}) collective-permute-start(bf16[512,256]{1,0:T(8,128)(2,1)S(1)} %bitcast.37), channel_id=1, source_target_pairs={{0,8},{8,16},{16,24},{1,9},{9,17},{17,25},{2,10},{10,18},{18,26},{... | collective-permute-start | bytes 786440 | tf_op jit(solution)/shard_map/ppermute | solution.py:340
  36.3 10.5 %collective-permute-start.2 = (bf16[256,256]{1,0:T(8,128)(2,1)S(1)}, bf16[256,256]{1,0:T(8,128)(2,1)S(1)}, u32[]{:S(2)}, u32[]{:S(2)}) collective-permute-start(bf16[256,256]{1,0:T(8,128)(2,1)S(1)} %shard_map.85), channel_id=1, source_target_pairs={{0,32},{32,64},{64,96},{96,128},{128,160},{160,192},{192,224},{224... | collective-permute-start | bytes 393224 | tf_op jit(solution)/shard_map/ppermute | solution.py:347
  44.8 10.2 %collective-permute-start.4 = (bf16[512,256]{1,0:T(8,128)(2,1)S(1)}, bf16[512,256]{1,0:T(8,128)(2,1)S(1)}, u32[]{:S(2)}, u32[]{:S(2)}) collective-permute-start(bf16[512,256]{1,0:T(8,128)(2,1)S(1)} %bitcast.39), channel_id=1, source_target_pairs={{0,16},{8,24},{1,17},{9,25},{2,18},{10,26},{3,19},{11,27},{4,20},{... | collective-permute-start | bytes 786440 | tf_op jit(solution)/shard_map/ppermute | solution.py:340
  46.1 8.9 %collective-permute-start.5 = (bf16[512,256]{1,0:T(8,128)(2,1)S(1)}, bf16[512,256]{1,0:T(8,128)(2,1)S(1)}, u32[]{:S(2)}, u32[]{:S(2)}) collective-permute-start(bf16[512,256]{1,0:T(8,128)(2,1)S(1)} %bitcast.40), channel_id=1, source_target_pairs={{0,24},{1,25},{2,26},{3,27},{4,28},{5,29},{6,30},{7,31},{32,56},{3... | collective-permute-start | bytes 786440 | tf_op jit(solution)/shard_map/ppermute | solution.py:340
  46.8 8.2 %collective-permute-start.6 = (bf16[256,256]{1,0:T(8,128)(2,1)S(1)}, bf16[256,256]{1,0:T(8,128)(2,1)S(1)}, u32[]{:S(2)}, u32[]{:S(2)}) collective-permute-start(bf16[256,256]{1,0:T(8,128)(2,1)S(1)} %collective-permute-done.2.refs_4_), channel_id=1, source_target_pairs={{8,0},{16,8},{24,16},{9,1},{17,9},{25,17},{10,2},{18,10},{26,18},{... | collective-permute-start | bytes 393224 | tf_op jit(solution)/shard_map/ppermute | solution.py:340
  49.8 6.4 %collective-permute-start.7 = (bf16[256,256]{1,0:T(8,128)(2,1)S(1)}, bf16[256,256]{1,0:T(8,128)(2,1)S(1)}, u32[]{:S(2)}, u32[]{:S(2)}) collective-permute-start(bf16[256,256]{1,0:T(8,128)(2,1)S(1)} %collective-permute-done.2.refs_4_), channel_id=1, source_target_pairs={{16,0},{24,8},{17,1},{25,9},{18,2},{26,10},{19,3},{27,11},{20,4},{... | collective-permute-start | bytes 393224 | tf_op jit(solution)/shard_map/ppermute | solution.py:340
  54.3 1.9 %collective-permute-start.8 = (bf16[256,256]{1,0:T(8,128)(2,1)S(1)}, bf16[256,256]{1,0:T(8,128)(2,1)S(1)}, u32[]{:S(2)}, u32[]{:S(2)}) collective-permute-start(bf16[256,256]{1,0:T(8,128)(2,1)S(1)} %collective-permute-done.2.refs_4_), channel_id=1, source_target_pairs={{24,0},{25,1},{26,2},{27,3},{28,4},{29,5},{30,6},{31,7},{56,32},{5... | collective-permute-start | bytes 393224 | tf_op jit(solution)/shard_map/ppermute | solution.py:340
  57.1 6.4 %collective-permute-start.9 = (bf16[1280,256]{1,0:T(8,128)(2,1)S(1)}, bf16[1280,256]{1,0:T(8,128)(2,1)S(1)}, u32[]{:S(2)}, u32[]{:S(2)}) collective-permute-start(bf16[1280,256]{1,0:T(8,128)(2,1)S(1)} %shard_map.86), channel_id=1, source_target_pairs={{0,4},{4,0},{1,5},{5,1},{2,6},{6,2},{3,7},{7,3},{8,12},{12,8},{9,1... | collective-permute-start | bytes 1966088 | tf_op jit(solution)/shard_map/ppermute | solution.py:353
  70.0 60.0 %all-to-all-start.2 = ((bf16[4,64,1024]{2,1,0:T(8,128)(2,1)}), bf16[4,64,1024]{2,1,0:T(8,128)(2,1)S(1)}, u32[]{:S(2)}, u32[]{:S(2)}) async-start(bf16[4,64,1024]{2,1,0:T(8,128)(2,1)} %bitcast.44), calls=%async_computation.2 | async-start | bytes 1048576 | tf_op jit(solution)/shard_map/all_to_all | solution.py:383
  81.8 4.3 %collective-permute-start.10 = (bf16[1280,256]{1,0:T(8,128)(2,1)S(1)}, bf16[1280,256]{1,0:T(8,128)(2,1)S(1)}, u32[]{:S(2)}, u32[]{:S(2)}) collective-permute-start(bf16[1280,256]{1,0:T(8,128)(2,1)S(1)} %copy-done.5), channel_id=1, source_target_pairs={{0,4},{4,0},{1,5},{5,1},{2,6},{6,2},{3,7},{7,3},{8,12},{12,8},{9,1... | collective-permute-start | bytes 1966088 | tf_op jit(solution)/shard_map/ppermute | solution.py:353
  87.2 15.4 %collective-permute-start.14 = (bf16[256,256]{1,0:T(8,128)(2,1)S(1)}, bf16[256,256]{1,0:T(8,128)(2,1)S(1)}, u32[]{:S(2)}, u32[]{:S(2)}) collective-permute-start(bf16[256,256]{1,0:T(8,128)(2,1)S(1)} %get-tuple-element.37), channel_id=1, source_target_pairs={{0,8},{8,16},{16,24},{1,9},{9,17},{17,25},{2,10},{10,18},{18,26},{... | collective-permute-start | bytes 393224 | tf_op jit(solution)/shard_map/ppermute | solution.py:340
  93.1 10.2 %collective-permute-start.15 = (bf16[256,256]{1,0:T(8,128)(2,1)S(1)}, bf16[256,256]{1,0:T(8,128)(2,1)S(1)}, u32[]{:S(2)}, u32[]{:S(2)}) collective-permute-start(bf16[256,256]{1,0:T(8,128)(2,1)S(1)} %get-tuple-element.38), channel_id=1, source_target_pairs={{0,16},{8,24},{1,17},{9,25},{2,18},{10,26},{3,19},{11,27},{4,20},{... | collective-permute-start | bytes 393224 | tf_op jit(solution)/shard_map/ppermute | solution.py:340
  94.4 8.9 %collective-permute-start.16 = (bf16[256,256]{1,0:T(8,128)(2,1)S(1)}, bf16[256,256]{1,0:T(8,128)(2,1)S(1)}, u32[]{:S(2)}, u32[]{:S(2)}) collective-permute-start(bf16[256,256]{1,0:T(8,128)(2,1)S(1)} %get-tuple-element.39), channel_id=1, source_target_pairs={{0,24},{1,25},{2,26},{3,27},{4,28},{5,29},{6,30},{7,31},{32,56},{3... | collective-permute-start | bytes 393224 | tf_op jit(solution)/shard_map/ppermute | solution.py:340
  95.1 27.2 %collective-permute-start.11 = (bf16[512,256]{1,0:T(8,128)(2,1)S(1)}, bf16[512,256]{1,0:T(8,128)(2,1)S(1)}, u32[]{:S(2)}, u32[]{:S(2)}) collective-permute-start(bf16[512,256]{1,0:T(8,128)(2,1)S(1)} %get-tuple-element.33), channel_id=1, source_target_pairs={{8,0},{16,8},{24,16},{9,1},{17,9},{25,17},{10,2},{18,10},{26,18},{... | collective-permute-start | bytes 786440 | tf_op jit(solution)/shard_map/ppermute | solution.py:340
  98.2 24.2 %collective-permute-start.12 = (bf16[512,256]{1,0:T(8,128)(2,1)S(1)}, bf16[512,256]{1,0:T(8,128)(2,1)S(1)}, u32[]{:S(2)}, u32[]{:S(2)}) collective-permute-start(bf16[512,256]{1,0:T(8,128)(2,1)S(1)} %get-tuple-element.34), channel_id=1, source_target_pairs={{16,0},{24,8},{17,1},{25,9},{18,2},{26,10},{19,3},{27,11},{20,4},{... | collective-permute-start | bytes 786440 | tf_op jit(solution)/shard_map/ppermute | solution.py:340
  102.6 19.8 %collective-permute-start.13 = (bf16[512,256]{1,0:T(8,128)(2,1)S(1)}, bf16[512,256]{1,0:T(8,128)(2,1)S(1)}, u32[]{:S(2)}, u32[]{:S(2)}) collective-permute-start(bf16[512,256]{1,0:T(8,128)(2,1)S(1)} %get-tuple-element.35), channel_id=1, source_target_pairs={{24,0},{25,1},{26,2},{27,3},{28,4},{29,5},{30,6},{31,7},{56,32},{5... | collective-permute-start | bytes 786440 | tf_op jit(solution)/shard_map/ppermute | solution.py:340
  103.4 12.8 %collective-permute-start.17 = (bf16[256,256]{1,0:T(8,128)(2,1)S(1)}, bf16[256,256]{1,0:T(8,128)(2,1)S(1)}, u32[]{:S(2)}, u32[]{:S(2)}) collective-permute-start(bf16[256,256]{1,0:T(8,128)(2,1)S(1)} %shard_map.90), channel_id=1, source_target_pairs={{32,0},{64,32},{96,64},{128,96},{160,128},{192,160},{224,192},{256... | collective-permute-start | bytes 393224 | tf_op jit(solution)/shard_map/ppermute | solution.py:347
  116.2 6.8 %collective-permute-start.18 = (bf16[256,256]{1,0:T(8,128)(2,1)S(1)}, bf16[256,256]{1,0:T(8,128)(2,1)S(1)}, u32[]{:S(2)}, u32[]{:S(2)}) collective-permute-start(bf16[256,256]{1,0:T(8,128)(2,1)S(1)} %collective-permute-done.17.refs_0_), channel_id=1, source_target_pairs={{0,8},{8,16},{16,24},{1,9},{9,17},{17,25},{2,10},{10,18},{18,26},{... | collective-permute-start | bytes 393224 | tf_op jit(solution)/shard_map/ppermute | solution.py:340
  121.1 7.6 %collective-permute-start.19 = (bf16[256,256]{1,0:T(8,128)(2,1)S(1)}, bf16[256,256]{1,0:T(8,128)(2,1)S(1)}, u32[]{:S(2)}, u32[]{:S(2)}) collective-permute-start(bf16[256,256]{1,0:T(8,128)(2,1)S(1)} %collective-permute-done.17.refs_0_), channel_id=1, source_target_pairs={{0,16},{1,17},{2,18},{3,19},{4,20},{5,21},{6,22},{7,23},{32,48},{3... | collective-permute-start | bytes 393224 | tf_op jit(solution)/shard_map/ppermute | solution.py:340
  130.1 24.0 %all-to-all-start.3 = ((bf16[8,64,256]{2,1,0:T(8,128)(2,1)}), bf16[8,64,256]{2,1,0:T(8,128)(2,1)S(1)}, u32[]{:S(2)}, u32[]{:S(2)}) async-start(bf16[8,64,256]{2,1,0:T(8,128)(2,1)} %bitcast.7), calls=%async_computation.3 | async-start | bytes 524288 | tf_op jit(solution)/shard_map/all_to_all | solution.py:393
  (8 other events, 47.5 us)

commit v8 on v7

--- a/solution.py
+++ b/solution.py
@@ -22,7 +22,7 @@
 ROW = CHIPS * CORES
 HEADS = 4
 WIDE = 2 * HD
-OWN, OTHER, SEEN, SEND, LAND, CORE, DEPTHS, PAIRS, TABLE = 0, 5, 10, 14, 15, 18, 19, 24, 32
+OWN, OTHER, SEEN, SEND, LAND, CORE, DEPTHS, PAIRS, GIVE, TABLE = 0, 5, 10, 14, 15, 18, 19, 24, 26, 32
 BASE = 10000.0
 BF16 = jnp.bfloat16
 F32 = jnp.float32
@@ -85,9 +85,11 @@
             node = pick(rank == j, relay[j], node)
         return node
 
+    table[GIVE] = jnp.maximum(held(CHIPS - chip), 0) & 1
+    table[GIVE + 1] = jnp.maximum(relay[LEVELS - 1], 0) & 1
     node = held(CHIPS - 1 - chip)
-    code = 2 * (((node - first) >> 1) - chip) + (node & 1)
-    table[SEND] = jnp.clip(code, 0, 2 * CHIPS - 3)
+    far = ((node - first) >> 1) - chip
+    table[SEND] = jnp.clip(pick(far <= 0, node & 1, 1 + far), 0, CHIPS - 1)
     for i, rank in enumerate((CHIPS - 1 - chip, CHIPS - chip, pick(chip == 2, CHIPS - 1, CHIPS))):
         node = held(rank)
         here = (node >= first) & (((node - first) >> 1) == chip)
@@ -97,7 +99,7 @@
         table[DEPTHS + i] = own_depth - i
     for i in range(CORES):
         table[PAIRS + i] = pair_depth[i]
-    for i in range(PAIRS + CORES, TABLE):
+    for i in range(GIVE + 2, TABLE):
         table[i] = 0
 
 
@@ -143,6 +145,21 @@
     sources, o_ref = refs[:-1], refs[-1]
     for i in range(number):
         fetch(table[offset + i], sources, part(o_ref, i))
+
+
+def give_kernel(table, pair, *outs):
+    for i, out in enumerate(outs):
+        fetch(table[GIVE + i], (pair,), out)
+
+
+def call_give(table, pair):
+    return pl.pallas_call(
+        give_kernel,
+        compiler_params=room(4),
+        out_shape=(jax.ShapeDtypeStruct((TOK, HD), BF16),) * 2,
+        in_specs=[SMEM, VMEM],
+        out_specs=(VMEM,) * 2,
+    )(table, pair)
 
 
 def call_pick(table, sources, offset, number):
@@ -337,9 +354,7 @@
 
 
 def along(block, shift, starts=range(CHIPS)):
-    return lax.ppermute(
-        block, "chip", [(i, i + shift) for i in starts if 0 <= i + shift < CHIPS]
-    )
+    return lax.ppermute(block, "chip", [(i, i + shift) for i in starts if 0 <= i + shift < CHIPS])
 
 
 def next_row(block, shift):
@@ -363,11 +378,10 @@
     ).reshape(PAIR, HD)
     table = call_plan(parent_gap)
     slot_angles = angles_of(table[DEPTHS : DEPTHS + SLOTS])
-    pair_angles = angles_of(table[PAIRS : PAIRS + CORES])
     slot_cos, slot_sin = jnp.cos(slot_angles), jnp.sin(slot_angles)
-    pair_cos, pair_sin = jnp.cos(pair_angles), jnp.sin(pair_angles)
     both, slot_cos, slot_sin = lax.optimization_barrier((both, slot_cos, slot_sin))
-    pairs = [both, along(both, -1), along(both, -2, (2,))]
+    near, far = call_give(table, both)
+    pairs = [both, along(near, -1), along(far, -2, (2,))]
     query_grad = jnp.concatenate(
         [queries.reshape(tokens, HEADS, WIDE), grad_attn.reshape(tokens, HEADS, WIDE)], 2
     ).reshape(tokens, HEADS * 2 * WIDE)
@@ -384,7 +398,10 @@
     spread = call_spread(table, keep, got)
     own, within, stack = spread[0], spread[1:CHIPS], spread[CHIPS:]
     stack_sum = call_sum([stack[0]] + [along(stack[k], k) for k in (1, 2, 3)], BF16)
+    stack_sum, late_table = lax.optimization_barrier((stack_sum, table))
     back = next_row(stack_sum, -1)
+    pair_angles = angles_of(late_table[PAIRS : PAIRS + CORES])
+    pair_cos, pair_sin = jnp.cos(pair_angles), jnp.sin(pair_angles)
     back, pair_cos, pair_sin = lax.optimization_barrier((back, pair_cos, pair_sin))
     own = call_sum([own] + [along(within[k - 1], -k) for k in (1, 2, 3)], F32)
     backs = [back, along(back, 1), along(back, 2, (0,))]

time: 156 us -> 148 us (0.949)
  the two profiles are of different devices: /device:TPU:29 before, /device:TPU:31 now
where the time goes in v8:
time: 148 us; the launch traced here: 147 us
  starting transfers between devices  85.1 us (58%)
  waiting for transfers between devices  35.6 us (24%)
  Pallas kernels  11 us (7%)
  local copies, waits for them, and re-layouts  8.45 us (6%)
  other arithmetic  5.87 us (4%)
    ppermute x16, starting transfers between devices, along(): lax.ppermute(block, 'chip', [(i, i + shift) for i in starts if 0 <= i + s...  35.9 us
    ppermute x2, waiting for transfers between devices, next_row(): lax.ppermute(block, 'row', [(i, i + shift) for i in range(rows) if 0 <= i...  13.3 us
    all_to_all x1, starting transfers between devices, shards(): out = lax.all_to_all(out, 'head', split_axis=0, concat_axis=1, tiled=True)  11.8 us
    all_to_all x1, starting transfers between devices, shards(): lax.all_to_all(grad_both, ('core', 'head'), split_axis=0, concat_axis=1,...  10.8 us
    ppermute x2, starting transfers between devices, next_row(): lax.ppermute(block, 'row', [(i, i + shift) for i in range(rows) if 0 <= i...  10.4 us
    all_to_all x1, waiting for transfers between devices, shards(): lax.all_to_all(jnp.concatenate(chunks, 0), ('core', 'head'), split_axis=0...  8.1 us
    ppermute x16, waiting for transfers between devices, along(): lax.ppermute(block, 'chip', [(i, i + shift) for i in starts if 0 <= i + s...  7.75 us
    all_to_all x1, starting transfers between devices, shards(): lax.all_to_all(jnp.concatenate(chunks, 0), ('core', 'head'), split_axis=0...  6.7 us
  transfers between devices with their start and end apart: 24, of which 7 were waited for; matrix products, arithmetic and copies ran while one was open for 6% of the time, Pallas kernels for 4%

profile of v8, /device:TPU:31, one launch (start us, length us, event | category | flops | bytes accessed | tf_op | source)
XLA Modules:
  0.0 147.1 jit_solution(15773691003000424151)
XLA Ops:
  2.4 6.7 %all-to-all-start = ((bf16[8,64,256]{2,1,0:T(8,128)(2,1)}), bf16[8,64,256]{2,1,0:T(8,128)(2,1)S(1)}, u32[]{:S(2)}, u32[]{:S(2)}) async-start(bf16[8,64,256]{2,1,0:T(8,128)(2,1)} %pad_maximum_fusion.1), calls=%async_computation | async-start | bytes 524288 | tf_op jit(solution)/shard_map/all_to_all | solution.py:376
  10.0 8.1 %all-to-all-done = bf16[8,64,256]{2,1,0:T(8,128)(2,1)S(1)} async-done(((bf16[8,64,256]{2,1,0:T(8,128)(2,1)}), bf16[8,64,256]{2,1,0:T(8,128)(2,1)S(1)}, u32[]{:S(2)}, u32[]{:S(2)}) %all-to-all-start) | async-done | bytes 262176 | tf_op jit(solution)/shard_map/all_to_all | solution.py:376
  18.1 3.5 %all-to-all-start.1 = ((bf16[64,4,1024]{2,0,1:T(8,128)(2,1)}), bf16[64,4,1024]{2,0,1:T(8,128)(2,1)S(1)}, u32[]{:S(2)}, u32[]{:S(2)}) async-start(bf16[64,4,1024]{2,0,1:T(8,128)(2,1)} %pad_maximum_fusion), calls=%async_computation.1 | async-start | bytes 1048576 | tf_op jit(solution)/shard_map/all_to_all | solution.py:388
  21.6 1.5 %shard_map.84.table = s32[32]{0:T(128)} custom-call(s32[128]{0:T(128)} %gap_ref.1), custom_call_target="tpu_custom_call" | custom-call | tf_op jit(solution)/shard_map/pallas_call | solution.py:107
  23.9 2.3 %multiply_sine_fusion = (f32[1280,128]{1,0:T(8,128)S(1)}, f32[1280,128]{1,0:T(8,128)S(1)}) fusion(f32[128]{0:T(128)S(1)} %multiply_exponential_fusion, f32[1280]{0:T(1024)S(1)} %convert_element_type.21), kind=kLoop, calls=%fused_computation | loop fusion | flops 163840 | bytes 1316352 | tf_op jit(solution)/shard_map/sin | solution.py:381
  27.5 2.4 %collective-permute-start = (bf16[256,256]{1,0:T(8,128)(2,1)S(1)}, bf16[256,256]{1,0:T(8,128)(2,1)S(1)}, u32[]{:S(2)}, u32[]{:S(2)}) collective-permute-start(bf16[256,256]{1,0:T(8,128)(2,1)S(1)} %get-tuple-element.30), channel_id=1, source_target_pairs={{8,0},{16,8},{24,16},{9,1},{17,9},{25,17},{10,2},{18,10},{26,18},{... | collective-permute-start | bytes 393224 | tf_op jit(solution)/shard_map/ppermute | solution.py:357
  33.0 8.5 %collective-permute-start.2 = (bf16[256,256]{1,0:T(8,128)(2,1)S(1)}, bf16[256,256]{1,0:T(8,128)(2,1)S(1)}, u32[]{:S(2)}, u32[]{:S(2)}) collective-permute-start(bf16[256,256]{1,0:T(8,128)(2,1)S(1)} %shard_map.86), channel_id=1, source_target_pairs={{0,32},{32,64},{64,96},{96,128},{128,160},{160,192},{192,224},{224... | collective-permute-start | bytes 393224 | tf_op jit(solution)/shard_map/ppermute | solution.py:362
  44.2 7.1 %collective-permute-start.8 = (bf16[256,256]{1,0:T(8,128)(2,1)S(1)}, bf16[256,256]{1,0:T(8,128)(2,1)S(1)}, u32[]{:S(2)}, u32[]{:S(2)}) collective-permute-start(bf16[256,256]{1,0:T(8,128)(2,1)S(1)} %collective-permute-done.2.refs_4_), channel_id=1, source_target_pairs={{24,0},{25,1},{26,2},{27,3},{28,4},{29,5},{30,6},{31,7},{56,32},{5... | collective-permute-start | bytes 393224 | tf_op jit(solution)/shard_map/ppermute | solution.py:357
  52.7 2.5 %collective-permute-start.6 = (bf16[256,256]{1,0:T(8,128)(2,1)S(1)}, bf16[256,256]{1,0:T(8,128)(2,1)S(1)}, u32[]{:S(2)}, u32[]{:S(2)}) collective-permute-start(bf16[256,256]{1,0:T(8,128)(2,1)S(1)} %collective-permute-done.2.refs_4_), channel_id=1, source_target_pairs={{8,0},{16,8},{24,16},{9,1},{17,9},{25,17},{10,2},{18,10},{26,18},{... | collective-permute-start | bytes 393224 | tf_op jit(solution)/shard_map/ppermute | solution.py:357
  55.2 3.0 %collective-permute-done.6.refs_5_ = bf16[256,256]{1,0:T(8,128)(2,1)S(1)} collective-permute-done((bf16[256,256]{1,0:T(8,128)(2,1)S(1)}, bf16[256,256]{1,0:T(8,128)(2,1)S(1)}, u32[]{:S(2)}, u32[]{:S(2)}) %collective-permute-start.6) | collective-permute-done | bytes 131104 | tf_op jit(solution)/shard_map/ppermute | solution.py:357
  59.1 3.7 %collective-permute-start.9 = (bf16[1280,256]{1,0:T(8,128)(2,1)S(1)}, bf16[1280,256]{1,0:T(8,128)(2,1)S(1)}, u32[]{:S(2)}, u32[]{:S(2)}) collective-permute-start(bf16[1280,256]{1,0:T(8,128)(2,1)S(1)} %shard_map.87), channel_id=1, source_target_pairs={{0,4},{4,0},{1,5},{5,1},{2,6},{6,2},{3,7},{7,3},{8,12},{12,8},{9,1... | collective-permute-start | bytes 1966088 | tf_op jit(solution)/shard_map/ppermute | solution.py:368
  62.8 1.7 %collective-permute-done.9.other_ref = bf16[1280,256]{1,0:T(8,128)(2,1)S(1)} collective-permute-done((bf16[1280,256]{1,0:T(8,128)(2,1)S(1)}, bf16[1280,256]{1,0:T(8,128)(2,1)S(1)}, u32[]{:S(2)}, u32[]{:S(2)}) %collective-permute-start.9) | collective-permute-done | bytes 655392 | tf_op jit(solution)/shard_map/ppermute | solution.py:368
  65.4 4.8 %shard_map.88 = (bf16[256,1024]{1,0:T(8,128)(2,1)S(1)}, bf16[1280,256]{1,0:T(8,128)(2,1)S(1)}, bf16[1280,256]{1,0:T(8,128)(2,1)}) custom-call(s32[32]{0:T(128)S(1)} %copy-done.3, bf16[256,1024]{1,0:T(8,128)(2,1)S(1)} %bitcast.42, f32[1280,128]{1,0:T(8,128)S(1)} %get-tuple-element.33.cos_ref, f32[1280,128]{1,0:T(8,128)S(1)} %get-tuple-element.34.sin_ref, ...), custom_call_target="tpu_custom_call" | custom-call | tf_op jit(solution)/shard_map/pallas_call | solution.py:254
  71.0 2.3 %collective-permute-start.10 = (bf16[1280,256]{1,0:T(8,128)(2,1)}, bf16[1280,256]{1,0:T(8,128)(2,1)S(1)}, u32[]{:S(2)}, u32[]{:S(2)}) collective-permute-start(bf16[1280,256]{1,0:T(8,128)(2,1)} %get-tuple-element.37), channel_id=1, source_target_pairs={{0,4},{4,0},{1,5},{5,1},{2,6},{6,2},{3,7},{7,3},{8,12},{12,8},{9,1... | collective-permute-start | bytes 1966088 | tf_op jit(solution)/shard_map/ppermute | solution.py:368
  73.3 11.8 %all-to-all-start.2 = ((bf16[4,64,1024]{2,1,0:T(8,128)(2,1)}), bf16[4,64,1024]{2,1,0:T(8,128)(2,1)S(1)}, u32[]{:S(2)}, u32[]{:S(2)}) async-start(bf16[4,64,1024]{2,1,0:T(8,128)(2,1)} %bitcast.43), calls=%async_computation.2 | async-start | bytes 1048576 | tf_op jit(solution)/shard_map/all_to_all | solution.py:397
  90.1 4.1 %collective-permute-start.11 = (bf16[512,256]{1,0:T(8,128)(2,1)S(1)}, bf16[512,256]{1,0:T(8,128)(2,1)S(1)}, u32[]{:S(2)}, u32[]{:S(2)}) collective-permute-start(bf16[512,256]{1,0:T(8,128)(2,1)S(1)} %get-tuple-element.39), channel_id=1, source_target_pairs={{8,0},{16,8},{24,16},{9,1},{17,9},{25,17},{10,2},{18,10},{26,18},{... | collective-permute-start | bytes 786440 | tf_op jit(solution)/shard_map/ppermute | solution.py:357
  94.3 6.7 %collective-permute-start.12 = (bf16[512,256]{1,0:T(8,128)(2,1)S(1)}, bf16[512,256]{1,0:T(8,128)(2,1)S(1)}, u32[]{:S(2)}, u32[]{:S(2)}) collective-permute-start(bf16[512,256]{1,0:T(8,128)(2,1)S(1)} %get-tuple-element.40), channel_id=1, source_target_pairs={{16,0},{24,8},{17,1},{25,9},{18,2},{26,10},{19,3},{27,11},{20,4},{... | collective-permute-start | bytes 786440 | tf_op jit(solution)/shard_map/ppermute | solution.py:357
  102.6 1.9 %collective-permute-start.17 = (bf16[256,256]{1,0:T(8,128)(2,1)S(1)}, bf16[256,256]{1,0:T(8,128)(2,1)S(1)}, u32[]{:S(2)}, u32[]{:S(2)}) collective-permute-start(bf16[256,256]{1,0:T(8,128)(2,1)S(1)} %shard_map.91), channel_id=1, source_target_pairs={{32,0},{64,32},{96,64},{128,96},{160,128},{192,160},{224,192},{256... | collective-permute-start | bytes 393224 | tf_op jit(solution)/shard_map/ppermute | solution.py:362
  105.5 13.2 %collective-permute-done.17.refs_0_ = bf16[256,256]{1,0:T(8,128)(2,1)S(1)} collective-permute-done((bf16[256,256]{1,0:T(8,128)(2,1)S(1)}, bf16[256,256]{1,0:T(8,128)(2,1)S(1)}, u32[]{:S(2)}, u32[]{:S(2)}) %collective-permute-start.17) | collective-permute-done | bytes 131104 | tf_op jit(solution)/shard_map/ppermute | solution.py:362
  120.9 4.2 %collective-permute-done.18.refs_1_ = bf16[256,256]{1,0:T(8,128)(2,1)S(1)} collective-permute-done((bf16[256,256]{1,0:T(8,128)(2,1)S(1)}, bf16[256,256]{1,0:T(8,128)(2,1)S(1)}, u32[]{:S(2)}, u32[]{:S(2)}) %collective-permute-start.18) | collective-permute-done | bytes 131104 | tf_op jit(solution)/shard_map/ppermute | solution.py:357
  125.1 1.4 shard_map.92
  126.5 10.8 %all-to-all-start.3 = ((bf16[8,64,256]{2,1,0:T(8,128)(2,1)}), bf16[8,64,256]{2,1,0:T(8,128)(2,1)S(1)}, u32[]{:S(2)}, u32[]{:S(2)}) async-start(bf16[8,64,256]{2,1,0:T(8,128)(2,1)} %bitcast.7), calls=%async_computation.3 | async-start | bytes 524288 | tf_op jit(solution)/shard_map/all_to_all | solution.py:410
  137.7 2.4 %slice_reduce_fusion = (bf16[64,4,512]{2,1,0:T(4,128)(2,1)S(1)}, bf16[64,4,512]{2,1,0:T(4,128)(2,1)S(1)}) fusion(bf16[64,4,2,512]{3,2,1,0:T(2,128)(2,1)S(1)} %reshape.81), kind=kLoop, calls=%fused_computation.2 | loop fusion | bytes 1048576 | tf_op jit(solution)/shard_map/slice | solution.py:413
  141.6 4.8 %all-to-all-done.3 = bf16[8,64,256]{2,1,0:T(8,128)(2,1)S(1)} async-done(((bf16[8,64,256]{2,1,0:T(8,128)(2,1)}), bf16[8,64,256]{2,1,0:T(8,128)(2,1)S(1)}, u32[]{:S(2)}, u32[]{:S(2)}) %all-to-all-start.3) | async-done | bytes 262176 | tf_op jit(solution)/shard_map/all_to_all | solution.py:410
  (65 shorter events, 26.5 us)
Async XLA Ops:
  2.4 15.7 %all-to-all-start = ((bf16[8,64,256]{2,1,0:T(8,128)(2,1)}), bf16[8,64,256]{2,1,0:T(8,128)(2,1)S(1)}, u32[]{:S(2)}, u32[]{:S(2)}) async-start(bf16[8,64,256]{2,1,0:T(8,128)(2,1)} %pad_maximum_fusion.1), calls=%async_computation | async-start | bytes 524288 | tf_op jit(solution)/shard_map/all_to_all | solution.py:376
  18.1 26.1 %all-to-all-start.1 = ((bf16[64,4,1024]{2,0,1:T(8,128)(2,1)}), bf16[64,4,1024]{2,0,1:T(8,128)(2,1)S(1)}, u32[]{:S(2)}, u32[]{:S(2)}) async-start(bf16[64,4,1024]{2,0,1:T(8,128)(2,1)} %pad_maximum_fusion), calls=%async_computation.1 | async-start | bytes 1048576 | tf_op jit(solution)/shard_map/all_to_all | solution.py:388
  27.5 4.9 %collective-permute-start = (bf16[256,256]{1,0:T(8,128)(2,1)S(1)}, bf16[256,256]{1,0:T(8,128)(2,1)S(1)}, u32[]{:S(2)}, u32[]{:S(2)}) collective-permute-start(bf16[256,256]{1,0:T(8,128)(2,1)S(1)} %get-tuple-element.30), channel_id=1, source_target_pairs={{8,0},{16,8},{24,16},{9,1},{17,9},{25,17},{10,2},{18,10},{26,18},{... | collective-permute-start | bytes 393224 | tf_op jit(solution)/shard_map/ppermute | solution.py:357
  30.0 2.5 %collective-permute-start.1 = (bf16[256,256]{1,0:T(8,128)(2,1)S(1)}, bf16[256,256]{1,0:T(8,128)(2,1)S(1)}, u32[]{:S(2)}, u32[]{:S(2)}) collective-permute-start(bf16[256,256]{1,0:T(8,128)(2,1)S(1)} %get-tuple-element.31), channel_id=1, source_target_pairs={{16,0},{17,1},{18,2},{19,3},{20,4},{21,5},{22,6},{23,7},{48,32},{4... | collective-permute-start | bytes 393224 | tf_op jit(solution)/shard_map/ppermute | solution.py:357
  30.6 22.0 %collective-permute-start.5 = (bf16[512,256]{1,0:T(8,128)(2,1)S(1)}, bf16[512,256]{1,0:T(8,128)(2,1)S(1)}, u32[]{:S(2)}, u32[]{:S(2)}) collective-permute-start(bf16[512,256]{1,0:T(8,128)(2,1)S(1)} %bitcast.36), channel_id=1, source_target_pairs={{0,24},{1,25},{2,26},{3,27},{4,28},{5,29},{6,30},{7,31},{32,56},{3... | collective-permute-start | bytes 786440 | tf_op jit(solution)/shard_map/ppermute | solution.py:357
  33.0 11.1 %collective-permute-start.2 = (bf16[256,256]{1,0:T(8,128)(2,1)S(1)}, bf16[256,256]{1,0:T(8,128)(2,1)S(1)}, u32[]{:S(2)}, u32[]{:S(2)}) collective-permute-start(bf16[256,256]{1,0:T(8,128)(2,1)S(1)} %shard_map.86), channel_id=1, source_target_pairs={{0,32},{32,64},{64,96},{96,128},{128,160},{160,192},{192,224},{224... | collective-permute-start | bytes 393224 | tf_op jit(solution)/shard_map/ppermute | solution.py:362
  41.6 13.6 %collective-permute-start.4 = (bf16[512,256]{1,0:T(8,128)(2,1)S(1)}, bf16[512,256]{1,0:T(8,128)(2,1)S(1)}, u32[]{:S(2)}, u32[]{:S(2)}) collective-permute-start(bf16[512,256]{1,0:T(8,128)(2,1)S(1)} %bitcast.38), channel_id=1, source_target_pairs={{0,16},{8,24},{1,17},{9,25},{2,18},{10,26},{3,19},{11,27},{4,20},{... | collective-permute-start | bytes 786440 | tf_op jit(solution)/shard_map/ppermute | solution.py:357
  42.9 12.3 %collective-permute-start.3 = (bf16[512,256]{1,0:T(8,128)(2,1)S(1)}, bf16[512,256]{1,0:T(8,128)(2,1)S(1)}, u32[]{:S(2)}, u32[]{:S(2)}) collective-permute-start(bf16[512,256]{1,0:T(8,128)(2,1)S(1)} %bitcast.39), channel_id=1, source_target_pairs={{0,8},{8,16},{16,24},{1,9},{9,17},{17,25},{2,10},{10,18},{18,26},{... | collective-permute-start | bytes 786440 | tf_op jit(solution)/shard_map/ppermute | solution.py:357
  44.2 11.0 %collective-permute-start.8 = (bf16[256,256]{1,0:T(8,128)(2,1)S(1)}, bf16[256,256]{1,0:T(8,128)(2,1)S(1)}, u32[]{:S(2)}, u32[]{:S(2)}) collective-permute-start(bf16[256,256]{1,0:T(8,128)(2,1)S(1)} %collective-permute-done.2.refs_4_), channel_id=1, source_target_pairs={{24,0},{25,1},{26,2},{27,3},{28,4},{29,5},{30,6},{31,7},{56,32},{5... | collective-permute-start | bytes 393224 | tf_op jit(solution)/shard_map/ppermute | solution.py:357
  51.4 3.8 %collective-permute-start.7 = (bf16[256,256]{1,0:T(8,128)(2,1)S(1)}, bf16[256,256]{1,0:T(8,128)(2,1)S(1)}, u32[]{:S(2)}, u32[]{:S(2)}) collective-permute-start(bf16[256,256]{1,0:T(8,128)(2,1)S(1)} %collective-permute-done.2.refs_4_), channel_id=1, source_target_pairs={{16,0},{24,8},{17,1},{25,9},{18,2},{26,10},{19,3},{27,11},{20,4},{... | collective-permute-start | bytes 393224 | tf_op jit(solution)/shard_map/ppermute | solution.py:357
  52.7 5.5 %collective-permute-start.6 = (bf16[256,256]{1,0:T(8,128)(2,1)S(1)}, bf16[256,256]{1,0:T(8,128)(2,1)S(1)}, u32[]{:S(2)}, u32[]{:S(2)}) collective-permute-start(bf16[256,256]{1,0:T(8,128)(2,1)S(1)} %collective-permute-done.2.refs_4_), channel_id=1, source_target_pairs={{8,0},{16,8},{24,16},{9,1},{17,9},{25,17},{10,2},{18,10},{26,18},{... | collective-permute-start | bytes 393224 | tf_op jit(solution)/shard_map/ppermute | solution.py:357
  59.1 5.4 %collective-permute-start.9 = (bf16[1280,256]{1,0:T(8,128)(2,1)S(1)}, bf16[1280,256]{1,0:T(8,128)(2,1)S(1)}, u32[]{:S(2)}, u32[]{:S(2)}) collective-permute-start(bf16[1280,256]{1,0:T(8,128)(2,1)S(1)} %shard_map.87), channel_id=1, source_target_pairs={{0,4},{4,0},{1,5},{5,1},{2,6},{6,2},{3,7},{7,3},{8,12},{12,8},{9,1... | collective-permute-start | bytes 1966088 | tf_op jit(solution)/shard_map/ppermute | solution.py:368
  71.0 14.1 %collective-permute-start.10 = (bf16[1280,256]{1,0:T(8,128)(2,1)}, bf16[1280,256]{1,0:T(8,128)(2,1)S(1)}, u32[]{:S(2)}, u32[]{:S(2)}) collective-permute-start(bf16[1280,256]{1,0:T(8,128)(2,1)} %get-tuple-element.37), channel_id=1, source_target_pairs={{0,4},{4,0},{1,5},{5,1},{2,6},{6,2},{3,7},{7,3},{8,12},{12,8},{9,1... | collective-permute-start | bytes 1966088 | tf_op jit(solution)/shard_map/ppermute | solution.py:368
  73.3 53.2 %all-to-all-start.2 = ((bf16[4,64,1024]{2,1,0:T(8,128)(2,1)}), bf16[4,64,1024]{2,1,0:T(8,128)(2,1)S(1)}, u32[]{:S(2)}, u32[]{:S(2)}) async-start(bf16[4,64,1024]{2,1,0:T(8,128)(2,1)} %bitcast.43), calls=%async_computation.2 | async-start | bytes 1048576 | tf_op jit(solution)/shard_map/all_to_all | solution.py:397
  86.2 14.8 %collective-permute-start.14 = (bf16[256,256]{1,0:T(8,128)(2,1)S(1)}, bf16[256,256]{1,0:T(8,128)(2,1)S(1)}, u32[]{:S(2)}, u32[]{:S(2)}) collective-permute-start(bf16[256,256]{1,0:T(8,128)(2,1)S(1)} %get-tuple-element.43), channel_id=1, source_target_pairs={{0,8},{8,16},{16,24},{1,9},{9,17},{17,25},{2,10},{10,18},{18,26},{... | collective-permute-start | bytes 393224 | tf_op jit(solution)/shard_map/ppermute | solution.py:357
  87.5 14.8 %collective-permute-start.15 = (bf16[256,256]{1,0:T(8,128)(2,1)S(1)}, bf16[256,256]{1,0:T(8,128)(2,1)S(1)}, u32[]{:S(2)}, u32[]{:S(2)}) collective-permute-start(bf16[256,256]{1,0:T(8,128)(2,1)S(1)} %get-tuple-element.44), channel_id=1, source_target_pairs={{0,16},{8,24},{1,17},{9,25},{2,18},{10,26},{3,19},{11,27},{4,20},{... | collective-permute-start | bytes 393224 | tf_op jit(solution)/shard_map/ppermute | solution.py:357
  88.8 13.5 %collective-permute-start.16 = (bf16[256,256]{1,0:T(8,128)(2,1)S(1)}, bf16[256,256]{1,0:T(8,128)(2,1)S(1)}, u32[]{:S(2)}, u32[]{:S(2)}) collective-permute-start(bf16[256,256]{1,0:T(8,128)(2,1)S(1)} %get-tuple-element.45), channel_id=1, source_target_pairs={{0,24},{1,25},{2,26},{3,27},{4,28},{5,29},{6,30},{7,31},{32,56},{3... | collective-permute-start | bytes 393224 | tf_op jit(solution)/shard_map/ppermute | solution.py:357
  90.1 30.6 %collective-permute-start.11 = (bf16[512,256]{1,0:T(8,128)(2,1)S(1)}, bf16[512,256]{1,0:T(8,128)(2,1)S(1)}, u32[]{:S(2)}, u32[]{:S(2)}) collective-permute-start(bf16[512,256]{1,0:T(8,128)(2,1)S(1)} %get-tuple-element.39), channel_id=1, source_target_pairs={{8,0},{16,8},{24,16},{9,1},{17,9},{25,17},{10,2},{18,10},{26,18},{... | collective-permute-start | bytes 786440 | tf_op jit(solution)/shard_map/ppermute | solution.py:357
  94.3 26.4 %collective-permute-start.12 = (bf16[512,256]{1,0:T(8,128)(2,1)S(1)}, bf16[512,256]{1,0:T(8,128)(2,1)S(1)}, u32[]{:S(2)}, u32[]{:S(2)}) collective-permute-start(bf16[512,256]{1,0:T(8,128)(2,1)S(1)} %get-tuple-element.40), channel_id=1, source_target_pairs={{16,0},{24,8},{17,1},{25,9},{18,2},{26,10},{19,3},{27,11},{20,4},{... | collective-permute-start | bytes 786440 | tf_op jit(solution)/shard_map/ppermute | solution.py:357
  101.0 19.7 %collective-permute-start.13 = (bf16[512,256]{1,0:T(8,128)(2,1)S(1)}, bf16[512,256]{1,0:T(8,128)(2,1)S(1)}, u32[]{:S(2)}, u32[]{:S(2)}) collective-permute-start(bf16[512,256]{1,0:T(8,128)(2,1)S(1)} %get-tuple-element.41), channel_id=1, source_target_pairs={{24,0},{25,1},{26,2},{27,3},{28,4},{29,5},{30,6},{31,7},{56,32},{5... | collective-permute-start | bytes 786440 | tf_op jit(solution)/shard_map/ppermute | solution.py:357
  102.6 16.2 %collective-permute-start.17 = (bf16[256,256]{1,0:T(8,128)(2,1)S(1)}, bf16[256,256]{1,0:T(8,128)(2,1)S(1)}, u32[]{:S(2)}, u32[]{:S(2)}) collective-permute-start(bf16[256,256]{1,0:T(8,128)(2,1)S(1)} %shard_map.91), channel_id=1, source_target_pairs={{32,0},{64,32},{96,64},{128,96},{160,128},{192,160},{224,192},{256... | collective-permute-start | bytes 393224 | tf_op jit(solution)/shard_map/ppermute | solution.py:362
  118.8 2.1 %collective-permute-start.19 = (bf16[256,256]{1,0:T(8,128)(2,1)S(1)}, bf16[256,256]{1,0:T(8,128)(2,1)S(1)}, u32[]{:S(2)}, u32[]{:S(2)}) collective-permute-start(bf16[256,256]{1,0:T(8,128)(2,1)S(1)} %collective-permute-done.17.refs_0_), channel_id=1, source_target_pairs={{0,16},{1,17},{2,18},{3,19},{4,20},{5,21},{6,22},{7,23},{32,48},{3... | collective-permute-start | bytes 393224 | tf_op jit(solution)/shard_map/ppermute | solution.py:357
  119.4 5.7 %collective-permute-start.18 = (bf16[256,256]{1,0:T(8,128)(2,1)S(1)}, bf16[256,256]{1,0:T(8,128)(2,1)S(1)}, u32[]{:S(2)}, u32[]{:S(2)}) collective-permute-start(bf16[256,256]{1,0:T(8,128)(2,1)S(1)} %collective-permute-done.17.refs_0_), channel_id=1, source_target_pairs={{0,8},{8,16},{16,24},{1,9},{9,17},{17,25},{2,10},{10,18},{18,26},{... | collective-permute-start | bytes 393224 | tf_op jit(solution)/shard_map/ppermute | solution.py:357
  126.5 19.8 %all-to-all-start.3 = ((bf16[8,64,256]{2,1,0:T(8,128)(2,1)}), bf16[8,64,256]{2,1,0:T(8,128)(2,1)S(1)}, u32[]{:S(2)}, u32[]{:S(2)}) async-start(bf16[8,64,256]{2,1,0:T(8,128)(2,1)} %bitcast.7), calls=%async_computation.3 | async-start | bytes 524288 | tf_op jit(solution)/shard_map/all_to_all | solution.py:410
  (6 other events, 30.7 us)

commit v9 on v8

--- a/solution.py
+++ b/solution.py
@@ -407,12 +407,21 @@
     backs = [back, along(back, 1), along(back, 2, (0,))]
     grad_both = call_close(table, own, backs, pair_cos, pair_sin)
     grad_both, out = lax.optimization_barrier((grad_both, out))
-    grad_both = lax.all_to_all(grad_both, ("core", "head"), split_axis=0, concat_axis=1, tiled=True)
+    grad_both = lax.all_to_all(
+        grad_both.reshape(CORES * HEADS, tokens, HD),
+        ("core", "head"),
+        split_axis=0,
+        concat_axis=0,
+        tiled=True,
+    )
+    grad_key, grad_value = (
+        x.transpose(1, 0, 2).reshape(tokens, HEADS * HD)
+        for x in (grad_both[:HEADS], grad_both[HEADS:])
+    )
     out = out.reshape(tokens, HEADS, 2, WIDE)
     attended = out[:, :, 0].reshape(tokens, HEADS * WIDE)
     grad_query = out[:, :, 1].reshape(tokens, HEADS * WIDE)
-    half = HEADS * HD
-    return attended, grad_query, grad_both[:, :half], grad_both[:, half:]
+    return attended, grad_query, grad_key, grad_value
 
 
 def solution(mesh):

time: 148 us -> 149 us (level)
    unnamed x15 -> x16, local copies, waits for them, and re-layouts: 3.91 us -> 3.92 us
where the time goes in v9:
time: 149 us; the launch traced here: 148 us
  starting transfers between devices  85.1 us (57%)
  waiting for transfers between devices  35.6 us (24%)
  Pallas kernels  11 us (7%)
  local copies, waits for them, and re-layouts  9.06 us (6%)
  other arithmetic  5.87 us (4%)
    ppermute x16, starting transfers between devices, along(): lax.ppermute(block, 'chip', [(i, i + shift) for i in starts if 0 <= i + s...  35.9 us
    ppermute x2, waiting for transfers between devices, next_row(): lax.ppermute(block, 'row', [(i, i + shift) for i in range(rows) if 0 <= i...  13.3 us
    all_to_all x1, starting transfers between devices, shards(): out = lax.all_to_all(out, 'head', split_axis=0, concat_axis=1, tiled=True)  11.8 us
    all_to_all x1, starting transfers between devices, shards(): lax.all_to_all(grad_both.reshape(CORES * HEADS, tokens, HD), ('core', 'he...  10.8 us
    ppermute x2, starting transfers between devices, next_row(): lax.ppermute(block, 'row', [(i, i + shift) for i in range(rows) if 0 <= i...  10.4 us
    all_to_all x1, waiting for transfers between devices, shards(): lax.all_to_all(jnp.concatenate(chunks, 0), ('core', 'head'), split_axis=0...  8.1 us
    ppermute x16, waiting for transfers between devices, along(): lax.ppermute(block, 'chip', [(i, i + shift) for i in starts if 0 <= i + s...  7.75 us
    all_to_all x1, starting transfers between devices, shards(): lax.all_to_all(jnp.concatenate(chunks, 0), ('core', 'head'), split_axis=0...  6.7 us
  transfers between devices with their start and end apart: 24, of which 7 were waited for; matrix products, arithmetic and copies ran while one was open for 6% of the time, Pallas kernels for 4%

profile of v9, /device:TPU:31, one launch (start us, length us, event | category | flops | bytes accessed | tf_op | source)
XLA Modules:
  0.0 147.7 jit_solution(1596711193503592786)
XLA Ops:
  2.4 6.7 %all-to-all-start = ((bf16[8,64,256]{2,1,0:T(8,128)(2,1)}), bf16[8,64,256]{2,1,0:T(8,128)(2,1)S(1)}, u32[]{:S(2)}, u32[]{:S(2)}) async-start(bf16[8,64,256]{2,1,0:T(8,128)(2,1)} %pad_maximum_fusion.1), calls=%async_computation | async-start | bytes 524288 | tf_op jit(solution)/shard_map/all_to_all | solution.py:376
  10.0 8.1 %all-to-all-done = bf16[8,64,256]{2,1,0:T(8,128)(2,1)S(1)} async-done(((bf16[8,64,256]{2,1,0:T(8,128)(2,1)}), bf16[8,64,256]{2,1,0:T(8,128)(2,1)S(1)}, u32[]{:S(2)}, u32[]{:S(2)}) %all-to-all-start) | async-done | bytes 262176 | tf_op jit(solution)/shard_map/all_to_all | solution.py:376
  18.1 3.5 %all-to-all-start.1 = ((bf16[64,4,1024]{2,0,1:T(8,128)(2,1)}), bf16[64,4,1024]{2,0,1:T(8,128)(2,1)S(1)}, u32[]{:S(2)}, u32[]{:S(2)}) async-start(bf16[64,4,1024]{2,0,1:T(8,128)(2,1)} %pad_maximum_fusion), calls=%async_computation.1 | async-start | bytes 1048576 | tf_op jit(solution)/shard_map/all_to_all | solution.py:388
  21.6 1.5 %shard_map.84.table = s32[32]{0:T(128)} custom-call(s32[128]{0:T(128)} %gap_ref.1), custom_call_target="tpu_custom_call" | custom-call | tf_op jit(solution)/shard_map/pallas_call | solution.py:107
  23.9 2.3 %multiply_sine_fusion = (f32[1280,128]{1,0:T(8,128)S(1)}, f32[1280,128]{1,0:T(8,128)S(1)}) fusion(f32[128]{0:T(128)S(1)} %multiply_exponential_fusion, f32[1280]{0:T(1024)S(1)} %convert_element_type.21), kind=kLoop, calls=%fused_computation | loop fusion | flops 163840 | bytes 1316352 | tf_op jit(solution)/shard_map/sin | solution.py:381
  27.5 2.4 %collective-permute-start = (bf16[256,256]{1,0:T(8,128)(2,1)S(1)}, bf16[256,256]{1,0:T(8,128)(2,1)S(1)}, u32[]{:S(2)}, u32[]{:S(2)}) collective-permute-start(bf16[256,256]{1,0:T(8,128)(2,1)S(1)} %get-tuple-element.30), channel_id=1, source_target_pairs={{8,0},{16,8},{24,16},{9,1},{17,9},{25,17},{10,2},{18,10},{26,18},{... | collective-permute-start | bytes 393224 | tf_op jit(solution)/shard_map/ppermute | solution.py:357
  33.0 8.5 %collective-permute-start.2 = (bf16[256,256]{1,0:T(8,128)(2,1)S(1)}, bf16[256,256]{1,0:T(8,128)(2,1)S(1)}, u32[]{:S(2)}, u32[]{:S(2)}) collective-permute-start(bf16[256,256]{1,0:T(8,128)(2,1)S(1)} %shard_map.86), channel_id=1, source_target_pairs={{0,32},{32,64},{64,96},{96,128},{128,160},{160,192},{192,224},{224... | collective-permute-start | bytes 393224 | tf_op jit(solution)/shard_map/ppermute | solution.py:362
  44.2 7.1 %collective-permute-start.8 = (bf16[256,256]{1,0:T(8,128)(2,1)S(1)}, bf16[256,256]{1,0:T(8,128)(2,1)S(1)}, u32[]{:S(2)}, u32[]{:S(2)}) collective-permute-start(bf16[256,256]{1,0:T(8,128)(2,1)S(1)} %collective-permute-done.2.refs_4_), channel_id=1, source_target_pairs={{24,0},{25,1},{26,2},{27,3},{28,4},{29,5},{30,6},{31,7},{56,32},{5... | collective-permute-start | bytes 393224 | tf_op jit(solution)/shard_map/ppermute | solution.py:357
  52.7 2.5 %collective-permute-start.6 = (bf16[256,256]{1,0:T(8,128)(2,1)S(1)}, bf16[256,256]{1,0:T(8,128)(2,1)S(1)}, u32[]{:S(2)}, u32[]{:S(2)}) collective-permute-start(bf16[256,256]{1,0:T(8,128)(2,1)S(1)} %collective-permute-done.2.refs_4_), channel_id=1, source_target_pairs={{8,0},{16,8},{24,16},{9,1},{17,9},{25,17},{10,2},{18,10},{26,18},{... | collective-permute-start | bytes 393224 | tf_op jit(solution)/shard_map/ppermute | solution.py:357
  55.2 3.0 %collective-permute-done.6.refs_5_ = bf16[256,256]{1,0:T(8,128)(2,1)S(1)} collective-permute-done((bf16[256,256]{1,0:T(8,128)(2,1)S(1)}, bf16[256,256]{1,0:T(8,128)(2,1)S(1)}, u32[]{:S(2)}, u32[]{:S(2)}) %collective-permute-start.6) | collective-permute-done | bytes 131104 | tf_op jit(solution)/shard_map/ppermute | solution.py:357
  59.1 3.7 %collective-permute-start.9 = (bf16[1280,256]{1,0:T(8,128)(2,1)S(1)}, bf16[1280,256]{1,0:T(8,128)(2,1)S(1)}, u32[]{:S(2)}, u32[]{:S(2)}) collective-permute-start(bf16[1280,256]{1,0:T(8,128)(2,1)S(1)} %shard_map.87), channel_id=1, source_target_pairs={{0,4},{4,0},{1,5},{5,1},{2,6},{6,2},{3,7},{7,3},{8,12},{12,8},{9,1... | collective-permute-start | bytes 1966088 | tf_op jit(solution)/shard_map/ppermute | solution.py:368
  62.8 1.7 %collective-permute-done.9.other_ref = bf16[1280,256]{1,0:T(8,128)(2,1)S(1)} collective-permute-done((bf16[1280,256]{1,0:T(8,128)(2,1)S(1)}, bf16[1280,256]{1,0:T(8,128)(2,1)S(1)}, u32[]{:S(2)}, u32[]{:S(2)}) %collective-permute-start.9) | collective-permute-done | bytes 655392 | tf_op jit(solution)/shard_map/ppermute | solution.py:368
  65.4 4.8 %shard_map.88 = (bf16[256,1024]{1,0:T(8,128)(2,1)S(1)}, bf16[1280,256]{1,0:T(8,128)(2,1)S(1)}, bf16[1280,256]{1,0:T(8,128)(2,1)}) custom-call(s32[32]{0:T(128)S(1)} %copy-done.3, bf16[256,1024]{1,0:T(8,128)(2,1)S(1)} %bitcast.47, f32[1280,128]{1,0:T(8,128)S(1)} %get-tuple-element.33.cos_ref, f32[1280,128]{1,0:T(8,128)S(1)} %get-tuple-element.34.sin_ref, ...), custom_call_target="tpu_custom_call" | custom-call | tf_op jit(solution)/shard_map/pallas_call | solution.py:254
  71.0 2.3 %collective-permute-start.10 = (bf16[1280,256]{1,0:T(8,128)(2,1)}, bf16[1280,256]{1,0:T(8,128)(2,1)S(1)}, u32[]{:S(2)}, u32[]{:S(2)}) collective-permute-start(bf16[1280,256]{1,0:T(8,128)(2,1)} %get-tuple-element.37), channel_id=1, source_target_pairs={{0,4},{4,0},{1,5},{5,1},{2,6},{6,2},{3,7},{7,3},{8,12},{12,8},{9,1... | collective-permute-start | bytes 1966088 | tf_op jit(solution)/shard_map/ppermute | solution.py:368
  73.3 11.8 %all-to-all-start.2 = ((bf16[4,64,1024]{2,1,0:T(8,128)(2,1)}), bf16[4,64,1024]{2,1,0:T(8,128)(2,1)S(1)}, u32[]{:S(2)}, u32[]{:S(2)}) async-start(bf16[4,64,1024]{2,1,0:T(8,128)(2,1)} %bitcast.48), calls=%async_computation.2 | async-start | bytes 1048576 | tf_op jit(solution)/shard_map/all_to_all | solution.py:397
  90.1 4.1 %collective-permute-start.11 = (bf16[512,256]{1,0:T(8,128)(2,1)S(1)}, bf16[512,256]{1,0:T(8,128)(2,1)S(1)}, u32[]{:S(2)}, u32[]{:S(2)}) collective-permute-start(bf16[512,256]{1,0:T(8,128)(2,1)S(1)} %get-tuple-element.39), channel_id=1, source_target_pairs={{8,0},{16,8},{24,16},{9,1},{17,9},{25,17},{10,2},{18,10},{26,18},{... | collective-permute-start | bytes 786440 | tf_op jit(solution)/shard_map/ppermute | solution.py:357
  94.3 6.7 %collective-permute-start.12 = (bf16[512,256]{1,0:T(8,128)(2,1)S(1)}, bf16[512,256]{1,0:T(8,128)(2,1)S(1)}, u32[]{:S(2)}, u32[]{:S(2)}) collective-permute-start(bf16[512,256]{1,0:T(8,128)(2,1)S(1)} %get-tuple-element.40), channel_id=1, source_target_pairs={{16,0},{24,8},{17,1},{25,9},{18,2},{26,10},{19,3},{27,11},{20,4},{... | collective-permute-start | bytes 786440 | tf_op jit(solution)/shard_map/ppermute | solution.py:357
  102.6 1.9 %collective-permute-start.17 = (bf16[256,256]{1,0:T(8,128)(2,1)S(1)}, bf16[256,256]{1,0:T(8,128)(2,1)S(1)}, u32[]{:S(2)}, u32[]{:S(2)}) collective-permute-start(bf16[256,256]{1,0:T(8,128)(2,1)S(1)} %shard_map.91), channel_id=1, source_target_pairs={{32,0},{64,32},{96,64},{128,96},{160,128},{192,160},{224,192},{256... | collective-permute-start | bytes 393224 | tf_op jit(solution)/shard_map/ppermute | solution.py:362
  105.5 13.2 %collective-permute-done.17.refs_0_ = bf16[256,256]{1,0:T(8,128)(2,1)S(1)} collective-permute-done((bf16[256,256]{1,0:T(8,128)(2,1)S(1)}, bf16[256,256]{1,0:T(8,128)(2,1)S(1)}, u32[]{:S(2)}, u32[]{:S(2)}) %collective-permute-start.17) | collective-permute-done | bytes 131104 | tf_op jit(solution)/shard_map/ppermute | solution.py:362
  120.9 4.2 %collective-permute-done.18.refs_1_ = bf16[256,256]{1,0:T(8,128)(2,1)S(1)} collective-permute-done((bf16[256,256]{1,0:T(8,128)(2,1)S(1)}, bf16[256,256]{1,0:T(8,128)(2,1)S(1)}, u32[]{:S(2)}, u32[]{:S(2)}) %collective-permute-start.18) | collective-permute-done | bytes 131104 | tf_op jit(solution)/shard_map/ppermute | solution.py:357
  125.1 1.4 shard_map.92
  126.5 10.8 %all-to-all-start.3 = ((bf16[8,64,256]{2,1,0:T(8,128)(2,1)}), bf16[8,64,256]{2,1,0:T(8,128)(2,1)S(1)}, u32[]{:S(2)}, u32[]{:S(2)}) async-start(bf16[8,64,256]{2,1,0:T(8,128)(2,1)} %bitcast.7), calls=%async_computation.3 | async-start | bytes 524288 | tf_op jit(solution)/shard_map/all_to_all | solution.py:410
  137.7 2.4 %slice_reduce_fusion = (bf16[64,4,512]{2,1,0:T(4,128)(2,1)S(1)}, bf16[64,4,512]{2,1,0:T(4,128)(2,1)S(1)}) fusion(bf16[64,4,2,512]{3,2,1,0:T(2,128)(2,1)S(1)} %reshape.87), kind=kLoop, calls=%fused_computation.2 | loop fusion | bytes 1048576 | tf_op jit(solution)/shard_map/slice | solution.py:423
  141.6 4.8 %all-to-all-done.3 = bf16[8,64,256]{2,1,0:T(8,128)(2,1)S(1)} async-done(((bf16[8,64,256]{2,1,0:T(8,128)(2,1)}), bf16[8,64,256]{2,1,0:T(8,128)(2,1)S(1)}, u32[]{:S(2)}, u32[]{:S(2)}) %all-to-all-start.3) | async-done | bytes 262176 | tf_op jit(solution)/shard_map/all_to_all | solution.py:410
  (66 shorter events, 27.1 us)
Async XLA Ops:
  2.4 15.7 %all-to-all-start = ((bf16[8,64,256]{2,1,0:T(8,128)(2,1)}), bf16[8,64,256]{2,1,0:T(8,128)(2,1)S(1)}, u32[]{:S(2)}, u32[]{:S(2)}) async-start(bf16[8,64,256]{2,1,0:T(8,128)(2,1)} %pad_maximum_fusion.1), calls=%async_computation | async-start | bytes 524288 | tf_op jit(solution)/shard_map/all_to_all | solution.py:376
  18.1 26.1 %all-to-all-start.1 = ((bf16[64,4,1024]{2,0,1:T(8,128)(2,1)}), bf16[64,4,1024]{2,0,1:T(8,128)(2,1)S(1)}, u32[]{:S(2)}, u32[]{:S(2)}) async-start(bf16[64,4,1024]{2,0,1:T(8,128)(2,1)} %pad_maximum_fusion), calls=%async_computation.1 | async-start | bytes 1048576 | tf_op jit(solution)/shard_map/all_to_all | solution.py:388
  27.5 4.9 %collective-permute-start = (bf16[256,256]{1,0:T(8,128)(2,1)S(1)}, bf16[256,256]{1,0:T(8,128)(2,1)S(1)}, u32[]{:S(2)}, u32[]{:S(2)}) collective-permute-start(bf16[256,256]{1,0:T(8,128)(2,1)S(1)} %get-tuple-element.30), channel_id=1, source_target_pairs={{8,0},{16,8},{24,16},{9,1},{17,9},{25,17},{10,2},{18,10},{26,18},{... | collective-permute-start | bytes 393224 | tf_op jit(solution)/shard_map/ppermute | solution.py:357
  30.0 2.5 %collective-permute-start.1 = (bf16[256,256]{1,0:T(8,128)(2,1)S(1)}, bf16[256,256]{1,0:T(8,128)(2,1)S(1)}, u32[]{:S(2)}, u32[]{:S(2)}) collective-permute-start(bf16[256,256]{1,0:T(8,128)(2,1)S(1)} %get-tuple-element.31), channel_id=1, source_target_pairs={{16,0},{17,1},{18,2},{19,3},{20,4},{21,5},{22,6},{23,7},{48,32},{4... | collective-permute-start | bytes 393224 | tf_op jit(solution)/shard_map/ppermute | solution.py:357
  30.6 22.0 %collective-permute-start.5 = (bf16[512,256]{1,0:T(8,128)(2,1)S(1)}, bf16[512,256]{1,0:T(8,128)(2,1)S(1)}, u32[]{:S(2)}, u32[]{:S(2)}) collective-permute-start(bf16[512,256]{1,0:T(8,128)(2,1)S(1)} %bitcast.41), channel_id=1, source_target_pairs={{0,24},{1,25},{2,26},{3,27},{4,28},{5,29},{6,30},{7,31},{32,56},{3... | collective-permute-start | bytes 786440 | tf_op jit(solution)/shard_map/ppermute | solution.py:357
  33.0 11.1 %collective-permute-start.2 = (bf16[256,256]{1,0:T(8,128)(2,1)S(1)}, bf16[256,256]{1,0:T(8,128)(2,1)S(1)}, u32[]{:S(2)}, u32[]{:S(2)}) collective-permute-start(bf16[256,256]{1,0:T(8,128)(2,1)S(1)} %shard_map.86), channel_id=1, source_target_pairs={{0,32},{32,64},{64,96},{96,128},{128,160},{160,192},{192,224},{224... | collective-permute-start | bytes 393224 | tf_op jit(solution)/shard_map/ppermute | solution.py:362
  41.6 13.6 %collective-permute-start.4 = (bf16[512,256]{1,0:T(8,128)(2,1)S(1)}, bf16[512,256]{1,0:T(8,128)(2,1)S(1)}, u32[]{:S(2)}, u32[]{:S(2)}) collective-permute-start(bf16[512,256]{1,0:T(8,128)(2,1)S(1)} %bitcast.43), channel_id=1, source_target_pairs={{0,16},{8,24},{1,17},{9,25},{2,18},{10,26},{3,19},{11,27},{4,20},{... | collective-permute-start | bytes 786440 | tf_op jit(solution)/shard_map/ppermute | solution.py:357
  42.9 12.3 %collective-permute-start.3 = (bf16[512,256]{1,0:T(8,128)(2,1)S(1)}, bf16[512,256]{1,0:T(8,128)(2,1)S(1)}, u32[]{:S(2)}, u32[]{:S(2)}) collective-permute-start(bf16[512,256]{1,0:T(8,128)(2,1)S(1)} %bitcast.44), channel_id=1, source_target_pairs={{0,8},{8,16},{16,24},{1,9},{9,17},{17,25},{2,10},{10,18},{18,26},{... | collective-permute-start | bytes 786440 | tf_op jit(solution)/shard_map/ppermute | solution.py:357
  44.2 11.0 %collective-permute-start.8 = (bf16[256,256]{1,0:T(8,128)(2,1)S(1)}, bf16[256,256]{1,0:T(8,128)(2,1)S(1)}, u32[]{:S(2)}, u32[]{:S(2)}) collective-permute-start(bf16[256,256]{1,0:T(8,128)(2,1)S(1)} %collective-permute-done.2.refs_4_), channel_id=1, source_target_pairs={{24,0},{25,1},{26,2},{27,3},{28,4},{29,5},{30,6},{31,7},{56,32},{5... | collective-permute-start | bytes 393224 | tf_op jit(solution)/shard_map/ppermute | solution.py:357
  51.4 3.8 %collective-permute-start.7 = (bf16[256,256]{1,0:T(8,128)(2,1)S(1)}, bf16[256,256]{1,0:T(8,128)(2,1)S(1)}, u32[]{:S(2)}, u32[]{:S(2)}) collective-permute-start(bf16[256,256]{1,0:T(8,128)(2,1)S(1)} %collective-permute-done.2.refs_4_), channel_id=1, source_target_pairs={{16,0},{24,8},{17,1},{25,9},{18,2},{26,10},{19,3},{27,11},{20,4},{... | collective-permute-start | bytes 393224 | tf_op jit(solution)/shard_map/ppermute | solution.py:357
  52.7 5.5 %collective-permute-start.6 = (bf16[256,256]{1,0:T(8,128)(2,1)S(1)}, bf16[256,256]{1,0:T(8,128)(2,1)S(1)}, u32[]{:S(2)}, u32[]{:S(2)}) collective-permute-start(bf16[256,256]{1,0:T(8,128)(2,1)S(1)} %collective-permute-done.2.refs_4_), channel_id=1, source_target_pairs={{8,0},{16,8},{24,16},{9,1},{17,9},{25,17},{10,2},{18,10},{26,18},{... | collective-permute-start | bytes 393224 | tf_op jit(solution)/shard_map/ppermute | solution.py:357
  59.1 5.4 %collective-permute-start.9 = (bf16[1280,256]{1,0:T(8,128)(2,1)S(1)}, bf16[1280,256]{1,0:T(8,128)(2,1)S(1)}, u32[]{:S(2)}, u32[]{:S(2)}) collective-permute-start(bf16[1280,256]{1,0:T(8,128)(2,1)S(1)} %shard_map.87), channel_id=1, source_target_pairs={{0,4},{4,0},{1,5},{5,1},{2,6},{6,2},{3,7},{7,3},{8,12},{12,8},{9,1... | collective-permute-start | bytes 1966088 | tf_op jit(solution)/shard_map/ppermute | solution.py:368
  71.0 14.1 %collective-permute-start.10 = (bf16[1280,256]{1,0:T(8,128)(2,1)}, bf16[1280,256]{1,0:T(8,128)(2,1)S(1)}, u32[]{:S(2)}, u32[]{:S(2)}) collective-permute-start(bf16[1280,256]{1,0:T(8,128)(2,1)} %get-tuple-element.37), channel_id=1, source_target_pairs={{0,4},{4,0},{1,5},{5,1},{2,6},{6,2},{3,7},{7,3},{8,12},{12,8},{9,1... | collective-permute-start | bytes 1966088 | tf_op jit(solution)/shard_map/ppermute | solution.py:368
  73.3 53.2 %all-to-all-start.2 = ((bf16[4,64,1024]{2,1,0:T(8,128)(2,1)}), bf16[4,64,1024]{2,1,0:T(8,128)(2,1)S(1)}, u32[]{:S(2)}, u32[]{:S(2)}) async-start(bf16[4,64,1024]{2,1,0:T(8,128)(2,1)} %bitcast.48), calls=%async_computation.2 | async-start | bytes 1048576 | tf_op jit(solution)/shard_map/all_to_all | solution.py:397
  86.2 14.8 %collective-permute-start.14 = (bf16[256,256]{1,0:T(8,128)(2,1)S(1)}, bf16[256,256]{1,0:T(8,128)(2,1)S(1)}, u32[]{:S(2)}, u32[]{:S(2)}) collective-permute-start(bf16[256,256]{1,0:T(8,128)(2,1)S(1)} %get-tuple-element.43), channel_id=1, source_target_pairs={{0,8},{8,16},{16,24},{1,9},{9,17},{17,25},{2,10},{10,18},{18,26},{... | collective-permute-start | bytes 393224 | tf_op jit(solution)/shard_map/ppermute | solution.py:357
  87.5 14.8 %collective-permute-start.15 = (bf16[256,256]{1,0:T(8,128)(2,1)S(1)}, bf16[256,256]{1,0:T(8,128)(2,1)S(1)}, u32[]{:S(2)}, u32[]{:S(2)}) collective-permute-start(bf16[256,256]{1,0:T(8,128)(2,1)S(1)} %get-tuple-element.44), channel_id=1, source_target_pairs={{0,16},{8,24},{1,17},{9,25},{2,18},{10,26},{3,19},{11,27},{4,20},{... | collective-permute-start | bytes 393224 | tf_op jit(solution)/shard_map/ppermute | solution.py:357
  88.8 13.5 %collective-permute-start.16 = (bf16[256,256]{1,0:T(8,128)(2,1)S(1)}, bf16[256,256]{1,0:T(8,128)(2,1)S(1)}, u32[]{:S(2)}, u32[]{:S(2)}) collective-permute-start(bf16[256,256]{1,0:T(8,128)(2,1)S(1)} %get-tuple-element.45), channel_id=1, source_target_pairs={{0,24},{1,25},{2,26},{3,27},{4,28},{5,29},{6,30},{7,31},{32,56},{3... | collective-permute-start | bytes 393224 | tf_op jit(solution)/shard_map/ppermute | solution.py:357
  90.1 30.6 %collective-permute-start.11 = (bf16[512,256]{1,0:T(8,128)(2,1)S(1)}, bf16[512,256]{1,0:T(8,128)(2,1)S(1)}, u32[]{:S(2)}, u32[]{:S(2)}) collective-permute-start(bf16[512,256]{1,0:T(8,128)(2,1)S(1)} %get-tuple-element.39), channel_id=1, source_target_pairs={{8,0},{16,8},{24,16},{9,1},{17,9},{25,17},{10,2},{18,10},{26,18},{... | collective-permute-start | bytes 786440 | tf_op jit(solution)/shard_map/ppermute | solution.py:357
  94.3 26.4 %collective-permute-start.12 = (bf16[512,256]{1,0:T(8,128)(2,1)S(1)}, bf16[512,256]{1,0:T(8,128)(2,1)S(1)}, u32[]{:S(2)}, u32[]{:S(2)}) collective-permute-start(bf16[512,256]{1,0:T(8,128)(2,1)S(1)} %get-tuple-element.40), channel_id=1, source_target_pairs={{16,0},{24,8},{17,1},{25,9},{18,2},{26,10},{19,3},{27,11},{20,4},{... | collective-permute-start | bytes 786440 | tf_op jit(solution)/shard_map/ppermute | solution.py:357
  101.0 19.7 %collective-permute-start.13 = (bf16[512,256]{1,0:T(8,128)(2,1)S(1)}, bf16[512,256]{1,0:T(8,128)(2,1)S(1)}, u32[]{:S(2)}, u32[]{:S(2)}) collective-permute-start(bf16[512,256]{1,0:T(8,128)(2,1)S(1)} %get-tuple-element.41), channel_id=1, source_target_pairs={{24,0},{25,1},{26,2},{27,3},{28,4},{29,5},{30,6},{31,7},{56,32},{5... | collective-permute-start | bytes 786440 | tf_op jit(solution)/shard_map/ppermute | solution.py:357
  102.6 16.2 %collective-permute-start.17 = (bf16[256,256]{1,0:T(8,128)(2,1)S(1)}, bf16[256,256]{1,0:T(8,128)(2,1)S(1)}, u32[]{:S(2)}, u32[]{:S(2)}) collective-permute-start(bf16[256,256]{1,0:T(8,128)(2,1)S(1)} %shard_map.91), channel_id=1, source_target_pairs={{32,0},{64,32},{96,64},{128,96},{160,128},{192,160},{224,192},{256... | collective-permute-start | bytes 393224 | tf_op jit(solution)/shard_map/ppermute | solution.py:362
  118.8 2.1 %collective-permute-start.19 = (bf16[256,256]{1,0:T(8,128)(2,1)S(1)}, bf16[256,256]{1,0:T(8,128)(2,1)S(1)}, u32[]{:S(2)}, u32[]{:S(2)}) collective-permute-start(bf16[256,256]{1,0:T(8,128)(2,1)S(1)} %collective-permute-done.17.refs_0_), channel_id=1, source_target_pairs={{0,16},{1,17},{2,18},{3,19},{4,20},{5,21},{6,22},{7,23},{32,48},{3... | collective-permute-start | bytes 393224 | tf_op jit(solution)/shard_map/ppermute | solution.py:357
  119.4 5.7 %collective-permute-start.18 = (bf16[256,256]{1,0:T(8,128)(2,1)S(1)}, bf16[256,256]{1,0:T(8,128)(2,1)S(1)}, u32[]{:S(2)}, u32[]{:S(2)}) collective-permute-start(bf16[256,256]{1,0:T(8,128)(2,1)S(1)} %collective-permute-done.17.refs_0_), channel_id=1, source_target_pairs={{0,8},{8,16},{16,24},{1,9},{9,17},{17,25},{2,10},{10,18},{18,26},{... | collective-permute-start | bytes 393224 | tf_op jit(solution)/shard_map/ppermute | solution.py:357
  126.5 19.8 %all-to-all-start.3 = ((bf16[8,64,256]{2,1,0:T(8,128)(2,1)}), bf16[8,64,256]{2,1,0:T(8,128)(2,1)S(1)}, u32[]{:S(2)}, u32[]{:S(2)}) async-start(bf16[8,64,256]{2,1,0:T(8,128)(2,1)} %bitcast.7), calls=%async_computation.3 | async-start | bytes 524288 | tf_op jit(solution)/shard_map/all_to_all | solution.py:410
  (6 other events, 30.7 us)

commit v10 on v7

--- a/solution.py
+++ b/solution.py
@@ -337,9 +337,7 @@
 
 
 def along(block, shift, starts=range(CHIPS)):
-    return lax.ppermute(
-        block, "chip", [(i, i + shift) for i in starts if 0 <= i + shift < CHIPS]
-    )
+    return lax.ppermute(block, "chip", [(i, i + shift) for i in starts if 0 <= i + shift < CHIPS])
 
 
 def next_row(block, shift):
@@ -363,9 +361,7 @@
     ).reshape(PAIR, HD)
     table = call_plan(parent_gap)
     slot_angles = angles_of(table[DEPTHS : DEPTHS + SLOTS])
-    pair_angles = angles_of(table[PAIRS : PAIRS + CORES])
     slot_cos, slot_sin = jnp.cos(slot_angles), jnp.sin(slot_angles)
-    pair_cos, pair_sin = jnp.cos(pair_angles), jnp.sin(pair_angles)
     both, slot_cos, slot_sin = lax.optimization_barrier((both, slot_cos, slot_sin))
     pairs = [both, along(both, -1), along(both, -2, (2,))]
     query_grad = jnp.concatenate(
@@ -384,7 +380,10 @@
     spread = call_spread(table, keep, got)
     own, within, stack = spread[0], spread[1:CHIPS], spread[CHIPS:]
     stack_sum = call_sum([stack[0]] + [along(stack[k], k) for k in (1, 2, 3)], BF16)
+    stack_sum, late_table = lax.optimization_barrier((stack_sum, table))
     back = next_row(stack_sum, -1)
+    pair_angles = angles_of(late_table[PAIRS : PAIRS + CORES])
+    pair_cos, pair_sin = jnp.cos(pair_angles), jnp.sin(pair_angles)
     back, pair_cos, pair_sin = lax.optimization_barrier((back, pair_cos, pair_sin))
     own = call_sum([own] + [along(within[k - 1], -k) for k in (1, 2, 3)], F32)
     backs = [back, along(back, 1), along(back, 2, (0,))]

time: 156 us -> 149 us (0.955)
  the two profiles are of different devices: /device:TPU:29 before, /device:TPU:31 now
where the time goes in v10:
time: 149 us; the launch traced here: 148 us
  starting transfers between devices  83.8 us (56%)
  waiting for transfers between devices  39.1 us (26%)
  Pallas kernels  10.5 us (7%)
  local copies, waits for them, and re-layouts  7.78 us (5%)
  other arithmetic  5.87 us (4%)
    ppermute x16, starting transfers between devices, along(): lax.ppermute(block, 'chip', [(i, i + shift) for i in starts if 0 <= i + s...  37.4 us
    ppermute x2, waiting for transfers between devices, next_row(): lax.ppermute(block, 'row', [(i, i + shift) for i in range(rows) if 0 <= i...  13.3 us
    ppermute x16, waiting for transfers between devices, along(): lax.ppermute(block, 'chip', [(i, i + shift) for i in starts if 0 <= i + s...  11.2 us
    all_to_all x1, starting transfers between devices, shards(): lax.all_to_all(grad_both, ('core', 'head'), split_axis=0, concat_axis=1,...  10.8 us
    ppermute x2, starting transfers between devices, next_row(): lax.ppermute(block, 'row', [(i, i + shift) for i in range(rows) if 0 <= i...  10.4 us
    all_to_all x1, starting transfers between devices, shards(): out = lax.all_to_all(out, 'head', split_axis=0, concat_axis=1, tiled=True)  9.06 us
    all_to_all x1, waiting for transfers between devices, shards(): lax.all_to_all(jnp.concatenate(chunks, 0), ('core', 'head'), split_axis=0...  8.1 us
    all_to_all x1, starting transfers between devices, shards(): lax.all_to_all(jnp.concatenate(chunks, 0), ('core', 'head'), split_axis=0...  6.7 us
  transfers between devices with their start and end apart: 24, of which 7 were waited for; matrix products, arithmetic and copies ran while one was open for 6% of the time, Pallas kernels for 3%

profile of v10, /device:TPU:31, one launch (start us, length us, event | category | flops | bytes accessed | tf_op | source)
XLA Modules:
  0.0 148.1 jit_solution(3309280877577503838)
XLA Ops:
  2.4 6.7 %all-to-all-start = ((bf16[8,64,256]{2,1,0:T(8,128)(2,1)}), bf16[8,64,256]{2,1,0:T(8,128)(2,1)S(1)}, u32[]{:S(2)}, u32[]{:S(2)}) async-start(bf16[8,64,256]{2,1,0:T(8,128)(2,1)} %pad_maximum_fusion.1), calls=%async_computation | async-start | bytes 524288 | tf_op jit(solution)/shard_map/all_to_all | solution.py:359
  10.0 8.1 %all-to-all-done = bf16[8,64,256]{2,1,0:T(8,128)(2,1)S(1)} async-done(((bf16[8,64,256]{2,1,0:T(8,128)(2,1)}), bf16[8,64,256]{2,1,0:T(8,128)(2,1)S(1)}, u32[]{:S(2)}, u32[]{:S(2)}) %all-to-all-start) | async-done | bytes 262176 | tf_op jit(solution)/shard_map/all_to_all | solution.py:359
  18.1 3.5 %all-to-all-start.1 = ((bf16[64,4,1024]{2,0,1:T(8,128)(2,1)}), bf16[64,4,1024]{2,0,1:T(8,128)(2,1)S(1)}, u32[]{:S(2)}, u32[]{:S(2)}) async-start(bf16[64,4,1024]{2,0,1:T(8,128)(2,1)} %pad_maximum_fusion), calls=%async_computation.1 | async-start | bytes 1048576 | tf_op jit(solution)/shard_map/all_to_all | solution.py:370
  21.6 1.5 %shard_map.84.table = s32[32]{0:T(128)} custom-call(s32[128]{0:T(128)} %gap_ref.1), custom_call_target="tpu_custom_call" | custom-call | tf_op jit(solution)/shard_map/pallas_call | solution.py:105
  23.9 2.3 %multiply_sine_fusion = (f32[1280,128]{1,0:T(8,128)S(1)}, f32[1280,128]{1,0:T(8,128)S(1)}) fusion(f32[128]{0:T(128)S(1)} %multiply_exponential_fusion, f32[1280]{0:T(1024)S(1)} %convert_element_type.21), kind=kLoop, calls=%fused_computation | loop fusion | flops 163840 | bytes 1316352 | tf_op jit(solution)/shard_map/sin | solution.py:364
  27.0 3.9 %collective-permute-start = (bf16[512,256]{1,0:T(8,128)(2,1)S(1)}, bf16[512,256]{1,0:T(8,128)(2,1)S(1)}, u32[]{:S(2)}, u32[]{:S(2)}) collective-permute-start(bf16[512,256]{1,0:T(8,128)(2,1)S(1)} %bitcast.36), channel_id=1, source_target_pairs={{8,0},{16,8},{24,16},{9,1},{17,9},{25,17},{10,2},{18,10},{26,18},{... | collective-permute-start | bytes 786440 | tf_op jit(solution)/shard_map/ppermute | solution.py:340
  32.2 3.7 %collective-permute-done.refs_1_ = bf16[512,256]{1,0:T(8,128)(2,1)S(1)} collective-permute-done((bf16[512,256]{1,0:T(8,128)(2,1)S(1)}, bf16[512,256]{1,0:T(8,128)(2,1)S(1)}, u32[]{:S(2)}, u32[]{:S(2)}) %collective-permute-start) | collective-permute-done | bytes 262176 | tf_op jit(solution)/shard_map/ppermute | solution.py:340
  36.5 8.5 %collective-permute-start.2 = (bf16[256,256]{1,0:T(8,128)(2,1)S(1)}, bf16[256,256]{1,0:T(8,128)(2,1)S(1)}, u32[]{:S(2)}, u32[]{:S(2)}) collective-permute-start(bf16[256,256]{1,0:T(8,128)(2,1)S(1)} %shard_map.85), channel_id=1, source_target_pairs={{0,32},{32,64},{64,96},{96,128},{128,160},{160,192},{192,224},{224... | collective-permute-start | bytes 393224 | tf_op jit(solution)/shard_map/ppermute | solution.py:345
  47.6 7.1 %collective-permute-start.8 = (bf16[256,256]{1,0:T(8,128)(2,1)S(1)}, bf16[256,256]{1,0:T(8,128)(2,1)S(1)}, u32[]{:S(2)}, u32[]{:S(2)}) collective-permute-start(bf16[256,256]{1,0:T(8,128)(2,1)S(1)} %collective-permute-done.2.refs_4_), channel_id=1, source_target_pairs={{24,0},{25,1},{26,2},{27,3},{28,4},{29,5},{30,6},{31,7},{56,32},{5... | collective-permute-start | bytes 393224 | tf_op jit(solution)/shard_map/ppermute | solution.py:340
  56.1 2.5 %collective-permute-start.6 = (bf16[256,256]{1,0:T(8,128)(2,1)S(1)}, bf16[256,256]{1,0:T(8,128)(2,1)S(1)}, u32[]{:S(2)}, u32[]{:S(2)}) collective-permute-start(bf16[256,256]{1,0:T(8,128)(2,1)S(1)} %collective-permute-done.2.refs_4_), channel_id=1, source_target_pairs={{8,0},{16,8},{24,16},{9,1},{17,9},{25,17},{10,2},{18,10},{26,18},{... | collective-permute-start | bytes 393224 | tf_op jit(solution)/shard_map/ppermute | solution.py:340
  58.6 3.2 %collective-permute-done.6.refs_5_ = bf16[256,256]{1,0:T(8,128)(2,1)S(1)} collective-permute-done((bf16[256,256]{1,0:T(8,128)(2,1)S(1)}, bf16[256,256]{1,0:T(8,128)(2,1)S(1)}, u32[]{:S(2)}, u32[]{:S(2)}) %collective-permute-start.6) | collective-permute-done | bytes 131104 | tf_op jit(solution)/shard_map/ppermute | solution.py:340
  62.8 3.7 %collective-permute-start.9 = (bf16[1280,256]{1,0:T(8,128)(2,1)S(1)}, bf16[1280,256]{1,0:T(8,128)(2,1)S(1)}, u32[]{:S(2)}, u32[]{:S(2)}) collective-permute-start(bf16[1280,256]{1,0:T(8,128)(2,1)S(1)} %shard_map.86), channel_id=1, source_target_pairs={{0,4},{4,0},{1,5},{5,1},{2,6},{6,2},{3,7},{7,3},{8,12},{12,8},{9,1... | collective-permute-start | bytes 1966088 | tf_op jit(solution)/shard_map/ppermute | solution.py:351
  66.5 1.7 %collective-permute-done.9.other_ref = bf16[1280,256]{1,0:T(8,128)(2,1)S(1)} collective-permute-done((bf16[1280,256]{1,0:T(8,128)(2,1)S(1)}, bf16[1280,256]{1,0:T(8,128)(2,1)S(1)}, u32[]{:S(2)}, u32[]{:S(2)}) %collective-permute-start.9) | collective-permute-done | bytes 655392 | tf_op jit(solution)/shard_map/ppermute | solution.py:351
  69.1 4.8 %shard_map.87 = (bf16[256,1024]{1,0:T(8,128)(2,1)S(1)}, bf16[1280,256]{1,0:T(8,128)(2,1)S(1)}, bf16[1280,256]{1,0:T(8,128)(2,1)}) custom-call(s32[32]{0:T(128)S(1)} %copy-done.3, bf16[256,1024]{1,0:T(8,128)(2,1)S(1)} %bitcast.43, f32[1280,128]{1,0:T(8,128)S(1)} %get-tuple-element.29.cos_ref, f32[1280,128]{1,0:T(8,128)S(1)} %get-tuple-element.30.sin_ref, ...), custom_call_target="tpu_custom_call" | custom-call | tf_op jit(solution)/shard_map/pallas_call | solution.py:237
  74.7 2.3 %collective-permute-start.10 = (bf16[1280,256]{1,0:T(8,128)(2,1)}, bf16[1280,256]{1,0:T(8,128)(2,1)S(1)}, u32[]{:S(2)}, u32[]{:S(2)}) collective-permute-start(bf16[1280,256]{1,0:T(8,128)(2,1)} %get-tuple-element.33), channel_id=1, source_target_pairs={{0,4},{4,0},{1,5},{5,1},{2,6},{6,2},{3,7},{7,3},{8,12},{12,8},{9,1... | collective-permute-start | bytes 1966088 | tf_op jit(solution)/shard_map/ppermute | solution.py:351
  77.0 9.1 %all-to-all-start.2 = ((bf16[4,64,1024]{2,1,0:T(8,128)(2,1)}), bf16[4,64,1024]{2,1,0:T(8,128)(2,1)S(1)}, u32[]{:S(2)}, u32[]{:S(2)}) async-start(bf16[4,64,1024]{2,1,0:T(8,128)(2,1)} %bitcast.44), calls=%async_computation.2 | async-start | bytes 1048576 | tf_op jit(solution)/shard_map/all_to_all | solution.py:379
  91.1 4.1 %collective-permute-start.11 = (bf16[512,256]{1,0:T(8,128)(2,1)S(1)}, bf16[512,256]{1,0:T(8,128)(2,1)S(1)}, u32[]{:S(2)}, u32[]{:S(2)}) collective-permute-start(bf16[512,256]{1,0:T(8,128)(2,1)S(1)} %get-tuple-element.35), channel_id=1, source_target_pairs={{8,0},{16,8},{24,16},{9,1},{17,9},{25,17},{10,2},{18,10},{26,18},{... | collective-permute-start | bytes 786440 | tf_op jit(solution)/shard_map/ppermute | solution.py:340
  95.2 6.7 %collective-permute-start.12 = (bf16[512,256]{1,0:T(8,128)(2,1)S(1)}, bf16[512,256]{1,0:T(8,128)(2,1)S(1)}, u32[]{:S(2)}, u32[]{:S(2)}) collective-permute-start(bf16[512,256]{1,0:T(8,128)(2,1)S(1)} %get-tuple-element.36), channel_id=1, source_target_pairs={{16,0},{24,8},{17,1},{25,9},{18,2},{26,10},{19,3},{27,11},{20,4},{... | collective-permute-start | bytes 786440 | tf_op jit(solution)/shard_map/ppermute | solution.py:340
  103.5 1.9 %collective-permute-start.17 = (bf16[256,256]{1,0:T(8,128)(2,1)S(1)}, bf16[256,256]{1,0:T(8,128)(2,1)S(1)}, u32[]{:S(2)}, u32[]{:S(2)}) collective-permute-start(bf16[256,256]{1,0:T(8,128)(2,1)S(1)} %shard_map.90), channel_id=1, source_target_pairs={{32,0},{64,32},{96,64},{128,96},{160,128},{192,160},{224,192},{256... | collective-permute-start | bytes 393224 | tf_op jit(solution)/shard_map/ppermute | solution.py:345
  106.4 13.2 %collective-permute-done.17.refs_0_ = bf16[256,256]{1,0:T(8,128)(2,1)S(1)} collective-permute-done((bf16[256,256]{1,0:T(8,128)(2,1)S(1)}, bf16[256,256]{1,0:T(8,128)(2,1)S(1)}, u32[]{:S(2)}, u32[]{:S(2)}) %collective-permute-start.17) | collective-permute-done | bytes 131104 | tf_op jit(solution)/shard_map/ppermute | solution.py:345
  121.8 4.2 %collective-permute-done.18.refs_1_ = bf16[256,256]{1,0:T(8,128)(2,1)S(1)} collective-permute-done((bf16[256,256]{1,0:T(8,128)(2,1)S(1)}, bf16[256,256]{1,0:T(8,128)(2,1)S(1)}, u32[]{:S(2)}, u32[]{:S(2)}) %collective-permute-start.18) | collective-permute-done | bytes 131104 | tf_op jit(solution)/shard_map/ppermute | solution.py:340
  127.5 10.8 %all-to-all-start.3 = ((bf16[8,64,256]{2,1,0:T(8,128)(2,1)}), bf16[8,64,256]{2,1,0:T(8,128)(2,1)S(1)}, u32[]{:S(2)}, u32[]{:S(2)}) async-start(bf16[8,64,256]{2,1,0:T(8,128)(2,1)} %bitcast.7), calls=%async_computation.3 | async-start | bytes 524288 | tf_op jit(solution)/shard_map/all_to_all | solution.py:392
  138.7 2.4 %slice_reduce_fusion = (bf16[64,4,512]{2,1,0:T(4,128)(2,1)S(1)}, bf16[64,4,512]{2,1,0:T(4,128)(2,1)S(1)}) fusion(bf16[64,4,2,512]{3,2,1,0:T(2,128)(2,1)S(1)} %reshape.81), kind=kLoop, calls=%fused_computation.2 | loop fusion | bytes 1048576 | tf_op jit(solution)/shard_map/slice | solution.py:395
  142.6 4.8 %all-to-all-done.3 = bf16[8,64,256]{2,1,0:T(8,128)(2,1)S(1)} async-done(((bf16[8,64,256]{2,1,0:T(8,128)(2,1)}), bf16[8,64,256]{2,1,0:T(8,128)(2,1)S(1)}, u32[]{:S(2)}, u32[]{:S(2)}) %all-to-all-start.3) | async-done | bytes 262176 | tf_op jit(solution)/shard_map/all_to_all | solution.py:392
  (64 shorter events, 26.1 us)
Async XLA Ops:
  2.4 15.7 %all-to-all-start = ((bf16[8,64,256]{2,1,0:T(8,128)(2,1)}), bf16[8,64,256]{2,1,0:T(8,128)(2,1)S(1)}, u32[]{:S(2)}, u32[]{:S(2)}) async-start(bf16[8,64,256]{2,1,0:T(8,128)(2,1)} %pad_maximum_fusion.1), calls=%async_computation | async-start | bytes 524288 | tf_op jit(solution)/shard_map/all_to_all | solution.py:359
  18.1 29.6 %all-to-all-start.1 = ((bf16[64,4,1024]{2,0,1:T(8,128)(2,1)}), bf16[64,4,1024]{2,0,1:T(8,128)(2,1)S(1)}, u32[]{:S(2)}, u32[]{:S(2)}) async-start(bf16[64,4,1024]{2,0,1:T(8,128)(2,1)} %pad_maximum_fusion), calls=%async_computation.1 | async-start | bytes 1048576 | tf_op jit(solution)/shard_map/all_to_all | solution.py:370
  26.3 5.9 %collective-permute-start.1 = (bf16[512,256]{1,0:T(8,128)(2,1)S(1)}, bf16[512,256]{1,0:T(8,128)(2,1)S(1)}, u32[]{:S(2)}, u32[]{:S(2)}) collective-permute-start(bf16[512,256]{1,0:T(8,128)(2,1)S(1)} %bitcast.35), channel_id=1, source_target_pairs={{16,0},{17,1},{18,2},{19,3},{20,4},{21,5},{22,6},{23,7},{48,32},{4... | collective-permute-start | bytes 786440 | tf_op jit(solution)/shard_map/ppermute | solution.py:340
  27.0 8.9 %collective-permute-start = (bf16[512,256]{1,0:T(8,128)(2,1)S(1)}, bf16[512,256]{1,0:T(8,128)(2,1)S(1)}, u32[]{:S(2)}, u32[]{:S(2)}) collective-permute-start(bf16[512,256]{1,0:T(8,128)(2,1)S(1)} %bitcast.36), channel_id=1, source_target_pairs={{8,0},{16,8},{24,16},{9,1},{17,9},{25,17},{10,2},{18,10},{26,18},{... | collective-permute-start | bytes 786440 | tf_op jit(solution)/shard_map/ppermute | solution.py:340
  30.9 25.2 %collective-permute-start.5 = (bf16[512,256]{1,0:T(8,128)(2,1)S(1)}, bf16[512,256]{1,0:T(8,128)(2,1)S(1)}, u32[]{:S(2)}, u32[]{:S(2)}) collective-permute-start(bf16[512,256]{1,0:T(8,128)(2,1)S(1)} %bitcast.37), channel_id=1, source_target_pairs={{0,24},{1,25},{2,26},{3,27},{4,28},{5,29},{6,30},{7,31},{32,56},{3... | collective-permute-start | bytes 786440 | tf_op jit(solution)/shard_map/ppermute | solution.py:340
  36.5 11.1 %collective-permute-start.2 = (bf16[256,256]{1,0:T(8,128)(2,1)S(1)}, bf16[256,256]{1,0:T(8,128)(2,1)S(1)}, u32[]{:S(2)}, u32[]{:S(2)}) collective-permute-start(bf16[256,256]{1,0:T(8,128)(2,1)S(1)} %shard_map.85), channel_id=1, source_target_pairs={{0,32},{32,64},{64,96},{96,128},{128,160},{160,192},{192,224},{224... | collective-permute-start | bytes 393224 | tf_op jit(solution)/shard_map/ppermute | solution.py:345
  45.0 13.6 %collective-permute-start.4 = (bf16[512,256]{1,0:T(8,128)(2,1)S(1)}, bf16[512,256]{1,0:T(8,128)(2,1)S(1)}, u32[]{:S(2)}, u32[]{:S(2)}) collective-permute-start(bf16[512,256]{1,0:T(8,128)(2,1)S(1)} %bitcast.39), channel_id=1, source_target_pairs={{0,16},{8,24},{1,17},{9,25},{2,18},{10,26},{3,19},{11,27},{4,20},{... | collective-permute-start | bytes 786440 | tf_op jit(solution)/shard_map/ppermute | solution.py:340
  46.3 12.3 %collective-permute-start.3 = (bf16[512,256]{1,0:T(8,128)(2,1)S(1)}, bf16[512,256]{1,0:T(8,128)(2,1)S(1)}, u32[]{:S(2)}, u32[]{:S(2)}) collective-permute-start(bf16[512,256]{1,0:T(8,128)(2,1)S(1)} %bitcast.40), channel_id=1, source_target_pairs={{0,8},{8,16},{16,24},{1,9},{9,17},{17,25},{2,10},{10,18},{18,26},{... | collective-permute-start | bytes 786440 | tf_op jit(solution)/shard_map/ppermute | solution.py:340
  47.6 11.0 %collective-permute-start.8 = (bf16[256,256]{1,0:T(8,128)(2,1)S(1)}, bf16[256,256]{1,0:T(8,128)(2,1)S(1)}, u32[]{:S(2)}, u32[]{:S(2)}) collective-permute-start(bf16[256,256]{1,0:T(8,128)(2,1)S(1)} %collective-permute-done.2.refs_4_), channel_id=1, source_target_pairs={{24,0},{25,1},{26,2},{27,3},{28,4},{29,5},{30,6},{31,7},{56,32},{5... | collective-permute-start | bytes 393224 | tf_op jit(solution)/shard_map/ppermute | solution.py:340
  54.8 3.8 %collective-permute-start.7 = (bf16[256,256]{1,0:T(8,128)(2,1)S(1)}, bf16[256,256]{1,0:T(8,128)(2,1)S(1)}, u32[]{:S(2)}, u32[]{:S(2)}) collective-permute-start(bf16[256,256]{1,0:T(8,128)(2,1)S(1)} %collective-permute-done.2.refs_4_), channel_id=1, source_target_pairs={{16,0},{24,8},{17,1},{25,9},{18,2},{26,10},{19,3},{27,11},{20,4},{... | collective-permute-start | bytes 393224 | tf_op jit(solution)/shard_map/ppermute | solution.py:340
  56.1 5.8 %collective-permute-start.6 = (bf16[256,256]{1,0:T(8,128)(2,1)S(1)}, bf16[256,256]{1,0:T(8,128)(2,1)S(1)}, u32[]{:S(2)}, u32[]{:S(2)}) collective-permute-start(bf16[256,256]{1,0:T(8,128)(2,1)S(1)} %collective-permute-done.2.refs_4_), channel_id=1, source_target_pairs={{8,0},{16,8},{24,16},{9,1},{17,9},{25,17},{10,2},{18,10},{26,18},{... | collective-permute-start | bytes 393224 | tf_op jit(solution)/shard_map/ppermute | solution.py:340
  62.8 5.4 %collective-permute-start.9 = (bf16[1280,256]{1,0:T(8,128)(2,1)S(1)}, bf16[1280,256]{1,0:T(8,128)(2,1)S(1)}, u32[]{:S(2)}, u32[]{:S(2)}) collective-permute-start(bf16[1280,256]{1,0:T(8,128)(2,1)S(1)} %shard_map.86), channel_id=1, source_target_pairs={{0,4},{4,0},{1,5},{5,1},{2,6},{6,2},{3,7},{7,3},{8,12},{12,8},{9,1... | collective-permute-start | bytes 1966088 | tf_op jit(solution)/shard_map/ppermute | solution.py:351
  74.7 11.3 %collective-permute-start.10 = (bf16[1280,256]{1,0:T(8,128)(2,1)}, bf16[1280,256]{1,0:T(8,128)(2,1)S(1)}, u32[]{:S(2)}, u32[]{:S(2)}) collective-permute-start(bf16[1280,256]{1,0:T(8,128)(2,1)} %get-tuple-element.33), channel_id=1, source_target_pairs={{0,4},{4,0},{1,5},{5,1},{2,6},{6,2},{3,7},{7,3},{8,12},{12,8},{9,1... | collective-permute-start | bytes 1966088 | tf_op jit(solution)/shard_map/ppermute | solution.py:351
  77.0 50.5 %all-to-all-start.2 = ((bf16[4,64,1024]{2,1,0:T(8,128)(2,1)}), bf16[4,64,1024]{2,1,0:T(8,128)(2,1)S(1)}, u32[]{:S(2)}, u32[]{:S(2)}) async-start(bf16[4,64,1024]{2,1,0:T(8,128)(2,1)} %bitcast.44), calls=%async_computation.2 | async-start | bytes 1048576 | tf_op jit(solution)/shard_map/all_to_all | solution.py:379
  87.2 14.8 %collective-permute-start.14 = (bf16[256,256]{1,0:T(8,128)(2,1)S(1)}, bf16[256,256]{1,0:T(8,128)(2,1)S(1)}, u32[]{:S(2)}, u32[]{:S(2)}) collective-permute-start(bf16[256,256]{1,0:T(8,128)(2,1)S(1)} %get-tuple-element.39), channel_id=1, source_target_pairs={{0,8},{8,16},{16,24},{1,9},{9,17},{17,25},{2,10},{10,18},{18,26},{... | collective-permute-start | bytes 393224 | tf_op jit(solution)/shard_map/ppermute | solution.py:340
  88.5 14.8 %collective-permute-start.15 = (bf16[256,256]{1,0:T(8,128)(2,1)S(1)}, bf16[256,256]{1,0:T(8,128)(2,1)S(1)}, u32[]{:S(2)}, u32[]{:S(2)}) collective-permute-start(bf16[256,256]{1,0:T(8,128)(2,1)S(1)} %get-tuple-element.40), channel_id=1, source_target_pairs={{0,16},{8,24},{1,17},{9,25},{2,18},{10,26},{3,19},{11,27},{4,20},{... | collective-permute-start | bytes 393224 | tf_op jit(solution)/shard_map/ppermute | solution.py:340
  89.8 13.5 %collective-permute-start.16 = (bf16[256,256]{1,0:T(8,128)(2,1)S(1)}, bf16[256,256]{1,0:T(8,128)(2,1)S(1)}, u32[]{:S(2)}, u32[]{:S(2)}) collective-permute-start(bf16[256,256]{1,0:T(8,128)(2,1)S(1)} %get-tuple-element.41), channel_id=1, source_target_pairs={{0,24},{1,25},{2,26},{3,27},{4,28},{5,29},{6,30},{7,31},{32,56},{3... | collective-permute-start | bytes 393224 | tf_op jit(solution)/shard_map/ppermute | solution.py:340
  91.1 30.6 %collective-permute-start.11 = (bf16[512,256]{1,0:T(8,128)(2,1)S(1)}, bf16[512,256]{1,0:T(8,128)(2,1)S(1)}, u32[]{:S(2)}, u32[]{:S(2)}) collective-permute-start(bf16[512,256]{1,0:T(8,128)(2,1)S(1)} %get-tuple-element.35), channel_id=1, source_target_pairs={{8,0},{16,8},{24,16},{9,1},{17,9},{25,17},{10,2},{18,10},{26,18},{... | collective-permute-start | bytes 786440 | tf_op jit(solution)/shard_map/ppermute | solution.py:340
  95.2 26.4 %collective-permute-start.12 = (bf16[512,256]{1,0:T(8,128)(2,1)S(1)}, bf16[512,256]{1,0:T(8,128)(2,1)S(1)}, u32[]{:S(2)}, u32[]{:S(2)}) collective-permute-start(bf16[512,256]{1,0:T(8,128)(2,1)S(1)} %get-tuple-element.36), channel_id=1, source_target_pairs={{16,0},{24,8},{17,1},{25,9},{18,2},{26,10},{19,3},{27,11},{20,4},{... | collective-permute-start | bytes 786440 | tf_op jit(solution)/shard_map/ppermute | solution.py:340
  102.0 19.7 %collective-permute-start.13 = (bf16[512,256]{1,0:T(8,128)(2,1)S(1)}, bf16[512,256]{1,0:T(8,128)(2,1)S(1)}, u32[]{:S(2)}, u32[]{:S(2)}) collective-permute-start(bf16[512,256]{1,0:T(8,128)(2,1)S(1)} %get-tuple-element.37), channel_id=1, source_target_pairs={{24,0},{25,1},{26,2},{27,3},{28,4},{29,5},{30,6},{31,7},{56,32},{5... | collective-permute-start | bytes 786440 | tf_op jit(solution)/shard_map/ppermute | solution.py:340
  103.5 16.2 %collective-permute-start.17 = (bf16[256,256]{1,0:T(8,128)(2,1)S(1)}, bf16[256,256]{1,0:T(8,128)(2,1)S(1)}, u32[]{:S(2)}, u32[]{:S(2)}) collective-permute-start(bf16[256,256]{1,0:T(8,128)(2,1)S(1)} %shard_map.90), channel_id=1, source_target_pairs={{32,0},{64,32},{96,64},{128,96},{160,128},{192,160},{224,192},{256... | collective-permute-start | bytes 393224 | tf_op jit(solution)/shard_map/ppermute | solution.py:345
  119.7 2.1 %collective-permute-start.19 = (bf16[256,256]{1,0:T(8,128)(2,1)S(1)}, bf16[256,256]{1,0:T(8,128)(2,1)S(1)}, u32[]{:S(2)}, u32[]{:S(2)}) collective-permute-start(bf16[256,256]{1,0:T(8,128)(2,1)S(1)} %collective-permute-done.17.refs_0_), channel_id=1, source_target_pairs={{0,16},{1,17},{2,18},{3,19},{4,20},{5,21},{6,22},{7,23},{32,48},{3... | collective-permute-start | bytes 393224 | tf_op jit(solution)/shard_map/ppermute | solution.py:340
  120.4 5.7 %collective-permute-start.18 = (bf16[256,256]{1,0:T(8,128)(2,1)S(1)}, bf16[256,256]{1,0:T(8,128)(2,1)S(1)}, u32[]{:S(2)}, u32[]{:S(2)}) collective-permute-start(bf16[256,256]{1,0:T(8,128)(2,1)S(1)} %collective-permute-done.17.refs_0_), channel_id=1, source_target_pairs={{0,8},{8,16},{16,24},{1,9},{9,17},{17,25},{2,10},{10,18},{18,26},{... | collective-permute-start | bytes 393224 | tf_op jit(solution)/shard_map/ppermute | solution.py:340
  127.5 19.8 %all-to-all-start.3 = ((bf16[8,64,256]{2,1,0:T(8,128)(2,1)}), bf16[8,64,256]{2,1,0:T(8,128)(2,1)S(1)}, u32[]{:S(2)}, u32[]{:S(2)}) async-start(bf16[8,64,256]{2,1,0:T(8,128)(2,1)} %bitcast.7), calls=%async_computation.3 | async-start | bytes 524288 | tf_op jit(solution)/shard_map/all_to_all | solution.py:392
  (6 other events, 39.9 us)
